TPU v7x, 128 devices: a whole 4x4x4 slice. The times are simulated.
128 devices in a mesh: ka: 32 (over y, z, core), ga: 4 (over x).
Axes of the slice: x: 4, y: 4, z: 4, core: 2. Of those that a mesh axis runs over, the one named last changes fastest.
Arguments:
- x_dens: bfloat16 [128, 64, 1500], P('ka', None, 'ga'), may hold values from -6 to 6
- y_dens: bfloat16 [128, 64, 1500], P('ka', None, 'ga'), may hold values from -0.15625 to 0.15625
- p_dens: bfloat16 [128, 64, 1500], P('ka', None, 'ga'), may hold values from -1 to 1
- coulomb: float32 [1500], P('ga'), may hold values from 0.1 to 2
- screened: bfloat16 [64, 1500, 1500], P('ka', 'ga'), may hold values from -0.15625 to 0.15625
- pairs: int32 [512, 3], P('ka'), may hold values from 0 to 127, as said below
- q_slot: int32 [64], replicated, may hold values from 0 to 63, as said below
Outputs:
- blocks: float32 [512, 4096], P('ka')
- mirrored: float32 [128, 4096], P('ka')
Inputs may be any that keep to these rules, and one draw needn't show every extreme that they name: `pairs`: column 0 of the rows held by index d of ka lies in d * 4 to (d + 1) * 4 - 1; column 1 is any k-point; column 2 is a momentum transfer below 64. Among one index's 16 rows at most 2 have a second k-point held by one same index, and this is reached; at most 2 have q_slot[q] // 2 equal to one same value, and this is reached. `q_slot`: A permutation of the slots; slot s of screened is held by index s // 2 of ka.
All inputs are finite; a program needn't handle non-finite values.
Results may differ from a plain program's by a relative error of at most 0.0014.
Values may be sent and summed in bfloat16 or wider, within the bound.
No kernel may reach another device: no remote copies, remote signals or barrier semaphores. Data moves between devices by JAX's collectives and lax.ppermute only.
A program may use at most 192 MiB of HBM per device.

v0:
```python
import jax
import jax.numpy as jnp
from jax import lax
from jax.sharding import PartitionSpec as P

CAPQ = 2
CAPK = 2


def from_everyone(x, axis):
    count = lax.axis_size(axis)
    return lax.all_to_all(jnp.broadcast_to(x[None], (count, *x.shape)), axis, 0, 0, tiled=True)


def over_copies(x, axis):
    everything = from_everyone(x, axis)
    return jnp.sum(everything, axis=0)


def split_up(x, dim, count):
    dims = x.shape
    pieces = x.reshape(*dims[:dim], count, dims[dim] // count, *dims[dim + 1 :])
    return jnp.moveaxis(pieces, dim, 0)


def sum_at_owner(x, axis, dim):
    count = lax.axis_size(axis)
    pieces = lax.all_to_all(split_up(x, dim, count), axis, 0, 0, tiled=True)
    return jnp.sum(pieces, axis=0)


def earlier_count(owners):
    places = jnp.arange(owners.shape[0])
    same_owner = owners[:, None] == owners[None, :]
    before = places[:, None] > places[None, :]
    return jnp.sum(jnp.logical_and(same_owner, before).astype(jnp.int32), axis=1)


def per_device(x_dens, y_dens, p_dens, coulomb, screened, pairs, q_slot):
    n_ka = lax.axis_size("ka")
    mine_index = lax.axis_index("ka")
    per_dev, transitions, g_local = x_dens.shape
    q_slots = screened.shape[0]
    pair_rows = pairs.shape[0]
    k_local = pairs[:, 0] - mine_index * per_dev
    partner = pairs[:, 1]
    q_index = pairs[:, 2]
    slot_of = jnp.sum(
        jnp.where(q_index[:, None] == jnp.arange(q_slot.shape[0])[None, :], q_slot[None, :], 0),
        axis=1,
    )
    q_owner = slot_of // q_slots
    q_local = slot_of % q_slots
    q_rank = earlier_count(q_owner)
    q_route = ((q_owner * CAPQ + q_rank)[:, None] == jnp.arange(n_ka * CAPQ)[None, :]).astype(
        jnp.bfloat16
    )
    pick_first = (k_local[:, None] == jnp.arange(per_dev)[None, :]).astype(jnp.bfloat16)
    x_rows = jnp.einsum(
        "jk,kig->jig", pick_first, x_dens, preferred_element_type=jnp.float32
    ).astype(jnp.bfloat16)
    p_rows = jnp.einsum(
        "jk,kig->jig", pick_first, p_dens, preferred_element_type=jnp.float32
    ).astype(jnp.bfloat16)
    send_x = jnp.einsum("js,jig->sig", q_route, x_rows, preferred_element_type=jnp.float32).astype(
        jnp.bfloat16
    )
    send_x = send_x.reshape(n_ka, CAPQ, transitions, g_local)
    send_q = jnp.sum(q_route.astype(jnp.int32) * q_local[:, None], axis=0).reshape(n_ka, CAPQ)
    got_x, got_q = (
        lax.all_to_all(send_x, "ka", split_axis=0, concat_axis=0, tiled=True),
        lax.all_to_all(send_q, "ka", split_axis=0, concat_axis=0, tiled=True),
    )
    chosen = (got_q[:, :, None] == jnp.arange(q_slots)[None, None, :]).astype(jnp.bfloat16)
    stacked = got_x[:, :, None, :, :] * chosen[:, :, :, None, None]
    partial_value = jnp.einsum(
        "ncsig,sgh->hnci", stacked, screened, preferred_element_type=jnp.float32
    )
    half_rows = lax.psum_scatter(
        partial_value.reshape(lax.axis_size("ga") * g_local, n_ka, CAPQ * transitions),
        "ga",
        scatter_dimension=0,
        tiled=True,
    ).astype(jnp.bfloat16)
    returned = lax.all_to_all(half_rows, "ka", split_axis=1, concat_axis=1, tiled=True)
    returned = returned.reshape(g_local, n_ka * CAPQ, transitions)
    u_rows = jnp.einsum(
        "js,gsi->jig", q_route, returned, preferred_element_type=jnp.float32
    ).astype(jnp.bfloat16)
    all_pairs = lax.all_gather(pairs, "ka", axis=0, tiled=True).reshape(n_ka, pair_rows, 3)
    seconds = all_pairs[:, :, 1]
    k_owners = seconds // per_dev
    k_ranks = jax.vmap(earlier_count)(k_owners)
    held_here = k_owners == mine_index
    rank_hot = (k_ranks[:, :, None] == jnp.arange(CAPK)[None, None, :]).astype(jnp.float32)
    local_hot = jnp.logical_and(
        (seconds - mine_index * per_dev)[:, :, None] == jnp.arange(per_dev)[None, None, :],
        held_here[:, :, None],
    ).astype(jnp.float32)
    selector = jnp.einsum("njc,njk->nck", rank_hot, local_hot).astype(jnp.bfloat16)
    send_y = jnp.einsum(
        "nck,kig->ncig", selector, y_dens, preferred_element_type=jnp.float32
    ).astype(jnp.bfloat16)
    send_p = jnp.einsum(
        "nck,kig->ncig", selector, p_dens, preferred_element_type=jnp.float32
    ).astype(jnp.bfloat16)
    got_y, got_p = (
        lax.all_to_all(send_y, "ka", split_axis=0, concat_axis=0, tiled=True),
        lax.all_to_all(send_p, "ka", split_axis=0, concat_axis=0, tiled=True),
    )
    own_rank = earlier_count(partner // per_dev)
    pick_second = (
        (partner // per_dev * CAPK + own_rank)[:, None] == jnp.arange(n_ka * CAPK)[None, :]
    ).astype(jnp.bfloat16)
    y_rows = jnp.einsum(
        "js,sig->jig",
        pick_second,
        got_y.reshape(n_ka * CAPK, transitions, g_local),
        preferred_element_type=jnp.float32,
    ).astype(jnp.bfloat16)
    pp_rows = jnp.einsum(
        "js,sig->jig",
        pick_second,
        got_p.reshape(n_ka * CAPK, transitions, g_local),
        preferred_element_type=jnp.float32,
    ).astype(jnp.bfloat16)
    direct = jnp.einsum("jig,jhg->jih", u_rows, y_rows, preferred_element_type=jnp.float32)
    weighted = p_rows.astype(jnp.float32) * coulomb[None, None, :]
    exchange_term = jnp.einsum(
        "jig,jhg->jih", weighted, pp_rows.astype(jnp.float32), precision=lax.Precision.HIGHEST
    )
    kernel_block = over_copies(2.0 * exchange_term - direct, "ga")
    blocks = kernel_block.reshape(pair_rows, transitions * transitions)
    flipped = jnp.transpose(kernel_block, (0, 2, 1)).reshape(pair_rows, transitions * transitions)
    selector = (partner[:, None] == jnp.arange(per_dev * lax.axis_size("ka"))[None, :]).astype(
        jnp.float32
    )
    mirrored = sum_at_owner(jnp.dot(selector.T, flipped, precision=lax.Precision.HIGHEST), "ka", 0)
    return (blocks, mirrored)


def solution(mesh):
    in_specs = (
        P("ka", None, "ga"),
        P("ka", None, "ga"),
        P("ka", None, "ga"),
        P("ga"),
        P("ka", "ga", None),
        P("ka", None),
        P(),
    )
    out_specs = (P("ka", None), P("ka", None))
    return jax.shard_map(
        per_device, mesh=mesh, in_specs=in_specs, out_specs=out_specs, check_vma=False
    )
```

profile of v0, /device:TPU:0, one launch (start us, length us, event | category | flops | bytes accessed | tf_op | source)
XLA Modules:
  0.0 472.0 jit_solution(160889449546015048)
XLA Ops:
  9.9 8.4 %all-to-all-start.2 = ((s32[32,1,2]{2,1,0:T(1,128)}), s32[32,1,2]{2,1,0:T(1,128)S(1)}, u32[]{:S(2)}, u32[]{:S(2)}) async-start(s32[32,1,2]{2,1,0:T(1,128)} %bitcast.18), calls=%async_computation.2 | async-start | bytes 32768 | tf_op jit(solution)/shard_map/all_to_all | solution.py:72
  18.3 4.0 convolution_convert_fusion
  22.3 7.3 %reshape.186 = bf16[32,2,64,375]{3,1,0,2:T(2,128)(2,1)} reshape(bf16[64,64,375]{2,0,1:T(8,128)(2,1)} %convolution_convert_fusion) | data formatting | bytes 6144000 | tf_op jit(solution)/shard_map/reshape | solution.py:68
  29.6 6.9 %copy.162 = bf16[32,2,64,375]{3,1,2,0:T(2,128)(2,1)} copy(bf16[32,2,64,375]{3,1,0,2:T(2,128)(2,1)} %reshape.186) | data formatting | bytes 6144000 | tf_op jit(solution)/shard_map/reshape | solution.py:68
  36.5 7.5 %all-to-all-start.1 = ((bf16[32,2,64,375]{3,1,2,0:T(2,128)(2,1)}), bf16[32,2,64,375]{3,1,2,0:T(2,128)(2,1)}, u32[]{:S(2)}, u32[]{:S(2)}) async-start(bf16[32,2,64,375]{3,1,2,0:T(2,128)(2,1)} %copy.162), calls=%async_computation.1 | async-start | bytes 6291456 | tf_op jit(solution)/shard_map/all_to_all | solution.py:71
  44.1 39.8 %all-to-all-done.1 = bf16[32,2,64,375]{3,1,2,0:T(2,128)(2,1)} async-done(((bf16[32,2,64,375]{3,1,2,0:T(2,128)(2,1)}), bf16[32,2,64,375]{3,1,2,0:T(2,128)(2,1)}, u32[]{:S(2)}, u32[]{:S(2)}) %all-to-all-start.1) | async-done | bytes 3072032 | tf_op jit(solution)/shard_map/all_to_all | solution.py:71
  86.5 13.6 %fusion = f32[32,2,64,1500,1]{3,2,4,1,0:T(8,128)} fusion(bf16[32,2,2]{2,1,0:T(2,128)(2,1)S(1)} %compare_convert_fusion, bf16[32,2,64,375]{3,2,1,0:T(8,128)(2,1)S(1)} %copy.163, bf16[2,375,1500,1,1]{2,0,1,4,3:T(2,128)(2,1)S(1)} %bitcast.82), kind=kOutput, calls=%fused_computation | convolution fusion | flops 9219072000 | bytes 29898256 | tf_op jit(solution)/shard_map/ncsig,sgh->hnci/dot_general | solution.py:76
  100.1 24.7 %copy.168 = f32[1500,32,128]{2,1,0:T(8,128)} copy(f32[1500,32,128]{0,2,1:T(8,128)} %bitcast.83) | data formatting | bytes 49152000 | tf_op jit(solution)/shard_map/reshape | solution.py:80
  125.5 23.2 %all-gather = s32[32,16,3]{1,2,0:T(4,128)S(1)} all-gather(s32[1,16,3]{1,2,0:T(4,128)S(1)} %bitcast.87), channel_id=1, replica_groups=mesh['ka'=32,'ga'=4] {'ka'}, dimensions={0}, use_global_device_ids=true | all-gather | bytes 6336 | tf_op jit(solution)/shard_map/all_gather | solution.py:90
  153.3 5.0 %all-to-all-start = ((bf16[32,2,64,375]{3,2,1,0:T(8,128)(2,1)}), bf16[32,2,64,375]{3,2,1,0:T(8,128)(2,1)}, u32[]{:S(2)}, u32[]{:S(2)}) async-start(bf16[32,2,64,375]{3,2,1,0:T(8,128)(2,1)} %copy.157), calls=%async_computation | async-start | bytes 6291456 | tf_op jit(solution)/shard_map/all_to_all | solution.py:109
  162.1 36.2 %all-to-all-done = bf16[32,2,64,375]{3,2,1,0:T(8,128)(2,1)} async-done(((bf16[32,2,64,375]{3,2,1,0:T(8,128)(2,1)}), bf16[32,2,64,375]{3,2,1,0:T(8,128)(2,1)}, u32[]{:S(2)}, u32[]{:S(2)}) %all-to-all-start) | async-done | bytes 3072032 | tf_op jit(solution)/shard_map/all_to_all | solution.py:109
  198.3 4.8 %all-to-all-start.4 = ((bf16[32,2,64,375]{3,2,1,0:T(8,128)(2,1)}), bf16[32,2,64,375]{3,2,1,0:T(8,128)(2,1)}, u32[]{:S(2)}, u32[]{:S(2)}) async-start(bf16[32,2,64,375]{3,2,1,0:T(8,128)(2,1)} %copy.173), calls=%async_computation.5 | async-start | bytes 6291456 | tf_op jit(solution)/shard_map/all_to_all | solution.py:108
  203.1 131.9 %reduce-scatter.2.cloned.1.call-done = f32[375,32,128]{2,1,0:T(8,128)} async-done(((f32[1500,32,128]{2,1,0:T(8,128)}), f32[375,32,128]{2,1,0:T(8,128)}) %reduce-scatter.2.cloned.1.call-update) | async-done | bytes 6144016 | tf_op jit(solution)/shard_map/reduce_scatter | solution.py:79
  341.4 7.7 %all-to-all-start.3 = ((bf16[375,32,128]{2,0,1:T(8,128)(2,1)}), bf16[375,32,128]{2,0,1:T(8,128)(2,1)}, u32[]{:S(2)}, u32[]{:S(2)}) async-start(bf16[375,32,128]{2,0,1:T(8,128)(2,1)} %copy.169), calls=%async_computation.4 | async-start | bytes 6160384 | tf_op jit(solution)/shard_map/all_to_all | solution.py:85
  349.7 4.2 fusion.13
  355.5 4.2 fusion.19
  359.7 28.7 %all-to-all-done.3 = bf16[375,32,128]{2,0,1:T(8,128)(2,1)} async-done(((bf16[375,32,128]{2,0,1:T(8,128)(2,1)}), bf16[375,32,128]{2,0,1:T(8,128)(2,1)}, u32[]{:S(2)}, u32[]{:S(2)}) %all-to-all-start.3) | async-done | bytes 3072032 | tf_op jit(solution)/shard_map/all_to_all | solution.py:85
  388.4 4.6 copy.170
  393.0 3.7 fusion.22
  399.8 3.7 all-to-all-start.5
  403.6 15.5 %all-to-all-done.5 = f32[4,1,65536]{2,1,0:T(1,128)S(1)} async-done(((f32[4,1,65536]{2,1,0:T(1,128)}), f32[4,1,65536]{2,1,0:T(1,128)S(1)}, u32[]{:S(2)}, u32[]{:S(2)}) %all-to-all-start.5) | async-done | bytes 1048608 | tf_op jit(solution)/shard_map/all_to_all | solution.py:12
  419.6 3.7 reduce
  428.7 4.8 %all-to-all-start.6 = ((f32[32,4,4096]{2,1,0:T(4,128)}), f32[32,4,4096]{2,1,0:T(4,128)}, u32[]{:S(2)}, u32[]{:S(2)}) async-start(f32[32,4,4096]{2,1,0:T(4,128)} %copy.178), calls=%async_computation.7 | async-start | bytes 4194304 | tf_op jit(solution)/shard_map/all_to_all | solution.py:28
  434.4 28.0 %all-to-all-done.6 = f32[32,4,4096]{2,1,0:T(4,128)} async-done(((f32[32,4,4096]{2,1,0:T(4,128)}), f32[32,4,4096]{2,1,0:T(4,128)}, u32[]{:S(2)}, u32[]{:S(2)}) %all-to-all-start.6) | async-done | bytes 2097184 | tf_op jit(solution)/shard_map/all_to_all | solution.py:28
  (61 shorter events, 35.5 us)
Async XLA Ops:
  7.2 79.3 %copy-start = (bf16[2,375,1500]{2,0,1:T(2,128)(2,1)S(1)}, bf16[2,375,1500]{2,0,1:T(2,128)(2,1)}, u32[]{:S(2)}) copy-start(bf16[2,375,1500]{2,0,1:T(2,128)(2,1)} %param.11) | copy-start | bytes 6750004
  9.9 26.5 %all-to-all-start.2 = ((s32[32,1,2]{2,1,0:T(1,128)}), s32[32,1,2]{2,1,0:T(1,128)S(1)}, u32[]{:S(2)}, u32[]{:S(2)}) async-start(s32[32,1,2]{2,1,0:T(1,128)} %bitcast.18), calls=%async_computation.2 | async-start | bytes 32768 | tf_op jit(solution)/shard_map/all_to_all | solution.py:72
  36.5 47.4 %all-to-all-start.1 = ((bf16[32,2,64,375]{3,1,2,0:T(2,128)(2,1)}), bf16[32,2,64,375]{3,1,2,0:T(2,128)(2,1)}, u32[]{:S(2)}, u32[]{:S(2)}) async-start(bf16[32,2,64,375]{3,1,2,0:T(2,128)(2,1)} %copy.162), calls=%async_computation.1 | async-start | bytes 6291456 | tf_op jit(solution)/shard_map/all_to_all | solution.py:71
  44.0 291.1 %reduce-scatter.2.cloned.1.call-start = ((), (), s32[]{:S(2)}) async-start(), calls=%async_computation.8 | async-start | bytes 30720000 | tf_op jit(solution)/shard_map/reduce_scatter | solution.py:79
  124.8 0.7 copy-start.4
  124.8 24.6 %copy-start.2 = (bf16[4,64,375]{2,1,0:T(8,128)(2,1)S(1)}, bf16[4,64,375]{2,1,0:T(8,128)(2,1)}, u32[]{:S(2)}) copy-start(bf16[4,64,375]{2,1,0:T(8,128)(2,1)} %param.9) | copy-start | bytes 576004
  153.3 5.0 %copy-start.3 = (bf16[4,64,375]{2,1,0:T(8,128)(2,1)S(1)}, bf16[4,64,375]{2,1,0:T(8,128)(2,1)}, u32[]{:S(2)}) copy-start(bf16[4,64,375]{2,1,0:T(8,128)(2,1)} %param.8) | copy-start | bytes 576004
  153.3 45.0 %all-to-all-start = ((bf16[32,2,64,375]{3,2,1,0:T(8,128)(2,1)}), bf16[32,2,64,375]{3,2,1,0:T(8,128)(2,1)}, u32[]{:S(2)}, u32[]{:S(2)}) async-start(bf16[32,2,64,375]{3,2,1,0:T(8,128)(2,1)} %copy.157), calls=%async_computation | async-start | bytes 6291456 | tf_op jit(solution)/shard_map/all_to_all | solution.py:109
  198.3 143.0 %all-to-all-start.4 = ((bf16[32,2,64,375]{3,2,1,0:T(8,128)(2,1)}), bf16[32,2,64,375]{3,2,1,0:T(8,128)(2,1)}, u32[]{:S(2)}, u32[]{:S(2)}) async-start(bf16[32,2,64,375]{3,2,1,0:T(8,128)(2,1)} %copy.173), calls=%async_computation.5 | async-start | bytes 6291456 | tf_op jit(solution)/shard_map/all_to_all | solution.py:108
  341.3 7.9 %copy-start.5 = (f32[375]{0:T(512)S(1)}, f32[375]{0:T(512)}, u32[]{:S(2)}) copy-start(f32[375]{0:T(512)} %param.10) | copy-start | bytes 4504
  341.4 47.0 %all-to-all-start.3 = ((bf16[375,32,128]{2,0,1:T(8,128)(2,1)}), bf16[375,32,128]{2,0,1:T(8,128)(2,1)}, u32[]{:S(2)}, u32[]{:S(2)}) async-start(bf16[375,32,128]{2,0,1:T(8,128)(2,1)} %copy.169), calls=%async_computation.4 | async-start | bytes 6160384 | tf_op jit(solution)/shard_map/all_to_all | solution.py:85
  399.8 19.2 %all-to-all-start.5 = ((f32[4,1,65536]{2,1,0:T(1,128)}), f32[4,1,65536]{2,1,0:T(1,128)S(1)}, u32[]{:S(2)}, u32[]{:S(2)}) async-start(f32[4,1,65536]{2,1,0:T(1,128)} %reshape.205), calls=%async_computation.6 | async-start | bytes 2097152 | tf_op jit(solution)/shard_map/all_to_all | solution.py:12
  426.0 38.8 %copy-start.1 = (bf16[2,375,1500]{2,0,1:T(2,128)(2,1)S(1)}, bf16[2,375,1500]{2,0,1:T(2,128)(2,1)}, u32[]{:S(2)}) copy-start(bf16[2,375,1500]{2,0,1:T(2,128)(2,1)} %param.11) | copy-start | bytes 6750004
  428.7 33.6 %all-to-all-start.6 = ((f32[32,4,4096]{2,1,0:T(4,128)}), f32[32,4,4096]{2,1,0:T(4,128)}, u32[]{:S(2)}, u32[]{:S(2)}) async-start(f32[32,4,4096]{2,1,0:T(4,128)} %copy.178), calls=%async_computation.7 | async-start | bytes 4194304 | tf_op jit(solution)/shard_map/all_to_all | solution.py:28
Sparse Core Ops, SparseCore 0:
  124.9 210.0 reduce-scatter.1
where the time goes:
time: 481 us; the launch traced here: 472 us
  waiting for transfers between devices  280 us (58%)
  local copies, waits for them, and re-layouts  64.4 us (13%)
  starting transfers between devices  41.9 us (9%)
  matrix products  35.5 us (7%)
  blocking collectives  23.2 us (5%)
  between operations  14.5 us (3%)
  other arithmetic  12.5 us (3%)
    reduce_scatter x1, waiting for transfers between devices, per_device(): lax.psum_scatter(partial_value.reshape(lax.axis_size('ga') * g_local, n_k...  132 us
    all_to_all x1, waiting for transfers between devices, per_device(): lax.all_to_all(send_x, 'ka', split_axis=0, concat_axis=0, tiled=True)  39.8 us
    all_to_all x1, waiting for transfers between devices, per_device(): lax.all_to_all(send_p, 'ka', split_axis=0, concat_axis=0, tiled=True)  36.2 us
    all_to_all x1, waiting for transfers between devices, per_device(): lax.all_to_all(half_rows, 'ka', split_axis=1, concat_axis=1, tiled=True)  28.7 us
    all_to_all x1, waiting for transfers between devices, sum_at_owner(): pieces = lax.all_to_all(split_up(x, dim, count), axis, 0, 0, tiled=True)  28 us
    reshape x1, local copies, waits for them, and re-layouts, per_device(): partial_value.reshape(lax.axis_size('ga') * g_local, n_ka, CAPQ * transit...  24.7 us
    all_gather x1, blocking collectives, per_device(): lax.all_gather(pairs, 'ka', axis=0, tiled=True).reshape(n_ka, pair_rows, 3)  23.2 us
    all_to_all x1, waiting for transfers between devices, from_everyone(): lax.all_to_all(jnp.broadcast_to(x[None], (count, *x.shape)), axis, 0, 0,...  15.5 us
  transfers between devices with their start and end apart: 8, of which 6 were waited for; matrix products, arithmetic and copies ran while one was open for 9% of the time, Pallas kernels for 0%

commit v1 on v0

v1 whole, which is shorter than its diff:
```python
import jax
import jax.numpy as jnp
from jax import lax
from jax.experimental import pallas as pl
from jax.experimental.pallas import tpu as pltpu
from jax.sharding import PartitionSpec as P

CAP = 2
QW = 384
CH = 8
F32 = jnp.float32
BF16 = jnp.bfloat16
NT_DIMS = (((1,), (1,)), ((), ()))


def rank_in_group(owners):
    n = owners.shape[-1]
    same = owners[..., :, None] == owners[..., None, :]
    before = jnp.arange(n)[:, None] > jnp.arange(n)[None, :]
    return jnp.sum(jnp.logical_and(same, before).astype(jnp.int32), axis=-1)


def widen(v):
    return jnp.pad(v, ((0, 0),) * (v.ndim - 1) + ((0, QW - v.shape[-1]),))


def flat_tiles(tmp, rows):
    even = tmp[pl.ds(0, rows // 2, stride=2), :]
    odd = tmp[pl.ds(1, rows // 2, stride=2), :]
    return jnp.concatenate([even, odd], axis=1)


def block_kernel(tab, own, big, wk, pk, cw, out, xs, ys, p2, whl, tmp, where_, sx, sy, sp):
    nslot = tab.shape[1]
    npair = own.shape[1]
    nk = pk.shape[0]
    nt = pk.shape[1]

    def p_copy(j):
        return pltpu.make_async_copy(big.at[own[1, j], :, pl.ds(4 * QW, QW)], p2.at[j], sp.at[j])

    def x_copy(k, pos):
        return pltpu.make_async_copy(big.at[k, :, pl.ds(0, 2 * QW)], xs.at[pos], sx.at[pos])

    def y_copy(k, pos):
        return pltpu.make_async_copy(big.at[k, :, pl.ds(2 * QW, 2 * QW)], ys.at[pos], sy.at[pos])

    for j in range(npair):
        p_copy(j).start()

    def clear(i, carry):
        where_[i] = nslot
        return carry

    lax.fori_loop(0, where_.shape[0], clear, 0)

    def count(t, n):
        return n + jnp.where((tab[0, t] == 1) & (tab[3, t] == 0), 1, 0)

    n_first = lax.fori_loop(0, nslot, count, 0)
    chunks_first = (n_first + CH - 1) // CH

    def place(t, carry):
        c0, c1 = carry
        first = tab[3, t] == 0
        used = tab[0, t] == 1
        pos = jnp.where(first, c0, chunks_first * CH + c1)

        @pl.when(used)
        def _():
            where_[pos] = t
            x_copy(tab[1, t], pos).start()
            y_copy(tab[2, t], pos).start()

        add = jnp.where(used, 1, 0)
        return c0 + jnp.where(first, add, 0), c1 + jnp.where(first, 0, add)

    _, n_second = lax.fori_loop(0, nslot, place, (0, 0))
    chunks = chunks_first + (n_second + CH - 1) // CH

    out[...] = jnp.zeros_like(out)
    for k in range(nk):
        w = pk[k].astype(F32) * cw[...]
        hi = w.astype(BF16)
        lo = (w - hi.astype(F32)).astype(BF16)
        whl[k, :nt, :] = hi
        whl[k, nt:, :] = lo
    for first in range(0, npair, CH):
        for i in range(CH):
            j = first + i
            p_copy(j).wait()
            e = lax.dot_general(whl[own[0, j]], p2[j], NT_DIMS, preferred_element_type=F32)
            tmp[i * nt : (i + 1) * nt, :] = 2.0 * (e[:nt] + e[nt:])
        z = flat_tiles(tmp, CH * nt)
        for i in range(CH):
            for q in range(4):
                row = i * (nt // 2) + q * 8
                out[q, nslot + first + i] = z[row : row + 8]

    def chunk(c, carry):
        for i in range(CH):
            pos = c * CH + i
            t = where_[pos]

            @pl.when(t < nslot)
            def _():
                x_copy(0, pos).wait()
                y_copy(0, pos).wait()

        slot = jnp.where(c < chunks_first, 0, 1)
        x = xs[pl.ds(c * CH, CH)].reshape(CH * nt, 2 * QW)
        u = jnp.dot(x, wk[slot], preferred_element_type=F32)
        hi = u.astype(BF16)
        lo = (u - hi.astype(F32)).astype(BF16)
        for i in range(CH):
            r = slice(i * nt, (i + 1) * nt)
            both = jnp.concatenate([hi[r], lo[r]], axis=0)
            d = lax.dot_general(both, ys[c * CH + i], NT_DIMS, preferred_element_type=F32)
            tmp[r, :] = d[:nt] + d[nt:]
        z = flat_tiles(tmp, CH * nt)
        for i in range(CH):
            t = where_[c * CH + i]

            @pl.when(t < nslot)
            def _():
                for q in range(4):
                    row = i * (nt // 2) + q * 8
                    out[q, t] = z[row : row + 8]

        return carry

    lax.fori_loop(0, chunks, chunk, 0)


def combine_kernel(own, e, d, blocks, send):
    send[...] = jnp.zeros_like(send)
    for j in range(e.shape[0]):
        v = e[j] - d[own[2, j]]
        blocks[j] = v
        send[own[3, j]] = v


def mirror_kernel(tab, got, b, out):
    n = b.shape[0]
    out[:n] = b[...]
    out[n:] = jnp.zeros((out.shape[0] - n, *out.shape[1:]), F32)
    for t in range(got.shape[0]):

        @pl.when(tab[4, t] == 1)
        def _():
            k = n + tab[5, t]
            out[k] = out[k] + got[t]


def in_vmem(count):
    return [pl.BlockSpec(memory_space=pltpu.VMEM)] * count


SMEM = pl.BlockSpec(memory_space=pltpu.SMEM)


def per_device(x, y, p, coulomb, w, pairs, q_slot):
    n_ka = lax.axis_size("ka")
    me = lax.axis_index("ka")
    a = lax.axis_index("ga")
    nk, nt, gl = x.shape
    qs = w.shape[0]
    npair = pairs.shape[0]
    nslot = n_ka * CAP

    with jax.named_scope("pack"):
        x_far = lax.ppermute(x, "ga", [(0, 1), (1, 0), (2, 3), (3, 2)])
        y_far = lax.ppermute(y, "ga", [(0, 3), (3, 0), (1, 2), (2, 1)])
        payload = jnp.concatenate([widen(v) for v in (x, x_far, y, y_far, p)], axis=2)
    with jax.named_scope("spread"):
        big = lax.all_gather(payload, "ka", axis=0, tiled=True)

    with jax.named_scope("weights"):
        cols = jnp.stack([w[:, :, i * gl : (i + 1) * gl] for i in range(4)])
        cols = jnp.pad(cols, ((0, 0), (0, 0), (0, QW - gl), (0, QW - gl)))

        def columns_of(b):
            return jnp.concatenate(
                [
                    lax.dynamic_index_in_dim(cols, b, 0, keepdims=False),
                    lax.dynamic_index_in_dim(cols, 3 - b, 0, keepdims=False),
                ],
                axis=2,
            )

        near = columns_of(a)
        far = lax.ppermute(
            columns_of(jnp.bitwise_xor(a, 1)), "ga", [(0, 1), (1, 0), (2, 3), (3, 2)]
        )
        wk = jnp.concatenate([near, far], axis=1)

    with jax.named_scope("tables"):
        every = lax.all_gather(pairs, "ka", axis=0, tiled=True).reshape(n_ka, npair, 3)

        def routes(rows):
            slot = jnp.sum(
                jnp.where(
                    rows[..., 2, None] == jnp.arange(q_slot.shape[0]), q_slot, 0
                ),
                axis=-1,
            )
            q_owner = slot // qs
            k_owner = rows[..., 1] // nk
            return slot % qs, q_owner, rank_in_group(q_owner), k_owner, rank_in_group(k_owner)

        local, q_owner, q_rank, k_owner, k_rank = routes(every)
        ranks = jnp.arange(CAP)
        hot_q = (q_owner == me)[..., None] & (q_rank[..., None] == ranks)
        hot_k = (k_owner == me)[..., None] & (k_rank[..., None] == ranks)

        def pick(hot, v):
            return jnp.sum(jnp.where(hot, v[..., None], 0), axis=1).reshape(nslot)

        ones = jnp.ones_like(local)
        tab = jnp.stack(
            [
                pick(hot_q, ones),
                pick(hot_q, every[..., 0]),
                pick(hot_q, every[..., 1]),
                pick(hot_q, local),
                pick(hot_k, ones),
                pick(hot_k, every[..., 1] - me * nk),
            ]
        )
        _, o1, r1, o2, r2 = routes(pairs)
        own = jnp.stack([pairs[:, 0] - me * nk, pairs[:, 1], o1 * CAP + r1, o2 * CAP + r2])

    cw = jnp.pad(coulomb[None], ((0, 0), (0, QW - gl)))
    npos = nslot + qs * CH
    part = pl.pallas_call(
        block_kernel,
        out_shape=jax.ShapeDtypeStruct((4, nslot + npair, 8, 128), F32),
        in_specs=[SMEM, SMEM, pl.BlockSpec(memory_space=pl.ANY), *in_vmem(3)],
        out_specs=pl.BlockSpec(memory_space=pltpu.VMEM),
        scratch_shapes=[
            pltpu.VMEM((npos, nt, 2 * QW), BF16),
            pltpu.VMEM((npos, nt, 2 * QW), BF16),
            pltpu.VMEM((npair, nt, QW), BF16),
            pltpu.VMEM((nk, 2 * nt, QW), BF16),
            pltpu.VMEM((CH * nt, nt), F32),
            pltpu.SMEM((npos,), jnp.int32),
            pltpu.SemaphoreType.DMA((npos,)),
            pltpu.SemaphoreType.DMA((npos,)),
            pltpu.SemaphoreType.DMA((npair,)),
        ],
        compiler_params=pltpu.CompilerParams(vmem_limit_bytes=48 * 1024 * 1024),
        name="pair_blocks",
    )(tab, own, big, wk, widen(p), cw)

    with jax.named_scope("sum_quarters"):
        quarter = jnp.sum(lax.all_to_all(part, "ga", 0, 0, tiled=True), axis=0)
    with jax.named_scope("to_pairs"):
        direct = lax.all_to_all(quarter[:nslot], "ka", 0, 0, tiled=True)
    blocks, send = pl.pallas_call(
        combine_kernel,
        out_shape=(
            jax.ShapeDtypeStruct((npair, 8, 128), F32),
            jax.ShapeDtypeStruct((nslot, 8, 128), F32),
        ),
        in_specs=[SMEM, *in_vmem(2)],
        out_specs=tuple(in_vmem(2)),
        name="combine",
    )(own, quarter[nslot:], direct)
    with jax.named_scope("to_seconds"):
        got = lax.all_to_all(send, "ka", 0, 0, tiled=True)
    both = pl.pallas_call(
        mirror_kernel,
        out_shape=jax.ShapeDtypeStruct((npair + nk, 8, 128), F32),
        in_specs=[SMEM, *in_vmem(2)],
        out_specs=pl.BlockSpec(memory_space=pltpu.VMEM),
        name="mirror",
    )(tab, got, blocks)
    with jax.named_scope("copies"):
        whole = lax.all_gather(both, "ga", axis=0)
        whole = jnp.transpose(whole, (1, 0, 2, 3)).reshape(npair + nk, nt, nt)
        mirrored = jnp.transpose(whole[npair:], (0, 2, 1)).reshape(nk, nt * nt)
    return whole[:npair].reshape(npair, nt * nt), mirrored


def solution(mesh):
    in_specs = (
        P("ka", None, "ga"),
        P("ka", None, "ga"),
        P("ka", None, "ga"),
        P("ga"),
        P("ka", "ga", None),
        P("ka", None),
        P(),
    )
    out_specs = (P("ka", None), P("ka", None))
    return jax.shard_map(
        per_device, mesh=mesh, in_specs=in_specs, out_specs=out_specs, check_vma=False
    )
```

time: 481 us -> 222 us (0.46); the launches traced: 472 us -> 222 us
  waiting for transfers between devices: 280 us -> 79 us
  blocking collectives: 23.2 us -> 74.2 us
  local copies, waits for them, and re-layouts: 64.4 us -> 15.1 us
  matrix products: 35.5 us -> 0 us
  starting transfers between devices: 41.9 us -> 14.2 us
  Pallas kernels: 0 us -> 15 us
    all_to_all x7 -> x1, waiting for transfers between devices: 148 us -> 8.3 us  [per_device(): direct = lax.all_to_all(quarter[:nslot], 'ka', 0, 0, tiled=True)]
    reduce_scatter x1 -> x0, waiting for transfers between devices: 132 us -> none  [per_device(): lax.psum_scatter(partial_value.reshape(lax.axis_size('ga') * g_local, n_k...]
    all_gather x0 -> x1, waiting for transfers between devices: none -> 67 us  [per_device(): big = lax.all_gather(payload, 'ka', axis=0, tiled=True)]
    reshape x5 -> x7, local copies, waits for them, and re-layouts: 39.9 us -> 1.37 us  [the longest x1 0.74 us: per_device(): mirrored = jnp.transpose(whole[npair:], (0, 2, 1)).reshape(nk, nt * nt)]
    all_to_all x0 -> x2, blocking collectives: none -> 35.9 us  [the longest x1 22.4 us: per_device(): quarter = jnp.sum(lax.all_to_all(part, 'ga', 0, 0, tiled=True), axis=0)]
    dot_general x12 -> x0, matrix products: 35.5 us -> none  [the longest x1 13.6 us: per_device(): jnp.einsum('ncsig,sgh->hnci', stacked, screened, preferred_element_type=j...]
    all_to_all x7 -> x1, starting transfers between devices: 41.9 us -> 10.2 us  [per_device(): direct = lax.all_to_all(quarter[:nslot], 'ka', 0, 0, tiled=True)]
    all_gather x1 -> x2, blocking collectives: 23.2 us -> 38.2 us  [the longest x1 25.6 us: per_device(): lax.all_gather(pairs, 'ka', axis=0, tiled=True).reshape(n_ka, npair, 3)]
  transfers between devices with their start and end apart: 8 -> 5, of which waited for: 6 -> 4; matrix products, arithmetic and copies ran while one was open for 9% -> 9% of each run, Pallas kernels for 0% -> 0%
where the time goes in v1:
time: 222 us
  waiting for transfers between devices  79 us (36%)
  blocking collectives  74.2 us (33%)
  local copies, waits for them, and re-layouts  15.1 us (7%)
  Pallas kernels  15 us (7%)
  between operations  14.4 us (6%)
  starting transfers between devices  14.2 us (6%)
  other arithmetic  10.1 us (5%)
    all_gather x1, waiting for transfers between devices, per_device(): big = lax.all_gather(payload, 'ka', axis=0, tiled=True)  67 us
    all_gather x1, blocking collectives, per_device(): lax.all_gather(pairs, 'ka', axis=0, tiled=True).reshape(n_ka, npair, 3)  25.6 us
    all_to_all x1, blocking collectives, per_device(): quarter = jnp.sum(lax.all_to_all(part, 'ga', 0, 0, tiled=True), axis=0)  22.4 us
    all_to_all x1, blocking collectives, per_device(): got = lax.all_to_all(send, 'ka', 0, 0, tiled=True)  13.5 us
    all_gather x1, blocking collectives, per_device(): whole = lax.all_gather(both, 'ga', axis=0)  12.6 us
    pallas_call x1, Pallas kernels, per_device(): pl.pallas_call(block_kernel, out_shape=jax.ShapeDtypeStruct((4, nslot + n...  11.1 us
    all_to_all x1, starting transfers between devices, per_device(): direct = lax.all_to_all(quarter[:nslot], 'ka', 0, 0, tiled=True)  10.2 us
    all_to_all x1, waiting for transfers between devices, per_device(): direct = lax.all_to_all(quarter[:nslot], 'ka', 0, 0, tiled=True)  8.3 us
  transfers between devices with their start and end apart: 5, of which 4 were waited for; matrix products, arithmetic and copies ran while one was open for 9% of the time, Pallas kernels for 0%

profile of v1, /device:TPU:0, one launch (start us, length us, event | category | flops | bytes accessed | tf_op | source)
XLA Modules:
  0.0 221.8 jit_solution(5771784943268539134)
XLA Ops:
  7.2 1.7 collective-permute-start
  8.9 2.1 collective-permute-start.1
  11.0 0.9 pad_dynamic-update-slice_fusion.3
  11.9 2.1 collective-permute-done
  14.0 1.0 pad_dynamic-update-slice_fusion.1
  15.0 1.7 collective-permute-done.1
  16.7 1.0 fusion.21
  17.7 1.0 copy-done.3
  18.7 3.6 %slice_bitcast_fusion.3 = (bf16[1,2,375,375]{3,1,2,0:T(2,128)(2,1)S(1)}, bf16[1,2,375,375]{3,1,2,0:T(2,128)(2,1)S(1)}, bf16[1,2,375,375]{3,1,2,0:T(2,128)(2,1)S(1)}, bf16[1,2,375,375]{3,1,2,0:T(2,128)(2,1)S(1)}) fusion(bf16[2,375,1500]{2,0,1:T(2,128)(2,1)S(1)} %copy-done.2), kind=kLoop, calls=%fused_computation.22 | loop fusion | bytes 4500000 | tf_op jit(solution)/shard_map/weights/stack | solution.py:179
  22.3 6.5 %fusion.10 = bf16[4,2,384,384]{3,1,2,0:T(2,128)(2,1)S(1)} fusion(bf16[1,2,375,375]{3,1,2,0:T(2,128)(2,1)S(1)} %get-tuple-element.22, bf16[1,2,375,375]{3,1,2,0:T(2,128)(2,1)S(1)} %get-tuple-element.23, bf16[1,2,375,375]{3,1,2,0:T(2,128)(2,1)S(1)} %get-tuple-element.21, bf16[1,2,375,375]{3,1,2,0:T(2,128)(2,1)S(1)} %get-tuple-element.20), kind=kLoop, calls=%fused_computation.12 | loop fusion | flops 22413312 | bytes 4609296 | tf_op jit(solution)/shard_map/weights/stack | solution.py:179
  28.8 1.6 constant_dynamic-slice_fusion.3
  31.2 25.6 %all-gather.1 = s32[32,16,3]{1,2,0:T(4,128)S(1)} all-gather(s32[1,16,3]{1,2,0:T(4,128)S(1)} %bitcast.80), channel_id=1, replica_groups=mesh['ka'=32,'ga'=4] {'ka'}, dimensions={0}, use_global_device_ids=true | all-gather | bytes 6336 | tf_op jit(solution)/shard_map/tables/all_gather | solution.py:198
  60.1 1.8 pad_maximum_fusion.wk
  61.9 67.0 %all-gather.4.cloned.1.call-done.big = bf16[128,64,1920]{2,1,0:T(8,128)(2,1)} async-done(((bf16[4,64,1920]{2,1,0:T(8,128)(2,1)}), bf16[128,64,1920]{2,1,0:T(8,128)(2,1)}) %all-gather.4.cloned.1.call-update) | async-done | bytes 31457296 | tf_op jit(solution)/shard_map/spread/all_gather | solution.py:176
  128.9 11.1 %pair_blocks.1 = f32[4,80,8,128]{3,2,1,0:T(8,128)S(1)} custom-call(s32[6,64]{1,0:T(8,128)S(1)} %stack.24.tab, s32[4,16]{1,0:T(4,128)S(1)} %pad_add_fusion.own, bf16[128,64,1920]{2,1,0:T(8,128)(2,1)} %all-gather.4.cloned.1.call-done.big, bf16[2,768,768]{2,1,0:T(8,128)(2,1)S(1)} %pad_maximum_fusion.wk, bf16[4,64,384]{2,1,0:T(8,128)(2,1)S(1)} %get-tuple-element.24.pk, ...), custom_call_target="tpu_custom_call" | custom-call | tf_op jit(solution)/shard_map/pair_blocks/pallas_call | solution.py:235
  140.0 22.4 %all_to_all.15 = f32[4,80,8,128]{3,2,1,0:T(8,128)S(1)} all-to-all(f32[4,80,8,128]{3,2,1,0:T(8,128)S(1)} %pair_blocks.1), channel_id=1, replica_groups=mesh['ka'=32,'ga'=4] {'ga'}, dimensions={0} | all-to-all | bytes 2621440 | tf_op jit(solution)/shard_map/sum_quarters/all_to_all | solution.py:256
  163.3 10.2 %all-to-all-start.1 = ((f32[64,8,128]{2,1,0:T(8,128)}), f32[64,8,128]{2,1,0:T(8,128)S(1)}, u32[]{:S(2)}, u32[]{:S(2)}) async-start(f32[64,8,128]{2,1,0:T(8,128)} %slice.68), calls=%async_computation.1 | async-start | bytes 524288 | tf_op jit(solution)/shard_map/to_pairs/all_to_all | solution.py:258
  174.1 8.3 %all-to-all-done.1.d = f32[64,8,128]{2,1,0:T(8,128)S(1)} async-done(((f32[64,8,128]{2,1,0:T(8,128)}), f32[64,8,128]{2,1,0:T(8,128)S(1)}, u32[]{:S(2)}, u32[]{:S(2)}) %all-to-all-start.1) | async-done | bytes 262176 | tf_op jit(solution)/shard_map/to_pairs/all_to_all | solution.py:258
  183.1 1.8 combine.1
  184.9 13.5 %all_to_all.16.got = f32[64,8,128]{2,1,0:T(8,128)} all-to-all(f32[64,8,128]{2,1,0:T(8,128)} %get-tuple-element.4), channel_id=1, replica_groups=mesh['ka'=32,'ga'=4] {'ka'}, dimensions={0} | all-to-all | bytes 524288 | tf_op jit(solution)/shard_map/to_seconds/all_to_all | solution.py:270
  198.4 2.2 mirror.1
  200.5 12.6 %all-gather = f32[80,8,128]{2,1,0:T(8,128)S(1)} all-gather(f32[20,8,128]{2,1,0:T(8,128)} %mirror.1), channel_id=2, replica_groups=mesh['ka'=32,'ga'=4] {'ga'}, dimensions={0}, use_global_device_ids=true | all-gather | bytes 409600 | tf_op jit(solution)/shard_map/copies/all_gather | solution.py:279
  213.2 0.9 copy.95
  214.3 0.7 reshape.314
  (69 shorter events, 6.4 us)
Async XLA Ops:
  7.2 11.5 %copy-start.2 = (bf16[2,375,1500]{2,0,1:T(2,128)(2,1)S(1)}, bf16[2,375,1500]{2,0,1:T(2,128)(2,1)}, u32[]{:S(2)}) copy-start(bf16[2,375,1500]{2,0,1:T(2,128)(2,1)} %param.11) | copy-start | bytes 6750004
  7.2 121.8 %all-gather.4.cloned.1.call-start = ((), (), s32[]{:S(2)}) async-start(), calls=%async_computation.3 | async-start | bytes 32440320 | tf_op jit(solution)/shard_map/spread/all_gather | solution.py:176
  7.2 6.8 %collective-permute-start = (bf16[4,64,375]{2,1,0:T(8,128)(2,1)}, bf16[4,64,375]{2,1,0:T(8,128)(2,1)S(1)}, u32[]{:S(2)}, u32[]{:S(2)}) collective-permute-start(bf16[4,64,375]{2,1,0:T(8,128)(2,1)} %param.7), channel_id=1, source_target_pairs={{0,1},{1,0},{2,3},{3,2},{4,5},{5,4},{6,7},{7,6},{8,9},{9,8},{10,11... | collective-permute-start | bytes 576008 | tf_op jit(solution)/shard_map/pack/ppermute | solution.py:172
  8.9 7.8 %collective-permute-start.1 = (bf16[4,64,375]{2,1,0:T(8,128)(2,1)}, bf16[4,64,375]{2,1,0:T(8,128)(2,1)S(1)}, u32[]{:S(2)}, u32[]{:S(2)}) collective-permute-start(bf16[4,64,375]{2,1,0:T(8,128)(2,1)} %param.8), channel_id=1, source_target_pairs={{0,3},{3,0},{1,2},{2,1},{4,7},{7,4},{5,6},{6,5},{8,11},{11,8},{9,1... | collective-permute-start | bytes 576008 | tf_op jit(solution)/shard_map/pack/ppermute | solution.py:173
  17.7 1.0 copy-start.3
  30.5 0.7 copy-start.5
  30.5 26.4 %copy-start.7 = (s32[64]{0:T(128)S(1)}, s32[64]{0:T(128)}, u32[]{:S(2)}) copy-start(s32[64]{0:T(128)} %param.13) | copy-start | bytes 772
  30.5 28.8 %copy-start.6 = (f32[375]{0:T(512)S(1)}, f32[375]{0:T(512)}, u32[]{:S(2)}) copy-start(f32[375]{0:T(512)} %param.10) | copy-start | bytes 4504
  30.8 29.4 %collective-permute-start.2 = (bf16[2,384,768]{2,1,0:T(8,128)(2,1)S(1)}, bf16[2,384,768]{2,1,0:T(8,128)(2,1)}, u32[]{:S(2)}, u32[]{:S(2)}) collective-permute-start(bf16[2,384,768]{2,1,0:T(8,128)(2,1)S(1)} %pad_maximum_fusion.1), channel_id=1, source_target_pairs={{0,1},{1,0},{2,3},{3,2},{4,5},{5,4},{6,7},{7,6},{8,9},{9,8},{10,11... | collective-permute-start | bytes 3538952 | tf_op jit(solution)/shard_map/weights/ppermute | solution.py:192
  59.3 69.6 %copy-start = (s32[6,64]{1,0:T(8,128)}, s32[6,64]{1,0:T(8,128)S(1)}, u32[]{:S(2)}) copy-start(s32[6,64]{1,0:T(8,128)S(1)} %stack.24.tab) | copy-start | bytes 4612
  60.0 69.0 %copy-start.1 = (s32[4,16]{1,0:T(4,128)}, s32[4,16]{1,0:T(4,128)S(1)}, u32[]{:S(2)}) copy-start(s32[4,16]{1,0:T(4,128)S(1)} %pad_add_fusion.own) | copy-start | bytes 772
  163.3 19.2 %all-to-all-start.1 = ((f32[64,8,128]{2,1,0:T(8,128)}), f32[64,8,128]{2,1,0:T(8,128)S(1)}, u32[]{:S(2)}, u32[]{:S(2)}) async-start(f32[64,8,128]{2,1,0:T(8,128)} %slice.68), calls=%async_computation.1 | async-start | bytes 524288 | tf_op jit(solution)/shard_map/to_pairs/all_to_all | solution.py:258
  182.4 0.7 copy-start.4
Sparse Core Ops, SparseCore 0:
  18.8 110.0 all-gather.3

commit v2 on v1

v2 whole, which is shorter than its diff:
```python
import jax
import jax.numpy as jnp
from jax import lax
from jax.experimental import pallas as pl
from jax.experimental.pallas import tpu as pltpu
from jax.sharding import PartitionSpec as P

CAP = 2
QW = 384
CH = 8
F32 = jnp.float32
BF16 = jnp.bfloat16
NT_DIMS = (((1,), (1,)), ((), ()))


def rank_in_group(owners):
    n = owners.shape[-1]
    same = owners[..., :, None] == owners[..., None, :]
    before = jnp.arange(n)[:, None] > jnp.arange(n)[None, :]
    return jnp.sum(jnp.logical_and(same, before).astype(jnp.int32), axis=-1)


def widen(v):
    return jnp.pad(v, ((0, 0),) * (v.ndim - 1) + ((0, QW - v.shape[-1]),))


def flat_tiles(tmp, rows):
    even = tmp[pl.ds(0, rows // 2, stride=2), :]
    odd = tmp[pl.ds(1, rows // 2, stride=2), :]
    return jnp.concatenate([even, odd], axis=1)


def direct_kernel(tab, big, wk, out, xs, ys, tmp, where_, sx, sy):
    nslot = tab.shape[1]
    nt = xs.shape[1]
    wide = xs.shape[2]

    def x_copy(k, pos):
        return pltpu.make_async_copy(big.at[k, :, pl.ds(0, wide)], xs.at[pos], sx.at[pos])

    def y_copy(k, pos):
        return pltpu.make_async_copy(big.at[k, :, pl.ds(wide, wide)], ys.at[pos], sy.at[pos])

    def clear(i, carry):
        where_[i] = nslot
        return carry

    lax.fori_loop(0, where_.shape[0], clear, 0)

    def count(t, n):
        return n + jnp.where((tab[0, t] == 1) & (tab[3, t] == 0), 1, 0)

    n_first = lax.fori_loop(0, nslot, count, 0)
    chunks_first = (n_first + CH - 1) // CH

    def place(t, carry):
        c0, c1 = carry
        first = tab[3, t] == 0
        used = tab[0, t] == 1
        pos = jnp.where(first, c0, chunks_first * CH + c1)

        @pl.when(used)
        def _():
            where_[pos] = t
            x_copy(tab[1, t], pos).start()
            y_copy(tab[2, t], pos).start()

        add = jnp.where(used, 1, 0)
        return c0 + jnp.where(first, add, 0), c1 + jnp.where(first, 0, add)

    _, n_second = lax.fori_loop(0, nslot, place, (0, 0))
    chunks = chunks_first + (n_second + CH - 1) // CH
    out[...] = jnp.zeros_like(out)

    def chunk(c, carry):
        for i in range(CH):
            pos = c * CH + i
            t = where_[pos]

            @pl.when(t < nslot)
            def _():
                x_copy(0, pos).wait()
                y_copy(0, pos).wait()

        slot = jnp.where(c < chunks_first, 0, 1)
        x = xs[pl.ds(c * CH, CH)].reshape(CH * nt, wide)
        u = jnp.dot(x, wk[slot], preferred_element_type=F32)
        hi = u.astype(BF16)
        lo = (u - hi.astype(F32)).astype(BF16)
        for i in range(CH):
            r = slice(i * nt, (i + 1) * nt)
            both = jnp.concatenate([hi[r], lo[r]], axis=0)
            d = lax.dot_general(ys[c * CH + i], both, NT_DIMS, preferred_element_type=F32)
            tmp[r, :] = d[:, :nt] + d[:, nt:]
        z = flat_tiles(tmp, CH * nt)
        for i in range(CH):
            t = where_[c * CH + i]

            @pl.when(t < nslot)
            def _():
                for q in range(4):
                    row = i * (nt // 2) + q * 8
                    out[q, t] = z[row : row + 8]

        return carry

    lax.fori_loop(0, chunks, chunk, 0)


def route_kernel(tab, parts, send):
    nk = send.shape[1] - CAP
    send[:, CAP:] = jnp.zeros((send.shape[0], nk, *send.shape[2:]), F32)
    for t in range(tab.shape[1]):
        v = (parts[0, t] + parts[1, t]) + (parts[2, t] + parts[3, t])
        send[t // CAP, t % CAP] = v
        owner = tab[2, t] // nk
        row = CAP + tab[2, t] % nk
        send[owner, row] = send[owner, row] + v


def exchange_kernel(tab, own, big, mine, whi, wlo, cw, out, p1, p2, tot, prod, flat, s1, s2):
    nslot = tab.shape[1]
    npair = own.shape[1]
    nk = tot.shape[0]
    rows = p2.shape[1]
    nt = mine.shape[0] // nk
    wide = p2.shape[2]

    def second(j):
        return pltpu.make_async_copy(big.at[own[1, j]], p2.at[j], s2.at[j])

    def first(t):
        return pltpu.make_async_copy(big.at[tab[6, t]], p1.at[t], s1.at[t])

    for j in range(npair):
        second(j).start()

    def begin(t, carry):
        @pl.when(tab[4, t] == 1)
        def _():
            first(t).start()

        return carry

    lax.fori_loop(0, nslot, begin, 0)
    tot[...] = jnp.zeros_like(tot)
    for j in range(npair):
        second(j).wait()
    b = p2[...].reshape(npair * rows, wide)
    e = lax.dot_general(b, whi[...], NT_DIMS, preferred_element_type=F32)
    e = e + lax.dot_general(b, wlo[...], NT_DIMS, preferred_element_type=F32)
    e = e + e
    for k in range(nk):
        prod[k] = e[:, k * nt : (k + 1) * nt]
    for j in range(npair):
        r = pl.ds(j * rows, rows)
        flat[r, :] = prod[own[0, j], r, :]

    def gather(t, carry):
        @pl.when(tab[4, t] == 1)
        def _():
            first(t).wait()
            k = tab[5, t]
            tot[k] = tot[k] + p1[t].astype(F32)

        return carry

    lax.fori_loop(0, nslot, gather, 0)
    w = tot[...].reshape(nk * rows, wide) * cw[...]
    hi = w.astype(BF16)
    lo = (w - hi.astype(F32)).astype(BF16)
    m = lax.dot_general(
        jnp.concatenate([hi, lo], axis=0), mine[...], NT_DIMS, preferred_element_type=F32
    )
    m = m[: nk * rows] + m[nk * rows :]
    m = m + m
    for k in range(nk):
        flat[pl.ds((npair + k) * rows, rows), :] = m[
            k * rows : (k + 1) * rows, k * nt : (k + 1) * nt
        ]
    z = flat_tiles(flat, (npair + nk) * rows)
    for j in range(npair + nk):
        out[j] = z[8 * j : 8 * j + 8]


def combine_kernel(own, e, got, out):
    nk = got.shape[1] - CAP
    npair = own.shape[1]
    for j in range(npair):
        out[j] = e[j] - got[own[2, j], own[3, j]]
    for k in range(nk):
        out[npair + k] = e[npair + k]
        out[npair + nk + k] = -jnp.sum(got[:, CAP + k], axis=0)


def in_vmem(count):
    return [pl.BlockSpec(memory_space=pltpu.VMEM)] * count


SMEM = pl.BlockSpec(memory_space=pltpu.SMEM)
ANY = pl.BlockSpec(memory_space=pl.ANY)


def per_device(x, y, p, coulomb, w, pairs, q_slot):
    n_ka = lax.axis_size("ka")
    me = lax.axis_index("ka")
    a = lax.axis_index("ga")
    nk, nt, gl = x.shape
    qs = w.shape[0]
    npair = pairs.shape[0]
    nslot = n_ka * CAP

    with jax.named_scope("pack"):
        x_far = lax.ppermute(x, "ga", [(0, 1), (1, 0), (2, 3), (3, 2)])
        y_far = lax.ppermute(y, "ga", [(0, 3), (3, 0), (1, 2), (2, 1)])
        payload = jnp.concatenate([widen(v) for v in (x, x_far, y, y_far)], axis=2)
    with jax.named_scope("spread"):
        big = lax.all_gather(payload, "ka", axis=0, tiled=True)

    with jax.named_scope("exchange_pack"):
        rows = nt // 4
        c1 = lax.reduce_precision(coulomb, 8, 7)
        c2 = lax.reduce_precision(coulomb - c1, 8, 7)
        c3 = coulomb - c1 - c2
        pieces = jnp.pad(jnp.stack([c1, c2, c3]).astype(BF16), ((0, 13), (0, 0)))
        held = jnp.concatenate([p.reshape(nk * nt, gl), pieces], axis=0)
        held = lax.all_gather(widen(held), "ga", axis=1, tiled=True)
        full = held[: nk * nt]
        c_full = jnp.sum(held[nk * nt : nk * nt + 3].astype(F32), axis=0, keepdims=True)
        p_rows = lax.dynamic_slice_in_dim(full.reshape(nk, nt, 4 * QW), a * rows, rows, axis=1)
        p_big = lax.all_gather(p_rows, "ka", axis=0, tiled=True)
        weighted = full.astype(F32) * c_full
        w_hi = lax.reduce_precision(weighted, 8, 7)
        w_lo = (weighted - w_hi).astype(BF16)
        w_hi = w_hi.astype(BF16)

    with jax.named_scope("weights"):
        cols = jnp.stack([w[:, :, i * gl : (i + 1) * gl] for i in range(4)])
        cols = jnp.pad(cols, ((0, 0), (0, 0), (0, QW - gl), (0, QW - gl)))

        def columns_of(b):
            return jnp.concatenate(
                [
                    lax.dynamic_index_in_dim(cols, b, 0, keepdims=False),
                    lax.dynamic_index_in_dim(cols, 3 - b, 0, keepdims=False),
                ],
                axis=2,
            )

        near = columns_of(a)
        far = lax.ppermute(
            columns_of(jnp.bitwise_xor(a, 1)), "ga", [(0, 1), (1, 0), (2, 3), (3, 2)]
        )
        wk = jnp.concatenate([near, far], axis=1)

    with jax.named_scope("tables"):
        every = lax.all_gather(pairs, "ka", axis=0, tiled=True).reshape(n_ka, npair, 3)

        def routes(rows):
            slot = jnp.sum(
                jnp.where(
                    rows[..., 2, None] == jnp.arange(q_slot.shape[0]), q_slot, 0
                ),
                axis=-1,
            )
            q_owner = slot // qs
            k_owner = rows[..., 1] // nk
            return slot % qs, q_owner, rank_in_group(q_owner), k_owner, rank_in_group(k_owner)

        local, q_owner, q_rank, k_owner, k_rank = routes(every)
        ranks = jnp.arange(CAP)
        hot_q = (q_owner == me)[..., None] & (q_rank[..., None] == ranks)
        hot_k = (k_owner == me)[..., None] & (k_rank[..., None] == ranks)

        def pick(hot, v):
            return jnp.sum(jnp.where(hot, v[..., None], 0), axis=1).reshape(nslot)

        ones = jnp.ones_like(local)
        tab = jnp.stack(
            [
                pick(hot_q, ones),
                pick(hot_q, every[..., 0]),
                pick(hot_q, every[..., 1]),
                pick(hot_q, local),
                pick(hot_k, ones),
                pick(hot_k, every[..., 1] - me * nk),
                pick(hot_k, every[..., 0]),
            ]
        )
        _, o1, r1, _, _ = routes(pairs)
        own = jnp.stack([pairs[:, 0] - me * nk, pairs[:, 1], o1, r1])

    npos = nslot + qs * CH
    part = pl.pallas_call(
        direct_kernel,
        out_shape=jax.ShapeDtypeStruct((4, nslot, 8, 128), F32),
        in_specs=[SMEM, ANY, *in_vmem(1)],
        out_specs=pl.BlockSpec(memory_space=pltpu.VMEM),
        scratch_shapes=[
            pltpu.VMEM((npos, nt, 2 * QW), BF16),
            pltpu.VMEM((npos, nt, 2 * QW), BF16),
            pltpu.VMEM((CH * nt, nt), F32),
            pltpu.SMEM((npos,), jnp.int32),
            pltpu.SemaphoreType.DMA((npos,)),
            pltpu.SemaphoreType.DMA((npos,)),
        ],
        compiler_params=pltpu.CompilerParams(vmem_limit_bytes=48 * 1024 * 1024),
        name="direct",
    )(tab, big, wk)
    with jax.named_scope("to_quarters"):
        parts = lax.all_to_all(part, "ga", 0, 0, tiled=True)
    send = pl.pallas_call(
        route_kernel,
        out_shape=jax.ShapeDtypeStruct((n_ka, CAP + nk, 8, 128), F32),
        in_specs=[SMEM, *in_vmem(1)],
        out_specs=pl.BlockSpec(memory_space=pltpu.VMEM),
        name="route",
    )(tab, parts)
    with jax.named_scope("to_holders"):
        got = lax.all_to_all(send, "ka", 0, 0, tiled=True)
    exch = pl.pallas_call(
        exchange_kernel,
        out_shape=jax.ShapeDtypeStruct((npair + nk, 8, 128), F32),
        in_specs=[SMEM, SMEM, ANY, *in_vmem(4)],
        out_specs=pl.BlockSpec(memory_space=pltpu.VMEM),
        scratch_shapes=[
            pltpu.VMEM((nslot, rows, 4 * QW), BF16),
            pltpu.VMEM((npair, rows, 4 * QW), BF16),
            pltpu.VMEM((nk, rows, 4 * QW), F32),
            pltpu.VMEM((nk, npair * rows, nt), F32),
            pltpu.VMEM(((npair + nk) * rows, nt), F32),
            pltpu.SemaphoreType.DMA((nslot,)),
            pltpu.SemaphoreType.DMA((npair,)),
        ],
        compiler_params=pltpu.CompilerParams(vmem_limit_bytes=32 * 1024 * 1024),
        name="exchange",
    )(tab, own, p_big, full, w_hi, w_lo, c_full)
    both = pl.pallas_call(
        combine_kernel,
        out_shape=jax.ShapeDtypeStruct((npair + 2 * nk, 8, 128), F32),
        in_specs=[SMEM, *in_vmem(2)],
        out_specs=pl.BlockSpec(memory_space=pltpu.VMEM),
        name="combine",
    )(own, exch, got)
    with jax.named_scope("copies"):
        whole = lax.all_gather(both, "ga", axis=0)
        whole = jnp.transpose(whole, (1, 0, 2, 3)).reshape(npair + 2 * nk, nt, nt)
        flipped = jnp.transpose(whole[: npair + nk], (0, 2, 1))
        mirrored = flipped[npair:] + whole[npair + nk :]
    return flipped[:npair].reshape(npair, nt * nt), mirrored.reshape(nk, nt * nt)


def solution(mesh):
    in_specs = (
        P("ka", None, "ga"),
        P("ka", None, "ga"),
        P("ka", None, "ga"),
        P("ga"),
        P("ka", "ga", None),
        P("ka", None),
        P(),
    )
    out_specs = (P("ka", None), P("ka", None))
    return jax.shard_map(
        per_device, mesh=mesh, in_specs=in_specs, out_specs=out_specs, check_vma=False
    )
```

time: 222 us -> 206 us (0.928); the launches traced: 222 us -> 203 us
  waiting for transfers between devices: 79 us -> 54.8 us
  Pallas kernels: 15 us -> 31.8 us
  blocking collectives: 74.2 us -> 58.2 us
    all_to_all x2 -> x0, blocking collectives: 35.9 us -> none  [the longest x1 22.4 us: per_device(): quarter = jnp.sum(lax.all_to_all(part, 'ga', 0, 0, tiled=True), axis=0)]
    all_gather x1, waiting for transfers between devices: 67 us -> 33.9 us  [per_device(): big = lax.all_gather(payload, 'ka', axis=0, tiled=True)]
    pallas_call x3 -> x4, Pallas kernels: 15 us -> 31.8 us  [the longest x1 20.6 us: per_device(): pl.pallas_call(direct_kernel, out_shape=jax.ShapeDtypeStruct((4, nslot, 8...]
    all_gather x0 -> x1, blocking collectives: none -> 14.8 us  [per_device(): held = lax.all_gather(widen(held), 'ga', axis=1, tiled=True)]
    all_gather x1, blocking collectives: 12.6 us -> 17.7 us  [per_device(): whole = lax.all_gather(both, 'ga', axis=0)]
    all_gather x0 -> x1, waiting for transfers between devices: none -> 4.45 us  [per_device(): p_big = lax.all_gather(p_rows, 'ka', axis=0, tiled=True)]
    all_to_all x1 -> x2, waiting for transfers between devices: 8.3 us -> 10.7 us  [the longest x1 10.7 us: per_device(): parts = lax.all_to_all(part, 'ga', 0, 0, tiled=True)]
    all_to_all x1 -> x2, starting transfers between devices: 10.2 us -> 11.5 us  [the longest x1 7.12 us: per_device(): got = lax.all_to_all(send, 'ka', 0, 0, tiled=True)]
  transfers between devices with their start and end apart: 5 -> 7, of which waited for: 4 -> 5; matrix products, arithmetic and copies ran while one was open for 9% -> 9% of each run, Pallas kernels for 0% -> 15%
where the time goes in v2:
time: 206 us; the launch traced here: 203 us
  blocking collectives  58.2 us (28%)
  waiting for transfers between devices  54.8 us (27%)
  Pallas kernels  31.8 us (15%)
  starting transfers between devices  16.3 us (8%)
  local copies, waits for them, and re-layouts  15.7 us (8%)
  between operations  14.5 us (7%)
  other arithmetic  12.1 us (6%)
    all_gather x1, waiting for transfers between devices, per_device(): big = lax.all_gather(payload, 'ka', axis=0, tiled=True)  33.9 us
    all_gather x1, blocking collectives, per_device(): lax.all_gather(pairs, 'ka', axis=0, tiled=True).reshape(n_ka, npair, 3)  25.7 us
    pallas_call x1, Pallas kernels, per_device(): pl.pallas_call(direct_kernel, out_shape=jax.ShapeDtypeStruct((4, nslot, 8...  20.6 us
    all_gather x1, blocking collectives, per_device(): whole = lax.all_gather(both, 'ga', axis=0)  17.7 us
    all_gather x1, blocking collectives, per_device(): held = lax.all_gather(widen(held), 'ga', axis=1, tiled=True)  14.8 us
    all_to_all x1, waiting for transfers between devices, per_device(): parts = lax.all_to_all(part, 'ga', 0, 0, tiled=True)  10.7 us
    all_to_all x1, starting transfers between devices, per_device(): got = lax.all_to_all(send, 'ka', 0, 0, tiled=True)  7.12 us
    pallas_call x1, Pallas kernels, per_device(): pl.pallas_call(exchange_kernel, out_shape=jax.ShapeDtypeStruct((npair + n...  6.82 us
  transfers between devices with their start and end apart: 7, of which 5 were waited for; matrix products, arithmetic and copies ran while one was open for 9% of the time, Pallas kernels for 15%

profile of v2, /device:TPU:0, one launch (start us, length us, event | category | flops | bytes accessed | tf_op | source)
XLA Modules:
  0.0 203.4 jit_solution(8528680034320752960)
XLA Ops:
  7.2 1.7 collective-permute-start
  8.9 2.1 %collective-permute-start.1 = (bf16[4,64,375]{2,1,0:T(8,128)(2,1)}, bf16[4,64,375]{2,1,0:T(8,128)(2,1)S(1)}, u32[]{:S(2)}, u32[]{:S(2)}) collective-permute-start(bf16[4,64,375]{2,1,0:T(8,128)(2,1)} %param.8), channel_id=1, source_target_pairs={{0,3},{3,0},{1,2},{2,1},{4,7},{7,4},{5,6},{6,5},{8,11},{11,8},{9,1... | collective-permute-start | bytes 576008 | tf_op jit(solution)/shard_map/pack/ppermute | solution.py:215
  11.0 3.0 %collective-permute-done = bf16[4,64,375]{2,1,0:T(8,128)(2,1)S(1)} collective-permute-done((bf16[4,64,375]{2,1,0:T(8,128)(2,1)}, bf16[4,64,375]{2,1,0:T(8,128)(2,1)S(1)}, u32[]{:S(2)}, u32[]{:S(2)}) %collective-permute-start) | collective-permute-done | bytes 192032 | tf_op jit(solution)/shard_map/pack/ppermute | solution.py:214
  14.0 2.7 %collective-permute-done.1 = bf16[4,64,375]{2,1,0:T(8,128)(2,1)S(1)} collective-permute-done((bf16[4,64,375]{2,1,0:T(8,128)(2,1)}, bf16[4,64,375]{2,1,0:T(8,128)(2,1)S(1)}, u32[]{:S(2)}, u32[]{:S(2)}) %collective-permute-start.1) | collective-permute-done | bytes 192032 | tf_op jit(solution)/shard_map/pack/ppermute | solution.py:215
  16.7 2.0 fusion.19
  18.9 14.8 %all_gather.19 = bf16[272,1536]{1,0:T(8,128)(2,1)S(1)} all-gather(bf16[272,384]{1,0:T(8,128)(2,1)S(1)} %fusion.23), channel_id=1, replica_groups=mesh['ka'=32,'ga'=4] {'ga'}, dimensions={1}, use_global_device_ids=true | all-gather | bytes 1044480 | tf_op jit(solution)/shard_map/exchange_pack/all_gather | solution.py:227
  35.5 3.6 %slice_bitcast_fusion.3 = (bf16[1,2,375,375]{3,1,2,0:T(2,128)(2,1)S(1)}, bf16[1,2,375,375]{3,1,2,0:T(2,128)(2,1)S(1)}, bf16[1,2,375,375]{3,1,2,0:T(2,128)(2,1)S(1)}, bf16[1,2,375,375]{3,1,2,0:T(2,128)(2,1)S(1)}) fusion(bf16[2,375,1500]{2,0,1:T(2,128)(2,1)S(1)} %copy-done.8), kind=kLoop, calls=%fused_computation.41 | loop fusion | bytes 4500000 | tf_op jit(solution)/shard_map/weights/stack | solution.py:238
  39.1 6.5 %fusion.10 = bf16[4,2,384,384]{3,1,2,0:T(2,128)(2,1)S(1)} fusion(bf16[1,2,375,375]{3,1,2,0:T(2,128)(2,1)S(1)} %get-tuple-element.22, bf16[1,2,375,375]{3,1,2,0:T(2,128)(2,1)S(1)} %get-tuple-element.23, bf16[1,2,375,375]{3,1,2,0:T(2,128)(2,1)S(1)} %get-tuple-element.21, bf16[1,2,375,375]{3,1,2,0:T(2,128)(2,1)S(1)} %get-tuple-element.20), kind=kLoop, calls=%fused_computation.16 | loop fusion | flops 22413312 | bytes 4609296 | tf_op jit(solution)/shard_map/weights/stack | solution.py:238
  45.6 1.6 constant_dynamic-slice_fusion.3
  47.5 1.0 collective-permute-start.2
  48.5 25.7 %all-gather.1 = s32[32,16,3]{1,2,0:T(4,128)S(1)} all-gather(s32[1,16,3]{1,2,0:T(4,128)S(1)} %bitcast.63), channel_id=1, replica_groups=mesh['ka'=32,'ga'=4] {'ka'}, dimensions={0}, use_global_device_ids=true | all-gather | bytes 6336 | tf_op jit(solution)/shard_map/tables/all_gather | solution.py:257
  77.1 1.8 pad_maximum_fusion.wk
  78.8 33.9 %all-gather.7.cloned.1.call-done.big = bf16[128,64,1536]{2,1,0:T(8,128)(2,1)} async-done(((bf16[4,64,1536]{2,1,0:T(8,128)(2,1)}), bf16[128,64,1536]{2,1,0:T(8,128)(2,1)}) %all-gather.7.cloned.1.call-update) | async-done | bytes 25165840 | tf_op jit(solution)/shard_map/spread/all_gather | solution.py:218
  112.7 20.6 %direct.1 = f32[4,64,8,128]{3,2,1,0:T(8,128)} custom-call(s32[7,64]{1,0:T(8,128)S(1)} %stack.44.tab, bf16[128,64,1536]{2,1,0:T(8,128)(2,1)} %all-gather.7.cloned.1.call-done.big, bf16[2,768,768]{2,1,0:T(8,128)(2,1)S(1)} %pad_maximum_fusion.wk), custom_call_target="tpu_custom_call" | custom-call | tf_op jit(solution)/shard_map/direct/pallas_call | solution.py:294
  133.3 4.4 %all-to-all-start = ((f32[4,64,8,128]{3,2,1,0:T(8,128)}), f32[4,64,8,128]{3,2,1,0:T(8,128)S(1)}, u32[]{:S(2)}, u32[]{:S(2)}) async-start(f32[4,64,8,128]{3,2,1,0:T(8,128)} %direct.1), calls=%async_computation | async-start | bytes 2097152 | tf_op jit(solution)/shard_map/to_quarters/all_to_all | solution.py:311
  137.9 10.7 %all-to-all-done.parts = f32[4,64,8,128]{3,2,1,0:T(8,128)S(1)} async-done(((f32[4,64,8,128]{3,2,1,0:T(8,128)}), f32[4,64,8,128]{3,2,1,0:T(8,128)S(1)}, u32[]{:S(2)}, u32[]{:S(2)}) %all-to-all-start) | async-done | bytes 1048608 | tf_op jit(solution)/shard_map/to_quarters/all_to_all | solution.py:311
  148.6 1.0 copy-done.7
  149.6 2.5 %route.1 = f32[32,6,8,128]{3,2,1,0:T(8,128)} custom-call(s32[7,64]{1,0:T(8,128)} %copy-done.2, f32[4,64,8,128]{3,2,1,0:T(8,128)} %copy-done.7), custom_call_target="tpu_custom_call" | custom-call | tf_op jit(solution)/shard_map/route/pallas_call | solution.py:312
  152.1 7.1 %all-to-all-start.1 = ((f32[32,6,8,128]{3,2,1,0:T(8,128)}), f32[32,6,8,128]{3,2,1,0:T(8,128)}, u32[]{:S(2)}, u32[]{:S(2)}) async-start(f32[32,6,8,128]{3,2,1,0:T(8,128)} %route.1), calls=%async_computation.1 | async-start | bytes 1572864 | tf_op jit(solution)/shard_map/to_holders/all_to_all | solution.py:320
  159.8 4.4 %all-gather.5.cloned.1.call-done.big = bf16[128,16,1536]{2,1,0:T(8,128)(2,1)} async-done(((bf16[4,16,1536]{2,1,0:T(8,128)(2,1)}), bf16[128,16,1536]{2,1,0:T(8,128)(2,1)}) %all-gather.5.cloned.1.call-update) | async-done | bytes 6291472 | tf_op jit(solution)/shard_map/exchange_pack/all_gather | solution.py:231
  164.2 2.8 %copy-done = bf16[128,16,1536]{2,1,0:T(8,128)(2,1)S(1)} copy-done((bf16[128,16,1536]{2,1,0:T(8,128)(2,1)S(1)}, bf16[128,16,1536]{2,1,0:T(8,128)(2,1)}, u32[]{:S(2)}) %copy-start) | copy-done | bytes 6291480
  167.0 6.8 %exchange.1.e = f32[20,8,128]{2,1,0:T(8,128)S(1)} custom-call(s32[7,64]{1,0:T(8,128)S(1)} %copy-done.3, s32[4,16]{1,0:T(4,128)S(1)} %pad_add_fusion.own, bf16[128,16,1536]{2,1,0:T(8,128)(2,1)S(1)} %copy-done, bf16[256,1536]{1,0:T(8,128)(2,1)S(1)} %slice.78.mine, bf16[256,1536]{1,0:T(8,128)(2,1)S(1)} %get-tuple-element.25.whi, ...), custom_call_target="tpu_custom_call" | custom-call | tf_op jit(solution)/shard_map/exchange/pallas_call | solution.py:321
  174.5 1.9 combine.1
  176.4 17.7 %all-gather = f32[96,8,128]{2,1,0:T(8,128)S(1)} all-gather(f32[24,8,128]{2,1,0:T(8,128)} %combine.1), channel_id=2, replica_groups=mesh['ka'=32,'ga'=4] {'ga'}, dimensions={0}, use_global_device_ids=true | all-gather | bytes 491520 | tf_op jit(solution)/shard_map/copies/all_gather | solution.py:346
  (90 shorter events, 8.6 us)
Async XLA Ops:
  7.2 11.6 %copy-start.11 = (f32[375]{0:T(512)S(1)}, f32[375]{0:T(512)}, u32[]{:S(2)}) copy-start(f32[375]{0:T(512)} %param.10) | copy-start | bytes 4504
  7.2 11.7 %copy-start.9 = (bf16[4,64,375]{2,1,0:T(8,128)(2,1)S(1)}, bf16[4,64,375]{2,1,0:T(8,128)(2,1)}, u32[]{:S(2)}) copy-start(bf16[4,64,375]{2,1,0:T(8,128)(2,1)} %param.9) | copy-start | bytes 576004
  7.2 105.6 %all-gather.7.cloned.1.call-start = ((), (), s32[]{:S(2)}) async-start(), calls=%async_computation.3 | async-start | bytes 25952256 | tf_op jit(solution)/shard_map/spread/all_gather | solution.py:218
  7.2 6.8 %collective-permute-start = (bf16[4,64,375]{2,1,0:T(8,128)(2,1)}, bf16[4,64,375]{2,1,0:T(8,128)(2,1)S(1)}, u32[]{:S(2)}, u32[]{:S(2)}) collective-permute-start(bf16[4,64,375]{2,1,0:T(8,128)(2,1)} %param.7), channel_id=1, source_target_pairs={{0,1},{1,0},{2,3},{3,2},{4,5},{5,4},{6,7},{7,6},{8,9},{9,8},{10,11... | collective-permute-start | bytes 576008 | tf_op jit(solution)/shard_map/pack/ppermute | solution.py:214
  8.9 7.8 %collective-permute-start.1 = (bf16[4,64,375]{2,1,0:T(8,128)(2,1)}, bf16[4,64,375]{2,1,0:T(8,128)(2,1)S(1)}, u32[]{:S(2)}, u32[]{:S(2)}) collective-permute-start(bf16[4,64,375]{2,1,0:T(8,128)(2,1)} %param.8), channel_id=1, source_target_pairs={{0,3},{3,0},{1,2},{2,1},{4,7},{7,4},{5,6},{6,5},{8,11},{11,8},{9,1... | collective-permute-start | bytes 576008 | tf_op jit(solution)/shard_map/pack/ppermute | solution.py:215
  18.7 16.8 %copy-start.8 = (bf16[2,375,1500]{2,0,1:T(2,128)(2,1)S(1)}, bf16[2,375,1500]{2,0,1:T(2,128)(2,1)}, u32[]{:S(2)}) copy-start(bf16[2,375,1500]{2,0,1:T(2,128)(2,1)} %param.11) | copy-start | bytes 6750004
  18.7 145.5 %all-gather.5.cloned.1.call-start = ((), (), s32[]{:S(2)}) async-start(), calls=%async_computation.2 | async-start | bytes 6488064 | tf_op jit(solution)/shard_map/exchange_pack/all_gather | solution.py:231
  33.7 0.9 copy-start.5
  47.2 1.3 copy-start.10
  47.3 27.1 %copy-start.12 = (s32[64]{0:T(128)S(1)}, s32[64]{0:T(128)}, u32[]{:S(2)}) copy-start(s32[64]{0:T(128)} %param.13) | copy-start | bytes 772
  47.5 29.5 %collective-permute-start.2 = (bf16[2,384,768]{2,1,0:T(8,128)(2,1)S(1)}, bf16[2,384,768]{2,1,0:T(8,128)(2,1)}, u32[]{:S(2)}, u32[]{:S(2)}) collective-permute-start(bf16[2,384,768]{2,1,0:T(8,128)(2,1)S(1)} %pad_maximum_fusion.1), channel_id=1, source_target_pairs={{0,1},{1,0},{2,3},{3,2},{4,5},{5,4},{6,7},{7,6},{8,9},{9,8},{10,11... | collective-permute-start | bytes 3538952 | tf_op jit(solution)/shard_map/weights/ppermute | solution.py:251
  76.9 35.9 %copy-start.2 = (s32[7,64]{1,0:T(8,128)}, s32[7,64]{1,0:T(8,128)S(1)}, u32[]{:S(2)}) copy-start(s32[7,64]{1,0:T(8,128)S(1)} %stack.44.tab) | copy-start | bytes 5380
  133.3 26.0 %copy-start.6 = (bf16[272,1536]{1,0:T(8,128)(2,1)S(1)}, bf16[272,1536]{1,0:T(8,128)(2,1)}, u32[]{:S(2)}) copy-start(bf16[272,1536]{1,0:T(8,128)(2,1)} %copy-done.5) | copy-start | bytes 2506756
  133.3 15.3 %all-to-all-start = ((f32[4,64,8,128]{3,2,1,0:T(8,128)}), f32[4,64,8,128]{3,2,1,0:T(8,128)S(1)}, u32[]{:S(2)}, u32[]{:S(2)}) async-start(f32[4,64,8,128]{3,2,1,0:T(8,128)} %direct.1), calls=%async_computation | async-start | bytes 2097152 | tf_op jit(solution)/shard_map/to_quarters/all_to_all | solution.py:311
  148.6 1.0 copy-start.7
  152.1 12.1 %copy-start.3 = (s32[7,64]{1,0:T(8,128)S(1)}, s32[7,64]{1,0:T(8,128)}, u32[]{:S(2)}) copy-start(s32[7,64]{1,0:T(8,128)} %copy-done.2) | copy-start | bytes 5380
  152.1 22.4 %all-to-all-start.1 = ((f32[32,6,8,128]{3,2,1,0:T(8,128)}), f32[32,6,8,128]{3,2,1,0:T(8,128)}, u32[]{:S(2)}, u32[]{:S(2)}) async-start(f32[32,6,8,128]{3,2,1,0:T(8,128)} %route.1), calls=%async_computation.1 | async-start | bytes 1572864 | tf_op jit(solution)/shard_map/to_holders/all_to_all | solution.py:320
  159.5 14.3 %copy-start.4 = (s32[4,16]{1,0:T(4,128)}, s32[4,16]{1,0:T(4,128)S(1)}, u32[]{:S(2)}) copy-start(s32[4,16]{1,0:T(4,128)S(1)} %pad_add_fusion.own) | copy-start | bytes 772
  164.2 2.8 %copy-start = (bf16[128,16,1536]{2,1,0:T(8,128)(2,1)S(1)}, bf16[128,16,1536]{2,1,0:T(8,128)(2,1)}, u32[]{:S(2)}) copy-start(bf16[128,16,1536]{2,1,0:T(8,128)(2,1)} %all-gather.5.cloned.1.call-done.big) | copy-start | bytes 18874372
  173.9 0.6 copy-start.1
Sparse Core Ops, SparseCore 0:
  18.8 93.8 all-gather.6
  115.6 48.6 all-gather.4

commit v3 on v2

--- a/solution.py
+++ b/solution.py
@@ -30,16 +30,16 @@
     return jnp.concatenate([even, odd], axis=1)
 
 
-def direct_kernel(tab, big, wk, out, xs, ys, tmp, where_, sx, sy):
+def direct_kernel(tab, big, w, send, xs, ys, prod, where_, sx, sy):
     nslot = tab.shape[1]
-    nt = xs.shape[1]
-    wide = xs.shape[2]
+    half = xs.shape[1]
+    nk = send.shape[1] - CAP
 
     def x_copy(k, pos):
-        return pltpu.make_async_copy(big.at[k, :, pl.ds(0, wide)], xs.at[pos], sx.at[pos])
+        return pltpu.make_async_copy(big.at[k, pl.ds(0, half)], xs.at[pos], sx.at[pos])
 
     def y_copy(k, pos):
-        return pltpu.make_async_copy(big.at[k, :, pl.ds(wide, wide)], ys.at[pos], sy.at[pos])
+        return pltpu.make_async_copy(big.at[k, pl.ds(half, half)], ys.at[pos], sy.at[pos])
 
     def clear(i, carry):
         where_[i] = nslot
@@ -70,7 +70,7 @@
 
     _, n_second = lax.fori_loop(0, nslot, place, (0, 0))
     chunks = chunks_first + (n_second + CH - 1) // CH
-    out[...] = jnp.zeros_like(out)
+    send[...] = jnp.zeros_like(send)
 
     def chunk(c, carry):
         for i in range(CH):
@@ -83,39 +83,30 @@
                 y_copy(0, pos).wait()
 
         slot = jnp.where(c < chunks_first, 0, 1)
-        x = xs[pl.ds(c * CH, CH)].reshape(CH * nt, wide)
-        u = jnp.dot(x, wk[slot], preferred_element_type=F32)
-        hi = u.astype(BF16)
-        lo = (u - hi.astype(F32)).astype(BF16)
-        for i in range(CH):
-            r = slice(i * nt, (i + 1) * nt)
-            both = jnp.concatenate([hi[r], lo[r]], axis=0)
-            d = lax.dot_general(ys[c * CH + i], both, NT_DIMS, preferred_element_type=F32)
-            tmp[r, :] = d[:, :nt] + d[:, nt:]
-        z = flat_tiles(tmp, CH * nt)
+        x = xs[pl.ds(c * CH, CH)].reshape(CH * half, xs.shape[2])
+        y = ys[pl.ds(c * CH, CH)].reshape(CH * half, ys.shape[2])
+        u = jnp.dot(x, w[slot], preferred_element_type=F32).astype(BF16)
+        d = lax.dot_general(u, y, NT_DIMS, preferred_element_type=F32)
+        for i in range(0, CH * half, 128):
+            prod[i : i + 128] = d[i : i + 128, i : i + 128]
+        quads = [prod[pl.ds(q, CH * half // 4, stride=4), :] for q in range(4)]
         for i in range(CH):
             t = where_[c * CH + i]
+            tile = jnp.concatenate(
+                [v[8 * i : 8 * i + 8, half * i % 128 : half * i % 128 + half] for v in quads],
+                axis=1,
+            )
 
             @pl.when(t < nslot)
             def _():
-                for q in range(4):
-                    row = i * (nt // 2) + q * 8
-                    out[q, t] = z[row : row + 8]
+                send[t // CAP, t % CAP] = tile
+                owner = tab[2, t] // nk
+                row = CAP + tab[2, t] % nk
+                send[owner, row] = send[owner, row] + tile
 
         return carry
 
     lax.fori_loop(0, chunks, chunk, 0)
-
-
-def route_kernel(tab, parts, send):
-    nk = send.shape[1] - CAP
-    send[:, CAP:] = jnp.zeros((send.shape[0], nk, *send.shape[2:]), F32)
-    for t in range(tab.shape[1]):
-        v = (parts[0, t] + parts[1, t]) + (parts[2, t] + parts[3, t])
-        send[t // CAP, t % CAP] = v
-        owner = tab[2, t] // nk
-        row = CAP + tab[2, t] % nk
-        send[owner, row] = send[owner, row] + v
 
 
 def exchange_kernel(tab, own, big, mine, whi, wlo, cw, out, p1, p2, tot, prod, flat, s1, s2):
@@ -127,10 +118,10 @@
     wide = p2.shape[2]
 
     def second(j):
-        return pltpu.make_async_copy(big.at[own[1, j]], p2.at[j], s2.at[j])
+        return pltpu.make_async_copy(big.at[own[1, j], pl.ds(nt, rows)], p2.at[j], s2.at[j])
 
     def first(t):
-        return pltpu.make_async_copy(big.at[tab[6, t]], p1.at[t], s1.at[t])
+        return pltpu.make_async_copy(big.at[tab[6, t], pl.ds(nt, rows)], p1.at[t], s1.at[t])
 
     for j in range(npair):
         second(j).start()
@@ -183,14 +174,45 @@
         out[j] = z[8 * j : 8 * j + 8]
 
 
-def combine_kernel(own, e, got, out):
+def collect_kernel(own, e, got, out):
     nk = got.shape[1] - CAP
     npair = own.shape[1]
     for j in range(npair):
-        out[j] = e[j] - got[own[2, j], own[3, j]]
+        out[j] = got[own[2, j], own[3, j]]
     for k in range(nk):
-        out[npair + k] = e[npair + k]
-        out[npair + nk + k] = -jnp.sum(got[:, CAP + k], axis=0)
+        out[npair + k] = jnp.sum(got[:, CAP + k], axis=0)
+    out[npair + nk :] = e[...]
+
+
+def finish_kernel(whole, blocks, mirrored, dmat, emat, rows):
+    npair, nk = blocks.shape[0], mirrored.shape[0]
+    nt = dmat.shape[1]
+    half = nt // 2
+    n = npair + nk
+    for j in range(n):
+        for a in range(2):
+            left, right = whole[2 * a, j], whole[2 * a + 1, j]
+            for q in range(4):
+                cut = slice(half * q, half * (q + 1))
+                dmat[j, pl.ds(half * a + q, 8, stride=4), :] = jnp.concatenate(
+                    [left[:, cut], right[:, cut]], axis=1
+                )
+        for a in range(4):
+            tile = whole[a, n + j]
+            emat[j, pl.ds(16 * a, 8, stride=2), :] = tile[:, :nt]
+            emat[j, pl.ds(16 * a + 1, 8, stride=2), :] = tile[:, nt:]
+    for j in range(n):
+        if j < npair:
+            dmat[j] = emat[j].T - dmat[j]
+        else:
+            dmat[j] = (emat[j] - dmat[j]).T
+        even = dmat[j, pl.ds(0, half, stride=2), :]
+        odd = dmat[j, pl.ds(1, half, stride=2), :]
+        rows[pl.ds(j * half, half), :] = jnp.concatenate([even, odd], axis=1)
+    for r in range(half):
+        lanes = pl.ds(2 * nt * r, 2 * nt)
+        blocks[:, lanes] = rows[pl.ds(r, npair, stride=half), :]
+        mirrored[:, lanes] = rows[pl.ds(npair * half + r, nk, stride=half), :]
 
 
 def in_vmem(count):
@@ -210,15 +232,40 @@
     npair = pairs.shape[0]
     nslot = n_ka * CAP
 
+    half, rows = nt // 2, nt // 4
     with jax.named_scope("pack"):
-        x_far = lax.ppermute(x, "ga", [(0, 1), (1, 0), (2, 3), (3, 2)])
-        y_far = lax.ppermute(y, "ga", [(0, 3), (3, 0), (1, 2), (2, 1)])
-        payload = jnp.concatenate([widen(v) for v in (x, x_far, y, y_far)], axis=2)
+        sent = [
+            jnp.concatenate(
+                [
+                    x[:, half * (b // 2) : half * (b // 2) + half],
+                    y[:, half * (b % 2) : half * (b % 2) + half],
+                    p[:, rows * b : rows * (b + 1)],
+                ],
+                axis=1,
+            )
+            for b in range(4)
+        ]
+        parts = lax.all_to_all(widen(jnp.stack(sent)), "ga", 0, 0, tiled=True)
+        payload = jnp.concatenate([parts[b] for b in range(4)], axis=2)
     with jax.named_scope("spread"):
         big = lax.all_gather(payload, "ka", axis=0, tiled=True)
 
+    with jax.named_scope("weights"):
+        up = [(i, (i + 1) % 4) for i in range(4)]
+        down = [(i, (i - 1) % 4) for i in range(4)]
+        here = jnp.concatenate([widen(w[:, :, i * gl : (i + 1) * gl]) for i in range(4)], axis=2)
+        here = jnp.pad(here, ((0, 0), (0, QW - gl), (0, 0)))
+        below = lax.ppermute(here, "ga", up)
+        above = lax.ppermute(here, "ga", down)
+        across = [lax.ppermute(below[:1], "ga", up), lax.ppermute(above[1:], "ga", down)]
+        wk = jnp.zeros((qs, 4, QW, 4 * QW), BF16)
+        for step, v in ((0, here), (1, above), (3, below)):
+            wk = lax.dynamic_update_slice_in_dim(wk, v[:, None], (a + step) % 4, 1)
+        for i, v in enumerate(across):
+            wk = lax.dynamic_update_slice(wk, v[:, None], (i, (a + 2) % 4, 0, 0))
+        wk = wk.reshape(qs, 4 * QW, 4 * QW)
+
     with jax.named_scope("exchange_pack"):
-        rows = nt // 4
         c1 = lax.reduce_precision(coulomb, 8, 7)
         c2 = lax.reduce_precision(coulomb - c1, 8, 7)
         c3 = coulomb - c1 - c2
@@ -227,31 +274,10 @@
         held = lax.all_gather(widen(held), "ga", axis=1, tiled=True)
         full = held[: nk * nt]
         c_full = jnp.sum(held[nk * nt : nk * nt + 3].astype(F32), axis=0, keepdims=True)
-        p_rows = lax.dynamic_slice_in_dim(full.reshape(nk, nt, 4 * QW), a * rows, rows, axis=1)
-        p_big = lax.all_gather(p_rows, "ka", axis=0, tiled=True)
         weighted = full.astype(F32) * c_full
         w_hi = lax.reduce_precision(weighted, 8, 7)
         w_lo = (weighted - w_hi).astype(BF16)
         w_hi = w_hi.astype(BF16)
-
-    with jax.named_scope("weights"):
-        cols = jnp.stack([w[:, :, i * gl : (i + 1) * gl] for i in range(4)])
-        cols = jnp.pad(cols, ((0, 0), (0, 0), (0, QW - gl), (0, QW - gl)))
-
-        def columns_of(b):
-            return jnp.concatenate(
-                [
-                    lax.dynamic_index_in_dim(cols, b, 0, keepdims=False),
-                    lax.dynamic_index_in_dim(cols, 3 - b, 0, keepdims=False),
-                ],
-                axis=2,
-            )
-
-        near = columns_of(a)
-        far = lax.ppermute(
-            columns_of(jnp.bitwise_xor(a, 1)), "ga", [(0, 1), (1, 0), (2, 3), (3, 2)]
-        )
-        wk = jnp.concatenate([near, far], axis=1)
 
     with jax.named_scope("tables"):
         every = lax.all_gather(pairs, "ka", axis=0, tiled=True).reshape(n_ka, npair, 3)
@@ -291,15 +317,15 @@
         own = jnp.stack([pairs[:, 0] - me * nk, pairs[:, 1], o1, r1])
 
     npos = nslot + qs * CH
-    part = pl.pallas_call(
+    send = pl.pallas_call(
         direct_kernel,
-        out_shape=jax.ShapeDtypeStruct((4, nslot, 8, 128), F32),
+        out_shape=jax.ShapeDtypeStruct((n_ka, CAP + nk, 8, 128), F32),
         in_specs=[SMEM, ANY, *in_vmem(1)],
         out_specs=pl.BlockSpec(memory_space=pltpu.VMEM),
         scratch_shapes=[
-            pltpu.VMEM((npos, nt, 2 * QW), BF16),
-            pltpu.VMEM((npos, nt, 2 * QW), BF16),
-            pltpu.VMEM((CH * nt, nt), F32),
+            pltpu.VMEM((npos, half, 4 * QW), BF16),
+            pltpu.VMEM((npos, half, 4 * QW), BF16),
+            pltpu.VMEM((CH * half, 128), F32),
             pltpu.SMEM((npos,), jnp.int32),
             pltpu.SemaphoreType.DMA((npos,)),
             pltpu.SemaphoreType.DMA((npos,)),
@@ -307,15 +333,6 @@
         compiler_params=pltpu.CompilerParams(vmem_limit_bytes=48 * 1024 * 1024),
         name="direct",
     )(tab, big, wk)
-    with jax.named_scope("to_quarters"):
-        parts = lax.all_to_all(part, "ga", 0, 0, tiled=True)
-    send = pl.pallas_call(
-        route_kernel,
-        out_shape=jax.ShapeDtypeStruct((n_ka, CAP + nk, 8, 128), F32),
-        in_specs=[SMEM, *in_vmem(1)],
-        out_specs=pl.BlockSpec(memory_space=pltpu.VMEM),
-        name="route",
-    )(tab, parts)
     with jax.named_scope("to_holders"):
         got = lax.all_to_all(send, "ka", 0, 0, tiled=True)
     exch = pl.pallas_call(
@@ -334,20 +351,31 @@
         ],
         compiler_params=pltpu.CompilerParams(vmem_limit_bytes=32 * 1024 * 1024),
         name="exchange",
-    )(tab, own, p_big, full, w_hi, w_lo, c_full)
+    )(tab, own, big, full, w_hi, w_lo, c_full)
     both = pl.pallas_call(
-        combine_kernel,
-        out_shape=jax.ShapeDtypeStruct((npair + 2 * nk, 8, 128), F32),
+        collect_kernel,
+        out_shape=jax.ShapeDtypeStruct((2 * (npair + nk), 8, 128), F32),
         in_specs=[SMEM, *in_vmem(2)],
         out_specs=pl.BlockSpec(memory_space=pltpu.VMEM),
-        name="combine",
+        name="collect",
     )(own, exch, got)
     with jax.named_scope("copies"):
         whole = lax.all_gather(both, "ga", axis=0)
-        whole = jnp.transpose(whole, (1, 0, 2, 3)).reshape(npair + 2 * nk, nt, nt)
-        flipped = jnp.transpose(whole[: npair + nk], (0, 2, 1))
-        mirrored = flipped[npair:] + whole[npair + nk :]
-    return flipped[:npair].reshape(npair, nt * nt), mirrored.reshape(nk, nt * nt)
+    return pl.pallas_call(
+        finish_kernel,
+        out_shape=(
+            jax.ShapeDtypeStruct((npair, nt * nt), F32),
+            jax.ShapeDtypeStruct((nk, nt * nt), F32),
+        ),
+        in_specs=in_vmem(1),
+        out_specs=tuple(in_vmem(2)),
+        scratch_shapes=[
+            pltpu.VMEM((npair + nk, nt, nt), F32),
+            pltpu.VMEM((npair + nk, nt, nt), F32),
+            pltpu.VMEM(((npair + nk) * half, 2 * nt), F32),
+        ],
+        name="finish",
+    )(whole)
 
 
 def solution(mesh):

time: 206 us -> 216 us (1.049); the launches traced: 203 us -> 216 us
  blocking collectives: 58.2 us -> 88.6 us
  waiting for transfers between devices: 54.8 us -> 27.8 us
  local copies, waits for them, and re-layouts: 15.7 us -> 32.1 us
  starting transfers between devices: 16.3 us -> 26.1 us
  other arithmetic: 12.1 us -> 3.42 us
  Pallas kernels: 31.8 us -> 23.3 us
    all_gather x1, waiting for transfers between devices: 33.9 us -> 8.39 us  [per_device(): big = lax.all_gather(payload, 'ka', axis=0, tiled=True)]
    all_to_all x0 -> x1, blocking collectives: none -> 18.6 us  [per_device(): parts = lax.all_to_all(widen(jnp.stack(sent)), 'ga', 0, 0, tiled=True)]
    all_to_all x1, starting transfers between devices: 7.12 us -> 20.9 us  [per_device(): got = lax.all_to_all(send, 'ka', 0, 0, tiled=True)]
    all_gather x1, blocking collectives: 14.8 us -> 27.7 us  [per_device(): held = lax.all_gather(widen(held), 'ga', axis=1, tiled=True)]
    all_to_all x1 -> x0, waiting for transfers between devices: 10.7 us -> none  [per_device(): parts = lax.all_to_all(part, 'ga', 0, 0, tiled=True)]
    dynamic_update_slice x0 -> x5, local copies, waits for them, and re-layouts: none -> 10.3 us  [the longest x3 8.1 us: per_device(): wk = lax.dynamic_update_slice_in_dim(wk, v[:, None], (a + step) % 4, 1)]
    slice x7, local copies, waits for them, and re-layouts: 0.61 us -> 9.12 us  [the longest x1 3.33 us: per_device(): w[:, :, i * gl:(i + 1) * gl]]
    all_to_all x1, waiting for transfers between devices: 0.01 us -> 7.36 us  [per_device(): got = lax.all_to_all(send, 'ka', 0, 0, tiled=True)]
  transfers between devices with their start and end apart: 7 -> 6, of which waited for: 5 -> 3; matrix products, arithmetic and copies ran while one was open for 9% -> 13% of each run, Pallas kernels for 15% -> 2%
where the time goes in v3:
time: 216 us
  blocking collectives  88.6 us (41%)
  local copies, waits for them, and re-layouts  32.1 us (15%)
  waiting for transfers between devices  27.8 us (13%)
  starting transfers between devices  26.1 us (12%)
  Pallas kernels  23.3 us (11%)
  between operations  14.5 us (7%)
  other arithmetic  3.42 us (2%)
    all_gather x1, blocking collectives, per_device(): held = lax.all_gather(widen(held), 'ga', axis=1, tiled=True)  27.7 us
    all_gather x1, blocking collectives, per_device(): lax.all_gather(pairs, 'ka', axis=0, tiled=True).reshape(n_ka, npair, 3)  25.7 us
    all_to_all x1, starting transfers between devices, per_device(): got = lax.all_to_all(send, 'ka', 0, 0, tiled=True)  20.9 us
    all_to_all x1, blocking collectives, per_device(): parts = lax.all_to_all(widen(jnp.stack(sent)), 'ga', 0, 0, tiled=True)  18.6 us
    all_gather x1, blocking collectives, per_device(): whole = lax.all_gather(both, 'ga', axis=0)  16.6 us
    pallas_call x1, Pallas kernels, per_device(): pl.pallas_call(direct_kernel, out_shape=jax.ShapeDtypeStruct((n_ka, CAP +...  13.4 us
    ppermute x1, waiting for transfers between devices, per_device(): lax.ppermute(below[:1], 'ga', up)  12 us
    all_gather x1, waiting for transfers between devices, per_device(): big = lax.all_gather(payload, 'ka', axis=0, tiled=True)  8.39 us
  transfers between devices with their start and end apart: 6, of which 3 were waited for; matrix products, arithmetic and copies ran while one was open for 13% of the time, Pallas kernels for 2%

profile of v3, /device:TPU:0, one launch (start us, length us, event | category | flops | bytes accessed | tf_op | source)
XLA Modules:
  0.0 215.7 jit_solution(1582470148051900346)
XLA Ops:
  9.5 18.6 %all_to_all.10 = bf16[4,4,80,384]{3,2,1,0:T(8,128)(2,1)S(1)} all-to-all(bf16[4,4,80,384]{3,2,1,0:T(8,128)(2,1)S(1)} %fusion.15), channel_id=1, replica_groups=mesh['ka'=32,'ga'=4] {'ga'}, dimensions={0} | all-to-all | bytes 1966080 | tf_op jit(solution)/shard_map/pack/all_to_all | solution.py:248
  30.2 3.3 %fusion.42 = (bf16[2,375,375]{2,0,1:T(2,128)(2,1)S(1)}, bf16[2,375,375]{2,0,1:T(2,128)(2,1)S(1)}, bf16[2,375,375]{2,0,1:T(2,128)(2,1)S(1)}) fusion(bf16[2,375,1500]{2,0,1:T(2,128)(2,1)S(1)} %copy-done.3), kind=kLoop, calls=%fused_computation.122 | loop fusion | bytes 3375000 | tf_op jit(solution)/shard_map/weights/slice | solution.py:256
  35.0 1.6 pad.36
  36.6 1.2 collective-permute-start
  38.7 25.7 %all-gather.1 = s32[32,16,3]{1,2,0:T(4,128)S(1)} all-gather(s32[1,16,3]{1,2,0:T(4,128)S(1)} %bitcast.66), channel_id=1, replica_groups=mesh['ka'=32,'ga'=4] {'ka'}, dimensions={0}, use_global_device_ids=true | all-gather | bytes 6336 | tf_op jit(solution)/shard_map/tables/all_gather | solution.py:283
  67.4 6.5 %broadcast_in_dim.125 = bf16[2,4,384,1536]{3,2,1,0:T(8,128)(2,1)} broadcast(bf16[]{:T(256)} %constant.85.clone.1), dimensions={} | broadcast | bytes 9437186 | tf_op jit(solution)/shard_map/weights/broadcast_in_dim | solution.py:261
  73.9 1.5 bitcast_dynamic-update-slice_fusion.2
  75.5 27.7 %all_gather.17 = bf16[272,1536]{1,0:T(8,128)(2,1)S(1)} all-gather(bf16[272,384]{1,0:T(8,128)(2,1)S(1)} %fusion.26), channel_id=1, replica_groups=mesh['ka'=32,'ga'=4] {'ga'}, dimensions={1}, use_global_device_ids=true | all-gather | bytes 1044480 | tf_op jit(solution)/shard_map/exchange_pack/all_gather | solution.py:274
  103.2 1.3 slice.121
  104.7 1.7 slice.122
  106.3 3.0 %collective-permute-start.3 = (bf16[1,384,1536]{2,1,0:T(8,128)(2,1)S(1)}, bf16[1,384,1536]{2,1,0:T(8,128)(2,1)S(1)}, u32[]{:S(2)}, u32[]{:S(2)}) collective-permute-start(bf16[1,384,1536]{2,1,0:T(8,128)(2,1)S(1)} %slice.122), channel_id=1, source_target_pairs={{0,3},{1,0},{2,1},{3,2},{4,7},{5,4},{6,5},{7,6},{8,11},{9,8},{10,9... | collective-permute-start | bytes 3538952 | tf_op jit(solution)/shard_map/weights/ppermute | solution.py:260
  109.4 3.3 %bitcast_dynamic-update-slice_fusion.1 = bf16[2,4,384,1536]{3,2,1,0:T(8,128)(2,1)} fusion(bf16[2,4,384,1536]{3,2,1,0:T(8,128)(2,1)} %bitcast_dynamic-update-slice_fusion.2, s32[]{:T(128)S(6)} %select_n.138, bf16[2,384,1536]{2,1,0:T(8,128)(2,1)} %collective-permute-done), kind=kLoop, calls=%fused_computation.11 | loop fusion | bytes 4718596 | tf_op jit(solution)/shard_map/weights/dynamic_update_slice | solution.py:263
  112.7 3.2 %bitcast_dynamic-update-slice_fusion = bf16[2,4,384,1536]{3,2,1,0:T(8,128)(2,1)} fusion(bf16[2,4,384,1536]{3,2,1,0:T(8,128)(2,1)} %bitcast_dynamic-update-slice_fusion.1, s32[]{:T(128)S(6)} %select_n.140, bf16[2,384,1536]{2,1,0:T(8,128)(2,1)} %collective-permute-done.1), kind=kLoop, calls=%fused_computation.10 | loop fusion | bytes 4718596 | tf_op jit(solution)/shard_map/weights/dynamic_update_slice | solution.py:263
  115.9 12.0 %collective-permute-done.2 = bf16[1,384,1536]{2,1,0:T(8,128)(2,1)S(1)} collective-permute-done((bf16[1,384,1536]{2,1,0:T(8,128)(2,1)S(1)}, bf16[1,384,1536]{2,1,0:T(8,128)(2,1)S(1)}, u32[]{:S(2)}, u32[]{:S(2)}) %collective-permute-start.2) | collective-permute-done | bytes 1179680 | tf_op jit(solution)/shard_map/weights/ppermute | solution.py:260
  127.9 1.1 bitcast_dynamic-update-slice_fusion.4
  129.1 1.1 bitcast_dynamic-update-slice_fusion.3
  130.2 8.4 %all-gather.4.cloned.1.call-done.big = bf16[128,80,1536]{2,1,0:T(8,128)(2,1)} async-done(((bf16[4,80,1536]{2,1,0:T(8,128)(2,1)}), bf16[128,80,1536]{2,1,0:T(8,128)(2,1)}) %all-gather.4.cloned.1.call-update) | async-done | bytes 31457296 | tf_op jit(solution)/shard_map/spread/all_gather | solution.py:251
  138.6 13.4 %direct.1 = f32[32,6,8,128]{3,2,1,0:T(8,128)} custom-call(s32[7,64]{1,0:T(8,128)S(1)} %stack.44.tab, bf16[128,80,1536]{2,1,0:T(8,128)(2,1)} %all-gather.4.cloned.1.call-done.big, bf16[2,1536,1536]{2,1,0:T(8,128)(2,1)} %bitcast.29.w), custom_call_target="tpu_custom_call" | custom-call | tf_op jit(solution)/shard_map/direct/pallas_call | solution.py:320
  152.0 20.9 %all-to-all-start.1 = ((f32[32,6,8,128]{3,2,1,0:T(8,128)}), f32[32,6,8,128]{3,2,1,0:T(8,128)S(1)}, u32[]{:S(2)}, u32[]{:S(2)}) async-start(f32[32,6,8,128]{3,2,1,0:T(8,128)} %direct.1), calls=%async_computation.1 | async-start | bytes 1572864 | tf_op jit(solution)/shard_map/to_holders/all_to_all | solution.py:337
  173.5 5.2 %exchange.1.e = f32[20,8,128]{2,1,0:T(8,128)S(1)} custom-call(s32[7,64]{1,0:T(8,128)S(1)} %stack.44.tab, s32[4,16]{1,0:T(4,128)S(1)} %pad_add_fusion.own, bf16[128,80,1536]{2,1,0:T(8,128)(2,1)} %all-gather.4.cloned.1.call-done.big, bf16[256,1536]{1,0:T(8,128)(2,1)S(1)} %slice.119.mine, bf16[256,1536]{1,0:T(8,128)(2,1)S(1)} %get-tuple-element.24.whi, ...), custom_call_target="tpu_custom_call" | custom-call | tf_op jit(solution)/shard_map/exchange/pallas_call | solution.py:338
  179.4 7.4 %all-to-all-done.1.got = f32[32,6,8,128]{3,2,1,0:T(8,128)S(1)} async-done(((f32[32,6,8,128]{3,2,1,0:T(8,128)}), f32[32,6,8,128]{3,2,1,0:T(8,128)S(1)}, u32[]{:S(2)}, u32[]{:S(2)}) %all-to-all-start.1) | async-done | bytes 786464 | tf_op jit(solution)/shard_map/to_holders/all_to_all | solution.py:337
  187.7 1.9 collect.1
  189.6 16.6 %all-gather = f32[160,8,128]{2,1,0:T(8,128)} all-gather(f32[40,8,128]{2,1,0:T(8,128)} %collect.1), channel_id=2, replica_groups=mesh['ka'=32,'ga'=4] {'ga'}, dimensions={0}, use_global_device_ids=true | all-gather | bytes 819200 | tf_op jit(solution)/shard_map/copies/all_gather | solution.py:363
  206.2 2.7 %finish.1 = (f32[16,4096]{1,0:T(8,128)}, f32[4,4096]{1,0:T(4,128)}) custom-call(f32[4,40,8,128]{3,2,1,0:T(8,128)} %bitcast.61), custom_call_target="tpu_custom_call" | custom-call | tf_op jit(solution)/shard_map/finish/pallas_call | solution.py:364
  (82 shorter events, 11.7 us)
Async XLA Ops:
  7.2 131.4 %all-gather.4.cloned.1.call-start = ((), (), s32[]{:S(2)}) async-start(), calls=%async_computation.2 | async-start | bytes 32440320 | tf_op jit(solution)/shard_map/spread/all_gather | solution.py:251
  28.2 2.0 copy-start.3
  33.5 1.1 slice-start
  33.5 1.1 copy-start.8
  35.0 3.7 %copy-start.5 = (s32[16,3]{0,1:T(4,128)S(1)}, s32[16,3]{0,1:T(4,128)}, u32[]{:S(2)}) copy-start(s32[16,3]{0,1:T(4,128)} %param.12) | copy-start | bytes 580
  35.0 29.4 %copy-start.7 = (s32[64]{0:T(128)S(1)}, s32[64]{0:T(128)}, u32[]{:S(2)}) copy-start(s32[64]{0:T(128)} %param.13) | copy-start | bytes 772
  35.0 32.0 %copy-start.6 = (f32[375]{0:T(512)S(1)}, f32[375]{0:T(512)}, u32[]{:S(2)}) copy-start(f32[375]{0:T(512)} %param.10) | copy-start | bytes 4504
  35.0 32.3 %copy-start.4 = (bf16[4,64,375]{2,1,0:T(8,128)(2,1)S(1)}, bf16[4,64,375]{2,1,0:T(8,128)(2,1)}, u32[]{:S(2)}) copy-start(bf16[4,64,375]{2,1,0:T(8,128)(2,1)} %param.9) | copy-start | bytes 576004
  36.6 68.0 %collective-permute-start = (bf16[2,384,1536]{2,1,0:T(8,128)(2,1)}, bf16[2,384,1536]{2,1,0:T(8,128)(2,1)}, u32[]{:S(2)}, u32[]{:S(2)}) collective-permute-start(bf16[2,384,1536]{2,1,0:T(8,128)(2,1)} %pad.36), channel_id=1, source_target_pairs={{0,3},{1,0},{2,1},{3,2},{4,7},{5,4},{6,5},{7,6},{8,11},{9,8},{10,9... | collective-permute-start | bytes 7077896 | tf_op jit(solution)/shard_map/weights/ppermute | solution.py:259
  37.8 65.4 %collective-permute-start.1 = (bf16[2,384,1536]{2,1,0:T(8,128)(2,1)}, bf16[2,384,1536]{2,1,0:T(8,128)(2,1)}, u32[]{:S(2)}, u32[]{:S(2)}) collective-permute-start(bf16[2,384,1536]{2,1,0:T(8,128)(2,1)} %pad.36), channel_id=1, source_target_pairs={{0,1},{1,2},{2,3},{3,0},{4,5},{5,6},{6,7},{7,4},{8,9},{9,10},{10,1... | collective-permute-start | bytes 7077896 | tf_op jit(solution)/shard_map/weights/ppermute | solution.py:258
  104.6 23.3 %collective-permute-start.2 = (bf16[1,384,1536]{2,1,0:T(8,128)(2,1)S(1)}, bf16[1,384,1536]{2,1,0:T(8,128)(2,1)S(1)}, u32[]{:S(2)}, u32[]{:S(2)}) collective-permute-start(bf16[1,384,1536]{2,1,0:T(8,128)(2,1)S(1)} %slice.121), channel_id=1, source_target_pairs={{0,1},{1,2},{2,3},{3,0},{4,5},{5,6},{6,7},{7,4},{8,9},{9,10},{10,1... | collective-permute-start | bytes 3538952 | tf_op jit(solution)/shard_map/weights/ppermute | solution.py:260
  106.3 22.7 %collective-permute-start.3 = (bf16[1,384,1536]{2,1,0:T(8,128)(2,1)S(1)}, bf16[1,384,1536]{2,1,0:T(8,128)(2,1)S(1)}, u32[]{:S(2)}, u32[]{:S(2)}) collective-permute-start(bf16[1,384,1536]{2,1,0:T(8,128)(2,1)S(1)} %slice.122), channel_id=1, source_target_pairs={{0,3},{1,0},{2,1},{3,2},{4,7},{5,4},{6,5},{7,6},{8,11},{9,8},{10,9... | collective-permute-start | bytes 3538952 | tf_op jit(solution)/shard_map/weights/ppermute | solution.py:260
  152.0 34.8 %all-to-all-start.1 = ((f32[32,6,8,128]{3,2,1,0:T(8,128)}), f32[32,6,8,128]{3,2,1,0:T(8,128)S(1)}, u32[]{:S(2)}, u32[]{:S(2)}) async-start(f32[32,6,8,128]{3,2,1,0:T(8,128)} %direct.1), calls=%async_computation.1 | async-start | bytes 1572864 | tf_op jit(solution)/shard_map/to_holders/all_to_all | solution.py:337
  173.2 5.5 %copy-start.1 = (s32[4,16]{1,0:T(4,128)}, s32[4,16]{1,0:T(4,128)S(1)}, u32[]{:S(2)}) copy-start(s32[4,16]{1,0:T(4,128)S(1)} %pad_add_fusion.own) | copy-start | bytes 772
  178.8 0.6 copy-start
  186.8 0.9 copy-start.2
Sparse Core Ops, SparseCore 0:
  29.4 109.1 all-gather.3

commit v4 on v3

v4 whole, which is shorter than its diff:
```python
import jax
import jax.numpy as jnp
from jax import lax
from jax.experimental import pallas as pl
from jax.experimental.pallas import tpu as pltpu
from jax.sharding import PartitionSpec as P

CAP = 2
QW = 384
CH = 8
F32 = jnp.float32
BF16 = jnp.bfloat16
NT_DIMS = (((1,), (1,)), ((), ()))


def rank_in_group(owners):
    n = owners.shape[-1]
    same = owners[..., :, None] == owners[..., None, :]
    before = jnp.arange(n)[:, None] > jnp.arange(n)[None, :]
    return jnp.sum(jnp.logical_and(same, before).astype(jnp.int32), axis=-1)


def widen(v):
    return jnp.pad(v, ((0, 0),) * (v.ndim - 1) + ((0, QW - v.shape[-1]),))


def flat_tiles(tmp, rows):
    even = tmp[pl.ds(0, rows // 2, stride=2), :]
    odd = tmp[pl.ds(1, rows // 2, stride=2), :]
    return jnp.concatenate([even, odd], axis=1)


def direct_kernel(plan, big, wk, keep, away, w, xs, ys, prod, sw, sx, sy):
    half = prod.shape[0] // CH
    nt = 2 * half
    deep = xs.shape[3]
    nslot = keep.shape[0]
    chunks_first, chunks, parity = plan[3, 0], plan[3, 1], plan[3, 2]

    def x_copy(pos, buf, i):
        return pltpu.make_async_copy(big.at[plan[1, pos], pl.ds(0, nt)], xs.at[buf, i], sx.at[buf, i])

    def y_copy(pos, buf, i):
        return pltpu.make_async_copy(big.at[plan[2, pos], pl.ds(nt, nt)], ys.at[buf, i], sy.at[buf, i])

    def w_copy(slot):
        return pltpu.make_async_copy(wk.at[slot], w.at[slot], sw.at[slot])

    def begin(c, buf):
        for i in range(CH):
            x_copy(c * CH + i, buf, i).start()
            y_copy(c * CH + i, buf, i).start()

    @pl.when(chunks > 0)
    def _():
        begin(0, 0)

    for slot in range(w.shape[0]):
        w_copy(slot).start()
    for slot in range(w.shape[0]):
        w_copy(slot).wait()

    def chunk(c, carry):
        buf = lax.rem(c, 2)

        @pl.when(c + 1 < chunks)
        def _():
            begin(c + 1, 1 - buf)

        for i in range(CH):
            x_copy(c * CH + i, buf, i).wait()
            y_copy(c * CH + i, buf, i).wait()
        slot = jnp.where(c < chunks_first, 0, 1)
        u = jnp.dot(
            xs[buf, :, :half].reshape(CH * half, deep),
            w[slot, :deep],
            preferred_element_type=F32,
        )
        u = u + jnp.dot(
            xs[buf, :, half:].reshape(CH * half, deep),
            w[slot, deep:],
            preferred_element_type=F32,
        )
        y = ys[buf].reshape(CH * nt, deep)
        d = lax.dot_general(u.astype(BF16), y, NT_DIMS, preferred_element_type=F32)
        for i in range(CH * nt // 128):
            prod[nt * i : nt * i + nt] = d[nt * i : nt * i + nt, 128 * i : 128 * i + 128]
        quads = [prod[pl.ds(q, CH * half // 4, stride=4), :] for q in range(4)]
        for i in range(CH):
            t = plan[0, c * CH + i]
            tiles = []
            for h in range(2):
                lane = nt * i % 128 + half * h
                tiles.append(
                    jnp.concatenate(
                        [v[8 * i : 8 * i + 8, lane : lane + half] for v in quads], axis=1
                    )
                )

            @pl.when(t < nslot)
            def _():
                keep[t] = jnp.where(parity == 0, tiles[0], tiles[1])
                away[t] = jnp.where(parity == 0, tiles[1], tiles[0])

        return carry

    lax.fori_loop(0, chunks, chunk, 0)


def route_kernel(tab, keep, came, send):
    nk = send.shape[1] - CAP
    send[:, CAP:] = jnp.zeros((send.shape[0], nk, *send.shape[2:]), F32)
    for t in range(tab.shape[1]):
        v = keep[t] + came[t]
        send[t // CAP, t % CAP] = v

        @pl.when(tab[0, t] == 1)
        def _():
            owner = tab[2, t] // nk
            row = CAP + tab[2, t] % nk
            send[owner, row] = send[owner, row] + v


def exchange_kernel(tab, own, big, got, mine, whi, wlo, cw, out, p1, p2, tot, prod, flat, s1, s2):
    nslot = tab.shape[1]
    npair = own.shape[1]
    nk = tot.shape[0]
    rows = p2.shape[1]
    nt = mine.shape[0] // nk
    wide = p2.shape[2]

    def second(j):
        return pltpu.make_async_copy(big.at[own[1, j]], p2.at[j], s2.at[j])

    def first(t):
        return pltpu.make_async_copy(big.at[tab[6, t]], p1.at[t], s1.at[t])

    for j in range(npair):
        second(j).start()

    def begin(t, carry):
        @pl.when(tab[4, t] == 1)
        def _():
            first(t).start()

        return carry

    lax.fori_loop(0, nslot, begin, 0)
    tot[...] = jnp.zeros_like(tot)
    for j in range(npair):
        second(j).wait()
    b = p2[...].reshape(npair * rows, wide)
    e = lax.dot_general(b, whi[...], NT_DIMS, preferred_element_type=F32)
    e = e + lax.dot_general(b, wlo[...], NT_DIMS, preferred_element_type=F32)
    e = e + e
    for k in range(nk):
        prod[k] = e[:, k * nt : (k + 1) * nt]
    for j in range(npair):
        r = pl.ds(j * rows, rows)
        flat[r, :] = prod[own[0, j], r, :]

    def gather(t, carry):
        @pl.when(tab[4, t] == 1)
        def _():
            first(t).wait()
            k = tab[5, t]
            tot[k] = tot[k] + p1[t].astype(F32)

        return carry

    lax.fori_loop(0, nslot, gather, 0)
    w = tot[...].reshape(nk * rows, wide) * cw[...]
    hi = w.astype(BF16)
    lo = (w - hi.astype(F32)).astype(BF16)
    m = lax.dot_general(
        jnp.concatenate([hi, lo], axis=0), mine[...], NT_DIMS, preferred_element_type=F32
    )
    m = m[: nk * rows] + m[nk * rows :]
    m = m + m
    for k in range(nk):
        flat[pl.ds((npair + k) * rows, rows), :] = m[
            k * rows : (k + 1) * rows, k * nt : (k + 1) * nt
        ]
    z = flat_tiles(flat, (npair + nk) * rows)
    n = npair + nk
    for j in range(n):
        out[n + j] = z[8 * j : 8 * j + 8]
    for j in range(npair):
        out[j] = got[own[2, j], own[3, j]]
    for k in range(nk):
        out[npair + k] = jnp.sum(got[:, CAP + k], axis=0)


def finish_kernel(place, r0, r1, r2, r3, blocks, mirrored, whole, dmat, emat, rows):
    npair, nk = blocks.shape[0], mirrored.shape[0]
    nt = dmat.shape[1]
    half = nt // 2
    n = npair + nk
    for i, r in enumerate((r0, r1, r2, r3)):
        whole[place[i]] = r[...]
    for j in range(n):
        for a in range(2):
            left, right = whole[2 * a, j], whole[2 * a + 1, j]
            for q in range(4):
                cut = slice(half * q, half * (q + 1))
                dmat[j, pl.ds(half * a + q, 8, stride=4), :] = jnp.concatenate(
                    [left[:, cut], right[:, cut]], axis=1
                )
        for a in range(4):
            tile = whole[a, n + j]
            emat[j, pl.ds(16 * a, 8, stride=2), :] = tile[:, :nt]
            emat[j, pl.ds(16 * a + 1, 8, stride=2), :] = tile[:, nt:]
    for j in range(n):
        if j < npair:
            dmat[j] = emat[j].T - dmat[j]
        else:
            dmat[j] = (emat[j] - dmat[j]).T
        even = dmat[j, pl.ds(0, half, stride=2), :]
        odd = dmat[j, pl.ds(1, half, stride=2), :]
        rows[pl.ds(j * half, half), :] = jnp.concatenate([even, odd], axis=1)
    for r in range(half):
        lanes = pl.ds(2 * nt * r, 2 * nt)
        blocks[:, lanes] = rows[pl.ds(r, npair, stride=half), :]
        mirrored[:, lanes] = rows[pl.ds(npair * half + r, nk, stride=half), :]


def in_vmem(count):
    return [pl.BlockSpec(memory_space=pltpu.VMEM)] * count


SMEM = pl.BlockSpec(memory_space=pltpu.SMEM)
HBM = pl.BlockSpec(memory_space=pltpu.HBM)
ANY = pl.BlockSpec(memory_space=pl.ANY)


def per_device(x, y, p, coulomb, w, pairs, q_slot):
    n_ka = lax.axis_size("ka")
    me = lax.axis_index("ka")
    a = lax.axis_index("ga")
    nk, nt, gl = x.shape
    qs = w.shape[0]
    npair = pairs.shape[0]
    nslot = n_ka * CAP

    half, rows = nt // 2, nt // 4

    def shift(r):
        return [(i, (i + r) % 4) for i in range(4)]

    with jax.named_scope("pack"):
        y_far = lax.ppermute(y, "ga", [(i, 3 - i) for i in range(4)])
        cut = [jnp.where((a + r) % 4 < 2, x[:, :half], x[:, half:]) for r in range(4)]
        cut = cut[:1] + [lax.ppermute(cut[r], "ga", shift(r)) for r in range(1, 4)]
        payload = jnp.concatenate(
            [
                jnp.concatenate([widen(cut[0]), widen(cut[1])], axis=2),
                jnp.concatenate([widen(cut[2]), widen(cut[3])], axis=2),
                jnp.concatenate(
                    [widen(jnp.where(a < 2, y, y_far)), widen(jnp.where(a < 2, y_far, y))], axis=2
                ),
            ],
            axis=1,
        )
    with jax.named_scope("spread"):
        big = lax.all_gather(payload, "ka", axis=0, tiled=True)

    with jax.named_scope("weights"):
        cols = [
            jnp.pad(w[:, :, i * gl : (i + 1) * gl], ((0, 0), (0, QW - gl), (0, QW - gl)))
            for i in range(4)
        ]
        outer = jnp.concatenate([cols[0], cols[3]], axis=2)
        inner = jnp.concatenate([cols[1], cols[2]], axis=2)
        wk = []
        for r in range(4):
            to = (a + r) % 4
            v = jnp.where((to == 0) | (to == 3), outer, inner)
            wk.append(lax.ppermute(v, "ga", shift(r)) if r else v)
        wk = jnp.concatenate(wk, axis=1)

    with jax.named_scope("exchange_pack"):
        c1 = lax.reduce_precision(coulomb, 8, 7)
        c2 = lax.reduce_precision(coulomb - c1, 8, 7)
        c3 = coulomb - c1 - c2
        pieces = jnp.pad(jnp.stack([c1, c2, c3]).astype(BF16), ((0, 13), (0, 0)))
        held = jnp.concatenate([p.reshape(nk * nt, gl), pieces], axis=0)
        held = lax.all_gather(widen(held), "ga", axis=1, tiled=True)
        full = held[: nk * nt]
        p_rows = lax.dynamic_slice_in_dim(full.reshape(nk, nt, 4 * QW), a * rows, rows, axis=1)
        p_big = lax.all_gather(p_rows, "ka", axis=0, tiled=True)
        c_full = jnp.sum(held[nk * nt : nk * nt + 3].astype(F32), axis=0, keepdims=True)
        weighted = full.astype(F32) * c_full
        w_hi = lax.reduce_precision(weighted, 8, 7)
        w_lo = (weighted - w_hi).astype(BF16)
        w_hi = w_hi.astype(BF16)

    with jax.named_scope("tables"):
        every = lax.all_gather(pairs, "ka", axis=0, tiled=True).reshape(n_ka, npair, 3)

        def routes(rows):
            slot = jnp.sum(
                jnp.where(
                    rows[..., 2, None] == jnp.arange(q_slot.shape[0]), q_slot, 0
                ),
                axis=-1,
            )
            q_owner = slot // qs
            k_owner = rows[..., 1] // nk
            return slot % qs, q_owner, rank_in_group(q_owner), k_owner, rank_in_group(k_owner)

        local, q_owner, q_rank, k_owner, k_rank = routes(every)
        ranks = jnp.arange(CAP)
        hot_q = (q_owner == me)[..., None] & (q_rank[..., None] == ranks)
        hot_k = (k_owner == me)[..., None] & (k_rank[..., None] == ranks)

        def pick(hot, v):
            return jnp.sum(jnp.where(hot, v[..., None], 0), axis=1).reshape(nslot)

        ones = jnp.ones_like(local)
        tab = jnp.stack(
            [
                pick(hot_q, ones),
                pick(hot_q, every[..., 0]),
                pick(hot_q, every[..., 1]),
                pick(hot_q, local),
                pick(hot_k, ones),
                pick(hot_k, every[..., 1] - me * nk),
                pick(hot_k, every[..., 0]),
            ]
        )
        _, o1, r1, _, _ = routes(pairs)
        own = jnp.stack([pairs[:, 0] - me * nk, pairs[:, 1], o1, r1])

    with jax.named_scope("plan"):
        npos = nslot + qs * CH
        used, slot = tab[0], tab[3]
        same = (slot[:, None] == slot[None, :]) & (used[None, :] == 1)
        order = jnp.arange(nslot)
        rank = jnp.sum((same & (order[:, None] > order[None, :])).astype(jnp.int32), axis=1)
        first = jnp.sum(used * (slot == 0))
        second = jnp.sum(used * (slot == 1))
        chunks_first = (first + CH - 1) // CH
        chunks = chunks_first + (second + CH - 1) // CH
        pos = jnp.where(slot == 0, rank, chunks_first * CH + rank)
        hot = (pos[None, :] == jnp.arange(npos)[:, None]) & (used == 1)[None, :]

        def at_pos(v):
            return jnp.sum(jnp.where(hot, v[None, :], 0), axis=1)

        heads = jnp.pad(jnp.stack([chunks_first, chunks, a % 2]), (0, npos - 3))
        plan = jnp.stack([at_pos(order - nslot) + nslot, at_pos(tab[1]), at_pos(tab[2]), heads])
    keep, away = pl.pallas_call(
        direct_kernel,
        out_shape=(jax.ShapeDtypeStruct((nslot, 8, 128), F32),) * 2,
        in_specs=[SMEM, ANY, ANY],
        out_specs=tuple(in_vmem(2)),
        scratch_shapes=[
            pltpu.VMEM((qs, 4 * QW, 2 * QW), BF16),
            pltpu.VMEM((2, CH, nt, 2 * QW), BF16),
            pltpu.VMEM((2, CH, nt, 2 * QW), BF16),
            pltpu.VMEM((CH * half, 128), F32),
            pltpu.SemaphoreType.DMA((qs,)),
            pltpu.SemaphoreType.DMA((2, CH)),
            pltpu.SemaphoreType.DMA((2, CH)),
        ],
        compiler_params=pltpu.CompilerParams(vmem_limit_bytes=60 * 1024 * 1024),
        name="direct",
    )(plan, big, wk)
    with jax.named_scope("to_neighbour"):
        came = lax.ppermute(away, "ga", [(0, 1), (1, 0), (2, 3), (3, 2)])
    send = pl.pallas_call(
        route_kernel,
        out_shape=jax.ShapeDtypeStruct((n_ka, CAP + nk, 8, 128), F32),
        in_specs=[SMEM, *in_vmem(2)],
        out_specs=pl.BlockSpec(memory_space=pltpu.VMEM),
        name="route",
    )(tab, keep, came)
    with jax.named_scope("to_holders"):
        got = lax.all_to_all(send, "ka", 0, 0, tiled=True)
    both = pl.pallas_call(
        exchange_kernel,
        out_shape=jax.ShapeDtypeStruct((2 * (npair + nk), 8, 128), F32),
        in_specs=[SMEM, SMEM, HBM, *in_vmem(5)],
        out_specs=pl.BlockSpec(memory_space=pltpu.VMEM),
        scratch_shapes=[
            pltpu.VMEM((nslot, rows, 4 * QW), BF16),
            pltpu.VMEM((npair, rows, 4 * QW), BF16),
            pltpu.VMEM((nk, rows, 4 * QW), F32),
            pltpu.VMEM((nk, npair * rows, nt), F32),
            pltpu.VMEM(((npair + nk) * rows, nt), F32),
            pltpu.SemaphoreType.DMA((nslot,)),
            pltpu.SemaphoreType.DMA((npair,)),
        ],
        compiler_params=pltpu.CompilerParams(vmem_limit_bytes=60 * 1024 * 1024),
        name="exchange",
    )(tab, own, p_big, got, full, w_hi, w_lo, c_full)
    with jax.named_scope("copies"):
        others = [lax.ppermute(both, "ga", shift(r)) for r in range(1, 4)]
        place = jnp.stack([(a - r) % 4 for r in range(4)])
    return pl.pallas_call(
        finish_kernel,
        out_shape=(
            jax.ShapeDtypeStruct((npair, nt * nt), F32),
            jax.ShapeDtypeStruct((nk, nt * nt), F32),
        ),
        in_specs=[SMEM, *in_vmem(4)],
        out_specs=tuple(in_vmem(2)),
        scratch_shapes=[
            pltpu.VMEM((4, 2 * (npair + nk), 8, 128), F32),
            pltpu.VMEM((npair + nk, nt, nt), F32),
            pltpu.VMEM((npair + nk, nt, nt), F32),
            pltpu.VMEM(((npair + nk) * half, 2 * nt), F32),
        ],
        name="finish",
    )(place, both, *others)


def solution(mesh):
    in_specs = (
        P("ka", None, "ga"),
        P("ka", None, "ga"),
        P("ka", None, "ga"),
        P("ga"),
        P("ka", "ga", None),
        P("ka", None),
        P(),
    )
    out_specs = (P("ka", None), P("ka", None))
    return jax.shard_map(
        per_device, mesh=mesh, in_specs=in_specs, out_specs=out_specs, check_vma=False
    )
```

time: 216 us -> 207 us (0.958)
  blocking collectives: 88.6 us -> 40.2 us
  waiting for transfers between devices: 27.8 us -> 62.8 us
  local copies, waits for them, and re-layouts: 32.1 us -> 12.5 us
  other arithmetic: 3.42 us -> 17.5 us
  starting transfers between devices: 26.1 us -> 36.3 us
  Pallas kernels: 23.3 us -> 21.1 us
    ppermute x4 -> x11, waiting for transfers between devices: 12 us -> 32.5 us  [the longest x3 15.9 us: per_device(): wk.append(lax.ppermute(v, 'ga', shift(r)) if r else v)]
    all_to_all x1 -> x0, blocking collectives: 18.6 us -> none  [per_device(): parts = lax.all_to_all(widen(jnp.stack(sent)), 'ga', 0, 0, tiled=True)]
    all_gather x0 -> x1, waiting for transfers between devices: none -> 16.9 us  [per_device(): p_big = lax.all_gather(p_rows, 'ka', axis=0, tiled=True)]
    all_gather x1 -> x0, blocking collectives: 16.6 us -> none  [per_device(): whole = lax.all_gather(both, 'ga', axis=0)]
    all_gather x1, blocking collectives: 27.7 us -> 14.5 us  [per_device(): held = lax.all_gather(widen(held), 'ga', axis=1, tiled=True)]
    ppermute x4 -> x11, starting transfers between devices: 5.13 us -> 17.7 us  [the longest x3 5.07 us: per_device(): others = [lax.ppermute(both, 'ga', shift(r)) for r in range(1, 4)]]
    dynamic_update_slice x5 -> x0, local copies, waits for them, and re-layouts: 10.3 us -> none  [the longest x3 8.1 us: per_device(): wk = lax.dynamic_update_slice_in_dim(wk, v[:, None], (a + step) % 4, 1)]
    all_to_all x1, waiting for transfers between devices: 7.36 us -> 0.01 us  [per_device(): got = lax.all_to_all(send, 'ka', 0, 0, tiled=True)]
  transfers between devices with their start and end apart: 6 -> 14, of which waited for: 3 -> 9; matrix products, arithmetic and copies ran while one was open for 13% -> 13% of each run, Pallas kernels for 2% -> 5%
where the time goes in v4:
time: 207 us; the launch traced here: 206 us
  waiting for transfers between devices  62.8 us (30%)
  blocking collectives  40.2 us (19%)
  starting transfers between devices  36.3 us (18%)
  Pallas kernels  21.1 us (10%)
  other arithmetic  17.5 us (8%)
  between operations  15.7 us (8%)
  local copies, waits for them, and re-layouts  12.5 us (6%)
    all_gather x1, blocking collectives, per_device(): lax.all_gather(pairs, 'ka', axis=0, tiled=True).reshape(n_ka, npair, 3)  25.7 us
    all_to_all x1, starting transfers between devices, per_device(): got = lax.all_to_all(send, 'ka', 0, 0, tiled=True)  18.5 us
    all_gather x1, waiting for transfers between devices, per_device(): p_big = lax.all_gather(p_rows, 'ka', axis=0, tiled=True)  16.9 us
    ppermute x3, waiting for transfers between devices, per_device(): wk.append(lax.ppermute(v, 'ga', shift(r)) if r else v)  15.9 us
    all_gather x1, blocking collectives, per_device(): held = lax.all_gather(widen(held), 'ga', axis=1, tiled=True)  14.5 us
    all_gather x1, waiting for transfers between devices, per_device(): big = lax.all_gather(payload, 'ka', axis=0, tiled=True)  13.4 us
    pallas_call x1, Pallas kernels, per_device(): pl.pallas_call(direct_kernel, out_shape=(jax.ShapeDtypeStruct((nslot, 8,...  8.48 us
    ppermute x3, waiting for transfers between devices, per_device(): others = [lax.ppermute(both, 'ga', shift(r)) for r in range(1, 4)]  7.78 us
  transfers between devices with their start and end apart: 14, of which 9 were waited for; matrix products, arithmetic and copies ran while one was open for 13% of the time, Pallas kernels for 5%

profile of v4, /device:TPU:0, one launch (start us, length us, event | category | flops | bytes accessed | tf_op | source)
XLA Modules:
  0.0 206.2 jit_solution(9529046012132325991)
XLA Ops:
  7.2 2.9 %collective-permute-start.3 = (bf16[4,64,375]{2,1,0:T(8,128)(2,1)}, bf16[4,64,375]{2,1,0:T(8,128)(2,1)S(1)}, u32[]{:S(2)}, u32[]{:S(2)}) collective-permute-start(bf16[4,64,375]{2,1,0:T(8,128)(2,1)} %param.8), channel_id=1, source_target_pairs={{0,3},{1,2},{2,1},{3,0},{4,7},{5,6},{6,5},{7,4},{8,11},{9,10},{10,... | collective-permute-start | bytes 576008 | tf_op jit(solution)/shard_map/pack/ppermute | solution.py:251
  11.4 1.6 collective-permute-start.1
  13.0 1.6 collective-permute-start.2
  14.6 3.4 %collective-permute-done.3 = bf16[4,64,375]{2,1,0:T(8,128)(2,1)S(1)} collective-permute-done((bf16[4,64,375]{2,1,0:T(8,128)(2,1)}, bf16[4,64,375]{2,1,0:T(8,128)(2,1)S(1)}, u32[]{:S(2)}, u32[]{:S(2)}) %collective-permute-start.3) | collective-permute-done | bytes 192032 | tf_op jit(solution)/shard_map/pack/ppermute | solution.py:251
  20.6 14.5 %all_gather.13 = bf16[272,1536]{1,0:T(8,128)(2,1)S(1)} all-gather(bf16[272,384]{1,0:T(8,128)(2,1)S(1)} %fusion.33), channel_id=1, replica_groups=mesh['ka'=32,'ga'=4] {'ga'}, dimensions={1}, use_global_device_ids=true | all-gather | bytes 1044480 | tf_op jit(solution)/shard_map/exchange_pack/all_gather | solution.py:287
  36.0 5.1 %fusion.53 = (bf16[2,375,375]{2,0,1:T(2,128)(2,1)S(1)}, bf16[2,375,375]{2,0,1:T(2,128)(2,1)S(1)}, bf16[2,375,375]{2,0,1:T(2,128)(2,1)S(1)}, bf16[2,375,375]{2,0,1:T(2,128)(2,1)S(1)}) fusion(bf16[2,375,1500]{2,0,1:T(2,128)(2,1)} %param.11), kind=kLoop, calls=%fused_computation.148 | loop fusion | bytes 4500000 | tf_op jit(solution)/shard_map/weights/slice | solution.py:269
  41.5 2.4 %broadcast_select_fusion.3 = (bf16[2,384,768]{2,1,0:T(8,128)(2,1)}, bf16[2,384,768]{2,1,0:T(8,128)(2,1)}, bf16[2,384,768]{2,1,0:T(8,128)(2,1)}) fusion(pred[]{:T(512)S(6)} %or.12, bf16[2,375,375]{2,1,0:T(8,128)(2,1)S(1)} %copy.84, bf16[2,375,375]{2,1,0:T(8,128)(2,1)S(1)} %copy.83, bf16[2,375,375]{2,1,0:T(8,128)(2,1)S(1)} %copy.82, ...), kind=kLoop, calls=%fused_computation.39 | loop fusion | flops 10027008 | bytes 5788947 | tf_op jit(solution)/shard_map/weights/jit(_where)/select_n | solution.py:277
  43.8 2.0 collective-permute-start.4
  45.8 2.5 %collective-permute-start.5 = (bf16[2,384,768]{2,1,0:T(8,128)(2,1)}, bf16[2,384,768]{2,1,0:T(8,128)(2,1)}, u32[]{:S(2)}, u32[]{:S(2)}) collective-permute-start(bf16[2,384,768]{2,1,0:T(8,128)(2,1)} %get-tuple-element.27), channel_id=1, source_target_pairs={{0,2},{1,3},{2,0},{3,1},{4,6},{5,7},{6,4},{7,5},{8,10},{9,11},{10,... | collective-permute-start | bytes 3538952 | tf_op jit(solution)/shard_map/weights/ppermute | solution.py:278
  49.9 25.7 %all-gather = s32[32,16,3]{1,2,0:T(4,128)S(1)} all-gather(s32[1,16,3]{1,2,0:T(4,128)S(1)} %bitcast.46), channel_id=1, replica_groups=mesh['ka'=32,'ga'=4] {'ka'}, dimensions={0}, use_global_device_ids=true | all-gather | bytes 6336 | tf_op jit(solution)/shard_map/tables/all_gather | solution.py:298
  80.8 15.4 %collective-permute-done.4 = bf16[2,384,768]{2,1,0:T(8,128)(2,1)} collective-permute-done((bf16[2,384,768]{2,1,0:T(8,128)(2,1)}, bf16[2,384,768]{2,1,0:T(8,128)(2,1)}, u32[]{:S(2)}, u32[]{:S(2)}) %collective-permute-start.4) | collective-permute-done | bytes 1179680 | tf_op jit(solution)/shard_map/weights/ppermute | solution.py:278
  96.7 5.2 %pad_maximum_fusion.wk = bf16[2,1536,768]{2,1,0:T(8,128)(2,1)} fusion(bf16[2,384,768]{2,1,0:T(8,128)(2,1)S(1)} %collective-permute-done.6, bf16[2,384,768]{2,1,0:T(8,128)(2,1)} %collective-permute-done.5, bf16[2,384,768]{2,1,0:T(8,128)(2,1)} %collective-permute-done.4, bf16[2,384,768]{2,1,0:T(8,128)(2,1)} %get-tuple-element.25), kind=kLoop, calls=%fused_computation | loop fusion | flops 18874368 | bytes 9437184 | tf_op jit(solution)/shard_map/weights/concatenate | solution.py:279
  101.9 13.4 %all-gather.6.cloned.1.call-done.big = bf16[128,128,768]{2,1,0:T(8,128)(2,1)} async-done(((bf16[4,128,768]{2,1,0:T(8,128)(2,1)}), bf16[128,128,768]{2,1,0:T(8,128)(2,1)}) %all-gather.6.cloned.1.call-update) | async-done | bytes 25165840 | tf_op jit(solution)/shard_map/spread/all_gather | solution.py:265
  115.3 8.5 %direct.1 = (f32[64,8,128]{2,1,0:T(8,128)}, f32[64,8,128]{2,1,0:T(8,128)}) custom-call(s32[4,80]{1,0:T(4,128)} %pad_add_fusion.1.plan, bf16[128,128,768]{2,1,0:T(8,128)(2,1)} %all-gather.6.cloned.1.call-done.big, bf16[2,1536,768]{2,1,0:T(8,128)(2,1)} %pad_maximum_fusion.wk), custom_call_target="tpu_custom_call" | custom-call | tf_op jit(solution)/shard_map/direct/pallas_call | solution.py:352
  127.1 5.0 %collective-permute-done.7.came = f32[64,8,128]{2,1,0:T(8,128)S(1)} collective-permute-done((f32[64,8,128]{2,1,0:T(8,128)}, f32[64,8,128]{2,1,0:T(8,128)S(1)}, u32[]{:S(2)}, u32[]{:S(2)}) %collective-permute-start.7) | collective-permute-done | bytes 262176 | tf_op jit(solution)/shard_map/to_neighbour/ppermute | solution.py:370
  132.8 2.5 %route.1 = f32[32,6,8,128]{3,2,1,0:T(8,128)} custom-call(s32[7,64]{1,0:T(8,128)} %stack.72.tab, f32[64,8,128]{2,1,0:T(8,128)} %get-tuple-element.4.keep, f32[64,8,128]{2,1,0:T(8,128)} %copy-done.2), custom_call_target="tpu_custom_call" | custom-call | tf_op jit(solution)/shard_map/route/pallas_call | solution.py:371
  135.3 18.5 %all-to-all-start = ((f32[32,6,8,128]{3,2,1,0:T(8,128)}), f32[32,6,8,128]{3,2,1,0:T(8,128)S(1)}, u32[]{:S(2)}, u32[]{:S(2)}) async-start(f32[32,6,8,128]{3,2,1,0:T(8,128)} %route.1), calls=%async_computation | async-start | bytes 1572864 | tf_op jit(solution)/shard_map/to_holders/all_to_all | solution.py:379
  156.7 16.9 %all-gather.4.cloned.1.call-done.big = bf16[128,16,1536]{2,1,0:T(8,128)(2,1)} async-done(((bf16[4,16,1536]{2,1,0:T(8,128)(2,1)}), bf16[128,16,1536]{2,1,0:T(8,128)(2,1)}) %all-gather.4.cloned.1.call-update) | async-done | bytes 6291472 | tf_op jit(solution)/shard_map/exchange_pack/all_gather | solution.py:290
  174.5 7.3 %exchange.1.r0 = f32[40,8,128]{2,1,0:T(8,128)} custom-call(s32[7,64]{1,0:T(8,128)} %stack.72.tab, s32[4,16]{1,0:T(4,128)} %pad_add_fusion.own, bf16[128,16,1536]{2,1,0:T(8,128)(2,1)} %all-gather.4.cloned.1.call-done.big, f32[32,6,8,128]{3,2,1,0:T(8,128)} %copy-done.1, bf16[256,1536]{1,0:T(8,128)(2,1)} %copy-done, bf16[256,1536]{1,0:T(8,128)(2,1)} %get-tuple-element.33.whi, ...), custom_call_target="tpu_custom_call" | custom-call | tf_op jit(solution)/shard_map/exchange/pallas_call | solution.py:380
  181.8 2.8 %collective-permute-start.10 = (f32[40,8,128]{2,1,0:T(8,128)}, f32[40,8,128]{2,1,0:T(8,128)S(1)}, u32[]{:S(2)}, u32[]{:S(2)}) collective-permute-start(f32[40,8,128]{2,1,0:T(8,128)} %exchange.1.r0), channel_id=1, source_target_pairs={{0,3},{1,0},{2,1},{3,2},{4,7},{5,4},{6,5},{7,6},{8,11},{9,8},{10,9... | collective-permute-start | bytes 491528 | tf_op jit(solution)/shard_map/copies/ppermute | solution.py:398
  184.6 2.3 %collective-permute-start.9 = (f32[40,8,128]{2,1,0:T(8,128)}, f32[40,8,128]{2,1,0:T(8,128)S(1)}, u32[]{:S(2)}, u32[]{:S(2)}) collective-permute-start(f32[40,8,128]{2,1,0:T(8,128)} %exchange.1.r0), channel_id=1, source_target_pairs={{0,2},{1,3},{2,0},{3,1},{4,6},{5,7},{6,4},{7,5},{8,10},{9,11},{10,... | collective-permute-start | bytes 491528 | tf_op jit(solution)/shard_map/copies/ppermute | solution.py:398
  187.5 4.5 %collective-permute-done.10.r3 = f32[40,8,128]{2,1,0:T(8,128)S(1)} collective-permute-done((f32[40,8,128]{2,1,0:T(8,128)}, f32[40,8,128]{2,1,0:T(8,128)S(1)}, u32[]{:S(2)}, u32[]{:S(2)}) %collective-permute-start.10) | collective-permute-done | bytes 163872 | tf_op jit(solution)/shard_map/copies/ppermute | solution.py:398
  192.0 3.3 %collective-permute-done.8.r1 = f32[40,8,128]{2,1,0:T(8,128)S(1)} collective-permute-done((f32[40,8,128]{2,1,0:T(8,128)}, f32[40,8,128]{2,1,0:T(8,128)S(1)}, u32[]{:S(2)}, u32[]{:S(2)}) %collective-permute-start.8) | collective-permute-done | bytes 163872 | tf_op jit(solution)/shard_map/copies/ppermute | solution.py:398
  196.6 2.8 %finish.1 = (f32[16,4096]{1,0:T(8,128)}, f32[4,4096]{1,0:T(4,128)}) custom-call(s32[4]{0:T(128)} %pad_add_fusion.2.place, f32[40,8,128]{2,1,0:T(8,128)} %exchange.1.r0, f32[40,8,128]{2,1,0:T(8,128)} %copy-done.5, f32[40,8,128]{2,1,0:T(8,128)} %copy-done.6, f32[40,8,128]{2,1,0:T(8,128)} %copy-done.4), custom_call_target="tpu_custom_call" | custom-call | tf_op jit(solution)/shard_map/finish/pallas_call | solution.py:400
  (103 shorter events, 20.6 us)
Async XLA Ops:
  7.2 108.2 %all-gather.6.cloned.1.call-start = ((), (), s32[]{:S(2)}) async-start(), calls=%async_computation.2 | async-start | bytes 25952256 | tf_op jit(solution)/shard_map/spread/all_gather | solution.py:265
  7.2 10.8 %collective-permute-start.3 = (bf16[4,64,375]{2,1,0:T(8,128)(2,1)}, bf16[4,64,375]{2,1,0:T(8,128)(2,1)S(1)}, u32[]{:S(2)}, u32[]{:S(2)}) collective-permute-start(bf16[4,64,375]{2,1,0:T(8,128)(2,1)} %param.8), channel_id=1, source_target_pairs={{0,3},{1,2},{2,1},{3,0},{4,7},{5,6},{6,5},{7,4},{8,11},{9,10},{10,... | collective-permute-start | bytes 576008 | tf_op jit(solution)/shard_map/pack/ppermute | solution.py:251
  11.1 8.3 %collective-permute-start = (bf16[4,32,375]{2,1,0:T(8,128)(2,1)S(1)}, bf16[4,32,375]{2,1,0:T(8,128)(2,1)S(1)}, u32[]{:S(2)}, u32[]{:S(2)}) collective-permute-start(bf16[4,32,375]{2,1,0:T(8,128)(2,1)S(1)} %get-tuple-element.39), channel_id=1, source_target_pairs={{0,1},{1,2},{2,3},{3,0},{4,5},{5,6},{6,7},{7,4},{8,9},{9,10},{10,1... | collective-permute-start | bytes 288008 | tf_op jit(solution)/shard_map/pack/ppermute | solution.py:253
  11.4 8.1 %collective-permute-start.1 = (bf16[4,32,375]{2,1,0:T(8,128)(2,1)S(1)}, bf16[4,32,375]{2,1,0:T(8,128)(2,1)S(1)}, u32[]{:S(2)}, u32[]{:S(2)}) collective-permute-start(bf16[4,32,375]{2,1,0:T(8,128)(2,1)S(1)} %get-tuple-element.37), channel_id=1, source_target_pairs={{0,2},{1,3},{2,0},{3,1},{4,6},{5,7},{6,4},{7,5},{8,10},{9,11},{10,... | collective-permute-start | bytes 288008 | tf_op jit(solution)/shard_map/pack/ppermute | solution.py:253
  13.0 6.4 %collective-permute-start.2 = (bf16[4,32,375]{2,1,0:T(8,128)(2,1)S(1)}, bf16[4,32,375]{2,1,0:T(8,128)(2,1)S(1)}, u32[]{:S(2)}, u32[]{:S(2)}) collective-permute-start(bf16[4,32,375]{2,1,0:T(8,128)(2,1)S(1)} %get-tuple-element.38), channel_id=1, source_target_pairs={{0,3},{1,0},{2,1},{3,2},{4,7},{5,4},{6,5},{7,6},{8,11},{9,8},{10,9... | collective-permute-start | bytes 288008 | tf_op jit(solution)/shard_map/pack/ppermute | solution.py:253
  14.6 5.9 %copy-start.8 = (f32[375]{0:T(512)S(1)}, f32[375]{0:T(512)}, u32[]{:S(2)}) copy-start(f32[375]{0:T(512)} %param.10) | copy-start | bytes 4504
  14.6 6.0 %copy-start.3 = (bf16[4,64,375]{2,1,0:T(8,128)(2,1)S(1)}, bf16[4,64,375]{2,1,0:T(8,128)(2,1)}, u32[]{:S(2)}) copy-start(bf16[4,64,375]{2,1,0:T(8,128)(2,1)} %param.9) | copy-start | bytes 576004
  20.5 153.1 %all-gather.4.cloned.1.call-start = ((), (), s32[]{:S(2)}) async-start(), calls=%async_computation.1 | async-start | bytes 6488064 | tf_op jit(solution)/shard_map/exchange_pack/all_gather | solution.py:290
  35.2 5.9 %copy-start = (bf16[256,1536]{1,0:T(8,128)(2,1)}, bf16[256,1536]{1,0:T(8,128)(2,1)S(1)}, u32[]{:S(2)}) copy-start(bf16[256,1536]{1,0:T(8,128)(2,1)S(1)} %slice.68.mine) | copy-start | bytes 2359300
  43.8 52.4 %collective-permute-start.4 = (bf16[2,384,768]{2,1,0:T(8,128)(2,1)}, bf16[2,384,768]{2,1,0:T(8,128)(2,1)}, u32[]{:S(2)}, u32[]{:S(2)}) collective-permute-start(bf16[2,384,768]{2,1,0:T(8,128)(2,1)} %get-tuple-element.26), channel_id=1, source_target_pairs={{0,1},{1,2},{2,3},{3,0},{4,5},{5,6},{6,7},{7,4},{8,9},{9,10},{10,1... | collective-permute-start | bytes 3538952 | tf_op jit(solution)/shard_map/weights/ppermute | solution.py:278
  45.8 50.4 %collective-permute-start.5 = (bf16[2,384,768]{2,1,0:T(8,128)(2,1)}, bf16[2,384,768]{2,1,0:T(8,128)(2,1)}, u32[]{:S(2)}, u32[]{:S(2)}) collective-permute-start(bf16[2,384,768]{2,1,0:T(8,128)(2,1)} %get-tuple-element.27), channel_id=1, source_target_pairs={{0,2},{1,3},{2,0},{3,1},{4,6},{5,7},{6,4},{7,5},{8,10},{9,11},{10,... | collective-permute-start | bytes 3538952 | tf_op jit(solution)/shard_map/weights/ppermute | solution.py:278
  48.3 1.6 copy-start.7
  48.3 27.4 %copy-start.9 = (s32[64]{0:T(128)S(1)}, s32[64]{0:T(128)}, u32[]{:S(2)}) copy-start(s32[64]{0:T(128)} %param.13) | copy-start | bytes 772
  49.7 47.0 %collective-permute-start.6 = (bf16[2,384,768]{2,1,0:T(8,128)(2,1)}, bf16[2,384,768]{2,1,0:T(8,128)(2,1)S(1)}, u32[]{:S(2)}, u32[]{:S(2)}) collective-permute-start(bf16[2,384,768]{2,1,0:T(8,128)(2,1)} %broadcast_select_fusion), channel_id=1, source_target_pairs={{0,3},{1,0},{2,1},{3,2},{4,7},{5,4},{6,5},{7,6},{8,11},{9,8},{10,9... | collective-permute-start | bytes 3538952 | tf_op jit(solution)/shard_map/weights/ppermute | solution.py:278
  123.8 8.2 %collective-permute-start.7 = (f32[64,8,128]{2,1,0:T(8,128)}, f32[64,8,128]{2,1,0:T(8,128)S(1)}, u32[]{:S(2)}, u32[]{:S(2)}) collective-permute-start(f32[64,8,128]{2,1,0:T(8,128)} %get-tuple-element.5), channel_id=1, source_target_pairs={{0,1},{1,0},{2,3},{3,2},{4,5},{5,4},{6,7},{7,6},{8,9},{9,8},{10,11... | collective-permute-start | bytes 786440 | tf_op jit(solution)/shard_map/to_neighbour/ppermute | solution.py:370
  132.0 0.7 copy-start.2
  135.3 38.3 %all-to-all-start = ((f32[32,6,8,128]{3,2,1,0:T(8,128)}), f32[32,6,8,128]{3,2,1,0:T(8,128)S(1)}, u32[]{:S(2)}, u32[]{:S(2)}) async-start(f32[32,6,8,128]{3,2,1,0:T(8,128)} %route.1), calls=%async_computation | async-start | bytes 1572864 | tf_op jit(solution)/shard_map/to_holders/all_to_all | solution.py:379
  173.6 0.9 copy-start.1
  181.8 10.2 %collective-permute-start.10 = (f32[40,8,128]{2,1,0:T(8,128)}, f32[40,8,128]{2,1,0:T(8,128)S(1)}, u32[]{:S(2)}, u32[]{:S(2)}) collective-permute-start(f32[40,8,128]{2,1,0:T(8,128)} %exchange.1.r0), channel_id=1, source_target_pairs={{0,3},{1,0},{2,1},{3,2},{4,7},{5,4},{6,5},{7,6},{8,11},{9,8},{10,9... | collective-permute-start | bytes 491528 | tf_op jit(solution)/shard_map/copies/ppermute | solution.py:398
  184.6 10.7 %collective-permute-start.8 = (f32[40,8,128]{2,1,0:T(8,128)}, f32[40,8,128]{2,1,0:T(8,128)S(1)}, u32[]{:S(2)}, u32[]{:S(2)}) collective-permute-start(f32[40,8,128]{2,1,0:T(8,128)} %exchange.1.r0), channel_id=1, source_target_pairs={{0,1},{1,2},{2,3},{3,0},{4,5},{5,6},{6,7},{7,4},{8,9},{9,10},{10,1... | collective-permute-start | bytes 491528 | tf_op jit(solution)/shard_map/copies/ppermute | solution.py:398
  184.6 10.7 %collective-permute-start.9 = (f32[40,8,128]{2,1,0:T(8,128)}, f32[40,8,128]{2,1,0:T(8,128)S(1)}, u32[]{:S(2)}, u32[]{:S(2)}) collective-permute-start(f32[40,8,128]{2,1,0:T(8,128)} %exchange.1.r0), channel_id=1, source_target_pairs={{0,2},{1,3},{2,0},{3,1},{4,6},{5,7},{6,4},{7,5},{8,10},{9,11},{10,... | collective-permute-start | bytes 491528 | tf_op jit(solution)/shard_map/copies/ppermute | solution.py:398
  192.0 3.3 %copy-start.4 = (f32[40,8,128]{2,1,0:T(8,128)}, f32[40,8,128]{2,1,0:T(8,128)S(1)}, u32[]{:S(2)}) copy-start(f32[40,8,128]{2,1,0:T(8,128)S(1)} %collective-permute-done.10.r3) | copy-start | bytes 491524
  195.3 0.7 copy-start.5
  195.9 0.7 copy-start.6
Sparse Core Ops, SparseCore 0:
  20.6 94.6 all-gather.5
  117.6 55.9 all-gather.3

commit v5 on v4

--- a/solution.py
+++ b/solution.py
@@ -30,7 +30,7 @@
     return jnp.concatenate([even, odd], axis=1)
 
 
-def direct_kernel(plan, big, wk, keep, away, w, xs, ys, prod, sw, sx, sy):
+def direct_kernel(plan, big, w, keep, away, xs, ys, us, prod, kept, sent, sx, sy):
     half = prod.shape[0] // CH
     nt = 2 * half
     deep = xs.shape[3]
@@ -43,75 +43,87 @@
     def y_copy(pos, buf, i):
         return pltpu.make_async_copy(big.at[plan[2, pos], pl.ds(nt, nt)], ys.at[buf, i], sy.at[buf, i])
 
-    def w_copy(slot):
-        return pltpu.make_async_copy(wk.at[slot], w.at[slot], sw.at[slot])
-
-    def begin(c, buf):
+    def begin(c):
         for i in range(CH):
-            x_copy(c * CH + i, buf, i).start()
-            y_copy(c * CH + i, buf, i).start()
+            x_copy(c * CH + i, lax.rem(c, 2), i).start()
+            y_copy(c * CH + i, lax.rem(c, 3), i).start()
+
+    def products(c):
+        u = us[lax.rem(c + 2, 2)]
+        y = ys[lax.rem(c + 3, 3)].reshape(CH * nt, deep)
+        for i in range(0, CH, 4):
+            d = lax.dot_general(
+                u[half * i : half * (i + 4)],
+                y[nt * i : nt * (i + 4)],
+                NT_DIMS,
+                preferred_element_type=F32,
+            )
+            for j in range(2):
+                prod[half * i + nt * j : half * i + nt * j + nt] = d[
+                    nt * j : nt * j + nt, 128 * j : 128 * j + 128
+                ]
+        lane = lax.broadcasted_iota(jnp.int32, (8, 128), 1)
+        for i in range(CH):
+            t = jnp.where(c < 0, nslot, plan[0, jnp.maximum(c, 0) * CH + i])
+            rows = [prod[half * i + 8 * g : half * i + 8 * g + 8] for g in range(4)]
+            tiles = []
+            for h in range(2):
+                start = nt * (i % 2) + half * h
+                moved = [pltpu.roll(v, (half * g - start) % 128, 1) for g, v in enumerate(rows)]
+                low = jnp.where(lane < half, moved[0], moved[1])
+                high = jnp.where(lane < 3 * half, moved[2], moved[3])
+                tiles.append(jnp.where(lane < nt, low, high))
+            kept[t] = jnp.where(parity == 0, tiles[0], tiles[1])
+            sent[t] = jnp.where(parity == 0, tiles[1], tiles[0])
 
     @pl.when(chunks > 0)
     def _():
-        begin(0, 0)
-
-    for slot in range(w.shape[0]):
-        w_copy(slot).start()
-    for slot in range(w.shape[0]):
-        w_copy(slot).wait()
+        begin(0)
 
     def chunk(c, carry):
-        buf = lax.rem(c, 2)
-
         @pl.when(c + 1 < chunks)
         def _():
-            begin(c + 1, 1 - buf)
-
+            begin(c + 1)
+
+        bx, by = lax.rem(c, 2), lax.rem(c, 3)
         for i in range(CH):
-            x_copy(c * CH + i, buf, i).wait()
-            y_copy(c * CH + i, buf, i).wait()
+            x_copy(c * CH + i, bx, i).wait()
+            y_copy(c * CH + i, by, i).wait()
+        products(c - 1)
         slot = jnp.where(c < chunks_first, 0, 1)
         u = jnp.dot(
-            xs[buf, :, :half].reshape(CH * half, deep),
-            w[slot, :deep],
-            preferred_element_type=F32,
+            xs[bx, :, :half].reshape(CH * half, deep), w[slot, :deep], preferred_element_type=F32
         )
         u = u + jnp.dot(
-            xs[buf, :, half:].reshape(CH * half, deep),
-            w[slot, deep:],
-            preferred_element_type=F32,
+            xs[bx, :, half:].reshape(CH * half, deep), w[slot, deep:], preferred_element_type=F32
         )
-        y = ys[buf].reshape(CH * nt, deep)
-        d = lax.dot_general(u.astype(BF16), y, NT_DIMS, preferred_element_type=F32)
-        for i in range(CH * nt // 128):
-            prod[nt * i : nt * i + nt] = d[nt * i : nt * i + nt, 128 * i : 128 * i + 128]
-        quads = [prod[pl.ds(q, CH * half // 4, stride=4), :] for q in range(4)]
-        for i in range(CH):
-            t = plan[0, c * CH + i]
-            tiles = []
-            for h in range(2):
-                lane = nt * i % 128 + half * h
-                tiles.append(
-                    jnp.concatenate(
-                        [v[8 * i : 8 * i + 8, lane : lane + half] for v in quads], axis=1
-                    )
-                )
-
-            @pl.when(t < nslot)
-            def _():
-                keep[t] = jnp.where(parity == 0, tiles[0], tiles[1])
-                away[t] = jnp.where(parity == 0, tiles[1], tiles[0])
-
+        us[bx] = u.astype(BF16)
         return carry
 
     lax.fori_loop(0, chunks, chunk, 0)
 
-
-def route_kernel(tab, keep, came, send):
+    @pl.when(chunks > 0)
+    def _():
+        products(chunks - 1)
+
+    keep[...] = kept[:nslot]
+    away[...] = sent[:nslot]
+
+
+def route_kernel(tab, keep, came, exch, send, done, mine, theirs, sem):
+    copies = [
+        pltpu.make_async_copy(keep, mine, sem.at[0]),
+        pltpu.make_async_copy(came, theirs, sem.at[1]),
+    ]
+    for c in copies:
+        c.start()
     nk = send.shape[1] - CAP
     send[:, CAP:] = jnp.zeros((send.shape[0], nk, *send.shape[2:]), F32)
+    done[...] = exch[...]
+    for c in copies:
+        c.wait()
     for t in range(tab.shape[1]):
-        v = keep[t] + came[t]
+        v = mine[t] + theirs[t]
         send[t // CAP, t % CAP] = v
 
         @pl.when(tab[0, t] == 1)
@@ -121,19 +133,20 @@
             send[owner, row] = send[owner, row] + v
 
 
-def exchange_kernel(tab, own, big, got, mine, whi, wlo, cw, out, p1, p2, tot, prod, flat, s1, s2):
+def exchange_kernel(tab, own, big, full, whi, wlo, cw, out, p1, p2, tot, prod, flat, s1, s2):
     nslot = tab.shape[1]
     npair = own.shape[1]
     nk = tot.shape[0]
-    rows = p2.shape[1]
-    nt = mine.shape[0] // nk
-    wide = p2.shape[2]
+    rows = p2.shape[1] // 2
+    nt = whi.shape[0] // nk
+    deep = p2.shape[2]
+    start = big.shape[1] - 2 * rows
 
     def second(j):
-        return pltpu.make_async_copy(big.at[own[1, j]], p2.at[j], s2.at[j])
+        return pltpu.make_async_copy(big.at[own[1, j], pl.ds(start, 2 * rows)], p2.at[j], s2.at[j])
 
     def first(t):
-        return pltpu.make_async_copy(big.at[tab[6, t]], p1.at[t], s1.at[t])
+        return pltpu.make_async_copy(big.at[tab[6, t], pl.ds(start, 2 * rows)], p1.at[t], s1.at[t])
 
     for j in range(npair):
         second(j).start()
@@ -149,9 +162,16 @@
     tot[...] = jnp.zeros_like(tot)
     for j in range(npair):
         second(j).wait()
-    b = p2[...].reshape(npair * rows, wide)
-    e = lax.dot_general(b, whi[...], NT_DIMS, preferred_element_type=F32)
-    e = e + lax.dot_general(b, wlo[...], NT_DIMS, preferred_element_type=F32)
+
+    def contract(left, right):
+        return lax.dot_general(left, right, NT_DIMS, preferred_element_type=F32)
+
+    e = None
+    for h in range(2):
+        b = p2[:, rows * h : rows * (h + 1)].reshape(npair * rows, deep)
+        lanes = slice(deep * h, deep * (h + 1))
+        part = contract(b, whi[:, lanes]) + contract(b, wlo[:, lanes])
+        e = part if e is None else e + part
     e = e + e
     for k in range(nk):
         prod[k] = e[:, k * nt : (k + 1) * nt]
@@ -169,12 +189,14 @@
         return carry
 
     lax.fori_loop(0, nslot, gather, 0)
-    w = tot[...].reshape(nk * rows, wide) * cw[...]
-    hi = w.astype(BF16)
-    lo = (w - hi.astype(F32)).astype(BF16)
-    m = lax.dot_general(
-        jnp.concatenate([hi, lo], axis=0), mine[...], NT_DIMS, preferred_element_type=F32
-    )
+    m = None
+    for h in range(2):
+        lanes = slice(deep * h, deep * (h + 1))
+        w = tot[:, rows * h : rows * (h + 1)].reshape(nk * rows, deep) * cw[:, lanes]
+        hi = w.astype(BF16)
+        lo = (w - hi.astype(F32)).astype(BF16)
+        part = contract(jnp.concatenate([hi, lo], axis=0), full[: nk * nt, lanes])
+        m = part if m is None else m + part
     m = m[: nk * rows] + m[nk * rows :]
     m = m + m
     for k in range(nk):
@@ -182,28 +204,42 @@
             k * rows : (k + 1) * rows, k * nt : (k + 1) * nt
         ]
     z = flat_tiles(flat, (npair + nk) * rows)
-    n = npair + nk
-    for j in range(n):
-        out[n + j] = z[8 * j : 8 * j + 8]
+    for j in range(npair + nk):
+        out[j] = z[8 * j : 8 * j + 8]
+
+
+def collect_kernel(own, exch, got, out, here, sem):
+    copy = pltpu.make_async_copy(got, here, sem)
+    copy.start()
+    nk = got.shape[1] - CAP
+    npair = own.shape[1]
+    out[npair + nk :] = exch[...]
+    copy.wait()
     for j in range(npair):
-        out[j] = got[own[2, j], own[3, j]]
+        out[j] = here[own[2, j], own[3, j]]
     for k in range(nk):
-        out[npair + k] = jnp.sum(got[:, CAP + k], axis=0)
-
-
-def finish_kernel(place, r0, r1, r2, r3, blocks, mirrored, whole, dmat, emat, rows):
+        out[npair + k] = jnp.sum(here[:, CAP + k], axis=0)
+
+
+def finish_kernel(place, r0, r1, r2, r3, blocks, mirrored, whole, dmat, emat, rows, sem):
     npair, nk = blocks.shape[0], mirrored.shape[0]
     nt = dmat.shape[1]
     half = nt // 2
     n = npair + nk
-    for i, r in enumerate((r0, r1, r2, r3)):
-        whole[place[i]] = r[...]
+    copies = [
+        pltpu.make_async_copy(r, whole.at[place[i]], sem.at[i])
+        for i, r in enumerate((r0, r1, r2, r3))
+    ]
+    for c in copies:
+        c.start()
+    for c in copies:
+        c.wait()
     for j in range(n):
         for a in range(2):
             left, right = whole[2 * a, j], whole[2 * a + 1, j]
-            for q in range(4):
-                cut = slice(half * q, half * (q + 1))
-                dmat[j, pl.ds(half * a + q, 8, stride=4), :] = jnp.concatenate(
+            for g in range(4):
+                cut = slice(half * g, half * (g + 1))
+                dmat[j, pl.ds(half * a + 8 * g, 8), :] = jnp.concatenate(
                     [left[:, cut], right[:, cut]], axis=1
                 )
         for a in range(4):
@@ -229,7 +265,6 @@
 
 
 SMEM = pl.BlockSpec(memory_space=pltpu.SMEM)
-HBM = pl.BlockSpec(memory_space=pltpu.HBM)
 ANY = pl.BlockSpec(memory_space=pl.ANY)
 
 
@@ -249,17 +284,22 @@
 
     with jax.named_scope("pack"):
         y_far = lax.ppermute(y, "ga", [(i, 3 - i) for i in range(4)])
-        cut = [jnp.where((a + r) % 4 < 2, x[:, :half], x[:, half:]) for r in range(4)]
-        cut = cut[:1] + [lax.ppermute(cut[r], "ga", shift(r)) for r in range(1, 4)]
+        cut = []
+        for r in range(4):
+            to = (a + r) % 4
+            x_cut = jnp.where(to < 2, x[:, :half], x[:, half:])
+            p_low = jnp.where(to == 0, p[:, :rows], p[:, rows : 2 * rows])
+            p_high = jnp.where(to == 2, p[:, 2 * rows : 3 * rows], p[:, 3 * rows :])
+            v = jnp.concatenate([x_cut, jnp.where(to < 2, p_low, p_high)], axis=1)
+            cut.append(lax.ppermute(v, "ga", shift(r)) if r else v)
+
+        def side(left, right):
+            return jnp.concatenate([widen(left), widen(right)], axis=2)
+
+        near, far = side(cut[0], cut[1]), side(cut[2], cut[3])
+        y_both = side(jnp.where(a < 2, y, y_far), jnp.where(a < 2, y_far, y))
         payload = jnp.concatenate(
-            [
-                jnp.concatenate([widen(cut[0]), widen(cut[1])], axis=2),
-                jnp.concatenate([widen(cut[2]), widen(cut[3])], axis=2),
-                jnp.concatenate(
-                    [widen(jnp.where(a < 2, y, y_far)), widen(jnp.where(a < 2, y_far, y))], axis=2
-                ),
-            ],
-            axis=1,
+            [near[:, :half], far[:, :half], y_both, near[:, half:], far[:, half:]], axis=1
         )
     with jax.named_scope("spread"):
         big = lax.all_gather(payload, "ka", axis=0, tiled=True)
@@ -284,12 +324,11 @@
         c3 = coulomb - c1 - c2
         pieces = jnp.pad(jnp.stack([c1, c2, c3]).astype(BF16), ((0, 13), (0, 0)))
         held = jnp.concatenate([p.reshape(nk * nt, gl), pieces], axis=0)
-        held = lax.all_gather(widen(held), "ga", axis=1, tiled=True)
-        full = held[: nk * nt]
-        p_rows = lax.dynamic_slice_in_dim(full.reshape(nk, nt, 4 * QW), a * rows, rows, axis=1)
-        p_big = lax.all_gather(p_rows, "ka", axis=0, tiled=True)
-        c_full = jnp.sum(held[nk * nt : nk * nt + 3].astype(F32), axis=0, keepdims=True)
-        weighted = full.astype(F32) * c_full
+        held = widen(held)
+        held = [held] + [lax.ppermute(held, "ga", shift(r)) for r in range(1, 4)]
+        full = jnp.concatenate(held, axis=1)
+        c_full = jnp.sum(full[nk * nt : nk * nt + 3].astype(F32), axis=0, keepdims=True)
+        weighted = full[: nk * nt].astype(F32) * c_full
         w_hi = lax.reduce_precision(weighted, 8, 7)
         w_lo = (weighted - w_hi).astype(BF16)
         w_hi = w_hi.astype(BF16)
@@ -352,48 +391,67 @@
     keep, away = pl.pallas_call(
         direct_kernel,
         out_shape=(jax.ShapeDtypeStruct((nslot, 8, 128), F32),) * 2,
-        in_specs=[SMEM, ANY, ANY],
+        in_specs=[SMEM, ANY, *in_vmem(1)],
         out_specs=tuple(in_vmem(2)),
         scratch_shapes=[
-            pltpu.VMEM((qs, 4 * QW, 2 * QW), BF16),
             pltpu.VMEM((2, CH, nt, 2 * QW), BF16),
-            pltpu.VMEM((2, CH, nt, 2 * QW), BF16),
+            pltpu.VMEM((3, CH, nt, 2 * QW), BF16),
+            pltpu.VMEM((2, CH * half, 2 * QW), BF16),
             pltpu.VMEM((CH * half, 128), F32),
-            pltpu.SemaphoreType.DMA((qs,)),
+            pltpu.VMEM((nslot + 1, 8, 128), F32),
+            pltpu.VMEM((nslot + 1, 8, 128), F32),
             pltpu.SemaphoreType.DMA((2, CH)),
-            pltpu.SemaphoreType.DMA((2, CH)),
+            pltpu.SemaphoreType.DMA((3, CH)),
         ],
-        compiler_params=pltpu.CompilerParams(vmem_limit_bytes=60 * 1024 * 1024),
+        compiler_params=pltpu.CompilerParams(vmem_limit_bytes=32 * 1024 * 1024),
         name="direct",
     )(plan, big, wk)
     with jax.named_scope("to_neighbour"):
         came = lax.ppermute(away, "ga", [(0, 1), (1, 0), (2, 3), (3, 2)])
-    send = pl.pallas_call(
-        route_kernel,
-        out_shape=jax.ShapeDtypeStruct((n_ka, CAP + nk, 8, 128), F32),
-        in_specs=[SMEM, *in_vmem(2)],
-        out_specs=pl.BlockSpec(memory_space=pltpu.VMEM),
-        name="route",
-    )(tab, keep, came)
-    with jax.named_scope("to_holders"):
-        got = lax.all_to_all(send, "ka", 0, 0, tiled=True)
-    both = pl.pallas_call(
+    exch = pl.pallas_call(
         exchange_kernel,
-        out_shape=jax.ShapeDtypeStruct((2 * (npair + nk), 8, 128), F32),
-        in_specs=[SMEM, SMEM, HBM, *in_vmem(5)],
+        out_shape=jax.ShapeDtypeStruct((npair + nk, 8, 128), F32),
+        in_specs=[SMEM, SMEM, ANY, *in_vmem(4)],
         out_specs=pl.BlockSpec(memory_space=pltpu.VMEM),
         scratch_shapes=[
-            pltpu.VMEM((nslot, rows, 4 * QW), BF16),
-            pltpu.VMEM((npair, rows, 4 * QW), BF16),
-            pltpu.VMEM((nk, rows, 4 * QW), F32),
+            pltpu.VMEM((nslot, 2 * rows, 2 * QW), BF16),
+            pltpu.VMEM((npair, 2 * rows, 2 * QW), BF16),
+            pltpu.VMEM((nk, 2 * rows, 2 * QW), F32),
             pltpu.VMEM((nk, npair * rows, nt), F32),
             pltpu.VMEM(((npair + nk) * rows, nt), F32),
             pltpu.SemaphoreType.DMA((nslot,)),
             pltpu.SemaphoreType.DMA((npair,)),
         ],
-        compiler_params=pltpu.CompilerParams(vmem_limit_bytes=60 * 1024 * 1024),
+        compiler_params=pltpu.CompilerParams(vmem_limit_bytes=32 * 1024 * 1024),
         name="exchange",
-    )(tab, own, p_big, got, full, w_hi, w_lo, c_full)
+    )(tab, own, big, full, w_hi, w_lo, c_full)
+    send, exch = pl.pallas_call(
+        route_kernel,
+        out_shape=(
+            jax.ShapeDtypeStruct((n_ka, CAP + nk, 8, 128), F32),
+            jax.ShapeDtypeStruct(exch.shape, F32),
+        ),
+        in_specs=[SMEM, ANY, ANY, *in_vmem(1)],
+        out_specs=tuple(in_vmem(2)),
+        scratch_shapes=[
+            pltpu.VMEM((nslot, 8, 128), F32),
+            pltpu.VMEM((nslot, 8, 128), F32),
+            pltpu.SemaphoreType.DMA((2,)),
+        ],
+        compiler_params=pltpu.CompilerParams(vmem_limit_bytes=8 * 1024 * 1024),
+        name="route",
+    )(tab, keep, came, exch)
+    with jax.named_scope("to_holders"):
+        got = lax.all_to_all(send, "ka", 0, 0, tiled=True)
+    both = pl.pallas_call(
+        collect_kernel,
+        out_shape=jax.ShapeDtypeStruct((2 * (npair + nk), 8, 128), F32),
+        in_specs=[SMEM, *in_vmem(1), ANY],
+        out_specs=pl.BlockSpec(memory_space=pltpu.VMEM),
+        scratch_shapes=[pltpu.VMEM(send.shape, F32), pltpu.SemaphoreType.DMA],
+        compiler_params=pltpu.CompilerParams(vmem_limit_bytes=8 * 1024 * 1024),
+        name="collect",
+    )(own, exch, got)
     with jax.named_scope("copies"):
         others = [lax.ppermute(both, "ga", shift(r)) for r in range(1, 4)]
         place = jnp.stack([(a - r) % 4 for r in range(4)])
@@ -403,14 +461,16 @@
             jax.ShapeDtypeStruct((npair, nt * nt), F32),
             jax.ShapeDtypeStruct((nk, nt * nt), F32),
         ),
-        in_specs=[SMEM, *in_vmem(4)],
+        in_specs=[SMEM, ANY, ANY, ANY, ANY],
         out_specs=tuple(in_vmem(2)),
         scratch_shapes=[
             pltpu.VMEM((4, 2 * (npair + nk), 8, 128), F32),
             pltpu.VMEM((npair + nk, nt, nt), F32),
             pltpu.VMEM((npair + nk, nt, nt), F32),
             pltpu.VMEM(((npair + nk) * half, 2 * nt), F32),
+            pltpu.SemaphoreType.DMA((4,)),
         ],
+        compiler_params=pltpu.CompilerParams(vmem_limit_bytes=16 * 1024 * 1024),
         name="finish",
     )(place, both, *others)
 

time: 207 us -> 203 us (0.981)
  starting transfers between devices: 36.3 us -> 23.2 us
  blocking collectives: 40.2 us -> 49.2 us
  waiting for transfers between devices: 62.8 us -> 71 us
  Pallas kernels: 21.1 us -> 16.9 us
  local copies, waits for them, and re-layouts: 12.5 us -> 9.4 us
    all_to_all x0 -> x1, blocking collectives: none -> 23.5 us  [per_device(): got = lax.all_to_all(send, 'ka', 0, 0, tiled=True)]
    ppermute x3 -> x6, waiting for transfers between devices: 0.51 us -> 24 us  [the longest x3 19.5 us: per_device(): held = [held] + [lax.ppermute(held, 'ga', shift(r)) for r in range(1, 4)]]
    all_gather x1, waiting for transfers between devices: 13.4 us -> 36.5 us  [per_device(): big = lax.all_gather(payload, 'ka', axis=0, tiled=True)]
    all_to_all x1 -> x0, starting transfers between devices: 18.5 us -> none  [per_device(): got = lax.all_to_all(send, 'ka', 0, 0, tiled=True)]
    all_gather x1 -> x0, waiting for transfers between devices: 16.9 us -> none  [per_device(): p_big = lax.all_gather(p_rows, 'ka', axis=0, tiled=True)]
    ppermute x3, waiting for transfers between devices: 15.9 us -> 0.01 us  [per_device(): wk.append(lax.ppermute(v, 'ga', shift(r)) if r else v)]
    all_gather x1 -> x0, blocking collectives: 14.5 us -> none  [per_device(): held = lax.all_gather(widen(held), 'ga', axis=1, tiled=True)]
    ppermute x3 -> x6, starting transfers between devices: 3.5 us -> 11.2 us  [the longest x3 6.56 us: per_device(): cut.append(lax.ppermute(v, 'ga', shift(r)) if r else v)]
  transfers between devices with their start and end apart: 14 -> 15, of which waited for: 9 -> 8; matrix products, arithmetic and copies ran while one was open for 13% -> 9% of each run, Pallas kernels for 5% -> 3%
where the time goes in v5:
time: 203 us; the launch traced here: 202 us
  waiting for transfers between devices  71 us (35%)
  blocking collectives  49.2 us (24%)
  starting transfers between devices  23.2 us (11%)
  Pallas kernels  16.9 us (8%)
  other arithmetic  15.9 us (8%)
  between operations  15.9 us (8%)
  local copies, waits for them, and re-layouts  9.4 us (5%)
    all_gather x1, waiting for transfers between devices, per_device(): big = lax.all_gather(payload, 'ka', axis=0, tiled=True)  36.5 us
    all_gather x1, blocking collectives, per_device(): lax.all_gather(pairs, 'ka', axis=0, tiled=True).reshape(n_ka, npair, 3)  25.7 us
    all_to_all x1, blocking collectives, per_device(): got = lax.all_to_all(send, 'ka', 0, 0, tiled=True)  23.5 us
    ppermute x3, waiting for transfers between devices, per_device(): held = [held] + [lax.ppermute(held, 'ga', shift(r)) for r in range(1, 4)]  19.5 us
    ppermute x3, waiting for transfers between devices, per_device(): others = [lax.ppermute(both, 'ga', shift(r)) for r in range(1, 4)]  6.61 us
    ppermute x3, starting transfers between devices, per_device(): cut.append(lax.ppermute(v, 'ga', shift(r)) if r else v)  6.56 us
    pallas_call x1, Pallas kernels, per_device(): pl.pallas_call(direct_kernel, out_shape=(jax.ShapeDtypeStruct((nslot, 8,...  6.55 us
    ppermute x3, starting transfers between devices, per_device(): others = [lax.ppermute(both, 'ga', shift(r)) for r in range(1, 4)]  5.44 us
  transfers between devices with their start and end apart: 15, of which 8 were waited for; matrix products, arithmetic and copies ran while one was open for 9% of the time, Pallas kernels for 3%

profile of v5, /device:TPU:0, one launch (start us, length us, event | category | flops | bytes accessed | tf_op | source)
XLA Modules:
  0.0 201.6 jit_solution(7829720838791590881)
XLA Ops:
  9.2 3.2 %collective-permute-start.1 = (bf16[4,48,375]{2,1,0:T(8,128)(2,1)S(1)}, bf16[4,48,375]{2,1,0:T(8,128)(2,1)S(1)}, u32[]{:S(2)}, u32[]{:S(2)}) collective-permute-start(bf16[4,48,375]{2,1,0:T(8,128)(2,1)S(1)} %pad_maximum_fusion.3), channel_id=1, source_target_pairs={{0,2},{1,3},{2,0},{3,1},{4,6},{5,7},{6,4},{7,5},{8,10},{9,11},{10,... | collective-permute-start | bytes 432008 | tf_op jit(solution)/shard_map/pack/ppermute | solution.py:294
  13.1 2.7 %collective-permute-start.2 = (bf16[4,48,375]{2,1,0:T(8,128)(2,1)S(1)}, bf16[4,48,375]{2,1,0:T(8,128)(2,1)S(1)}, u32[]{:S(2)}, u32[]{:S(2)}) collective-permute-start(bf16[4,48,375]{2,1,0:T(8,128)(2,1)S(1)} %pad_maximum_fusion.4), channel_id=1, source_target_pairs={{0,3},{1,0},{2,1},{3,2},{4,7},{5,4},{6,5},{7,6},{8,11},{9,8},{10,9... | collective-permute-start | bytes 432008 | tf_op jit(solution)/shard_map/pack/ppermute | solution.py:294
  16.0 4.5 %collective-permute-done = bf16[4,48,375]{2,1,0:T(8,128)(2,1)S(1)} collective-permute-done((bf16[4,48,375]{2,1,0:T(8,128)(2,1)S(1)}, bf16[4,48,375]{2,1,0:T(8,128)(2,1)S(1)}, u32[]{:S(2)}, u32[]{:S(2)}) %collective-permute-start) | collective-permute-done | bytes 144032 | tf_op jit(solution)/shard_map/pack/ppermute | solution.py:294
  20.7 3.4 %collective-permute-done.3 = bf16[4,64,375]{2,1,0:T(8,128)(2,1)} collective-permute-done((bf16[4,64,375]{2,1,0:T(8,128)(2,1)}, bf16[4,64,375]{2,1,0:T(8,128)(2,1)}, u32[]{:S(2)}, u32[]{:S(2)}) %collective-permute-start.3) | collective-permute-done | bytes 192032 | tf_op jit(solution)/shard_map/pack/ppermute | solution.py:286
  27.0 3.1 %collective-permute-start.10 = (bf16[272,384]{1,0:T(8,128)(2,1)}, bf16[272,384]{1,0:T(8,128)(2,1)}, u32[]{:S(2)}, u32[]{:S(2)}) collective-permute-start(bf16[272,384]{1,0:T(8,128)(2,1)} %fusion.20), channel_id=1, source_target_pairs={{0,3},{1,0},{2,1},{3,2},{4,7},{5,4},{6,5},{7,6},{8,11},{9,8},{10,9... | collective-permute-start | bytes 626696 | tf_op jit(solution)/shard_map/exchange_pack/ppermute | solution.py:328
  30.1 3.6 %fusion.41 = (bf16[2,375,375]{2,0,1:T(2,128)(2,1)S(1)}, bf16[2,375,375]{2,0,1:T(2,128)(2,1)S(1)}, bf16[2,375,375]{2,0,1:T(2,128)(2,1)S(1)}, bf16[2,375,375]{2,0,1:T(2,128)(2,1)S(1)}) fusion(bf16[2,375,1500]{2,0,1:T(2,128)(2,1)S(1)} %copy-done.1), kind=kLoop, calls=%fused_computation.146 | loop fusion | bytes 4500000 | tf_op jit(solution)/shard_map/weights/slice | solution.py:309
  34.0 2.1 %broadcast_select_fusion.3 = (bf16[2,384,768]{2,1,0:T(8,128)(2,1)S(1)}, bf16[2,384,768]{2,1,0:T(8,128)(2,1)}, bf16[2,384,768]{2,1,0:T(8,128)(2,1)}) fusion(pred[]{:T(512)S(6)} %or.12, bf16[2,375,375]{2,1,0:T(8,128)(2,1)S(1)} %copy.84, bf16[2,375,375]{2,1,0:T(8,128)(2,1)S(1)} %copy.83, bf16[2,375,375]{2,1,0:T(8,128)(2,1)S(1)} %copy.82, ...), kind=kLoop, calls=%fused_computation.16 | loop fusion | flops 10027008 | bytes 5788947 | tf_op jit(solution)/shard_map/weights/jit(_where)/select_n | solution.py:317
  36.4 4.4 %collective-permute-start.5 = (bf16[2,384,768]{2,1,0:T(8,128)(2,1)}, bf16[2,384,768]{2,1,0:T(8,128)(2,1)}, u32[]{:S(2)}, u32[]{:S(2)}) collective-permute-start(bf16[2,384,768]{2,1,0:T(8,128)(2,1)} %get-tuple-element.31), channel_id=1, source_target_pairs={{0,2},{1,3},{2,0},{3,1},{4,6},{5,7},{6,4},{7,5},{8,10},{9,11},{10,... | collective-permute-start | bytes 3538952 | tf_op jit(solution)/shard_map/weights/ppermute | solution.py:318
  42.2 25.7 %all-gather = s32[32,16,3]{1,2,0:T(4,128)S(1)} all-gather(s32[1,16,3]{1,2,0:T(4,128)S(1)} %bitcast.44), channel_id=1, replica_groups=mesh['ka'=32,'ga'=4] {'ka'}, dimensions={0}, use_global_device_ids=true | all-gather | bytes 6336 | tf_op jit(solution)/shard_map/tables/all_gather | solution.py:337
  74.0 1.6 collective-permute-start.9
  75.6 19.5 %collective-permute-done.9 = bf16[272,384]{1,0:T(8,128)(2,1)S(1)} collective-permute-done((bf16[272,384]{1,0:T(8,128)(2,1)}, bf16[272,384]{1,0:T(8,128)(2,1)S(1)}, u32[]{:S(2)}, u32[]{:S(2)}) %collective-permute-start.9) | collective-permute-done | bytes 208928 | tf_op jit(solution)/shard_map/exchange_pack/ppermute | solution.py:328
  96.4 4.4 %pad_maximum_fusion.w = bf16[2,1536,768]{2,1,0:T(8,128)(2,1)} fusion(bf16[2,384,768]{2,1,0:T(8,128)(2,1)S(1)} %collective-permute-done.6, bf16[2,384,768]{2,1,0:T(8,128)(2,1)} %collective-permute-done.5, bf16[2,384,768]{2,1,0:T(8,128)(2,1)} %collective-permute-done.4, bf16[2,384,768]{2,1,0:T(8,128)(2,1)S(1)} %get-tuple-element.29), kind=kLoop, calls=%fused_computation | loop fusion | flops 18874368 | bytes 9437184 | tf_op jit(solution)/shard_map/weights/concatenate | solution.py:319
  100.9 36.5 %all-gather.3.cloned.1.call-done.big = bf16[128,160,768]{2,1,0:T(8,128)(2,1)} async-done(((bf16[4,160,768]{2,1,0:T(8,128)(2,1)}), bf16[128,160,768]{2,1,0:T(8,128)(2,1)}) %all-gather.3.cloned.1.call-update) | async-done | bytes 31457296 | tf_op jit(solution)/shard_map/spread/all_gather | solution.py:305
  137.4 2.3 %copy-done = bf16[2,1536,768]{2,1,0:T(8,128)(2,1)S(1)} copy-done((bf16[2,1536,768]{2,1,0:T(8,128)(2,1)S(1)}, bf16[2,1536,768]{2,1,0:T(8,128)(2,1)}, u32[]{:S(2)}) %copy-start) | copy-done | bytes 4718616
  139.7 6.6 %direct.1 = (f32[64,8,128]{2,1,0:T(8,128)S(1)}, f32[64,8,128]{2,1,0:T(8,128)S(1)}) custom-call(s32[4,80]{1,0:T(4,128)S(1)} %pad_add_fusion.1.plan, bf16[128,160,768]{2,1,0:T(8,128)(2,1)} %all-gather.3.cloned.1.call-done.big, bf16[2,1536,768]{2,1,0:T(8,128)(2,1)S(1)} %copy-done), custom_call_target="tpu_custom_call" | custom-call | tf_op jit(solution)/shard_map/direct/pallas_call | solution.py:391
  146.3 1.7 collective-permute-start.7
  148.3 5.2 %exchange.1.exch = f32[20,8,128]{2,1,0:T(8,128)S(1)} custom-call(s32[7,64]{1,0:T(8,128)S(1)} %stack.74.tab, s32[4,16]{1,0:T(4,128)S(1)} %pad_add_fusion.own, bf16[128,160,768]{2,1,0:T(8,128)(2,1)} %all-gather.3.cloned.1.call-done.big, bf16[272,1536]{1,0:T(8,128)(2,1)S(1)} %pad_maximum_fusion.1.full, bf16[256,1536]{1,0:T(8,128)(2,1)S(1)} %get-tuple-element.37.whi, ...), custom_call_target="tpu_custom_call" | custom-call | tf_op jit(solution)/shard_map/exchange/pallas_call | solution.py:411
  154.0 1.4 route.1
  155.4 23.5 %all_to_all.5.got = f32[32,6,8,128]{3,2,1,0:T(8,128)S(1)} all-to-all(f32[32,6,8,128]{3,2,1,0:T(8,128)S(1)} %get-tuple-element.9), channel_id=1, replica_groups=mesh['ka'=32,'ga'=4] {'ka'}, dimensions={0} | all-to-all | bytes 1572864 | tf_op jit(solution)/shard_map/to_holders/all_to_all | solution.py:445
  180.2 3.0 %collective-permute-start.12 = (f32[40,8,128]{2,1,0:T(8,128)S(1)}, f32[40,8,128]{2,1,0:T(8,128)S(1)}, u32[]{:S(2)}, u32[]{:S(2)}) collective-permute-start(f32[40,8,128]{2,1,0:T(8,128)S(1)} %collect.1.r0), channel_id=1, source_target_pairs={{0,2},{1,3},{2,0},{3,1},{4,6},{5,7},{6,4},{7,5},{8,10},{9,11},{10,... | collective-permute-start | bytes 491528 | tf_op jit(solution)/shard_map/copies/ppermute | solution.py:456
  183.2 1.8 collective-permute-start.13
  185.1 2.5 %collective-permute-done.11.r1 = f32[40,8,128]{2,1,0:T(8,128)S(1)} collective-permute-done((f32[40,8,128]{2,1,0:T(8,128)S(1)}, f32[40,8,128]{2,1,0:T(8,128)S(1)}, u32[]{:S(2)}, u32[]{:S(2)}) %collective-permute-start.11) | collective-permute-done | bytes 163872 | tf_op jit(solution)/shard_map/copies/ppermute | solution.py:456
  187.7 3.8 %collective-permute-done.12.r2 = f32[40,8,128]{2,1,0:T(8,128)S(1)} collective-permute-done((f32[40,8,128]{2,1,0:T(8,128)S(1)}, f32[40,8,128]{2,1,0:T(8,128)S(1)}, u32[]{:S(2)}, u32[]{:S(2)}) %collective-permute-start.12) | collective-permute-done | bytes 163872 | tf_op jit(solution)/shard_map/copies/ppermute | solution.py:456
  191.8 3.0 %finish.1 = (f32[16,4096]{1,0:T(8,128)}, f32[4,4096]{1,0:T(4,128)}) custom-call(s32[4]{0:T(128)S(1)} %pad_add_fusion.2.place, f32[40,8,128]{2,1,0:T(8,128)S(1)} %collect.1.r0, f32[40,8,128]{2,1,0:T(8,128)S(1)} %collective-permute-done.11.r1, f32[40,8,128]{2,1,0:T(8,128)S(1)} %collective-permute-done.12.r2, f32[40,8,128]{2,1,0:T(8,128)S(1)} %collective-permute-done.13.r3), custom_call_target="tpu_custom_call" | custom-call | tf_op jit(solution)/shard_map/finish/pallas_call | solution.py:458
  (110 shorter events, 16.1 us)
Async XLA Ops:
  7.2 5.9 %copy-start.2 = (bf16[4,64,375]{2,1,0:T(8,128)(2,1)S(1)}, bf16[4,64,375]{2,1,0:T(8,128)(2,1)}, u32[]{:S(2)}) copy-start(bf16[4,64,375]{2,1,0:T(8,128)(2,1)} %param.9) | copy-start | bytes 576004
  7.2 130.2 %all-gather.3.cloned.1.call-start = ((), (), s32[]{:S(2)}) async-start(), calls=%async_computation.1 | async-start | bytes 32440320 | tf_op jit(solution)/shard_map/spread/all_gather | solution.py:305
  9.2 11.3 %collective-permute-start.1 = (bf16[4,48,375]{2,1,0:T(8,128)(2,1)S(1)}, bf16[4,48,375]{2,1,0:T(8,128)(2,1)S(1)}, u32[]{:S(2)}, u32[]{:S(2)}) collective-permute-start(bf16[4,48,375]{2,1,0:T(8,128)(2,1)S(1)} %pad_maximum_fusion.3), channel_id=1, source_target_pairs={{0,2},{1,3},{2,0},{3,1},{4,6},{5,7},{6,4},{7,5},{8,10},{9,11},{10,... | collective-permute-start | bytes 432008 | tf_op jit(solution)/shard_map/pack/ppermute | solution.py:294
  12.4 8.1 %collective-permute-start = (bf16[4,48,375]{2,1,0:T(8,128)(2,1)S(1)}, bf16[4,48,375]{2,1,0:T(8,128)(2,1)S(1)}, u32[]{:S(2)}, u32[]{:S(2)}) collective-permute-start(bf16[4,48,375]{2,1,0:T(8,128)(2,1)S(1)} %pad_maximum_fusion.2), channel_id=1, source_target_pairs={{0,1},{1,2},{2,3},{3,0},{4,5},{5,6},{6,7},{7,4},{8,9},{9,10},{10,1... | collective-permute-start | bytes 432008 | tf_op jit(solution)/shard_map/pack/ppermute | solution.py:294
  13.1 7.4 %collective-permute-start.2 = (bf16[4,48,375]{2,1,0:T(8,128)(2,1)S(1)}, bf16[4,48,375]{2,1,0:T(8,128)(2,1)S(1)}, u32[]{:S(2)}, u32[]{:S(2)}) collective-permute-start(bf16[4,48,375]{2,1,0:T(8,128)(2,1)S(1)} %pad_maximum_fusion.4), channel_id=1, source_target_pairs={{0,3},{1,0},{2,1},{3,2},{4,7},{5,4},{6,5},{7,6},{8,11},{9,8},{10,9... | collective-permute-start | bytes 432008 | tf_op jit(solution)/shard_map/pack/ppermute | solution.py:294
  15.8 8.2 %collective-permute-start.3 = (bf16[4,64,375]{2,1,0:T(8,128)(2,1)}, bf16[4,64,375]{2,1,0:T(8,128)(2,1)}, u32[]{:S(2)}, u32[]{:S(2)}) collective-permute-start(bf16[4,64,375]{2,1,0:T(8,128)(2,1)} %param.8), channel_id=1, source_target_pairs={{0,3},{1,2},{2,1},{3,0},{4,7},{5,6},{6,5},{7,4},{8,11},{9,10},{10,... | collective-permute-start | bytes 576008 | tf_op jit(solution)/shard_map/pack/ppermute | solution.py:286
  20.6 5.6 %copy-start.5 = (f32[375]{0:T(512)S(1)}, f32[375]{0:T(512)}, u32[]{:S(2)}) copy-start(f32[375]{0:T(512)} %param.10) | copy-start | bytes 4504
  20.6 9.4 %copy-start.1 = (bf16[2,375,1500]{2,0,1:T(2,128)(2,1)S(1)}, bf16[2,375,1500]{2,0,1:T(2,128)(2,1)}, u32[]{:S(2)}) copy-start(bf16[2,375,1500]{2,0,1:T(2,128)(2,1)} %param.11) | copy-start | bytes 6750004
  25.2 1.0 copy-start.3
  27.0 47.0 %collective-permute-start.10 = (bf16[272,384]{1,0:T(8,128)(2,1)}, bf16[272,384]{1,0:T(8,128)(2,1)}, u32[]{:S(2)}, u32[]{:S(2)}) collective-permute-start(bf16[272,384]{1,0:T(8,128)(2,1)} %fusion.20), channel_id=1, source_target_pairs={{0,3},{1,0},{2,1},{3,2},{4,7},{5,4},{6,5},{7,6},{8,11},{9,8},{10,9... | collective-permute-start | bytes 626696 | tf_op jit(solution)/shard_map/exchange_pack/ppermute | solution.py:328
  30.1 45.5 %collective-permute-start.8 = (bf16[272,384]{1,0:T(8,128)(2,1)}, bf16[272,384]{1,0:T(8,128)(2,1)}, u32[]{:S(2)}, u32[]{:S(2)}) collective-permute-start(bf16[272,384]{1,0:T(8,128)(2,1)} %fusion.20), channel_id=1, source_target_pairs={{0,1},{1,2},{2,3},{3,0},{4,5},{5,6},{6,7},{7,4},{8,9},{9,10},{10,1... | collective-permute-start | bytes 626696 | tf_op jit(solution)/shard_map/exchange_pack/ppermute | solution.py:328
  36.1 60.3 %collective-permute-start.4 = (bf16[2,384,768]{2,1,0:T(8,128)(2,1)}, bf16[2,384,768]{2,1,0:T(8,128)(2,1)}, u32[]{:S(2)}, u32[]{:S(2)}) collective-permute-start(bf16[2,384,768]{2,1,0:T(8,128)(2,1)} %get-tuple-element.30), channel_id=1, source_target_pairs={{0,1},{1,2},{2,3},{3,0},{4,5},{5,6},{6,7},{7,4},{8,9},{9,10},{10,1... | collective-permute-start | bytes 3538952 | tf_op jit(solution)/shard_map/weights/ppermute | solution.py:318
  36.4 60.0 %collective-permute-start.5 = (bf16[2,384,768]{2,1,0:T(8,128)(2,1)}, bf16[2,384,768]{2,1,0:T(8,128)(2,1)}, u32[]{:S(2)}, u32[]{:S(2)}) collective-permute-start(bf16[2,384,768]{2,1,0:T(8,128)(2,1)} %get-tuple-element.31), channel_id=1, source_target_pairs={{0,2},{1,3},{2,0},{3,1},{4,6},{5,7},{6,4},{7,5},{8,10},{9,11},{10,... | collective-permute-start | bytes 3538952 | tf_op jit(solution)/shard_map/weights/ppermute | solution.py:318
  40.8 1.4 copy-start.4
  40.8 27.2 %copy-start.6 = (s32[64]{0:T(128)S(1)}, s32[64]{0:T(128)}, u32[]{:S(2)}) copy-start(s32[64]{0:T(128)} %param.13) | copy-start | bytes 772
  42.2 54.2 %collective-permute-start.6 = (bf16[2,384,768]{2,1,0:T(8,128)(2,1)}, bf16[2,384,768]{2,1,0:T(8,128)(2,1)S(1)}, u32[]{:S(2)}, u32[]{:S(2)}) collective-permute-start(bf16[2,384,768]{2,1,0:T(8,128)(2,1)} %broadcast_select_fusion), channel_id=1, source_target_pairs={{0,3},{1,0},{2,1},{3,2},{4,7},{5,4},{6,5},{7,6},{8,11},{9,8},{10,9... | collective-permute-start | bytes 3538952 | tf_op jit(solution)/shard_map/weights/ppermute | solution.py:318
  74.0 21.1 %collective-permute-start.9 = (bf16[272,384]{1,0:T(8,128)(2,1)}, bf16[272,384]{1,0:T(8,128)(2,1)S(1)}, u32[]{:S(2)}, u32[]{:S(2)}) collective-permute-start(bf16[272,384]{1,0:T(8,128)(2,1)} %fusion.20), channel_id=1, source_target_pairs={{0,2},{1,3},{2,0},{3,1},{4,6},{5,7},{6,4},{7,5},{8,10},{9,11},{10,... | collective-permute-start | bytes 626696 | tf_op jit(solution)/shard_map/exchange_pack/ppermute | solution.py:328
  137.4 2.3 %copy-start = (bf16[2,1536,768]{2,1,0:T(8,128)(2,1)S(1)}, bf16[2,1536,768]{2,1,0:T(8,128)(2,1)}, u32[]{:S(2)}) copy-start(bf16[2,1536,768]{2,1,0:T(8,128)(2,1)} %pad_maximum_fusion.w) | copy-start | bytes 14155780
  146.3 7.7 %collective-permute-start.7 = (f32[64,8,128]{2,1,0:T(8,128)S(1)}, f32[64,8,128]{2,1,0:T(8,128)S(1)}, u32[]{:S(2)}, u32[]{:S(2)}) collective-permute-start(f32[64,8,128]{2,1,0:T(8,128)S(1)} %get-tuple-element.7), channel_id=1, source_target_pairs={{0,1},{1,0},{2,3},{3,2},{4,5},{5,4},{6,7},{7,6},{8,9},{9,8},{10,11... | collective-permute-start | bytes 786440 | tf_op jit(solution)/shard_map/to_neighbour/ppermute | solution.py:410
  179.6 8.1 %collective-permute-start.11 = (f32[40,8,128]{2,1,0:T(8,128)S(1)}, f32[40,8,128]{2,1,0:T(8,128)S(1)}, u32[]{:S(2)}, u32[]{:S(2)}) collective-permute-start(f32[40,8,128]{2,1,0:T(8,128)S(1)} %collect.1.r0), channel_id=1, source_target_pairs={{0,1},{1,2},{2,3},{3,0},{4,5},{5,6},{6,7},{7,4},{8,9},{9,10},{10,1... | collective-permute-start | bytes 491528 | tf_op jit(solution)/shard_map/copies/ppermute | solution.py:456
  180.2 11.2 %collective-permute-start.12 = (f32[40,8,128]{2,1,0:T(8,128)S(1)}, f32[40,8,128]{2,1,0:T(8,128)S(1)}, u32[]{:S(2)}, u32[]{:S(2)}) collective-permute-start(f32[40,8,128]{2,1,0:T(8,128)S(1)} %collect.1.r0), channel_id=1, source_target_pairs={{0,2},{1,3},{2,0},{3,1},{4,6},{5,7},{6,4},{7,5},{8,10},{9,11},{10,... | collective-permute-start | bytes 491528 | tf_op jit(solution)/shard_map/copies/ppermute | solution.py:456
  183.2 8.5 %collective-permute-start.13 = (f32[40,8,128]{2,1,0:T(8,128)S(1)}, f32[40,8,128]{2,1,0:T(8,128)S(1)}, u32[]{:S(2)}, u32[]{:S(2)}) collective-permute-start(f32[40,8,128]{2,1,0:T(8,128)S(1)} %collect.1.r0), channel_id=1, source_target_pairs={{0,3},{1,0},{2,1},{3,2},{4,7},{5,4},{6,5},{7,6},{8,11},{9,8},{10,9... | collective-permute-start | bytes 491528 | tf_op jit(solution)/shard_map/copies/ppermute | solution.py:456
Sparse Core Ops, SparseCore 0:
  26.3 111.0 all-gather.2

commit v6 on v5

--- a/solution.py
+++ b/solution.py
@@ -110,7 +110,7 @@
     away[...] = sent[:nslot]
 
 
-def route_kernel(tab, keep, came, exch, send, done, mine, theirs, sem):
+def route_kernel(tab, keep, came, send, mine, theirs, sem):
     copies = [
         pltpu.make_async_copy(keep, mine, sem.at[0]),
         pltpu.make_async_copy(came, theirs, sem.at[1]),
@@ -119,7 +119,6 @@
         c.start()
     nk = send.shape[1] - CAP
     send[:, CAP:] = jnp.zeros((send.shape[0], nk, *send.shape[2:]), F32)
-    done[...] = exch[...]
     for c in copies:
         c.wait()
     for t in range(tab.shape[1]):
@@ -133,23 +132,29 @@
             send[owner, row] = send[owner, row] + v
 
 
-def exchange_kernel(tab, own, big, full, whi, wlo, cw, out, p1, p2, tot, prod, flat, s1, s2):
+def exchange_kernel(
+    tab, own, big, full_in, whi_in, wlo_in, dmat, cw, out, full, whi, wlo, p1, p2, tot, prod, flat, s0, s1, s2
+):
     nslot = tab.shape[1]
     npair = own.shape[1]
-    nk = tot.shape[0]
-    rows = p2.shape[1] // 2
-    nt = whi.shape[0] // nk
-    deep = p2.shape[2]
-    start = big.shape[1] - 2 * rows
+    nk, rows, wide = tot.shape
+    nt = whi_in.shape[0] // nk
 
     def second(j):
-        return pltpu.make_async_copy(big.at[own[1, j], pl.ds(start, 2 * rows)], p2.at[j], s2.at[j])
+        return pltpu.make_async_copy(big.at[own[1, j]], p2.at[j], s2.at[j])
 
     def first(t):
-        return pltpu.make_async_copy(big.at[tab[6, t], pl.ds(start, 2 * rows)], p1.at[t], s1.at[t])
-
+        return pltpu.make_async_copy(big.at[tab[6, t]], p1.at[t], s1.at[t])
+
+    loads = [
+        pltpu.make_async_copy(whi_in, whi, s0.at[0]),
+        pltpu.make_async_copy(wlo_in, wlo, s0.at[1]),
+        pltpu.make_async_copy(full_in.at[pl.ds(0, nk * nt)], full, s0.at[2]),
+    ]
     for j in range(npair):
         second(j).start()
+    for c in loads:
+        c.start()
 
     def begin(t, carry):
         @pl.when(tab[4, t] == 1)
@@ -162,16 +167,14 @@
     tot[...] = jnp.zeros_like(tot)
     for j in range(npair):
         second(j).wait()
+    for c in loads:
+        c.wait()
 
     def contract(left, right):
         return lax.dot_general(left, right, NT_DIMS, preferred_element_type=F32)
 
-    e = None
-    for h in range(2):
-        b = p2[:, rows * h : rows * (h + 1)].reshape(npair * rows, deep)
-        lanes = slice(deep * h, deep * (h + 1))
-        part = contract(b, whi[:, lanes]) + contract(b, wlo[:, lanes])
-        e = part if e is None else e + part
+    b = p2[...].reshape(npair * rows, wide)
+    e = contract(b, whi[...]) + contract(b, wlo[...])
     e = e + e
     for k in range(nk):
         prod[k] = e[:, k * nt : (k + 1) * nt]
@@ -189,14 +192,10 @@
         return carry
 
     lax.fori_loop(0, nslot, gather, 0)
-    m = None
-    for h in range(2):
-        lanes = slice(deep * h, deep * (h + 1))
-        w = tot[:, rows * h : rows * (h + 1)].reshape(nk * rows, deep) * cw[:, lanes]
-        hi = w.astype(BF16)
-        lo = (w - hi.astype(F32)).astype(BF16)
-        part = contract(jnp.concatenate([hi, lo], axis=0), full[: nk * nt, lanes])
-        m = part if m is None else m + part
+    w = tot[...].reshape(nk * rows, wide) * cw[...]
+    hi = w.astype(BF16)
+    lo = (w - hi.astype(F32)).astype(BF16)
+    m = contract(jnp.concatenate([hi, lo], axis=0), full[...])
     m = m[: nk * rows] + m[nk * rows :]
     m = m + m
     for k in range(nk):
@@ -208,33 +207,32 @@
         out[j] = z[8 * j : 8 * j + 8]
 
 
-def collect_kernel(own, exch, got, out, here, sem):
+def collect_kernel(own, got, out, here, sem):
     copy = pltpu.make_async_copy(got, here, sem)
     copy.start()
+    copy.wait()
     nk = got.shape[1] - CAP
     npair = own.shape[1]
-    out[npair + nk :] = exch[...]
-    copy.wait()
     for j in range(npair):
         out[j] = here[own[2, j], own[3, j]]
     for k in range(nk):
         out[npair + k] = jnp.sum(here[:, CAP + k], axis=0)
 
 
-def finish_kernel(place, r0, r1, r2, r3, blocks, mirrored, whole, dmat, emat, rows, sem):
-    npair, nk = blocks.shape[0], mirrored.shape[0]
-    nt = dmat.shape[1]
-    half = nt // 2
-    n = npair + nk
+def bring(place, refs, whole, sem):
     copies = [
-        pltpu.make_async_copy(r, whole.at[place[i]], sem.at[i])
-        for i, r in enumerate((r0, r1, r2, r3))
+        pltpu.make_async_copy(r, whole.at[place[i]], sem.at[i]) for i, r in enumerate(refs)
     ]
     for c in copies:
         c.start()
     for c in copies:
         c.wait()
-    for j in range(n):
+
+
+def arrange_kernel(place, r0, r1, r2, r3, dmat, whole, sem):
+    bring(place, (r0, r1, r2, r3), whole, sem)
+    half = dmat.shape[1] // 2
+    for j in range(dmat.shape[0]):
         for a in range(2):
             left, right = whole[2 * a, j], whole[2 * a + 1, j]
             for g in range(4):
@@ -242,17 +240,26 @@
                 dmat[j, pl.ds(half * a + 8 * g, 8), :] = jnp.concatenate(
                     [left[:, cut], right[:, cut]], axis=1
                 )
+
+
+def finish_kernel(place, dmat, r0, r1, r2, r3, blocks, mirrored, whole, emat, bmat, rows, sem):
+    bring(place, (r0, r1, r2, r3), whole, sem)
+    npair, nk = blocks.shape[0], mirrored.shape[0]
+    nt = dmat.shape[1]
+    half = nt // 2
+    n = npair + nk
+    for j in range(n):
         for a in range(4):
-            tile = whole[a, n + j]
+            tile = whole[a, j]
             emat[j, pl.ds(16 * a, 8, stride=2), :] = tile[:, :nt]
             emat[j, pl.ds(16 * a + 1, 8, stride=2), :] = tile[:, nt:]
     for j in range(n):
         if j < npair:
-            dmat[j] = emat[j].T - dmat[j]
+            bmat[j] = emat[j].T - dmat[j]
         else:
-            dmat[j] = (emat[j] - dmat[j]).T
-        even = dmat[j, pl.ds(0, half, stride=2), :]
-        odd = dmat[j, pl.ds(1, half, stride=2), :]
+            bmat[j] = (emat[j] - dmat[j]).T
+        even = bmat[j, pl.ds(0, half, stride=2), :]
+        odd = bmat[j, pl.ds(1, half, stride=2), :]
         rows[pl.ds(j * half, half), :] = jnp.concatenate([even, odd], axis=1)
     for r in range(half):
         lanes = pl.ds(2 * nt * r, 2 * nt)
@@ -284,22 +291,14 @@
 
     with jax.named_scope("pack"):
         y_far = lax.ppermute(y, "ga", [(i, 3 - i) for i in range(4)])
-        cut = []
-        for r in range(4):
-            to = (a + r) % 4
-            x_cut = jnp.where(to < 2, x[:, :half], x[:, half:])
-            p_low = jnp.where(to == 0, p[:, :rows], p[:, rows : 2 * rows])
-            p_high = jnp.where(to == 2, p[:, 2 * rows : 3 * rows], p[:, 3 * rows :])
-            v = jnp.concatenate([x_cut, jnp.where(to < 2, p_low, p_high)], axis=1)
-            cut.append(lax.ppermute(v, "ga", shift(r)) if r else v)
+        cut = [jnp.where((a + r) % 4 < 2, x[:, :half], x[:, half:]) for r in range(4)]
+        cut = cut[:1] + [lax.ppermute(cut[r], "ga", shift(r)) for r in range(1, 4)]
 
         def side(left, right):
             return jnp.concatenate([widen(left), widen(right)], axis=2)
 
-        near, far = side(cut[0], cut[1]), side(cut[2], cut[3])
-        y_both = side(jnp.where(a < 2, y, y_far), jnp.where(a < 2, y_far, y))
         payload = jnp.concatenate(
-            [near[:, :half], far[:, :half], y_both, near[:, half:], far[:, half:]], axis=1
+            [side(cut[0], cut[1]), side(cut[2], cut[3]), side(y, y_far)], axis=1
         )
     with jax.named_scope("spread"):
         big = lax.all_gather(payload, "ka", axis=0, tiled=True)
@@ -309,12 +308,16 @@
             jnp.pad(w[:, :, i * gl : (i + 1) * gl], ((0, 0), (0, QW - gl), (0, QW - gl)))
             for i in range(4)
         ]
-        outer = jnp.concatenate([cols[0], cols[3]], axis=2)
-        inner = jnp.concatenate([cols[1], cols[2]], axis=2)
         wk = []
         for r in range(4):
             to = (a + r) % 4
-            v = jnp.where((to == 0) | (to == 3), outer, inner)
+            left = jnp.where(
+                to < 2, jnp.where(to == 0, cols[0], cols[1]), jnp.where(to == 2, cols[2], cols[3])
+            )
+            right = jnp.where(
+                to < 2, jnp.where(to == 0, cols[3], cols[2]), jnp.where(to == 2, cols[1], cols[0])
+            )
+            v = jnp.concatenate([left, right], axis=2)
             wk.append(lax.ppermute(v, "ga", shift(r)) if r else v)
         wk = jnp.concatenate(wk, axis=1)
 
@@ -324,9 +327,10 @@
         c3 = coulomb - c1 - c2
         pieces = jnp.pad(jnp.stack([c1, c2, c3]).astype(BF16), ((0, 13), (0, 0)))
         held = jnp.concatenate([p.reshape(nk * nt, gl), pieces], axis=0)
-        held = widen(held)
-        held = [held] + [lax.ppermute(held, "ga", shift(r)) for r in range(1, 4)]
-        full = jnp.concatenate(held, axis=1)
+        full = lax.all_gather(widen(held), "ga", axis=1, tiled=True)
+        p_rows = full[: nk * nt].reshape(nk, nt, 4 * QW)
+        p_rows = lax.dynamic_slice_in_dim(p_rows, a * rows, rows, axis=1)
+        p_big = lax.all_gather(p_rows, "ka", axis=0, tiled=True)
         c_full = jnp.sum(full[nk * nt : nk * nt + 3].astype(F32), axis=0, keepdims=True)
         weighted = full[: nk * nt].astype(F32) * c_full
         w_hi = lax.reduce_precision(weighted, 8, 7)
@@ -408,31 +412,11 @@
     )(plan, big, wk)
     with jax.named_scope("to_neighbour"):
         came = lax.ppermute(away, "ga", [(0, 1), (1, 0), (2, 3), (3, 2)])
-    exch = pl.pallas_call(
-        exchange_kernel,
-        out_shape=jax.ShapeDtypeStruct((npair + nk, 8, 128), F32),
-        in_specs=[SMEM, SMEM, ANY, *in_vmem(4)],
+    send = pl.pallas_call(
+        route_kernel,
+        out_shape=jax.ShapeDtypeStruct((n_ka, CAP + nk, 8, 128), F32),
+        in_specs=[SMEM, ANY, ANY],
         out_specs=pl.BlockSpec(memory_space=pltpu.VMEM),
-        scratch_shapes=[
-            pltpu.VMEM((nslot, 2 * rows, 2 * QW), BF16),
-            pltpu.VMEM((npair, 2 * rows, 2 * QW), BF16),
-            pltpu.VMEM((nk, 2 * rows, 2 * QW), F32),
-            pltpu.VMEM((nk, npair * rows, nt), F32),
-            pltpu.VMEM(((npair + nk) * rows, nt), F32),
-            pltpu.SemaphoreType.DMA((nslot,)),
-            pltpu.SemaphoreType.DMA((npair,)),
-        ],
-        compiler_params=pltpu.CompilerParams(vmem_limit_bytes=32 * 1024 * 1024),
-        name="exchange",
-    )(tab, own, big, full, w_hi, w_lo, c_full)
-    send, exch = pl.pallas_call(
-        route_kernel,
-        out_shape=(
-            jax.ShapeDtypeStruct((n_ka, CAP + nk, 8, 128), F32),
-            jax.ShapeDtypeStruct(exch.shape, F32),
-        ),
-        in_specs=[SMEM, ANY, ANY, *in_vmem(1)],
-        out_specs=tuple(in_vmem(2)),
         scratch_shapes=[
             pltpu.VMEM((nslot, 8, 128), F32),
             pltpu.VMEM((nslot, 8, 128), F32),
@@ -440,39 +424,72 @@
         ],
         compiler_params=pltpu.CompilerParams(vmem_limit_bytes=8 * 1024 * 1024),
         name="route",
-    )(tab, keep, came, exch)
+    )(tab, keep, came)
     with jax.named_scope("to_holders"):
         got = lax.all_to_all(send, "ka", 0, 0, tiled=True)
-    both = pl.pallas_call(
+    n = npair + nk
+    mine = pl.pallas_call(
         collect_kernel,
-        out_shape=jax.ShapeDtypeStruct((2 * (npair + nk), 8, 128), F32),
-        in_specs=[SMEM, *in_vmem(1), ANY],
+        out_shape=jax.ShapeDtypeStruct((n, 8, 128), F32),
+        in_specs=[SMEM, ANY],
         out_specs=pl.BlockSpec(memory_space=pltpu.VMEM),
         scratch_shapes=[pltpu.VMEM(send.shape, F32), pltpu.SemaphoreType.DMA],
         compiler_params=pltpu.CompilerParams(vmem_limit_bytes=8 * 1024 * 1024),
         name="collect",
-    )(own, exch, got)
-    with jax.named_scope("copies"):
-        others = [lax.ppermute(both, "ga", shift(r)) for r in range(1, 4)]
+    )(own, got)
+    with jax.named_scope("direct_copies"):
+        others = [lax.ppermute(mine, "ga", shift(r)) for r in range(1, 4)]
         place = jnp.stack([(a - r) % 4 for r in range(4)])
+    dmat = pl.pallas_call(
+        arrange_kernel,
+        out_shape=jax.ShapeDtypeStruct((n, nt, nt), F32),
+        in_specs=[SMEM, ANY, ANY, ANY, ANY],
+        out_specs=pl.BlockSpec(memory_space=pltpu.VMEM),
+        scratch_shapes=[pltpu.VMEM((4, n, 8, 128), F32), pltpu.SemaphoreType.DMA((4,))],
+        compiler_params=pltpu.CompilerParams(vmem_limit_bytes=8 * 1024 * 1024),
+        name="arrange",
+    )(place, mine, *others)
+    exch = pl.pallas_call(
+        exchange_kernel,
+        out_shape=jax.ShapeDtypeStruct((n, 8, 128), F32),
+        in_specs=[SMEM, SMEM, ANY, ANY, ANY, ANY, ANY, *in_vmem(1)],
+        out_specs=pl.BlockSpec(memory_space=pltpu.VMEM),
+        scratch_shapes=[
+            pltpu.VMEM((nk * nt, 4 * QW), BF16),
+            pltpu.VMEM((nk * nt, 4 * QW), BF16),
+            pltpu.VMEM((nk * nt, 4 * QW), BF16),
+            pltpu.VMEM((nslot, rows, 4 * QW), BF16),
+            pltpu.VMEM((npair, rows, 4 * QW), BF16),
+            pltpu.VMEM((nk, rows, 4 * QW), F32),
+            pltpu.VMEM((nk, npair * rows, nt), F32),
+            pltpu.VMEM((n * rows, nt), F32),
+            pltpu.SemaphoreType.DMA((3,)),
+            pltpu.SemaphoreType.DMA((nslot,)),
+            pltpu.SemaphoreType.DMA((npair,)),
+        ],
+        compiler_params=pltpu.CompilerParams(vmem_limit_bytes=60 * 1024 * 1024),
+        name="exchange",
+    )(tab, own, p_big, full, w_hi, w_lo, dmat, c_full)
+    with jax.named_scope("exchange_copies"):
+        others = [lax.ppermute(exch, "ga", shift(r)) for r in range(1, 4)]
     return pl.pallas_call(
         finish_kernel,
         out_shape=(
             jax.ShapeDtypeStruct((npair, nt * nt), F32),
             jax.ShapeDtypeStruct((nk, nt * nt), F32),
         ),
-        in_specs=[SMEM, ANY, ANY, ANY, ANY],
+        in_specs=[SMEM, *in_vmem(1), ANY, ANY, ANY, ANY],
         out_specs=tuple(in_vmem(2)),
         scratch_shapes=[
-            pltpu.VMEM((4, 2 * (npair + nk), 8, 128), F32),
-            pltpu.VMEM((npair + nk, nt, nt), F32),
-            pltpu.VMEM((npair + nk, nt, nt), F32),
-            pltpu.VMEM(((npair + nk) * half, 2 * nt), F32),
+            pltpu.VMEM((4, n, 8, 128), F32),
+            pltpu.VMEM((n, nt, nt), F32),
+            pltpu.VMEM((n, nt, nt), F32),
+            pltpu.VMEM((n * half, 2 * nt), F32),
             pltpu.SemaphoreType.DMA((4,)),
         ],
         compiler_params=pltpu.CompilerParams(vmem_limit_bytes=16 * 1024 * 1024),
         name="finish",
-    )(place, both, *others)
+    )(place, dmat, exch, *others)
 
 
 def solution(mesh):

time: 203 us -> 205 us (level)
  Pallas kernels: 16.9 us -> 26.3 us
  blocking collectives: 49.2 us -> 40.3 us
  waiting for transfers between devices: 71 us -> 62.9 us
  starting transfers between devices: 23.2 us -> 27.6 us
  local copies, waits for them, and re-layouts: 9.4 us -> 13.4 us
  other arithmetic: 15.9 us -> 18.8 us
    all_gather x1, waiting for transfers between devices: 36.5 us -> 10.3 us  [per_device(): big = lax.all_gather(payload, 'ka', axis=0, tiled=True)]
    all_to_all x1 -> x0, blocking collectives: 23.5 us -> none  [per_device(): got = lax.all_to_all(send, 'ka', 0, 0, tiled=True)]
    all_to_all x0 -> x1, waiting for transfers between devices: none -> 17.8 us  [per_device(): got = lax.all_to_all(send, 'ka', 0, 0, tiled=True)]
    ppermute x3, waiting for transfers between devices: 0.01 us -> 16.1 us  [per_device(): wk.append(lax.ppermute(v, 'ga', shift(r)) if r else v)]
    ppermute x9, waiting for transfers between devices: 30.6 us -> 14.9 us  [the longest x3 5.38 us: per_device(): others = [lax.ppermute(mine, 'ga', shift(r)) for r in range(1, 4)]]
    all_gather x0 -> x1, blocking collectives: none -> 14.6 us  [per_device(): full = lax.all_gather(widen(held), 'ga', axis=1, tiled=True)]
    all_to_all x0 -> x1, starting transfers between devices: none -> 6.38 us  [per_device(): got = lax.all_to_all(send, 'ka', 0, 0, tiled=True)]
    pallas_call x1, Pallas kernels: 6.55 us -> 12.3 us  [per_device(): pl.pallas_call(direct_kernel, out_shape=(jax.ShapeDtypeStruct((nslot, 8,...]
  transfers between devices with their start and end apart: 15 -> 17, of which waited for: 8 -> 10; matrix products, arithmetic and copies ran while one was open for 9% -> 13% of each run, Pallas kernels for 3% -> 8%
where the time goes in v6:
time: 205 us
  waiting for transfers between devices  62.9 us (31%)
  blocking collectives  40.3 us (20%)
  starting transfers between devices  27.6 us (13%)
  Pallas kernels  26.3 us (13%)
  other arithmetic  18.8 us (9%)
  between operations  15.9 us (8%)
  local copies, waits for them, and re-layouts  13.4 us (7%)
    all_gather x1, blocking collectives, per_device(): lax.all_gather(pairs, 'ka', axis=0, tiled=True).reshape(n_ka, npair, 3)  25.7 us
    all_to_all x1, waiting for transfers between devices, per_device(): got = lax.all_to_all(send, 'ka', 0, 0, tiled=True)  17.8 us
    ppermute x3, waiting for transfers between devices, per_device(): wk.append(lax.ppermute(v, 'ga', shift(r)) if r else v)  16.1 us
    all_gather x1, blocking collectives, per_device(): full = lax.all_gather(widen(held), 'ga', axis=1, tiled=True)  14.6 us
    pallas_call x1, Pallas kernels, per_device(): pl.pallas_call(direct_kernel, out_shape=(jax.ShapeDtypeStruct((nslot, 8,...  12.3 us
    all_gather x1, waiting for transfers between devices, per_device(): big = lax.all_gather(payload, 'ka', axis=0, tiled=True)  10.3 us
    pallas_call x1, Pallas kernels, per_device(): pl.pallas_call(exchange_kernel, out_shape=jax.ShapeDtypeStruct((n, 8, 128...  7 us
    all_to_all x1, starting transfers between devices, per_device(): got = lax.all_to_all(send, 'ka', 0, 0, tiled=True)  6.38 us
  transfers between devices with their start and end apart: 17, of which 10 were waited for; matrix products, arithmetic and copies ran while one was open for 13% of the time, Pallas kernels for 8%

profile of v6, /device:TPU:0, one launch (start us, length us, event | category | flops | bytes accessed | tf_op | source)
XLA Modules:
  0.0 205.2 jit_solution(1376436583548189052)
XLA Ops:
  7.2 2.9 %collective-permute-start.3 = (bf16[4,64,375]{2,1,0:T(8,128)(2,1)}, bf16[4,64,375]{2,1,0:T(8,128)(2,1)S(1)}, u32[]{:S(2)}, u32[]{:S(2)}) collective-permute-start(bf16[4,64,375]{2,1,0:T(8,128)(2,1)} %param.8), channel_id=1, source_target_pairs={{0,3},{1,2},{2,1},{3,0},{4,7},{5,6},{6,5},{7,4},{8,11},{9,10},{10,... | collective-permute-start | bytes 576008 | tf_op jit(solution)/shard_map/pack/ppermute | solution.py:293
  14.6 4.8 %collective-permute-done = bf16[4,32,375]{2,1,0:T(8,128)(2,1)S(1)} collective-permute-done((bf16[4,32,375]{2,1,0:T(8,128)(2,1)S(1)}, bf16[4,32,375]{2,1,0:T(8,128)(2,1)S(1)}, u32[]{:S(2)}, u32[]{:S(2)}) %collective-permute-start) | collective-permute-done | bytes 96032 | tf_op jit(solution)/shard_map/pack/ppermute | solution.py:295
  21.6 14.6 %all_gather.14.full_in = bf16[272,1536]{1,0:T(8,128)(2,1)S(1)} all-gather(bf16[272,384]{1,0:T(8,128)(2,1)S(1)} %fusion.27), channel_id=1, replica_groups=mesh['ka'=32,'ga'=4] {'ga'}, dimensions={1}, use_global_device_ids=true | all-gather | bytes 1044480 | tf_op jit(solution)/shard_map/exchange_pack/all_gather | solution.py:330
  38.9 3.6 %fusion.47 = (bf16[2,375,375]{2,0,1:T(2,128)(2,1)S(1)}, bf16[2,375,375]{2,0,1:T(2,128)(2,1)S(1)}, bf16[2,375,375]{2,0,1:T(2,128)(2,1)S(1)}, bf16[2,375,375]{2,0,1:T(2,128)(2,1)S(1)}) fusion(bf16[2,375,1500]{2,0,1:T(2,128)(2,1)S(1)} %copy-done.9), kind=kLoop, calls=%fused_computation.145 | loop fusion | bytes 4500000 | tf_op jit(solution)/shard_map/weights/slice | solution.py:308
  45.5 2.0 collective-permute-start.4
  50.0 2.5 %collective-permute-start.5 = (bf16[2,384,768]{2,1,0:T(8,128)(2,1)}, bf16[2,384,768]{2,1,0:T(8,128)(2,1)}, u32[]{:S(2)}, u32[]{:S(2)}) collective-permute-start(bf16[2,384,768]{2,1,0:T(8,128)(2,1)} %pad_maximum_fusion.2), channel_id=1, source_target_pairs={{0,2},{1,3},{2,0},{3,1},{4,6},{5,7},{6,4},{7,5},{8,10},{9,11},{10,... | collective-permute-start | bytes 3538952 | tf_op jit(solution)/shard_map/weights/ppermute | solution.py:321
  54.4 25.7 %all-gather = s32[32,16,3]{1,2,0:T(4,128)S(1)} all-gather(s32[1,16,3]{1,2,0:T(4,128)S(1)} %bitcast.46), channel_id=1, replica_groups=mesh['ka'=32,'ga'=4] {'ka'}, dimensions={0}, use_global_device_ids=true | all-gather | bytes 6336 | tf_op jit(solution)/shard_map/tables/all_gather | solution.py:341
  84.8 13.0 %collective-permute-done.4 = bf16[2,384,768]{2,1,0:T(8,128)(2,1)} collective-permute-done((bf16[2,384,768]{2,1,0:T(8,128)(2,1)}, bf16[2,384,768]{2,1,0:T(8,128)(2,1)}, u32[]{:S(2)}, u32[]{:S(2)}) %collective-permute-start.4) | collective-permute-done | bytes 1179680 | tf_op jit(solution)/shard_map/weights/ppermute | solution.py:321
  97.8 3.1 %collective-permute-done.6 = bf16[2,384,768]{2,1,0:T(8,128)(2,1)S(1)} collective-permute-done((bf16[2,384,768]{2,1,0:T(8,128)(2,1)}, bf16[2,384,768]{2,1,0:T(8,128)(2,1)S(1)}, u32[]{:S(2)}, u32[]{:S(2)}) %collective-permute-start.6) | collective-permute-done | bytes 1179680 | tf_op jit(solution)/shard_map/weights/ppermute | solution.py:321
  100.9 5.1 %pad_maximum_fusion.w = bf16[2,1536,768]{2,1,0:T(8,128)(2,1)} fusion(bf16[2,384,768]{2,1,0:T(8,128)(2,1)S(1)} %collective-permute-done.6, bf16[2,384,768]{2,1,0:T(8,128)(2,1)} %collective-permute-done.5, bf16[2,384,768]{2,1,0:T(8,128)(2,1)} %collective-permute-done.4, bf16[2,384,384]{2,1,0:T(8,128)(2,1)S(1)} %copy-done.8, bf16[2,384,384]{2,1,0:T(8,128)(2,1)S(1)} %copy-done.7), kind=kLoop, calls=%fused_computation | loop fusion | flops 23592960 | bytes 9437184 | tf_op jit(solution)/shard_map/weights/concatenate | solution.py:322
  105.9 10.3 %all-gather.4.cloned.1.call-done.big = bf16[128,128,768]{2,1,0:T(8,128)(2,1)} async-done(((bf16[4,128,768]{2,1,0:T(8,128)(2,1)}), bf16[128,128,768]{2,1,0:T(8,128)(2,1)}) %all-gather.4.cloned.1.call-update) | async-done | bytes 25165840 | tf_op jit(solution)/shard_map/spread/all_gather | solution.py:304
  116.3 2.3 %copy-done = bf16[2,1536,768]{2,1,0:T(8,128)(2,1)S(1)} copy-done((bf16[2,1536,768]{2,1,0:T(8,128)(2,1)S(1)}, bf16[2,1536,768]{2,1,0:T(8,128)(2,1)}, u32[]{:S(2)}) %copy-start) | copy-done | bytes 4718616
  118.6 12.3 %direct.1 = (f32[64,8,128]{2,1,0:T(8,128)S(1)}, f32[64,8,128]{2,1,0:T(8,128)S(1)}) custom-call(s32[4,80]{1,0:T(4,128)S(1)} %pad_add_fusion.1.plan, bf16[128,128,768]{2,1,0:T(8,128)(2,1)} %all-gather.4.cloned.1.call-done.big, bf16[2,1536,768]{2,1,0:T(8,128)(2,1)S(1)} %copy-done), custom_call_target="tpu_custom_call" | custom-call | tf_op jit(solution)/shard_map/direct/pallas_call | solution.py:395
  133.8 3.7 %collective-permute-done.7.came = f32[64,8,128]{2,1,0:T(8,128)S(1)} collective-permute-done((f32[64,8,128]{2,1,0:T(8,128)S(1)}, f32[64,8,128]{2,1,0:T(8,128)S(1)}, u32[]{:S(2)}, u32[]{:S(2)}) %collective-permute-start.7) | collective-permute-done | bytes 262176 | tf_op jit(solution)/shard_map/to_neighbour/ppermute | solution.py:414
  137.6 2.7 %route.1 = f32[32,6,8,128]{3,2,1,0:T(8,128)} custom-call(s32[7,64]{1,0:T(8,128)S(1)} %stack.74.tab, f32[64,8,128]{2,1,0:T(8,128)S(1)} %get-tuple-element.4.keep, f32[64,8,128]{2,1,0:T(8,128)S(1)} %collective-permute-done.7.came), custom_call_target="tpu_custom_call" | custom-call | tf_op jit(solution)/shard_map/route/pallas_call | solution.py:415
  140.2 6.4 %all-to-all-start = ((f32[32,6,8,128]{3,2,1,0:T(8,128)}), f32[32,6,8,128]{3,2,1,0:T(8,128)S(1)}, u32[]{:S(2)}, u32[]{:S(2)}) async-start(f32[32,6,8,128]{3,2,1,0:T(8,128)} %route.1), calls=%async_computation | async-start | bytes 1572864 | tf_op jit(solution)/shard_map/to_holders/all_to_all | solution.py:429
  148.9 17.8 %all-to-all-done.got = f32[32,6,8,128]{3,2,1,0:T(8,128)S(1)} async-done(((f32[32,6,8,128]{3,2,1,0:T(8,128)}), f32[32,6,8,128]{3,2,1,0:T(8,128)S(1)}, u32[]{:S(2)}, u32[]{:S(2)}) %all-to-all-start) | async-done | bytes 786464 | tf_op jit(solution)/shard_map/to_holders/all_to_all | solution.py:429
  167.4 2.8 %collective-permute-start.10 = (f32[20,8,128]{2,1,0:T(8,128)S(1)}, f32[20,8,128]{2,1,0:T(8,128)S(1)}, u32[]{:S(2)}, u32[]{:S(2)}) collective-permute-start(f32[20,8,128]{2,1,0:T(8,128)S(1)} %collect.1.r0), channel_id=1, source_target_pairs={{0,3},{1,0},{2,1},{3,2},{4,7},{5,4},{6,5},{7,6},{8,11},{9,8},{10,9... | collective-permute-start | bytes 245768 | tf_op jit(solution)/shard_map/direct_copies/ppermute | solution.py:441
  170.2 2.3 %collective-permute-start.9 = (f32[20,8,128]{2,1,0:T(8,128)S(1)}, f32[20,8,128]{2,1,0:T(8,128)S(1)}, u32[]{:S(2)}, u32[]{:S(2)}) collective-permute-start(f32[20,8,128]{2,1,0:T(8,128)S(1)} %collect.1.r0), channel_id=1, source_target_pairs={{0,2},{1,3},{2,0},{3,1},{4,6},{5,7},{6,4},{7,5},{8,10},{9,11},{10,... | collective-permute-start | bytes 245768 | tf_op jit(solution)/shard_map/direct_copies/ppermute | solution.py:441
  172.8 5.2 %collective-permute-done.8.r1 = f32[20,8,128]{2,1,0:T(8,128)S(1)} collective-permute-done((f32[20,8,128]{2,1,0:T(8,128)S(1)}, f32[20,8,128]{2,1,0:T(8,128)S(1)}, u32[]{:S(2)}, u32[]{:S(2)}) %collective-permute-start.8) | collective-permute-done | bytes 81952 | tf_op jit(solution)/shard_map/direct_copies/ppermute | solution.py:441
  180.1 7.0 %exchange.1.r0 = f32[20,8,128]{2,1,0:T(8,128)} custom-call(s32[7,64]{1,0:T(8,128)} %copy-done.4, s32[4,16]{1,0:T(4,128)} %copy-done.5, bf16[128,16,1536]{2,1,0:T(8,128)(2,1)} %all-gather.6.cloned.1.call-done.big, bf16[272,1536]{1,0:T(8,128)(2,1)} %copy-done.6, bf16[256,1536]{1,0:T(8,128)(2,1)} %get-tuple-element.38.whi_in, ...), custom_call_target="tpu_custom_call" | custom-call | tf_op jit(solution)/shard_map/exchange/pallas_call | solution.py:452
  187.2 2.9 %collective-permute-start.12 = (f32[20,8,128]{2,1,0:T(8,128)}, f32[20,8,128]{2,1,0:T(8,128)S(1)}, u32[]{:S(2)}, u32[]{:S(2)}) collective-permute-start(f32[20,8,128]{2,1,0:T(8,128)} %exchange.1.r0), channel_id=1, source_target_pairs={{0,2},{1,3},{2,0},{3,1},{4,6},{5,7},{6,4},{7,5},{8,10},{9,11},{10,... | collective-permute-start | bytes 245768 | tf_op jit(solution)/shard_map/exchange_copies/ppermute | solution.py:474
  190.5 4.1 %collective-permute-done.11.r1 = f32[20,8,128]{2,1,0:T(8,128)S(1)} collective-permute-done((f32[20,8,128]{2,1,0:T(8,128)}, f32[20,8,128]{2,1,0:T(8,128)S(1)}, u32[]{:S(2)}, u32[]{:S(2)}) %collective-permute-start.11) | collective-permute-done | bytes 81952 | tf_op jit(solution)/shard_map/exchange_copies/ppermute | solution.py:474
  196.0 2.4 %finish.1 = (f32[16,4096]{1,0:T(8,128)}, f32[4,4096]{1,0:T(4,128)}) custom-call(s32[4]{0:T(128)S(1)} %pad_add_fusion.2.place, f32[20,64,64]{2,1,0:T(8,128)S(1)} %copy-done.2, f32[20,8,128]{2,1,0:T(8,128)S(1)} %copy-done.3, f32[20,8,128]{2,1,0:T(8,128)S(1)} %collective-permute-done.11.r1, f32[20,8,128]{2,1,0:T(8,128)S(1)} %collective-permute-done.12.r2, ...), custom_call_target="tpu_custom_call" | custom-call | tf_op jit(solution)/shard_map/finish/pallas_call | solution.py:475
  (122 shorter events, 29.9 us)
Async XLA Ops:
  7.2 109.1 %all-gather.4.cloned.1.call-start = ((), (), s32[]{:S(2)}) async-start(), calls=%async_computation.1 | async-start | bytes 25952256 | tf_op jit(solution)/shard_map/spread/all_gather | solution.py:304
  7.2 12.3 %collective-permute-start.3 = (bf16[4,64,375]{2,1,0:T(8,128)(2,1)}, bf16[4,64,375]{2,1,0:T(8,128)(2,1)S(1)}, u32[]{:S(2)}, u32[]{:S(2)}) collective-permute-start(bf16[4,64,375]{2,1,0:T(8,128)(2,1)} %param.8), channel_id=1, source_target_pairs={{0,3},{1,2},{2,1},{3,0},{4,7},{5,6},{6,5},{7,4},{8,11},{9,10},{10,... | collective-permute-start | bytes 576008 | tf_op jit(solution)/shard_map/pack/ppermute | solution.py:293
  11.1 8.3 %collective-permute-start = (bf16[4,32,375]{2,1,0:T(8,128)(2,1)S(1)}, bf16[4,32,375]{2,1,0:T(8,128)(2,1)S(1)}, u32[]{:S(2)}, u32[]{:S(2)}) collective-permute-start(bf16[4,32,375]{2,1,0:T(8,128)(2,1)S(1)} %get-tuple-element.42), channel_id=1, source_target_pairs={{0,1},{1,2},{2,3},{3,0},{4,5},{5,6},{6,7},{7,4},{8,9},{9,10},{10,1... | collective-permute-start | bytes 288008 | tf_op jit(solution)/shard_map/pack/ppermute | solution.py:295
  11.4 8.1 %collective-permute-start.1 = (bf16[4,32,375]{2,1,0:T(8,128)(2,1)S(1)}, bf16[4,32,375]{2,1,0:T(8,128)(2,1)S(1)}, u32[]{:S(2)}, u32[]{:S(2)}) collective-permute-start(bf16[4,32,375]{2,1,0:T(8,128)(2,1)S(1)} %get-tuple-element.40), channel_id=1, source_target_pairs={{0,2},{1,3},{2,0},{3,1},{4,6},{5,7},{6,4},{7,5},{8,10},{9,11},{10,... | collective-permute-start | bytes 288008 | tf_op jit(solution)/shard_map/pack/ppermute | solution.py:295
  13.1 6.4 %collective-permute-start.2 = (bf16[4,32,375]{2,1,0:T(8,128)(2,1)S(1)}, bf16[4,32,375]{2,1,0:T(8,128)(2,1)S(1)}, u32[]{:S(2)}, u32[]{:S(2)}) collective-permute-start(bf16[4,32,375]{2,1,0:T(8,128)(2,1)S(1)} %get-tuple-element.41), channel_id=1, source_target_pairs={{0,3},{1,0},{2,1},{3,2},{4,7},{5,4},{6,5},{7,6},{8,11},{9,8},{10,9... | collective-permute-start | bytes 288008 | tf_op jit(solution)/shard_map/pack/ppermute | solution.py:295
  21.4 158.7 %all-gather.6.cloned.1.call-start = ((), (), s32[]{:S(2)}) async-start(), calls=%async_computation.2 | async-start | bytes 6488064 | tf_op jit(solution)/shard_map/exchange_pack/all_gather | solution.py:333
  21.6 17.3 %copy-start.9 = (bf16[2,375,1500]{2,0,1:T(2,128)(2,1)S(1)}, bf16[2,375,1500]{2,0,1:T(2,128)(2,1)}, u32[]{:S(2)}) copy-start(bf16[2,375,1500]{2,0,1:T(2,128)(2,1)} %param.11) | copy-start | bytes 6750004
  36.2 111.2 %copy-start.6 = (bf16[272,1536]{1,0:T(8,128)(2,1)}, bf16[272,1536]{1,0:T(8,128)(2,1)S(1)}, u32[]{:S(2)}) copy-start(bf16[272,1536]{1,0:T(8,128)(2,1)S(1)} %all_gather.14.full_in) | copy-start | bytes 2506756
  45.5 52.3 %collective-permute-start.4 = (bf16[2,384,768]{2,1,0:T(8,128)(2,1)}, bf16[2,384,768]{2,1,0:T(8,128)(2,1)}, u32[]{:S(2)}, u32[]{:S(2)}) collective-permute-start(bf16[2,384,768]{2,1,0:T(8,128)(2,1)} %pad_maximum_fusion.1), channel_id=1, source_target_pairs={{0,1},{1,2},{2,3},{3,0},{4,5},{5,6},{6,7},{7,4},{8,9},{9,10},{10,1... | collective-permute-start | bytes 3538952 | tf_op jit(solution)/shard_map/weights/ppermute | solution.py:321
  50.0 47.7 %collective-permute-start.5 = (bf16[2,384,768]{2,1,0:T(8,128)(2,1)}, bf16[2,384,768]{2,1,0:T(8,128)(2,1)}, u32[]{:S(2)}, u32[]{:S(2)}) collective-permute-start(bf16[2,384,768]{2,1,0:T(8,128)(2,1)} %pad_maximum_fusion.2), channel_id=1, source_target_pairs={{0,2},{1,3},{2,0},{3,1},{4,6},{5,7},{6,4},{7,5},{8,10},{9,11},{10,... | collective-permute-start | bytes 3538952 | tf_op jit(solution)/shard_map/weights/ppermute | solution.py:321
  53.0 27.2 %copy-start.13 = (s32[64]{0:T(128)S(1)}, s32[64]{0:T(128)}, u32[]{:S(2)}) copy-start(s32[64]{0:T(128)} %param.13) | copy-start | bytes 772
  53.0 47.8 %copy-start.7 = (bf16[2,384,384]{2,1,0:T(8,128)(2,1)S(1)}, bf16[2,384,384]{2,1,0:T(8,128)(2,1)}, u32[]{:S(2)}) copy-start(bf16[2,384,384]{2,1,0:T(8,128)(2,1)} %get-tuple-element.25) | copy-start | bytes 1769476
  53.1 47.8 %copy-start.8 = (bf16[2,384,384]{2,1,0:T(8,128)(2,1)S(1)}, bf16[2,384,384]{2,1,0:T(8,128)(2,1)}, u32[]{:S(2)}) copy-start(bf16[2,384,384]{2,1,0:T(8,128)(2,1)} %get-tuple-element.28) | copy-start | bytes 1769476
  54.2 46.7 %collective-permute-start.6 = (bf16[2,384,768]{2,1,0:T(8,128)(2,1)}, bf16[2,384,768]{2,1,0:T(8,128)(2,1)S(1)}, u32[]{:S(2)}, u32[]{:S(2)}) collective-permute-start(bf16[2,384,768]{2,1,0:T(8,128)(2,1)} %pad_maximum_fusion.3), channel_id=1, source_target_pairs={{0,3},{1,0},{2,1},{3,2},{4,7},{5,4},{6,5},{7,6},{8,11},{9,8},{10,9... | collective-permute-start | bytes 3538952 | tf_op jit(solution)/shard_map/weights/ppermute | solution.py:321
  130.9 6.6 %collective-permute-start.7 = (f32[64,8,128]{2,1,0:T(8,128)S(1)}, f32[64,8,128]{2,1,0:T(8,128)S(1)}, u32[]{:S(2)}, u32[]{:S(2)}) collective-permute-start(f32[64,8,128]{2,1,0:T(8,128)S(1)} %get-tuple-element.5), channel_id=1, source_target_pairs={{0,1},{1,0},{2,3},{3,2},{4,5},{5,4},{6,7},{7,6},{8,9},{9,8},{10,11... | collective-permute-start | bytes 786440 | tf_op jit(solution)/shard_map/to_neighbour/ppermute | solution.py:414
  133.8 15.1 %copy-start.4 = (s32[7,64]{1,0:T(8,128)}, s32[7,64]{1,0:T(8,128)S(1)}, u32[]{:S(2)}) copy-start(s32[7,64]{1,0:T(8,128)S(1)} %stack.74.tab) | copy-start | bytes 5380
  140.2 26.5 %all-to-all-start = ((f32[32,6,8,128]{3,2,1,0:T(8,128)}), f32[32,6,8,128]{3,2,1,0:T(8,128)S(1)}, u32[]{:S(2)}, u32[]{:S(2)}) async-start(f32[32,6,8,128]{3,2,1,0:T(8,128)} %route.1), calls=%async_computation | async-start | bytes 1572864 | tf_op jit(solution)/shard_map/to_holders/all_to_all | solution.py:429
  147.5 19.9 %copy-start.5 = (s32[4,16]{1,0:T(4,128)}, s32[4,16]{1,0:T(4,128)S(1)}, u32[]{:S(2)}) copy-start(s32[4,16]{1,0:T(4,128)S(1)} %pad_add_fusion.own) | copy-start | bytes 772
  167.4 5.3 %collective-permute-start.10 = (f32[20,8,128]{2,1,0:T(8,128)S(1)}, f32[20,8,128]{2,1,0:T(8,128)S(1)}, u32[]{:S(2)}, u32[]{:S(2)}) collective-permute-start(f32[20,8,128]{2,1,0:T(8,128)S(1)} %collect.1.r0), channel_id=1, source_target_pairs={{0,3},{1,0},{2,1},{3,2},{4,7},{5,4},{6,5},{7,6},{8,11},{9,8},{10,9... | collective-permute-start | bytes 245768 | tf_op jit(solution)/shard_map/direct_copies/ppermute | solution.py:441
  170.2 7.8 %collective-permute-start.8 = (f32[20,8,128]{2,1,0:T(8,128)S(1)}, f32[20,8,128]{2,1,0:T(8,128)S(1)}, u32[]{:S(2)}, u32[]{:S(2)}) collective-permute-start(f32[20,8,128]{2,1,0:T(8,128)S(1)} %collect.1.r0), channel_id=1, source_target_pairs={{0,1},{1,2},{2,3},{3,0},{4,5},{5,6},{6,7},{7,4},{8,9},{9,10},{10,1... | collective-permute-start | bytes 245768 | tf_op jit(solution)/shard_map/direct_copies/ppermute | solution.py:441
  170.2 7.8 %collective-permute-start.9 = (f32[20,8,128]{2,1,0:T(8,128)S(1)}, f32[20,8,128]{2,1,0:T(8,128)S(1)}, u32[]{:S(2)}, u32[]{:S(2)}) collective-permute-start(f32[20,8,128]{2,1,0:T(8,128)S(1)} %collect.1.r0), channel_id=1, source_target_pairs={{0,2},{1,3},{2,0},{3,1},{4,6},{5,7},{6,4},{7,5},{8,10},{9,11},{10,... | collective-permute-start | bytes 245768 | tf_op jit(solution)/shard_map/direct_copies/ppermute | solution.py:441
  187.1 7.4 %collective-permute-start.11 = (f32[20,8,128]{2,1,0:T(8,128)}, f32[20,8,128]{2,1,0:T(8,128)S(1)}, u32[]{:S(2)}, u32[]{:S(2)}) collective-permute-start(f32[20,8,128]{2,1,0:T(8,128)} %exchange.1.r0), channel_id=1, source_target_pairs={{0,1},{1,2},{2,3},{3,0},{4,5},{5,6},{6,7},{7,4},{8,9},{9,10},{10,1... | collective-permute-start | bytes 245768 | tf_op jit(solution)/shard_map/exchange_copies/ppermute | solution.py:474
  187.2 7.3 %collective-permute-start.12 = (f32[20,8,128]{2,1,0:T(8,128)}, f32[20,8,128]{2,1,0:T(8,128)S(1)}, u32[]{:S(2)}, u32[]{:S(2)}) collective-permute-start(f32[20,8,128]{2,1,0:T(8,128)} %exchange.1.r0), channel_id=1, source_target_pairs={{0,2},{1,3},{2,0},{3,1},{4,6},{5,7},{6,4},{7,5},{8,10},{9,11},{10,... | collective-permute-start | bytes 245768 | tf_op jit(solution)/shard_map/exchange_copies/ppermute | solution.py:474
  190.2 5.0 %collective-permute-start.13 = (f32[20,8,128]{2,1,0:T(8,128)}, f32[20,8,128]{2,1,0:T(8,128)S(1)}, u32[]{:S(2)}, u32[]{:S(2)}) collective-permute-start(f32[20,8,128]{2,1,0:T(8,128)} %exchange.1.r0), channel_id=1, source_target_pairs={{0,3},{1,0},{2,1},{3,2},{4,7},{5,4},{6,5},{7,6},{8,11},{9,8},{10,9... | collective-permute-start | bytes 245768 | tf_op jit(solution)/shard_map/exchange_copies/ppermute | solution.py:474
  (7 other events, 49.1 us)
Sparse Core Ops, SparseCore 0:
  21.5 94.6 all-gather.3
  119.1 55.2 all-gather.5

commit v7 on v6

--- a/solution.py
+++ b/solution.py
@@ -133,9 +133,9 @@
 
 
 def exchange_kernel(
-    tab, own, big, full_in, whi_in, wlo_in, dmat, cw, out, full, whi, wlo, p1, p2, tot, prod, flat, s0, s1, s2
+    firsts, own, big, full_in, whi_in, wlo_in, early, late, cw, out, full, whi, wlo, p1, p2, tot, prod, flat, s0, s1, s2
 ):
-    nslot = tab.shape[1]
+    count = firsts[2, 0]
     npair = own.shape[1]
     nk, rows, wide = tot.shape
     nt = whi_in.shape[0] // nk
@@ -144,7 +144,7 @@
         return pltpu.make_async_copy(big.at[own[1, j]], p2.at[j], s2.at[j])
 
     def first(t):
-        return pltpu.make_async_copy(big.at[tab[6, t]], p1.at[t], s1.at[t])
+        return pltpu.make_async_copy(big.at[firsts[0, t]], p1.at[t], s1.at[t])
 
     loads = [
         pltpu.make_async_copy(whi_in, whi, s0.at[0]),
@@ -157,13 +157,10 @@
         c.start()
 
     def begin(t, carry):
-        @pl.when(tab[4, t] == 1)
-        def _():
-            first(t).start()
-
+        first(t).start()
         return carry
 
-    lax.fori_loop(0, nslot, begin, 0)
+    lax.fori_loop(0, count, begin, 0)
     tot[...] = jnp.zeros_like(tot)
     for j in range(npair):
         second(j).wait()
@@ -183,15 +180,12 @@
         flat[r, :] = prod[own[0, j], r, :]
 
     def gather(t, carry):
-        @pl.when(tab[4, t] == 1)
-        def _():
-            first(t).wait()
-            k = tab[5, t]
-            tot[k] = tot[k] + p1[t].astype(F32)
-
+        first(t).wait()
+        k = firsts[1, t]
+        tot[k] = tot[k] + p1[t].astype(F32)
         return carry
 
-    lax.fori_loop(0, nslot, gather, 0)
+    lax.fori_loop(0, count, gather, 0)
     w = tot[...].reshape(nk * rows, wide) * cw[...]
     hi = w.astype(BF16)
     lo = (w - hi.astype(F32)).astype(BF16)
@@ -297,9 +291,8 @@
         def side(left, right):
             return jnp.concatenate([widen(left), widen(right)], axis=2)
 
-        payload = jnp.concatenate(
-            [side(cut[0], cut[1]), side(cut[2], cut[3]), side(y, y_far)], axis=1
-        )
+        y_both = side(jnp.where(a < 2, y, y_far), jnp.where(a < 2, y_far, y))
+        payload = jnp.concatenate([side(cut[0], cut[1]), side(cut[2], cut[3]), y_both], axis=1)
     with jax.named_scope("spread"):
         big = lax.all_gather(payload, "ka", axis=0, tiled=True)
 
@@ -308,16 +301,12 @@
             jnp.pad(w[:, :, i * gl : (i + 1) * gl], ((0, 0), (0, QW - gl), (0, QW - gl)))
             for i in range(4)
         ]
+        outer = jnp.concatenate([cols[0], cols[3]], axis=2)
+        inner = jnp.concatenate([cols[1], cols[2]], axis=2)
         wk = []
         for r in range(4):
             to = (a + r) % 4
-            left = jnp.where(
-                to < 2, jnp.where(to == 0, cols[0], cols[1]), jnp.where(to == 2, cols[2], cols[3])
-            )
-            right = jnp.where(
-                to < 2, jnp.where(to == 0, cols[3], cols[2]), jnp.where(to == 2, cols[1], cols[0])
-            )
-            v = jnp.concatenate([left, right], axis=2)
+            v = jnp.where((to == 0) | (to == 3), outer, inner)
             wk.append(lax.ppermute(v, "ga", shift(r)) if r else v)
         wk = jnp.concatenate(wk, axis=1)
 
@@ -387,11 +376,18 @@
         pos = jnp.where(slot == 0, rank, chunks_first * CH + rank)
         hot = (pos[None, :] == jnp.arange(npos)[:, None]) & (used == 1)[None, :]
 
-        def at_pos(v):
+        def at_pos(v, hot):
             return jnp.sum(jnp.where(hot, v[None, :], 0), axis=1)
 
         heads = jnp.pad(jnp.stack([chunks_first, chunks, a % 2]), (0, npos - 3))
-        plan = jnp.stack([at_pos(order - nslot) + nslot, at_pos(tab[1]), at_pos(tab[2]), heads])
+        plan = jnp.stack(
+            [at_pos(order - nslot, hot) + nslot, at_pos(tab[1], hot), at_pos(tab[2], hot), heads]
+        )
+        named = tab[4]
+        rank = jnp.sum(jnp.where(order[:, None] > order[None, :], named[None, :], 0), axis=1)
+        hot = (rank[None, :] == order[:, None]) & (named == 1)[None, :]
+        total = jnp.broadcast_to(jnp.sum(named), (nslot,))
+        firsts = jnp.stack([at_pos(tab[6], hot), at_pos(tab[5], hot), total])
     keep, away = pl.pallas_call(
         direct_kernel,
         out_shape=(jax.ShapeDtypeStruct((nslot, 8, 128), F32),) * 2,
@@ -452,7 +448,7 @@
     exch = pl.pallas_call(
         exchange_kernel,
         out_shape=jax.ShapeDtypeStruct((n, 8, 128), F32),
-        in_specs=[SMEM, SMEM, ANY, ANY, ANY, ANY, ANY, *in_vmem(1)],
+        in_specs=[SMEM, SMEM, ANY, ANY, ANY, ANY, ANY, ANY, *in_vmem(1)],
         out_specs=pl.BlockSpec(memory_space=pltpu.VMEM),
         scratch_shapes=[
             pltpu.VMEM((nk * nt, 4 * QW), BF16),
@@ -467,18 +463,18 @@
             pltpu.SemaphoreType.DMA((nslot,)),
             pltpu.SemaphoreType.DMA((npair,)),
         ],
-        compiler_params=pltpu.CompilerParams(vmem_limit_bytes=60 * 1024 * 1024),
+        compiler_params=pltpu.CompilerParams(vmem_limit_bytes=50 * 1024 * 1024),
         name="exchange",
-    )(tab, own, p_big, full, w_hi, w_lo, dmat, c_full)
+    )(firsts, own, p_big, full, w_hi, w_lo, others[0], others[2], c_full)
     with jax.named_scope("exchange_copies"):
-        others = [lax.ppermute(exch, "ga", shift(r)) for r in range(1, 4)]
+        exch_others = [lax.ppermute(exch, "ga", shift(r)) for r in range(1, 4)]
     return pl.pallas_call(
         finish_kernel,
         out_shape=(
             jax.ShapeDtypeStruct((npair, nt * nt), F32),
             jax.ShapeDtypeStruct((nk, nt * nt), F32),
         ),
-        in_specs=[SMEM, *in_vmem(1), ANY, ANY, ANY, ANY],
+        in_specs=[SMEM, *in_vmem(2), ANY, ANY, ANY],
         out_specs=tuple(in_vmem(2)),
         scratch_shapes=[
             pltpu.VMEM((4, n, 8, 128), F32),
@@ -489,7 +485,7 @@
         ],
         compiler_params=pltpu.CompilerParams(vmem_limit_bytes=16 * 1024 * 1024),
         name="finish",
-    )(place, dmat, exch, *others)
+    )(place, dmat, exch, *exch_others)
 
 
 def solution(mesh):

time: 205 us -> 200 us (0.976)
  Pallas kernels: 26.3 us -> 16.1 us
  starting transfers between devices: 27.6 us -> 33.8 us
  waiting for transfers between devices: 62.9 us -> 66.4 us
  other arithmetic: 18.8 us -> 15.6 us
    pallas_call x1, Pallas kernels: 12.3 us -> 4.91 us  [per_device(): pl.pallas_call(direct_kernel, out_shape=(jax.ShapeDtypeStruct((nslot, 8,...]
    all_to_all x1, starting transfers between devices: 6.38 us -> 12.7 us  [per_device(): got = lax.all_to_all(send, 'ka', 0, 0, tiled=True)]
    ppermute x3, waiting for transfers between devices: 4.84 us -> 0.51 us  [per_device(): cut = cut[:1] + [lax.ppermute(cut[r], 'ga', shift(r)) for r in range(1, 4)]]
    concatenate x4 -> x1, other arithmetic: 5.28 us -> 1 us  [per_device(): jnp.concatenate([side(cut[0], cut[1]), side(cut[2], cut[3]), y_both], axi...]
    ppermute x1, waiting for transfers between devices: 0.01 us -> 3.36 us  [per_device(): y_far = lax.ppermute(y, 'ga', [(i, 3 - i) for i in range(4)])]
    all_gather x1, waiting for transfers between devices: 10.3 us -> 13.2 us  [per_device(): big = lax.all_gather(payload, 'ka', axis=0, tiled=True)]
    pallas_call x1, Pallas kernels: 7 us -> 4.41 us  [per_device(): pl.pallas_call(exchange_kernel, out_shape=jax.ShapeDtypeStruct((n, 8, 128...]
    ppermute x1, waiting for transfers between devices: 3.74 us -> 6.05 us  [per_device(): came = lax.ppermute(away, 'ga', [(0, 1), (1, 0), (2, 3), (3, 2)])]
  transfers between devices with their start and end apart: 17 -> 17, of which waited for: 10 -> 11; matrix products, arithmetic and copies ran while one was open for 13% -> 12% of each run, Pallas kernels for 8% -> 7%
where the time goes in v7:
time: 200 us
  waiting for transfers between devices  66.4 us (33%)
  blocking collectives  40.3 us (20%)
  starting transfers between devices  33.8 us (17%)
  Pallas kernels  16.1 us (8%)
  between operations  15.9 us (8%)
  other arithmetic  15.6 us (8%)
  local copies, waits for them, and re-layouts  12.1 us (6%)
    all_gather x1, blocking collectives, per_device(): lax.all_gather(pairs, 'ka', axis=0, tiled=True).reshape(n_ka, npair, 3)  25.7 us
    all_to_all x1, waiting for transfers between devices, per_device(): got = lax.all_to_all(send, 'ka', 0, 0, tiled=True)  18.9 us
    ppermute x3, waiting for transfers between devices, per_device(): wk.append(lax.ppermute(v, 'ga', shift(r)) if r else v)  15.2 us
    all_gather x1, blocking collectives, per_device(): full = lax.all_gather(widen(held), 'ga', axis=1, tiled=True)  14.6 us
    all_gather x1, waiting for transfers between devices, per_device(): big = lax.all_gather(payload, 'ka', axis=0, tiled=True)  13.2 us
    all_to_all x1, starting transfers between devices, per_device(): got = lax.all_to_all(send, 'ka', 0, 0, tiled=True)  12.7 us
    ppermute x1, waiting for transfers between devices, per_device(): came = lax.ppermute(away, 'ga', [(0, 1), (1, 0), (2, 3), (3, 2)])  6.05 us
    ppermute x3, starting transfers between devices, per_device(): others = [lax.ppermute(mine, 'ga', shift(r)) for r in range(1, 4)]  5.15 us
  transfers between devices with their start and end apart: 17, of which 11 were waited for; matrix products, arithmetic and copies ran while one was open for 12% of the time, Pallas kernels for 7%

profile of v7, /device:TPU:0, one launch (start us, length us, event | category | flops | bytes accessed | tf_op | source)
XLA Modules:
  0.0 200.1 jit_solution(11130982692180175956)
XLA Ops:
  7.2 2.9 %collective-permute-start.3 = (bf16[4,64,375]{2,1,0:T(8,128)(2,1)}, bf16[4,64,375]{2,1,0:T(8,128)(2,1)S(1)}, u32[]{:S(2)}, u32[]{:S(2)}) collective-permute-start(bf16[4,64,375]{2,1,0:T(8,128)(2,1)} %param.8), channel_id=1, source_target_pairs={{0,3},{1,2},{2,1},{3,0},{4,7},{5,6},{6,5},{7,4},{8,11},{9,10},{10,... | collective-permute-start | bytes 576008 | tf_op jit(solution)/shard_map/pack/ppermute | solution.py:287
  14.6 3.4 %collective-permute-done.3 = bf16[4,64,375]{2,1,0:T(8,128)(2,1)S(1)} collective-permute-done((bf16[4,64,375]{2,1,0:T(8,128)(2,1)}, bf16[4,64,375]{2,1,0:T(8,128)(2,1)S(1)}, u32[]{:S(2)}, u32[]{:S(2)}) %collective-permute-start.3) | collective-permute-done | bytes 192032 | tf_op jit(solution)/shard_map/pack/ppermute | solution.py:287
  20.7 14.6 %all_gather.14.full_in = bf16[272,1536]{1,0:T(8,128)(2,1)S(1)} all-gather(bf16[272,384]{1,0:T(8,128)(2,1)S(1)} %fusion.33), channel_id=1, replica_groups=mesh['ka'=32,'ga'=4] {'ga'}, dimensions={1}, use_global_device_ids=true | all-gather | bytes 1044480 | tf_op jit(solution)/shard_map/exchange_pack/all_gather | solution.py:319
  38.0 3.6 %fusion.54 = (bf16[2,375,375]{2,0,1:T(2,128)(2,1)S(1)}, bf16[2,375,375]{2,0,1:T(2,128)(2,1)S(1)}, bf16[2,375,375]{2,0,1:T(2,128)(2,1)S(1)}, bf16[2,375,375]{2,0,1:T(2,128)(2,1)S(1)}) fusion(bf16[2,375,1500]{2,0,1:T(2,128)(2,1)S(1)} %copy-done.1), kind=kLoop, calls=%fused_computation.156 | loop fusion | bytes 4500000 | tf_op jit(solution)/shard_map/weights/slice | solution.py:301
  41.9 2.4 %broadcast_select_fusion.3 = (bf16[2,384,768]{2,1,0:T(8,128)(2,1)}, bf16[2,384,768]{2,1,0:T(8,128)(2,1)}, bf16[2,384,768]{2,1,0:T(8,128)(2,1)}) fusion(pred[]{:T(512)S(6)} %or.12, bf16[2,375,375]{2,1,0:T(8,128)(2,1)S(1)} %copy.90, bf16[2,375,375]{2,1,0:T(8,128)(2,1)S(1)} %copy.89, bf16[2,375,375]{2,1,0:T(8,128)(2,1)S(1)} %copy.88, ...), kind=kLoop, calls=%fused_computation.39 | loop fusion | flops 10027008 | bytes 5788947 | tf_op jit(solution)/shard_map/weights/jit(_where)/select_n | solution.py:309
  44.3 2.0 collective-permute-start.4
  46.3 2.5 %collective-permute-start.5 = (bf16[2,384,768]{2,1,0:T(8,128)(2,1)}, bf16[2,384,768]{2,1,0:T(8,128)(2,1)}, u32[]{:S(2)}, u32[]{:S(2)}) collective-permute-start(bf16[2,384,768]{2,1,0:T(8,128)(2,1)} %get-tuple-element.27), channel_id=1, source_target_pairs={{0,2},{1,3},{2,0},{3,1},{4,6},{5,7},{6,4},{7,5},{8,10},{9,11},{10,... | collective-permute-start | bytes 3538952 | tf_op jit(solution)/shard_map/weights/ppermute | solution.py:310
  50.3 25.7 %all-gather = s32[32,16,3]{1,2,0:T(4,128)S(1)} all-gather(s32[1,16,3]{1,2,0:T(4,128)S(1)} %bitcast.49), channel_id=1, replica_groups=mesh['ka'=32,'ga'=4] {'ka'}, dimensions={0}, use_global_device_ids=true | all-gather | bytes 6336 | tf_op jit(solution)/shard_map/tables/all_gather | solution.py:330
  81.9 14.7 %collective-permute-done.4 = bf16[2,384,768]{2,1,0:T(8,128)(2,1)} collective-permute-done((bf16[2,384,768]{2,1,0:T(8,128)(2,1)}, bf16[2,384,768]{2,1,0:T(8,128)(2,1)}, u32[]{:S(2)}, u32[]{:S(2)}) %collective-permute-start.4) | collective-permute-done | bytes 1179680 | tf_op jit(solution)/shard_map/weights/ppermute | solution.py:310
  97.1 5.1 %pad_maximum_fusion.w = bf16[2,1536,768]{2,1,0:T(8,128)(2,1)} fusion(bf16[2,384,768]{2,1,0:T(8,128)(2,1)S(1)} %collective-permute-done.6, bf16[2,384,768]{2,1,0:T(8,128)(2,1)} %collective-permute-done.5, bf16[2,384,768]{2,1,0:T(8,128)(2,1)} %collective-permute-done.4, bf16[2,384,768]{2,1,0:T(8,128)(2,1)} %get-tuple-element.25), kind=kLoop, calls=%fused_computation | loop fusion | flops 18874368 | bytes 9437184 | tf_op jit(solution)/shard_map/weights/concatenate | solution.py:311
  102.1 13.2 %all-gather.4.cloned.1.call-done.big = bf16[128,128,768]{2,1,0:T(8,128)(2,1)} async-done(((bf16[4,128,768]{2,1,0:T(8,128)(2,1)}), bf16[128,128,768]{2,1,0:T(8,128)(2,1)}) %all-gather.4.cloned.1.call-update) | async-done | bytes 25165840 | tf_op jit(solution)/shard_map/spread/all_gather | solution.py:297
  115.3 2.3 %copy-done = bf16[2,1536,768]{2,1,0:T(8,128)(2,1)S(1)} copy-done((bf16[2,1536,768]{2,1,0:T(8,128)(2,1)S(1)}, bf16[2,1536,768]{2,1,0:T(8,128)(2,1)}, u32[]{:S(2)}) %copy-start) | copy-done | bytes 4718616
  117.7 4.9 %direct.1 = (f32[64,8,128]{2,1,0:T(8,128)S(1)}, f32[64,8,128]{2,1,0:T(8,128)S(1)}) custom-call(s32[4,80]{1,0:T(4,128)S(1)} %pad_add_fusion.1.plan, bf16[128,128,768]{2,1,0:T(8,128)(2,1)} %all-gather.4.cloned.1.call-done.big, bf16[2,1536,768]{2,1,0:T(8,128)(2,1)S(1)} %copy-done), custom_call_target="tpu_custom_call" | custom-call | tf_op jit(solution)/shard_map/direct/pallas_call | solution.py:391
  125.3 6.1 %collective-permute-done.7.came = f32[64,8,128]{2,1,0:T(8,128)S(1)} collective-permute-done((f32[64,8,128]{2,1,0:T(8,128)S(1)}, f32[64,8,128]{2,1,0:T(8,128)S(1)}, u32[]{:S(2)}, u32[]{:S(2)}) %collective-permute-start.7) | collective-permute-done | bytes 262176 | tf_op jit(solution)/shard_map/to_neighbour/ppermute | solution.py:410
  131.4 2.4 %route.1 = f32[32,6,8,128]{3,2,1,0:T(8,128)} custom-call(s32[7,64]{1,0:T(8,128)S(1)} %stack.83.tab, f32[64,8,128]{2,1,0:T(8,128)S(1)} %get-tuple-element.4.keep, f32[64,8,128]{2,1,0:T(8,128)S(1)} %collective-permute-done.7.came), custom_call_target="tpu_custom_call" | custom-call | tf_op jit(solution)/shard_map/route/pallas_call | solution.py:411
  133.8 12.7 %all-to-all-start = ((f32[32,6,8,128]{3,2,1,0:T(8,128)}), f32[32,6,8,128]{3,2,1,0:T(8,128)S(1)}, u32[]{:S(2)}, u32[]{:S(2)}) async-start(f32[32,6,8,128]{3,2,1,0:T(8,128)} %route.1), calls=%async_computation | async-start | bytes 1572864 | tf_op jit(solution)/shard_map/to_holders/all_to_all | solution.py:425
  147.8 18.9 %all-to-all-done.got = f32[32,6,8,128]{3,2,1,0:T(8,128)S(1)} async-done(((f32[32,6,8,128]{3,2,1,0:T(8,128)}), f32[32,6,8,128]{3,2,1,0:T(8,128)S(1)}, u32[]{:S(2)}, u32[]{:S(2)}) %all-to-all-start) | async-done | bytes 786464 | tf_op jit(solution)/shard_map/to_holders/all_to_all | solution.py:425
  167.4 2.8 %collective-permute-start.10 = (f32[20,8,128]{2,1,0:T(8,128)S(1)}, f32[20,8,128]{2,1,0:T(8,128)S(1)}, u32[]{:S(2)}, u32[]{:S(2)}) collective-permute-start(f32[20,8,128]{2,1,0:T(8,128)S(1)} %collect.1.r0), channel_id=1, source_target_pairs={{0,3},{1,0},{2,1},{3,2},{4,7},{5,4},{6,5},{7,6},{8,11},{9,8},{10,9... | collective-permute-start | bytes 245768 | tf_op jit(solution)/shard_map/direct_copies/ppermute | solution.py:437
  170.3 2.4 %collective-permute-start.9 = (f32[20,8,128]{2,1,0:T(8,128)S(1)}, f32[20,8,128]{2,1,0:T(8,128)S(1)}, u32[]{:S(2)}, u32[]{:S(2)}) collective-permute-start(f32[20,8,128]{2,1,0:T(8,128)S(1)} %collect.1.r0), channel_id=1, source_target_pairs={{0,2},{1,3},{2,0},{3,1},{4,6},{5,7},{6,4},{7,5},{8,10},{9,11},{10,... | collective-permute-start | bytes 245768 | tf_op jit(solution)/shard_map/direct_copies/ppermute | solution.py:437
  174.3 4.1 %collective-permute-done.8.r1.early = f32[20,8,128]{2,1,0:T(8,128)S(1)} collective-permute-done((f32[20,8,128]{2,1,0:T(8,128)S(1)}, f32[20,8,128]{2,1,0:T(8,128)S(1)}, u32[]{:S(2)}, u32[]{:S(2)}) %collective-permute-start.8) | collective-permute-done | bytes 81952 | tf_op jit(solution)/shard_map/direct_copies/ppermute | solution.py:437
  178.4 4.4 %exchange.1.r0 = f32[20,8,128]{2,1,0:T(8,128)S(1)} custom-call(s32[3,64]{1,0:T(4,128)S(1)} %add_add_fusion.firsts, s32[4,16]{1,0:T(4,128)S(1)} %pad_add_fusion.own, bf16[128,16,1536]{2,1,0:T(8,128)(2,1)} %all-gather.6.cloned.1.call-done.big, bf16[272,1536]{1,0:T(8,128)(2,1)S(1)} %all_gather.14.full_in, bf16[256,1536]{1,0:T(8,128)(2,1)S(1)} %get-tuple-element.33.whi_in, ...), custom_call_target="tpu_custom_call" | custom-call | tf_op jit(solution)/shard_map/exchange/pallas_call | solution.py:448
  183.8 2.3 %collective-permute-start.13 = (f32[20,8,128]{2,1,0:T(8,128)S(1)}, f32[20,8,128]{2,1,0:T(8,128)S(1)}, u32[]{:S(2)}, u32[]{:S(2)}) collective-permute-start(f32[20,8,128]{2,1,0:T(8,128)S(1)} %exchange.1.r0), channel_id=1, source_target_pairs={{0,3},{1,0},{2,1},{3,2},{4,7},{5,4},{6,5},{7,6},{8,11},{9,8},{10,9... | collective-permute-start | bytes 245768 | tf_op jit(solution)/shard_map/exchange_copies/ppermute | solution.py:470
  187.6 2.8 %collective-permute-done.11.r1 = f32[20,8,128]{2,1,0:T(8,128)S(1)} collective-permute-done((f32[20,8,128]{2,1,0:T(8,128)S(1)}, f32[20,8,128]{2,1,0:T(8,128)S(1)}, u32[]{:S(2)}, u32[]{:S(2)}) %collective-permute-start.11) | collective-permute-done | bytes 81952 | tf_op jit(solution)/shard_map/exchange_copies/ppermute | solution.py:470
  190.9 2.4 %finish.1 = (f32[16,4096]{1,0:T(8,128)}, f32[4,4096]{1,0:T(4,128)}) custom-call(s32[4]{0:T(128)S(1)} %pad_add_fusion.2.place, f32[20,64,64]{2,1,0:T(8,128)S(1)} %arrange.1.dmat, f32[20,8,128]{2,1,0:T(8,128)S(1)} %exchange.1.r0, f32[20,8,128]{2,1,0:T(8,128)S(1)} %collective-permute-done.11.r1, f32[20,8,128]{2,1,0:T(8,128)S(1)} %collective-permute-done.12.r2, ...), custom_call_target="tpu_custom_call" | custom-call | tf_op jit(solution)/shard_map/finish/pallas_call | solution.py:471
  (111 shorter events, 25.8 us)
Async XLA Ops:
  7.2 108.2 %all-gather.4.cloned.1.call-start = ((), (), s32[]{:S(2)}) async-start(), calls=%async_computation.1 | async-start | bytes 25952256 | tf_op jit(solution)/shard_map/spread/all_gather | solution.py:297
  7.2 10.8 %collective-permute-start.3 = (bf16[4,64,375]{2,1,0:T(8,128)(2,1)}, bf16[4,64,375]{2,1,0:T(8,128)(2,1)S(1)}, u32[]{:S(2)}, u32[]{:S(2)}) collective-permute-start(bf16[4,64,375]{2,1,0:T(8,128)(2,1)} %param.8), channel_id=1, source_target_pairs={{0,3},{1,2},{2,1},{3,0},{4,7},{5,6},{6,5},{7,4},{8,11},{9,10},{10,... | collective-permute-start | bytes 576008 | tf_op jit(solution)/shard_map/pack/ppermute | solution.py:287
  11.1 8.3 %collective-permute-start = (bf16[4,32,375]{2,1,0:T(8,128)(2,1)S(1)}, bf16[4,32,375]{2,1,0:T(8,128)(2,1)S(1)}, u32[]{:S(2)}, u32[]{:S(2)}) collective-permute-start(bf16[4,32,375]{2,1,0:T(8,128)(2,1)S(1)} %get-tuple-element.39), channel_id=1, source_target_pairs={{0,1},{1,2},{2,3},{3,0},{4,5},{5,6},{6,7},{7,4},{8,9},{9,10},{10,1... | collective-permute-start | bytes 288008 | tf_op jit(solution)/shard_map/pack/ppermute | solution.py:289
  11.4 8.1 %collective-permute-start.1 = (bf16[4,32,375]{2,1,0:T(8,128)(2,1)S(1)}, bf16[4,32,375]{2,1,0:T(8,128)(2,1)S(1)}, u32[]{:S(2)}, u32[]{:S(2)}) collective-permute-start(bf16[4,32,375]{2,1,0:T(8,128)(2,1)S(1)} %get-tuple-element.37), channel_id=1, source_target_pairs={{0,2},{1,3},{2,0},{3,1},{4,6},{5,7},{6,4},{7,5},{8,10},{9,11},{10,... | collective-permute-start | bytes 288008 | tf_op jit(solution)/shard_map/pack/ppermute | solution.py:289
  13.0 6.4 %collective-permute-start.2 = (bf16[4,32,375]{2,1,0:T(8,128)(2,1)S(1)}, bf16[4,32,375]{2,1,0:T(8,128)(2,1)S(1)}, u32[]{:S(2)}, u32[]{:S(2)}) collective-permute-start(bf16[4,32,375]{2,1,0:T(8,128)(2,1)S(1)} %get-tuple-element.38), channel_id=1, source_target_pairs={{0,3},{1,0},{2,1},{3,2},{4,7},{5,4},{6,5},{7,6},{8,11},{9,8},{10,9... | collective-permute-start | bytes 288008 | tf_op jit(solution)/shard_map/pack/ppermute | solution.py:289
  14.6 5.9 %copy-start.4 = (f32[375]{0:T(512)S(1)}, f32[375]{0:T(512)}, u32[]{:S(2)}) copy-start(f32[375]{0:T(512)} %param.10) | copy-start | bytes 4504
  14.6 6.0 %copy-start.2 = (bf16[4,64,375]{2,1,0:T(8,128)(2,1)S(1)}, bf16[4,64,375]{2,1,0:T(8,128)(2,1)}, u32[]{:S(2)}) copy-start(bf16[4,64,375]{2,1,0:T(8,128)(2,1)} %param.9) | copy-start | bytes 576004
  20.5 153.8 %all-gather.6.cloned.1.call-start = ((), (), s32[]{:S(2)}) async-start(), calls=%async_computation.2 | async-start | bytes 6488064 | tf_op jit(solution)/shard_map/exchange_pack/all_gather | solution.py:322
  20.7 17.3 %copy-start.1 = (bf16[2,375,1500]{2,0,1:T(2,128)(2,1)S(1)}, bf16[2,375,1500]{2,0,1:T(2,128)(2,1)}, u32[]{:S(2)}) copy-start(bf16[2,375,1500]{2,0,1:T(2,128)(2,1)} %param.11) | copy-start | bytes 6750004
  44.3 52.3 %collective-permute-start.4 = (bf16[2,384,768]{2,1,0:T(8,128)(2,1)}, bf16[2,384,768]{2,1,0:T(8,128)(2,1)}, u32[]{:S(2)}, u32[]{:S(2)}) collective-permute-start(bf16[2,384,768]{2,1,0:T(8,128)(2,1)} %get-tuple-element.26), channel_id=1, source_target_pairs={{0,1},{1,2},{2,3},{3,0},{4,5},{5,6},{6,7},{7,4},{8,9},{9,10},{10,1... | collective-permute-start | bytes 3538952 | tf_op jit(solution)/shard_map/weights/ppermute | solution.py:310
  46.3 50.3 %collective-permute-start.5 = (bf16[2,384,768]{2,1,0:T(8,128)(2,1)}, bf16[2,384,768]{2,1,0:T(8,128)(2,1)}, u32[]{:S(2)}, u32[]{:S(2)}) collective-permute-start(bf16[2,384,768]{2,1,0:T(8,128)(2,1)} %get-tuple-element.27), channel_id=1, source_target_pairs={{0,2},{1,3},{2,0},{3,1},{4,6},{5,7},{6,4},{7,5},{8,10},{9,11},{10,... | collective-permute-start | bytes 3538952 | tf_op jit(solution)/shard_map/weights/ppermute | solution.py:310
  48.7 1.6 copy-start.3
  48.7 27.4 %copy-start.5 = (s32[64]{0:T(128)S(1)}, s32[64]{0:T(128)}, u32[]{:S(2)}) copy-start(s32[64]{0:T(128)} %param.13) | copy-start | bytes 772
  50.1 46.9 %collective-permute-start.6 = (bf16[2,384,768]{2,1,0:T(8,128)(2,1)}, bf16[2,384,768]{2,1,0:T(8,128)(2,1)S(1)}, u32[]{:S(2)}, u32[]{:S(2)}) collective-permute-start(bf16[2,384,768]{2,1,0:T(8,128)(2,1)} %broadcast_select_fusion), channel_id=1, source_target_pairs={{0,3},{1,0},{2,1},{3,2},{4,7},{5,4},{6,5},{7,6},{8,11},{9,8},{10,9... | collective-permute-start | bytes 3538952 | tf_op jit(solution)/shard_map/weights/ppermute | solution.py:310
  115.3 2.3 %copy-start = (bf16[2,1536,768]{2,1,0:T(8,128)(2,1)S(1)}, bf16[2,1536,768]{2,1,0:T(8,128)(2,1)}, u32[]{:S(2)}) copy-start(bf16[2,1536,768]{2,1,0:T(8,128)(2,1)} %pad_maximum_fusion.w) | copy-start | bytes 14155780
  122.6 8.8 %collective-permute-start.7 = (f32[64,8,128]{2,1,0:T(8,128)S(1)}, f32[64,8,128]{2,1,0:T(8,128)S(1)}, u32[]{:S(2)}, u32[]{:S(2)}) collective-permute-start(f32[64,8,128]{2,1,0:T(8,128)S(1)} %get-tuple-element.5), channel_id=1, source_target_pairs={{0,1},{1,0},{2,3},{3,2},{4,5},{5,4},{6,7},{7,6},{8,9},{9,8},{10,11... | collective-permute-start | bytes 786440 | tf_op jit(solution)/shard_map/to_neighbour/ppermute | solution.py:410
  133.8 33.0 %all-to-all-start = ((f32[32,6,8,128]{3,2,1,0:T(8,128)}), f32[32,6,8,128]{3,2,1,0:T(8,128)S(1)}, u32[]{:S(2)}, u32[]{:S(2)}) async-start(f32[32,6,8,128]{3,2,1,0:T(8,128)} %route.1), calls=%async_computation | async-start | bytes 1572864 | tf_op jit(solution)/shard_map/to_holders/all_to_all | solution.py:425
  167.4 6.8 %collective-permute-start.10 = (f32[20,8,128]{2,1,0:T(8,128)S(1)}, f32[20,8,128]{2,1,0:T(8,128)S(1)}, u32[]{:S(2)}, u32[]{:S(2)}) collective-permute-start(f32[20,8,128]{2,1,0:T(8,128)S(1)} %collect.1.r0), channel_id=1, source_target_pairs={{0,3},{1,0},{2,1},{3,2},{4,7},{5,4},{6,5},{7,6},{8,11},{9,8},{10,9... | collective-permute-start | bytes 245768 | tf_op jit(solution)/shard_map/direct_copies/ppermute | solution.py:437
  170.2 8.2 %collective-permute-start.8 = (f32[20,8,128]{2,1,0:T(8,128)S(1)}, f32[20,8,128]{2,1,0:T(8,128)S(1)}, u32[]{:S(2)}, u32[]{:S(2)}) collective-permute-start(f32[20,8,128]{2,1,0:T(8,128)S(1)} %collect.1.r0), channel_id=1, source_target_pairs={{0,1},{1,2},{2,3},{3,0},{4,5},{5,6},{6,7},{7,4},{8,9},{9,10},{10,1... | collective-permute-start | bytes 245768 | tf_op jit(solution)/shard_map/direct_copies/ppermute | solution.py:437
  170.3 15.9 %collective-permute-start.9 = (f32[20,8,128]{2,1,0:T(8,128)S(1)}, f32[20,8,128]{2,1,0:T(8,128)S(1)}, u32[]{:S(2)}, u32[]{:S(2)}) collective-permute-start(f32[20,8,128]{2,1,0:T(8,128)S(1)} %collect.1.r0), channel_id=1, source_target_pairs={{0,2},{1,3},{2,0},{3,1},{4,6},{5,7},{6,4},{7,5},{8,10},{9,11},{10,... | collective-permute-start | bytes 245768 | tf_op jit(solution)/shard_map/direct_copies/ppermute | solution.py:437
  182.8 7.5 %collective-permute-start.11 = (f32[20,8,128]{2,1,0:T(8,128)S(1)}, f32[20,8,128]{2,1,0:T(8,128)S(1)}, u32[]{:S(2)}, u32[]{:S(2)}) collective-permute-start(f32[20,8,128]{2,1,0:T(8,128)S(1)} %exchange.1.r0), channel_id=1, source_target_pairs={{0,1},{1,2},{2,3},{3,0},{4,5},{5,6},{6,7},{7,4},{8,9},{9,10},{10,1... | collective-permute-start | bytes 245768 | tf_op jit(solution)/shard_map/exchange_copies/ppermute | solution.py:470
  182.9 7.4 %collective-permute-start.12 = (f32[20,8,128]{2,1,0:T(8,128)S(1)}, f32[20,8,128]{2,1,0:T(8,128)S(1)}, u32[]{:S(2)}, u32[]{:S(2)}) collective-permute-start(f32[20,8,128]{2,1,0:T(8,128)S(1)} %exchange.1.r0), channel_id=1, source_target_pairs={{0,2},{1,3},{2,0},{3,1},{4,6},{5,7},{6,4},{7,5},{8,10},{9,11},{10,... | collective-permute-start | bytes 245768 | tf_op jit(solution)/shard_map/exchange_copies/ppermute | solution.py:470
  183.8 7.1 %collective-permute-start.13 = (f32[20,8,128]{2,1,0:T(8,128)S(1)}, f32[20,8,128]{2,1,0:T(8,128)S(1)}, u32[]{:S(2)}, u32[]{:S(2)}) collective-permute-start(f32[20,8,128]{2,1,0:T(8,128)S(1)} %exchange.1.r0), channel_id=1, source_target_pairs={{0,3},{1,0},{2,1},{3,2},{4,7},{5,4},{6,5},{7,6},{8,11},{9,8},{10,9... | collective-permute-start | bytes 245768 | tf_op jit(solution)/shard_map/exchange_copies/ppermute | solution.py:470
Sparse Core Ops, SparseCore 0:
  20.6 94.6 all-gather.3
  118.2 56.0 all-gather.5

commit v8 on v7

--- a/solution.py
+++ b/solution.py
@@ -228,7 +228,7 @@
     half = dmat.shape[1] // 2
     for j in range(dmat.shape[0]):
         for a in range(2):
-            left, right = whole[2 * a, j], whole[2 * a + 1, j]
+            left, right = whole[a, j], whole[a + 2, j]
             for g in range(4):
                 cut = slice(half * g, half * (g + 1))
                 dmat[j, pl.ds(half * a + 8 * g, 8), :] = jnp.concatenate(
@@ -284,15 +284,16 @@
         return [(i, (i + r) % 4) for i in range(4)]
 
     with jax.named_scope("pack"):
-        y_far = lax.ppermute(y, "ga", [(i, 3 - i) for i in range(4)])
-        cut = [jnp.where((a + r) % 4 < 2, x[:, :half], x[:, half:]) for r in range(4)]
+        y_far = lax.ppermute(y, "ga", shift(3))
+        cut = [jnp.where((a + r) % 2 == 0, x[:, :half], x[:, half:]) for r in range(2)] * 2
         cut = cut[:1] + [lax.ppermute(cut[r], "ga", shift(r)) for r in range(1, 4)]
 
         def side(left, right):
             return jnp.concatenate([widen(left), widen(right)], axis=2)
 
-        y_both = side(jnp.where(a < 2, y, y_far), jnp.where(a < 2, y_far, y))
-        payload = jnp.concatenate([side(cut[0], cut[1]), side(cut[2], cut[3]), y_both], axis=1)
+        payload = jnp.concatenate(
+            [side(cut[0], cut[1]), side(cut[2], cut[3]), side(y, y_far)], axis=1
+        )
     with jax.named_scope("spread"):
         big = lax.all_gather(payload, "ka", axis=0, tiled=True)
 
@@ -301,12 +302,13 @@
             jnp.pad(w[:, :, i * gl : (i + 1) * gl], ((0, 0), (0, QW - gl), (0, QW - gl)))
             for i in range(4)
         ]
-        outer = jnp.concatenate([cols[0], cols[3]], axis=2)
-        inner = jnp.concatenate([cols[1], cols[2]], axis=2)
+        sets = [jnp.concatenate([cols[i], cols[(i + 1) % 4]], axis=2) for i in range(4)]
         wk = []
         for r in range(4):
             to = (a + r) % 4
-            v = jnp.where((to == 0) | (to == 3), outer, inner)
+            v = jnp.where(
+                to < 2, jnp.where(to == 0, sets[0], sets[1]), jnp.where(to == 2, sets[2], sets[3])
+            )
             wk.append(lax.ppermute(v, "ga", shift(r)) if r else v)
         wk = jnp.concatenate(wk, axis=1)
 
@@ -379,7 +381,7 @@
         def at_pos(v, hot):
             return jnp.sum(jnp.where(hot, v[None, :], 0), axis=1)
 
-        heads = jnp.pad(jnp.stack([chunks_first, chunks, a % 2]), (0, npos - 3))
+        heads = jnp.pad(jnp.stack([chunks_first, chunks, a // 2]), (0, npos - 3))
         plan = jnp.stack(
             [at_pos(order - nslot, hot) + nslot, at_pos(tab[1], hot), at_pos(tab[2], hot), heads]
         )
@@ -407,7 +409,7 @@
         name="direct",
     )(plan, big, wk)
     with jax.named_scope("to_neighbour"):
-        came = lax.ppermute(away, "ga", [(0, 1), (1, 0), (2, 3), (3, 2)])
+        came = lax.ppermute(away, "ga", shift(2))
     send = pl.pallas_call(
         route_kernel,
         out_shape=jax.ShapeDtypeStruct((n_ka, CAP + nk, 8, 128), F32),
@@ -465,7 +467,7 @@
         ],
         compiler_params=pltpu.CompilerParams(vmem_limit_bytes=50 * 1024 * 1024),
         name="exchange",
-    )(firsts, own, p_big, full, w_hi, w_lo, others[0], others[2], c_full)
+    )(firsts, own, p_big, full, w_hi, w_lo, others[2], others[2], c_full)
     with jax.named_scope("exchange_copies"):
         exch_others = [lax.ppermute(exch, "ga", shift(r)) for r in range(1, 4)]
     return pl.pallas_call(

time: 200 us -> 199 us (level)
  waiting for transfers between devices: 66.4 us -> 59.6 us
  starting transfers between devices: 33.8 us -> 36.4 us
    ppermute x3, waiting for transfers between devices: 0.51 us -> 4.76 us  [per_device(): cut = cut[:1] + [lax.ppermute(cut[r], 'ga', shift(r)) for r in range(1, 4)]]
    ppermute x3, waiting for transfers between devices: 4.14 us -> 0.01 us  [per_device(): others = [lax.ppermute(mine, 'ga', shift(r)) for r in range(1, 4)]]
    ppermute x2, waiting for transfers between devices: 9.41 us -> 6.27 us  [the longest x1 6.27 us: per_device(): came = lax.ppermute(away, 'ga', shift(2))]
    ppermute x3, starting transfers between devices: 3.3 us -> 5.68 us  [per_device(): exch_others = [lax.ppermute(exch, 'ga', shift(r)) for r in range(1, 4)]]
    select_n x4 -> x5, other arithmetic: 5.7 us -> 6.43 us  [the longest x4 5.47 us: per_device(): jnp.where(to < 2, jnp.where(to == 0, sets[0], sets[1]), jnp.where(to == 2...]
  transfers between devices with their start and end apart: 17 -> 17, of which waited for: 11 -> 9; matrix products, arithmetic and copies ran while one was open for 12% -> 13% of each run, Pallas kernels for 7% -> 7%
where the time goes in v8:
time: 199 us; the launch traced here: 198 us
  waiting for transfers between devices  59.6 us (30%)
  blocking collectives  40.4 us (20%)
  starting transfers between devices  36.4 us (18%)
  other arithmetic  17.2 us (9%)
  Pallas kernels  15.9 us (8%)
  between operations  15.9 us (8%)
  local copies, waits for them, and re-layouts  12.3 us (6%)
    all_gather x1, blocking collectives, per_device(): lax.all_gather(pairs, 'ka', axis=0, tiled=True).reshape(n_ka, npair, 3)  25.7 us
    all_to_all x1, waiting for transfers between devices, per_device(): got = lax.all_to_all(send, 'ka', 0, 0, tiled=True)  18.8 us
    all_gather x1, blocking collectives, per_device(): full = lax.all_gather(widen(held), 'ga', axis=1, tiled=True)  14.7 us
    ppermute x3, waiting for transfers between devices, per_device(): wk.append(lax.ppermute(v, 'ga', shift(r)) if r else v)  14.4 us
    all_gather x1, waiting for transfers between devices, per_device(): big = lax.all_gather(payload, 'ka', axis=0, tiled=True)  12 us
    all_to_all x1, starting transfers between devices, per_device(): got = lax.all_to_all(send, 'ka', 0, 0, tiled=True)  11.3 us
    ppermute x1, waiting for transfers between devices, per_device(): came = lax.ppermute(away, 'ga', shift(2))  6.27 us
    ppermute x3, starting transfers between devices, per_device(): exch_others = [lax.ppermute(exch, 'ga', shift(r)) for r in range(1, 4)]  5.68 us
  transfers between devices with their start and end apart: 17, of which 9 were waited for; matrix products, arithmetic and copies ran while one was open for 13% of the time, Pallas kernels for 7%

profile of v8, /device:TPU:0, one launch (start us, length us, event | category | flops | bytes accessed | tf_op | source)
XLA Modules:
  0.0 197.9 jit_solution(7422732506320134839)
XLA Ops:
  7.2 2.9 %collective-permute-start.3 = (bf16[4,64,375]{2,1,0:T(8,128)(2,1)}, bf16[4,64,375]{2,1,0:T(8,128)(2,1)S(1)}, u32[]{:S(2)}, u32[]{:S(2)}) collective-permute-start(bf16[4,64,375]{2,1,0:T(8,128)(2,1)} %param.8), channel_id=1, source_target_pairs={{0,3},{1,0},{2,1},{3,2},{4,7},{5,4},{6,5},{7,6},{8,11},{9,8},{10,9... | collective-permute-start | bytes 576008 | tf_op jit(solution)/shard_map/pack/ppermute | solution.py:287
  11.2 2.3 %collective-permute-start.1 = (bf16[4,32,375]{2,1,0:T(8,128)(2,1)S(1)}, bf16[4,32,375]{2,1,0:T(8,128)(2,1)S(1)}, u32[]{:S(2)}, u32[]{:S(2)}) collective-permute-start(bf16[4,32,375]{2,1,0:T(8,128)(2,1)S(1)} %get-tuple-element.31), channel_id=1, source_target_pairs={{0,2},{1,3},{2,0},{3,1},{4,6},{5,7},{6,4},{7,5},{8,10},{9,11},{10,... | collective-permute-start | bytes 288008 | tf_op jit(solution)/shard_map/pack/ppermute | solution.py:289
  14.6 4.1 %collective-permute-done = bf16[4,32,375]{2,1,0:T(8,128)(2,1)S(1)} collective-permute-done((bf16[4,32,375]{2,1,0:T(8,128)(2,1)S(1)}, bf16[4,32,375]{2,1,0:T(8,128)(2,1)S(1)}, u32[]{:S(2)}, u32[]{:S(2)}) %collective-permute-start) | collective-permute-done | bytes 96032 | tf_op jit(solution)/shard_map/pack/ppermute | solution.py:289
  21.5 14.7 %all_gather.14.full_in = bf16[272,1536]{1,0:T(8,128)(2,1)S(1)} all-gather(bf16[272,384]{1,0:T(8,128)(2,1)S(1)} %fusion.27), channel_id=1, replica_groups=mesh['ka'=32,'ga'=4] {'ga'}, dimensions={1}, use_global_device_ids=true | all-gather | bytes 1044480 | tf_op jit(solution)/shard_map/exchange_pack/all_gather | solution.py:321
  38.9 3.6 %fusion.48 = (bf16[2,375,375]{2,0,1:T(2,128)(2,1)S(1)}, bf16[2,375,375]{2,0,1:T(2,128)(2,1)S(1)}, bf16[2,375,375]{2,0,1:T(2,128)(2,1)S(1)}, bf16[2,375,375]{2,0,1:T(2,128)(2,1)S(1)}) fusion(bf16[2,375,1500]{2,0,1:T(2,128)(2,1)S(1)} %copy-done.1), kind=kLoop, calls=%fused_computation.148 | loop fusion | bytes 4500000 | tf_op jit(solution)/shard_map/weights/slice | solution.py:302
  44.8 2.0 %collective-permute-start.4 = (bf16[2,384,768]{2,1,0:T(8,128)(2,1)}, bf16[2,384,768]{2,1,0:T(8,128)(2,1)}, u32[]{:S(2)}, u32[]{:S(2)}) collective-permute-start(bf16[2,384,768]{2,1,0:T(8,128)(2,1)} %select_select_fusion.2), channel_id=1, source_target_pairs={{0,1},{1,2},{2,3},{3,0},{4,5},{5,6},{6,7},{7,4},{8,9},{9,10},{10,1... | collective-permute-start | bytes 3538952 | tf_op jit(solution)/shard_map/weights/ppermute | solution.py:312
  48.4 2.5 %collective-permute-start.5 = (bf16[2,384,768]{2,1,0:T(8,128)(2,1)}, bf16[2,384,768]{2,1,0:T(8,128)(2,1)}, u32[]{:S(2)}, u32[]{:S(2)}) collective-permute-start(bf16[2,384,768]{2,1,0:T(8,128)(2,1)} %select_select_fusion.1), channel_id=1, source_target_pairs={{0,2},{1,3},{2,0},{3,1},{4,6},{5,7},{6,4},{7,5},{8,10},{9,11},{10,... | collective-permute-start | bytes 3538952 | tf_op jit(solution)/shard_map/weights/ppermute | solution.py:312
  52.7 25.7 %all-gather = s32[32,16,3]{1,2,0:T(4,128)S(1)} all-gather(s32[1,16,3]{1,2,0:T(4,128)S(1)} %bitcast.49), channel_id=1, replica_groups=mesh['ka'=32,'ga'=4] {'ka'}, dimensions={0}, use_global_device_ids=true | all-gather | bytes 6336 | tf_op jit(solution)/shard_map/tables/all_gather | solution.py:332
  84.8 12.2 %collective-permute-done.4 = bf16[2,384,768]{2,1,0:T(8,128)(2,1)} collective-permute-done((bf16[2,384,768]{2,1,0:T(8,128)(2,1)}, bf16[2,384,768]{2,1,0:T(8,128)(2,1)}, u32[]{:S(2)}, u32[]{:S(2)}) %collective-permute-start.4) | collective-permute-done | bytes 1179680 | tf_op jit(solution)/shard_map/weights/ppermute | solution.py:312
  97.0 2.2 %collective-permute-done.6 = bf16[2,384,768]{2,1,0:T(8,128)(2,1)} collective-permute-done((bf16[2,384,768]{2,1,0:T(8,128)(2,1)}, bf16[2,384,768]{2,1,0:T(8,128)(2,1)}, u32[]{:S(2)}, u32[]{:S(2)}) %collective-permute-start.6) | collective-permute-done | bytes 1179680 | tf_op jit(solution)/shard_map/weights/ppermute | solution.py:312
  99.3 5.1 %pad_maximum_fusion.w = bf16[2,1536,768]{2,1,0:T(8,128)(2,1)} fusion(bf16[2,384,768]{2,1,0:T(8,128)(2,1)} %collective-permute-done.6, bf16[2,384,768]{2,1,0:T(8,128)(2,1)} %collective-permute-done.5, bf16[2,384,768]{2,1,0:T(8,128)(2,1)} %collective-permute-done.4, bf16[2,384,768]{2,1,0:T(8,128)(2,1)S(1)} %select_select_fusion.3), kind=kLoop, calls=%fused_computation | loop fusion | flops 18874368 | bytes 9437184 | tf_op jit(solution)/shard_map/weights/concatenate | solution.py:313
  104.3 12.0 %all-gather.4.cloned.1.call-done.big = bf16[128,128,768]{2,1,0:T(8,128)(2,1)} async-done(((bf16[4,128,768]{2,1,0:T(8,128)(2,1)}), bf16[128,128,768]{2,1,0:T(8,128)(2,1)}) %all-gather.4.cloned.1.call-update) | async-done | bytes 25165840 | tf_op jit(solution)/shard_map/spread/all_gather | solution.py:298
  116.3 2.3 %copy-done = bf16[2,1536,768]{2,1,0:T(8,128)(2,1)S(1)} copy-done((bf16[2,1536,768]{2,1,0:T(8,128)(2,1)S(1)}, bf16[2,1536,768]{2,1,0:T(8,128)(2,1)}, u32[]{:S(2)}) %copy-start) | copy-done | bytes 4718616
  118.6 5.3 %direct.1 = (f32[64,8,128]{2,1,0:T(8,128)S(1)}, f32[64,8,128]{2,1,0:T(8,128)S(1)}) custom-call(s32[4,80]{1,0:T(4,128)S(1)} %pad_add_fusion.1.plan, bf16[128,128,768]{2,1,0:T(8,128)(2,1)} %all-gather.4.cloned.1.call-done.big, bf16[2,1536,768]{2,1,0:T(8,128)(2,1)S(1)} %copy-done), custom_call_target="tpu_custom_call" | custom-call | tf_op jit(solution)/shard_map/direct/pallas_call | solution.py:393
  123.9 3.2 %collective-permute-start.7 = (f32[64,8,128]{2,1,0:T(8,128)S(1)}, f32[64,8,128]{2,1,0:T(8,128)S(1)}, u32[]{:S(2)}, u32[]{:S(2)}) collective-permute-start(f32[64,8,128]{2,1,0:T(8,128)S(1)} %get-tuple-element.5), channel_id=1, source_target_pairs={{0,2},{1,3},{2,0},{3,1},{4,6},{5,7},{6,4},{7,5},{8,10},{9,11},{10,... | collective-permute-start | bytes 786440 | tf_op jit(solution)/shard_map/to_neighbour/ppermute | solution.py:412
  128.3 6.3 %collective-permute-done.7.came = f32[64,8,128]{2,1,0:T(8,128)S(1)} collective-permute-done((f32[64,8,128]{2,1,0:T(8,128)S(1)}, f32[64,8,128]{2,1,0:T(8,128)S(1)}, u32[]{:S(2)}, u32[]{:S(2)}) %collective-permute-start.7) | collective-permute-done | bytes 262176 | tf_op jit(solution)/shard_map/to_neighbour/ppermute | solution.py:412
  134.6 2.2 %route.1 = f32[32,6,8,128]{3,2,1,0:T(8,128)} custom-call(s32[7,64]{1,0:T(8,128)S(1)} %stack.83.tab, f32[64,8,128]{2,1,0:T(8,128)S(1)} %get-tuple-element.4.keep, f32[64,8,128]{2,1,0:T(8,128)S(1)} %collective-permute-done.7.came), custom_call_target="tpu_custom_call" | custom-call | tf_op jit(solution)/shard_map/route/pallas_call | solution.py:413
  136.7 11.3 %all-to-all-start = ((f32[32,6,8,128]{3,2,1,0:T(8,128)}), f32[32,6,8,128]{3,2,1,0:T(8,128)S(1)}, u32[]{:S(2)}, u32[]{:S(2)}) async-start(f32[32,6,8,128]{3,2,1,0:T(8,128)} %route.1), calls=%async_computation | async-start | bytes 1572864 | tf_op jit(solution)/shard_map/to_holders/all_to_all | solution.py:427
  149.4 18.8 %all-to-all-done.got = f32[32,6,8,128]{3,2,1,0:T(8,128)S(1)} async-done(((f32[32,6,8,128]{3,2,1,0:T(8,128)}), f32[32,6,8,128]{3,2,1,0:T(8,128)S(1)}, u32[]{:S(2)}, u32[]{:S(2)}) %all-to-all-start) | async-done | bytes 786464 | tf_op jit(solution)/shard_map/to_holders/all_to_all | solution.py:427
  168.9 2.8 %collective-permute-start.10 = (f32[20,8,128]{2,1,0:T(8,128)S(1)}, f32[20,8,128]{2,1,0:T(8,128)S(1)}, u32[]{:S(2)}, u32[]{:S(2)}) collective-permute-start(f32[20,8,128]{2,1,0:T(8,128)S(1)} %collect.1.r0), channel_id=1, source_target_pairs={{0,3},{1,0},{2,1},{3,2},{4,7},{5,4},{6,5},{7,6},{8,11},{9,8},{10,9... | collective-permute-start | bytes 245768 | tf_op jit(solution)/shard_map/direct_copies/ppermute | solution.py:439
  171.8 2.3 %collective-permute-start.9 = (f32[20,8,128]{2,1,0:T(8,128)S(1)}, f32[20,8,128]{2,1,0:T(8,128)S(1)}, u32[]{:S(2)}, u32[]{:S(2)}) collective-permute-start(f32[20,8,128]{2,1,0:T(8,128)S(1)} %collect.1.r0), channel_id=1, source_target_pairs={{0,2},{1,3},{2,0},{3,1},{4,6},{5,7},{6,4},{7,5},{8,10},{9,11},{10,... | collective-permute-start | bytes 245768 | tf_op jit(solution)/shard_map/direct_copies/ppermute | solution.py:439
  175.8 4.1 %exchange.1.r0 = f32[20,8,128]{2,1,0:T(8,128)S(1)} custom-call(s32[3,64]{1,0:T(4,128)S(1)} %add_add_fusion.firsts, s32[4,16]{1,0:T(4,128)S(1)} %pad_add_fusion.own, bf16[128,16,1536]{2,1,0:T(8,128)(2,1)} %all-gather.6.cloned.1.call-done.big, bf16[272,1536]{1,0:T(8,128)(2,1)S(1)} %all_gather.14.full_in, bf16[256,1536]{1,0:T(8,128)(2,1)S(1)} %get-tuple-element.30.whi_in, ...), custom_call_target="tpu_custom_call" | custom-call | tf_op jit(solution)/shard_map/exchange/pallas_call | solution.py:450
  181.5 2.7 %collective-permute-start.12 = (f32[20,8,128]{2,1,0:T(8,128)S(1)}, f32[20,8,128]{2,1,0:T(8,128)S(1)}, u32[]{:S(2)}, u32[]{:S(2)}) collective-permute-start(f32[20,8,128]{2,1,0:T(8,128)S(1)} %exchange.1.r0), channel_id=1, source_target_pairs={{0,2},{1,3},{2,0},{3,1},{4,6},{5,7},{6,4},{7,5},{8,10},{9,11},{10,... | collective-permute-start | bytes 245768 | tf_op jit(solution)/shard_map/exchange_copies/ppermute | solution.py:472
  188.7 2.3 %finish.1 = (f32[16,4096]{1,0:T(8,128)}, f32[4,4096]{1,0:T(4,128)}) custom-call(s32[4]{0:T(128)S(1)} %pad_add_fusion.2.place, f32[20,64,64]{2,1,0:T(8,128)S(1)} %arrange.1.dmat, f32[20,8,128]{2,1,0:T(8,128)S(1)} %exchange.1.r0, f32[20,8,128]{2,1,0:T(8,128)S(1)} %collective-permute-done.11.r1, f32[20,8,128]{2,1,0:T(8,128)S(1)} %collective-permute-done.12.r2, ...), custom_call_target="tpu_custom_call" | custom-call | tf_op jit(solution)/shard_map/finish/pallas_call | solution.py:473
  (116 shorter events, 29.1 us)
Async XLA Ops:
  7.2 14.2 %copy-start.4 = (f32[375]{0:T(512)S(1)}, f32[375]{0:T(512)}, u32[]{:S(2)}) copy-start(f32[375]{0:T(512)} %param.10) | copy-start | bytes 4504
  7.2 14.3 %copy-start.2 = (bf16[4,64,375]{2,1,0:T(8,128)(2,1)S(1)}, bf16[4,64,375]{2,1,0:T(8,128)(2,1)}, u32[]{:S(2)}) copy-start(bf16[4,64,375]{2,1,0:T(8,128)(2,1)} %param.9) | copy-start | bytes 576004
  7.2 109.1 %all-gather.4.cloned.1.call-start = ((), (), s32[]{:S(2)}) async-start(), calls=%async_computation.1 | async-start | bytes 25952256 | tf_op jit(solution)/shard_map/spread/all_gather | solution.py:298
  7.2 12.1 %collective-permute-start.3 = (bf16[4,64,375]{2,1,0:T(8,128)(2,1)}, bf16[4,64,375]{2,1,0:T(8,128)(2,1)S(1)}, u32[]{:S(2)}, u32[]{:S(2)}) collective-permute-start(bf16[4,64,375]{2,1,0:T(8,128)(2,1)} %param.8), channel_id=1, source_target_pairs={{0,3},{1,0},{2,1},{3,2},{4,7},{5,4},{6,5},{7,6},{8,11},{9,8},{10,9... | collective-permute-start | bytes 576008 | tf_op jit(solution)/shard_map/pack/ppermute | solution.py:287
  11.1 7.6 %collective-permute-start = (bf16[4,32,375]{2,1,0:T(8,128)(2,1)S(1)}, bf16[4,32,375]{2,1,0:T(8,128)(2,1)S(1)}, u32[]{:S(2)}, u32[]{:S(2)}) collective-permute-start(bf16[4,32,375]{2,1,0:T(8,128)(2,1)S(1)} %get-tuple-element.32), channel_id=1, source_target_pairs={{0,1},{1,2},{2,3},{3,0},{4,5},{5,6},{6,7},{7,4},{8,9},{9,10},{10,1... | collective-permute-start | bytes 288008 | tf_op jit(solution)/shard_map/pack/ppermute | solution.py:289
  11.2 7.6 %collective-permute-start.1 = (bf16[4,32,375]{2,1,0:T(8,128)(2,1)S(1)}, bf16[4,32,375]{2,1,0:T(8,128)(2,1)S(1)}, u32[]{:S(2)}, u32[]{:S(2)}) collective-permute-start(bf16[4,32,375]{2,1,0:T(8,128)(2,1)S(1)} %get-tuple-element.31), channel_id=1, source_target_pairs={{0,2},{1,3},{2,0},{3,1},{4,6},{5,7},{6,4},{7,5},{8,10},{9,11},{10,... | collective-permute-start | bytes 288008 | tf_op jit(solution)/shard_map/pack/ppermute | solution.py:289
  13.5 5.9 %collective-permute-start.2 = (bf16[4,32,375]{2,1,0:T(8,128)(2,1)S(1)}, bf16[4,32,375]{2,1,0:T(8,128)(2,1)S(1)}, u32[]{:S(2)}, u32[]{:S(2)}) collective-permute-start(bf16[4,32,375]{2,1,0:T(8,128)(2,1)S(1)} %get-tuple-element.32), channel_id=1, source_target_pairs={{0,3},{1,0},{2,1},{3,2},{4,7},{5,4},{6,5},{7,6},{8,11},{9,8},{10,9... | collective-permute-start | bytes 288008 | tf_op jit(solution)/shard_map/pack/ppermute | solution.py:289
  21.3 154.5 %all-gather.6.cloned.1.call-start = ((), (), s32[]{:S(2)}) async-start(), calls=%async_computation.2 | async-start | bytes 6488064 | tf_op jit(solution)/shard_map/exchange_pack/all_gather | solution.py:324
  21.5 17.4 %copy-start.1 = (bf16[2,375,1500]{2,0,1:T(2,128)(2,1)S(1)}, bf16[2,375,1500]{2,0,1:T(2,128)(2,1)}, u32[]{:S(2)}) copy-start(bf16[2,375,1500]{2,0,1:T(2,128)(2,1)} %param.11) | copy-start | bytes 6750004
  44.8 52.3 %collective-permute-start.4 = (bf16[2,384,768]{2,1,0:T(8,128)(2,1)}, bf16[2,384,768]{2,1,0:T(8,128)(2,1)}, u32[]{:S(2)}, u32[]{:S(2)}) collective-permute-start(bf16[2,384,768]{2,1,0:T(8,128)(2,1)} %select_select_fusion.2), channel_id=1, source_target_pairs={{0,1},{1,2},{2,3},{3,0},{4,5},{5,6},{6,7},{7,4},{8,9},{9,10},{10,1... | collective-permute-start | bytes 3538952 | tf_op jit(solution)/shard_map/weights/ppermute | solution.py:312
  48.4 48.7 %collective-permute-start.5 = (bf16[2,384,768]{2,1,0:T(8,128)(2,1)}, bf16[2,384,768]{2,1,0:T(8,128)(2,1)}, u32[]{:S(2)}, u32[]{:S(2)}) collective-permute-start(bf16[2,384,768]{2,1,0:T(8,128)(2,1)} %select_select_fusion.1), channel_id=1, source_target_pairs={{0,2},{1,3},{2,0},{3,1},{4,6},{5,7},{6,4},{7,5},{8,10},{9,11},{10,... | collective-permute-start | bytes 3538952 | tf_op jit(solution)/shard_map/weights/ppermute | solution.py:312
  50.8 1.8 copy-start.3
  50.8 27.6 %copy-start.5 = (s32[64]{0:T(128)S(1)}, s32[64]{0:T(128)}, u32[]{:S(2)}) copy-start(s32[64]{0:T(128)} %param.13) | copy-start | bytes 772
  52.5 46.8 %collective-permute-start.6 = (bf16[2,384,768]{2,1,0:T(8,128)(2,1)}, bf16[2,384,768]{2,1,0:T(8,128)(2,1)}, u32[]{:S(2)}, u32[]{:S(2)}) collective-permute-start(bf16[2,384,768]{2,1,0:T(8,128)(2,1)} %select_select_fusion), channel_id=1, source_target_pairs={{0,3},{1,0},{2,1},{3,2},{4,7},{5,4},{6,5},{7,6},{8,11},{9,8},{10,9... | collective-permute-start | bytes 3538952 | tf_op jit(solution)/shard_map/weights/ppermute | solution.py:312
  116.3 2.3 %copy-start = (bf16[2,1536,768]{2,1,0:T(8,128)(2,1)S(1)}, bf16[2,1536,768]{2,1,0:T(8,128)(2,1)}, u32[]{:S(2)}) copy-start(bf16[2,1536,768]{2,1,0:T(8,128)(2,1)} %pad_maximum_fusion.w) | copy-start | bytes 14155780
  123.9 10.7 %collective-permute-start.7 = (f32[64,8,128]{2,1,0:T(8,128)S(1)}, f32[64,8,128]{2,1,0:T(8,128)S(1)}, u32[]{:S(2)}, u32[]{:S(2)}) collective-permute-start(f32[64,8,128]{2,1,0:T(8,128)S(1)} %get-tuple-element.5), channel_id=1, source_target_pairs={{0,2},{1,3},{2,0},{3,1},{4,6},{5,7},{6,4},{7,5},{8,10},{9,11},{10,... | collective-permute-start | bytes 786440 | tf_op jit(solution)/shard_map/to_neighbour/ppermute | solution.py:412
  136.7 31.5 %all-to-all-start = ((f32[32,6,8,128]{3,2,1,0:T(8,128)}), f32[32,6,8,128]{3,2,1,0:T(8,128)S(1)}, u32[]{:S(2)}, u32[]{:S(2)}) async-start(f32[32,6,8,128]{3,2,1,0:T(8,128)} %route.1), calls=%async_computation | async-start | bytes 1572864 | tf_op jit(solution)/shard_map/to_holders/all_to_all | solution.py:427
  168.9 6.9 %collective-permute-start.10 = (f32[20,8,128]{2,1,0:T(8,128)S(1)}, f32[20,8,128]{2,1,0:T(8,128)S(1)}, u32[]{:S(2)}, u32[]{:S(2)}) collective-permute-start(f32[20,8,128]{2,1,0:T(8,128)S(1)} %collect.1.r0), channel_id=1, source_target_pairs={{0,3},{1,0},{2,1},{3,2},{4,7},{5,4},{6,5},{7,6},{8,11},{9,8},{10,9... | collective-permute-start | bytes 245768 | tf_op jit(solution)/shard_map/direct_copies/ppermute | solution.py:439
  171.7 14.0 %collective-permute-start.8 = (f32[20,8,128]{2,1,0:T(8,128)S(1)}, f32[20,8,128]{2,1,0:T(8,128)S(1)}, u32[]{:S(2)}, u32[]{:S(2)}) collective-permute-start(f32[20,8,128]{2,1,0:T(8,128)S(1)} %collect.1.r0), channel_id=1, source_target_pairs={{0,1},{1,2},{2,3},{3,0},{4,5},{5,6},{6,7},{7,4},{8,9},{9,10},{10,1... | collective-permute-start | bytes 245768 | tf_op jit(solution)/shard_map/direct_copies/ppermute | solution.py:439
  171.8 13.9 %collective-permute-start.9 = (f32[20,8,128]{2,1,0:T(8,128)S(1)}, f32[20,8,128]{2,1,0:T(8,128)S(1)}, u32[]{:S(2)}, u32[]{:S(2)}) collective-permute-start(f32[20,8,128]{2,1,0:T(8,128)S(1)} %collect.1.r0), channel_id=1, source_target_pairs={{0,2},{1,3},{2,0},{3,1},{4,6},{5,7},{6,4},{7,5},{8,10},{9,11},{10,... | collective-permute-start | bytes 245768 | tf_op jit(solution)/shard_map/direct_copies/ppermute | solution.py:439
  180.0 7.1 %collective-permute-start.11 = (f32[20,8,128]{2,1,0:T(8,128)S(1)}, f32[20,8,128]{2,1,0:T(8,128)S(1)}, u32[]{:S(2)}, u32[]{:S(2)}) collective-permute-start(f32[20,8,128]{2,1,0:T(8,128)S(1)} %exchange.1.r0), channel_id=1, source_target_pairs={{0,1},{1,2},{2,3},{3,0},{4,5},{5,6},{6,7},{7,4},{8,9},{9,10},{10,1... | collective-permute-start | bytes 245768 | tf_op jit(solution)/shard_map/exchange_copies/ppermute | solution.py:472
  181.5 7.2 %collective-permute-start.12 = (f32[20,8,128]{2,1,0:T(8,128)S(1)}, f32[20,8,128]{2,1,0:T(8,128)S(1)}, u32[]{:S(2)}, u32[]{:S(2)}) collective-permute-start(f32[20,8,128]{2,1,0:T(8,128)S(1)} %exchange.1.r0), channel_id=1, source_target_pairs={{0,2},{1,3},{2,0},{3,1},{4,6},{5,7},{6,4},{7,5},{8,10},{9,11},{10,... | collective-permute-start | bytes 245768 | tf_op jit(solution)/shard_map/exchange_copies/ppermute | solution.py:472
  184.3 4.4 %collective-permute-start.13 = (f32[20,8,128]{2,1,0:T(8,128)S(1)}, f32[20,8,128]{2,1,0:T(8,128)S(1)}, u32[]{:S(2)}, u32[]{:S(2)}) collective-permute-start(f32[20,8,128]{2,1,0:T(8,128)S(1)} %exchange.1.r0), channel_id=1, source_target_pairs={{0,3},{1,0},{2,1},{3,2},{4,7},{5,4},{6,5},{7,6},{8,11},{9,8},{10,9... | collective-permute-start | bytes 245768 | tf_op jit(solution)/shard_map/exchange_copies/ppermute | solution.py:472
Sparse Core Ops, SparseCore 0:
  21.4 94.7 all-gather.3
  119.1 56.6 all-gather.5

commit v9 on v7

--- a/solution.py
+++ b/solution.py
@@ -133,12 +133,12 @@
 
 
 def exchange_kernel(
-    firsts, own, big, full_in, whi_in, wlo_in, early, late, cw, out, full, whi, wlo, p1, p2, tot, prod, flat, s0, s1, s2
+    firsts, own, big, early, full, whi, wlo, cw, out, p1, p2, tot, prod, flat, s1, s2
 ):
     count = firsts[2, 0]
     npair = own.shape[1]
     nk, rows, wide = tot.shape
-    nt = whi_in.shape[0] // nk
+    nt = whi.shape[0] // nk
 
     def second(j):
         return pltpu.make_async_copy(big.at[own[1, j]], p2.at[j], s2.at[j])
@@ -146,15 +146,8 @@
     def first(t):
         return pltpu.make_async_copy(big.at[firsts[0, t]], p1.at[t], s1.at[t])
 
-    loads = [
-        pltpu.make_async_copy(whi_in, whi, s0.at[0]),
-        pltpu.make_async_copy(wlo_in, wlo, s0.at[1]),
-        pltpu.make_async_copy(full_in.at[pl.ds(0, nk * nt)], full, s0.at[2]),
-    ]
     for j in range(npair):
         second(j).start()
-    for c in loads:
-        c.start()
 
     def begin(t, carry):
         first(t).start()
@@ -164,8 +157,6 @@
     tot[...] = jnp.zeros_like(tot)
     for j in range(npair):
         second(j).wait()
-    for c in loads:
-        c.wait()
 
     def contract(left, right):
         return lax.dot_general(left, right, NT_DIMS, preferred_element_type=F32)
@@ -189,7 +180,7 @@
     w = tot[...].reshape(nk * rows, wide) * cw[...]
     hi = w.astype(BF16)
     lo = (w - hi.astype(F32)).astype(BF16)
-    m = contract(jnp.concatenate([hi, lo], axis=0), full[...])
+    m = contract(jnp.concatenate([hi, lo], axis=0), full[: nk * nt])
     m = m[: nk * rows] + m[nk * rows :]
     m = m + m
     for k in range(nk):
@@ -448,24 +439,20 @@
     exch = pl.pallas_call(
         exchange_kernel,
         out_shape=jax.ShapeDtypeStruct((n, 8, 128), F32),
-        in_specs=[SMEM, SMEM, ANY, ANY, ANY, ANY, ANY, ANY, *in_vmem(1)],
+        in_specs=[SMEM, SMEM, ANY, ANY, *in_vmem(4)],
         out_specs=pl.BlockSpec(memory_space=pltpu.VMEM),
         scratch_shapes=[
-            pltpu.VMEM((nk * nt, 4 * QW), BF16),
-            pltpu.VMEM((nk * nt, 4 * QW), BF16),
-            pltpu.VMEM((nk * nt, 4 * QW), BF16),
             pltpu.VMEM((nslot, rows, 4 * QW), BF16),
             pltpu.VMEM((npair, rows, 4 * QW), BF16),
             pltpu.VMEM((nk, rows, 4 * QW), F32),
             pltpu.VMEM((nk, npair * rows, nt), F32),
             pltpu.VMEM((n * rows, nt), F32),
-            pltpu.SemaphoreType.DMA((3,)),
             pltpu.SemaphoreType.DMA((nslot,)),
             pltpu.SemaphoreType.DMA((npair,)),
         ],
         compiler_params=pltpu.CompilerParams(vmem_limit_bytes=50 * 1024 * 1024),
         name="exchange",
-    )(firsts, own, p_big, full, w_hi, w_lo, others[0], others[2], c_full)
+    )(firsts, own, p_big, others[2], full, w_hi, w_lo, c_full)
     with jax.named_scope("exchange_copies"):
         exch_others = [lax.ppermute(exch, "ga", shift(r)) for r in range(1, 4)]
     return pl.pallas_call(

time: 200 us -> 198 us (0.990); the launches traced: 200 us -> 196 us
  waiting for transfers between devices: 66.4 us -> 60.5 us
    ppermute x3, waiting for transfers between devices: 4.14 us -> 0.01 us  [per_device(): others = [lax.ppermute(mine, 'ga', shift(r)) for r in range(1, 4)]]
    ppermute x3, starting transfers between devices: 3.3 us -> 5.67 us  [per_device(): exch_others = [lax.ppermute(exch, 'ga', shift(r)) for r in range(1, 4)]]
  transfers between devices with their start and end apart: 17 -> 17, of which waited for: 11 -> 10; matrix products, arithmetic and copies ran while one was open for 12% -> 12% of each run, Pallas kernels for 7% -> 7%
where the time goes in v9:
time: 198 us; the launch traced here: 196 us
  waiting for transfers between devices  60.5 us (31%)
  blocking collectives  40.3 us (20%)
  starting transfers between devices  35.7 us (18%)
  Pallas kernels  16 us (8%)
  between operations  15.9 us (8%)
  other arithmetic  15.6 us (8%)
  local copies, waits for them, and re-layouts  12.1 us (6%)
    all_gather x1, blocking collectives, per_device(): lax.all_gather(pairs, 'ka', axis=0, tiled=True).reshape(n_ka, npair, 3)  25.7 us
    all_to_all x1, waiting for transfers between devices, per_device(): got = lax.all_to_all(send, 'ka', 0, 0, tiled=True)  18.9 us
    ppermute x3, waiting for transfers between devices, per_device(): wk.append(lax.ppermute(v, 'ga', shift(r)) if r else v)  15.2 us
    all_gather x1, blocking collectives, per_device(): full = lax.all_gather(widen(held), 'ga', axis=1, tiled=True)  14.6 us
    all_gather x1, waiting for transfers between devices, per_device(): big = lax.all_gather(payload, 'ka', axis=0, tiled=True)  13.2 us
    all_to_all x1, starting transfers between devices, per_device(): got = lax.all_to_all(send, 'ka', 0, 0, tiled=True)  12.2 us
    ppermute x1, waiting for transfers between devices, per_device(): came = lax.ppermute(away, 'ga', [(0, 1), (1, 0), (2, 3), (3, 2)])  6 us
    ppermute x3, starting transfers between devices, per_device(): exch_others = [lax.ppermute(exch, 'ga', shift(r)) for r in range(1, 4)]  5.67 us
  transfers between devices with their start and end apart: 17, of which 10 were waited for; matrix products, arithmetic and copies ran while one was open for 12% of the time, Pallas kernels for 7%

profile of v9, /device:TPU:0, one launch (start us, length us, event | category | flops | bytes accessed | tf_op | source)
XLA Modules:
  0.0 196.0 jit_solution(6141720939221059368)
XLA Ops:
  7.2 2.9 %collective-permute-start.3 = (bf16[4,64,375]{2,1,0:T(8,128)(2,1)}, bf16[4,64,375]{2,1,0:T(8,128)(2,1)S(1)}, u32[]{:S(2)}, u32[]{:S(2)}) collective-permute-start(bf16[4,64,375]{2,1,0:T(8,128)(2,1)} %param.8), channel_id=1, source_target_pairs={{0,3},{1,2},{2,1},{3,0},{4,7},{5,6},{6,5},{7,4},{8,11},{9,10},{10,... | collective-permute-start | bytes 576008 | tf_op jit(solution)/shard_map/pack/ppermute | solution.py:278
  11.4 1.6 collective-permute-start.1
  14.6 3.4 %collective-permute-done.3 = bf16[4,64,375]{2,1,0:T(8,128)(2,1)S(1)} collective-permute-done((bf16[4,64,375]{2,1,0:T(8,128)(2,1)}, bf16[4,64,375]{2,1,0:T(8,128)(2,1)S(1)}, u32[]{:S(2)}, u32[]{:S(2)}) %collective-permute-start.3) | collective-permute-done | bytes 192032 | tf_op jit(solution)/shard_map/pack/ppermute | solution.py:278
  20.7 14.6 %all_gather.14.full = bf16[272,1536]{1,0:T(8,128)(2,1)S(1)} all-gather(bf16[272,384]{1,0:T(8,128)(2,1)S(1)} %fusion.33), channel_id=1, replica_groups=mesh['ka'=32,'ga'=4] {'ga'}, dimensions={1}, use_global_device_ids=true | all-gather | bytes 1044480 | tf_op jit(solution)/shard_map/exchange_pack/all_gather | solution.py:310
  38.0 3.6 %fusion.54 = (bf16[2,375,375]{2,0,1:T(2,128)(2,1)S(1)}, bf16[2,375,375]{2,0,1:T(2,128)(2,1)S(1)}, bf16[2,375,375]{2,0,1:T(2,128)(2,1)S(1)}, bf16[2,375,375]{2,0,1:T(2,128)(2,1)S(1)}) fusion(bf16[2,375,1500]{2,0,1:T(2,128)(2,1)S(1)} %copy-done.1), kind=kLoop, calls=%fused_computation.156 | loop fusion | bytes 4500000 | tf_op jit(solution)/shard_map/weights/slice | solution.py:292
  41.9 2.4 %broadcast_select_fusion.3 = (bf16[2,384,768]{2,1,0:T(8,128)(2,1)}, bf16[2,384,768]{2,1,0:T(8,128)(2,1)}, bf16[2,384,768]{2,1,0:T(8,128)(2,1)}) fusion(pred[]{:T(512)S(6)} %or.12, bf16[2,375,375]{2,1,0:T(8,128)(2,1)S(1)} %copy.90, bf16[2,375,375]{2,1,0:T(8,128)(2,1)S(1)} %copy.89, bf16[2,375,375]{2,1,0:T(8,128)(2,1)S(1)} %copy.88, ...), kind=kLoop, calls=%fused_computation.39 | loop fusion | flops 10027008 | bytes 5788947 | tf_op jit(solution)/shard_map/weights/jit(_where)/select_n | solution.py:300
  44.3 2.0 %collective-permute-start.4 = (bf16[2,384,768]{2,1,0:T(8,128)(2,1)}, bf16[2,384,768]{2,1,0:T(8,128)(2,1)}, u32[]{:S(2)}, u32[]{:S(2)}) collective-permute-start(bf16[2,384,768]{2,1,0:T(8,128)(2,1)} %get-tuple-element.26), channel_id=1, source_target_pairs={{0,1},{1,2},{2,3},{3,0},{4,5},{5,6},{6,7},{7,4},{8,9},{9,10},{10,1... | collective-permute-start | bytes 3538952 | tf_op jit(solution)/shard_map/weights/ppermute | solution.py:301
  46.3 2.5 %collective-permute-start.5 = (bf16[2,384,768]{2,1,0:T(8,128)(2,1)}, bf16[2,384,768]{2,1,0:T(8,128)(2,1)}, u32[]{:S(2)}, u32[]{:S(2)}) collective-permute-start(bf16[2,384,768]{2,1,0:T(8,128)(2,1)} %get-tuple-element.27), channel_id=1, source_target_pairs={{0,2},{1,3},{2,0},{3,1},{4,6},{5,7},{6,4},{7,5},{8,10},{9,11},{10,... | collective-permute-start | bytes 3538952 | tf_op jit(solution)/shard_map/weights/ppermute | solution.py:301
  50.3 25.7 %all-gather = s32[32,16,3]{1,2,0:T(4,128)S(1)} all-gather(s32[1,16,3]{1,2,0:T(4,128)S(1)} %bitcast.49), channel_id=1, replica_groups=mesh['ka'=32,'ga'=4] {'ka'}, dimensions={0}, use_global_device_ids=true | all-gather | bytes 6336 | tf_op jit(solution)/shard_map/tables/all_gather | solution.py:321
  81.9 14.7 %collective-permute-done.4 = bf16[2,384,768]{2,1,0:T(8,128)(2,1)} collective-permute-done((bf16[2,384,768]{2,1,0:T(8,128)(2,1)}, bf16[2,384,768]{2,1,0:T(8,128)(2,1)}, u32[]{:S(2)}, u32[]{:S(2)}) %collective-permute-start.4) | collective-permute-done | bytes 1179680 | tf_op jit(solution)/shard_map/weights/ppermute | solution.py:301
  97.1 5.1 %pad_maximum_fusion.w = bf16[2,1536,768]{2,1,0:T(8,128)(2,1)} fusion(bf16[2,384,768]{2,1,0:T(8,128)(2,1)S(1)} %collective-permute-done.6, bf16[2,384,768]{2,1,0:T(8,128)(2,1)} %collective-permute-done.5, bf16[2,384,768]{2,1,0:T(8,128)(2,1)} %collective-permute-done.4, bf16[2,384,768]{2,1,0:T(8,128)(2,1)} %get-tuple-element.25), kind=kLoop, calls=%fused_computation | loop fusion | flops 18874368 | bytes 9437184 | tf_op jit(solution)/shard_map/weights/concatenate | solution.py:302
  102.1 13.2 %all-gather.4.cloned.1.call-done.big = bf16[128,128,768]{2,1,0:T(8,128)(2,1)} async-done(((bf16[4,128,768]{2,1,0:T(8,128)(2,1)}), bf16[128,128,768]{2,1,0:T(8,128)(2,1)}) %all-gather.4.cloned.1.call-update) | async-done | bytes 25165840 | tf_op jit(solution)/shard_map/spread/all_gather | solution.py:288
  115.3 2.3 %copy-done = bf16[2,1536,768]{2,1,0:T(8,128)(2,1)S(1)} copy-done((bf16[2,1536,768]{2,1,0:T(8,128)(2,1)S(1)}, bf16[2,1536,768]{2,1,0:T(8,128)(2,1)}, u32[]{:S(2)}) %copy-start) | copy-done | bytes 4718616
  117.7 5.1 %direct.1 = (f32[64,8,128]{2,1,0:T(8,128)S(1)}, f32[64,8,128]{2,1,0:T(8,128)S(1)}) custom-call(s32[4,80]{1,0:T(4,128)S(1)} %pad_add_fusion.1.plan, bf16[128,128,768]{2,1,0:T(8,128)(2,1)} %all-gather.4.cloned.1.call-done.big, bf16[2,1536,768]{2,1,0:T(8,128)(2,1)S(1)} %copy-done), custom_call_target="tpu_custom_call" | custom-call | tf_op jit(solution)/shard_map/direct/pallas_call | solution.py:382
  125.5 6.0 %collective-permute-done.7.came = f32[64,8,128]{2,1,0:T(8,128)S(1)} collective-permute-done((f32[64,8,128]{2,1,0:T(8,128)S(1)}, f32[64,8,128]{2,1,0:T(8,128)S(1)}, u32[]{:S(2)}, u32[]{:S(2)}) %collective-permute-start.7) | collective-permute-done | bytes 262176 | tf_op jit(solution)/shard_map/to_neighbour/ppermute | solution.py:401
  131.5 2.4 %route.1 = f32[32,6,8,128]{3,2,1,0:T(8,128)} custom-call(s32[7,64]{1,0:T(8,128)S(1)} %stack.83.tab, f32[64,8,128]{2,1,0:T(8,128)S(1)} %get-tuple-element.4.keep, f32[64,8,128]{2,1,0:T(8,128)S(1)} %collective-permute-done.7.came), custom_call_target="tpu_custom_call" | custom-call | tf_op jit(solution)/shard_map/route/pallas_call | solution.py:402
  133.9 12.2 %all-to-all-start = ((f32[32,6,8,128]{3,2,1,0:T(8,128)}), f32[32,6,8,128]{3,2,1,0:T(8,128)S(1)}, u32[]{:S(2)}, u32[]{:S(2)}) async-start(f32[32,6,8,128]{3,2,1,0:T(8,128)} %route.1), calls=%async_computation | async-start | bytes 1572864 | tf_op jit(solution)/shard_map/to_holders/all_to_all | solution.py:416
  147.5 18.9 %all-to-all-done.got = f32[32,6,8,128]{3,2,1,0:T(8,128)S(1)} async-done(((f32[32,6,8,128]{3,2,1,0:T(8,128)}), f32[32,6,8,128]{3,2,1,0:T(8,128)S(1)}, u32[]{:S(2)}, u32[]{:S(2)}) %all-to-all-start) | async-done | bytes 786464 | tf_op jit(solution)/shard_map/to_holders/all_to_all | solution.py:416
  167.1 2.7 %collective-permute-start.10 = (f32[20,8,128]{2,1,0:T(8,128)S(1)}, f32[20,8,128]{2,1,0:T(8,128)S(1)}, u32[]{:S(2)}, u32[]{:S(2)}) collective-permute-start(f32[20,8,128]{2,1,0:T(8,128)S(1)} %collect.1.r0), channel_id=1, source_target_pairs={{0,3},{1,0},{2,1},{3,2},{4,7},{5,4},{6,5},{7,6},{8,11},{9,8},{10,9... | collective-permute-start | bytes 245768 | tf_op jit(solution)/shard_map/direct_copies/ppermute | solution.py:428
  170.0 2.3 %collective-permute-start.9 = (f32[20,8,128]{2,1,0:T(8,128)S(1)}, f32[20,8,128]{2,1,0:T(8,128)S(1)}, u32[]{:S(2)}, u32[]{:S(2)}) collective-permute-start(f32[20,8,128]{2,1,0:T(8,128)S(1)} %collect.1.r0), channel_id=1, source_target_pairs={{0,2},{1,3},{2,0},{3,1},{4,6},{5,7},{6,4},{7,5},{8,10},{9,11},{10,... | collective-permute-start | bytes 245768 | tf_op jit(solution)/shard_map/direct_copies/ppermute | solution.py:428
  172.3 1.7 all-gather.6.cloned.1.call-done.big
  174.0 4.2 %exchange.1.r0 = f32[20,8,128]{2,1,0:T(8,128)S(1)} custom-call(s32[3,64]{1,0:T(4,128)S(1)} %add_add_fusion.firsts, s32[4,16]{1,0:T(4,128)S(1)} %pad_add_fusion.own, bf16[128,16,1536]{2,1,0:T(8,128)(2,1)} %all-gather.6.cloned.1.call-done.big, f32[20,8,128]{2,1,0:T(8,128)S(1)} %collective-permute-done.10.r3.early, bf16[272,1536]{1,0:T(8,128)(2,1)S(1)} %all_gather.14.full, ...), custom_call_target="tpu_custom_call" | custom-call | tf_op jit(solution)/shard_map/exchange/pallas_call | solution.py:439
  179.7 2.7 %collective-permute-start.12 = (f32[20,8,128]{2,1,0:T(8,128)S(1)}, f32[20,8,128]{2,1,0:T(8,128)S(1)}, u32[]{:S(2)}, u32[]{:S(2)}) collective-permute-start(f32[20,8,128]{2,1,0:T(8,128)S(1)} %exchange.1.r0), channel_id=1, source_target_pairs={{0,2},{1,3},{2,0},{3,1},{4,6},{5,7},{6,4},{7,5},{8,10},{9,11},{10,... | collective-permute-start | bytes 245768 | tf_op jit(solution)/shard_map/exchange_copies/ppermute | solution.py:457
  186.8 2.4 %finish.1 = (f32[16,4096]{1,0:T(8,128)}, f32[4,4096]{1,0:T(4,128)}) custom-call(s32[4]{0:T(128)S(1)} %pad_add_fusion.2.place, f32[20,64,64]{2,1,0:T(8,128)S(1)} %arrange.1.dmat, f32[20,8,128]{2,1,0:T(8,128)S(1)} %exchange.1.r0, f32[20,8,128]{2,1,0:T(8,128)S(1)} %collective-permute-done.11.r1, f32[20,8,128]{2,1,0:T(8,128)S(1)} %collective-permute-done.12.r2, ...), custom_call_target="tpu_custom_call" | custom-call | tf_op jit(solution)/shard_map/finish/pallas_call | solution.py:458
  (111 shorter events, 25.7 us)
Async XLA Ops:
  7.2 108.2 %all-gather.4.cloned.1.call-start = ((), (), s32[]{:S(2)}) async-start(), calls=%async_computation.1 | async-start | bytes 25952256 | tf_op jit(solution)/shard_map/spread/all_gather | solution.py:288
  7.2 10.8 %collective-permute-start.3 = (bf16[4,64,375]{2,1,0:T(8,128)(2,1)}, bf16[4,64,375]{2,1,0:T(8,128)(2,1)S(1)}, u32[]{:S(2)}, u32[]{:S(2)}) collective-permute-start(bf16[4,64,375]{2,1,0:T(8,128)(2,1)} %param.8), channel_id=1, source_target_pairs={{0,3},{1,2},{2,1},{3,0},{4,7},{5,6},{6,5},{7,4},{8,11},{9,10},{10,... | collective-permute-start | bytes 576008 | tf_op jit(solution)/shard_map/pack/ppermute | solution.py:278
  11.1 8.3 %collective-permute-start = (bf16[4,32,375]{2,1,0:T(8,128)(2,1)S(1)}, bf16[4,32,375]{2,1,0:T(8,128)(2,1)S(1)}, u32[]{:S(2)}, u32[]{:S(2)}) collective-permute-start(bf16[4,32,375]{2,1,0:T(8,128)(2,1)S(1)} %get-tuple-element.39), channel_id=1, source_target_pairs={{0,1},{1,2},{2,3},{3,0},{4,5},{5,6},{6,7},{7,4},{8,9},{9,10},{10,1... | collective-permute-start | bytes 288008 | tf_op jit(solution)/shard_map/pack/ppermute | solution.py:280
  11.4 8.1 %collective-permute-start.1 = (bf16[4,32,375]{2,1,0:T(8,128)(2,1)S(1)}, bf16[4,32,375]{2,1,0:T(8,128)(2,1)S(1)}, u32[]{:S(2)}, u32[]{:S(2)}) collective-permute-start(bf16[4,32,375]{2,1,0:T(8,128)(2,1)S(1)} %get-tuple-element.37), channel_id=1, source_target_pairs={{0,2},{1,3},{2,0},{3,1},{4,6},{5,7},{6,4},{7,5},{8,10},{9,11},{10,... | collective-permute-start | bytes 288008 | tf_op jit(solution)/shard_map/pack/ppermute | solution.py:280
  13.0 6.4 %collective-permute-start.2 = (bf16[4,32,375]{2,1,0:T(8,128)(2,1)S(1)}, bf16[4,32,375]{2,1,0:T(8,128)(2,1)S(1)}, u32[]{:S(2)}, u32[]{:S(2)}) collective-permute-start(bf16[4,32,375]{2,1,0:T(8,128)(2,1)S(1)} %get-tuple-element.38), channel_id=1, source_target_pairs={{0,3},{1,0},{2,1},{3,2},{4,7},{5,4},{6,5},{7,6},{8,11},{9,8},{10,9... | collective-permute-start | bytes 288008 | tf_op jit(solution)/shard_map/pack/ppermute | solution.py:280
  14.6 5.9 %copy-start.4 = (f32[375]{0:T(512)S(1)}, f32[375]{0:T(512)}, u32[]{:S(2)}) copy-start(f32[375]{0:T(512)} %param.10) | copy-start | bytes 4504
  14.6 6.0 %copy-start.2 = (bf16[4,64,375]{2,1,0:T(8,128)(2,1)S(1)}, bf16[4,64,375]{2,1,0:T(8,128)(2,1)}, u32[]{:S(2)}) copy-start(bf16[4,64,375]{2,1,0:T(8,128)(2,1)} %param.9) | copy-start | bytes 576004
  20.5 153.5 %all-gather.6.cloned.1.call-start = ((), (), s32[]{:S(2)}) async-start(), calls=%async_computation.2 | async-start | bytes 6488064 | tf_op jit(solution)/shard_map/exchange_pack/all_gather | solution.py:313
  20.7 17.3 %copy-start.1 = (bf16[2,375,1500]{2,0,1:T(2,128)(2,1)S(1)}, bf16[2,375,1500]{2,0,1:T(2,128)(2,1)}, u32[]{:S(2)}) copy-start(bf16[2,375,1500]{2,0,1:T(2,128)(2,1)} %param.11) | copy-start | bytes 6750004
  44.3 52.3 %collective-permute-start.4 = (bf16[2,384,768]{2,1,0:T(8,128)(2,1)}, bf16[2,384,768]{2,1,0:T(8,128)(2,1)}, u32[]{:S(2)}, u32[]{:S(2)}) collective-permute-start(bf16[2,384,768]{2,1,0:T(8,128)(2,1)} %get-tuple-element.26), channel_id=1, source_target_pairs={{0,1},{1,2},{2,3},{3,0},{4,5},{5,6},{6,7},{7,4},{8,9},{9,10},{10,1... | collective-permute-start | bytes 3538952 | tf_op jit(solution)/shard_map/weights/ppermute | solution.py:301
  46.3 50.3 %collective-permute-start.5 = (bf16[2,384,768]{2,1,0:T(8,128)(2,1)}, bf16[2,384,768]{2,1,0:T(8,128)(2,1)}, u32[]{:S(2)}, u32[]{:S(2)}) collective-permute-start(bf16[2,384,768]{2,1,0:T(8,128)(2,1)} %get-tuple-element.27), channel_id=1, source_target_pairs={{0,2},{1,3},{2,0},{3,1},{4,6},{5,7},{6,4},{7,5},{8,10},{9,11},{10,... | collective-permute-start | bytes 3538952 | tf_op jit(solution)/shard_map/weights/ppermute | solution.py:301
  48.7 1.6 copy-start.3
  48.7 27.4 %copy-start.5 = (s32[64]{0:T(128)S(1)}, s32[64]{0:T(128)}, u32[]{:S(2)}) copy-start(s32[64]{0:T(128)} %param.13) | copy-start | bytes 772
  50.1 46.9 %collective-permute-start.6 = (bf16[2,384,768]{2,1,0:T(8,128)(2,1)}, bf16[2,384,768]{2,1,0:T(8,128)(2,1)S(1)}, u32[]{:S(2)}, u32[]{:S(2)}) collective-permute-start(bf16[2,384,768]{2,1,0:T(8,128)(2,1)} %broadcast_select_fusion), channel_id=1, source_target_pairs={{0,3},{1,0},{2,1},{3,2},{4,7},{5,4},{6,5},{7,6},{8,11},{9,8},{10,9... | collective-permute-start | bytes 3538952 | tf_op jit(solution)/shard_map/weights/ppermute | solution.py:301
  115.3 2.3 %copy-start = (bf16[2,1536,768]{2,1,0:T(8,128)(2,1)S(1)}, bf16[2,1536,768]{2,1,0:T(8,128)(2,1)}, u32[]{:S(2)}) copy-start(bf16[2,1536,768]{2,1,0:T(8,128)(2,1)} %pad_maximum_fusion.w) | copy-start | bytes 14155780
  122.8 8.7 %collective-permute-start.7 = (f32[64,8,128]{2,1,0:T(8,128)S(1)}, f32[64,8,128]{2,1,0:T(8,128)S(1)}, u32[]{:S(2)}, u32[]{:S(2)}) collective-permute-start(f32[64,8,128]{2,1,0:T(8,128)S(1)} %get-tuple-element.5), channel_id=1, source_target_pairs={{0,1},{1,0},{2,3},{3,2},{4,5},{5,4},{6,7},{7,6},{8,9},{9,8},{10,11... | collective-permute-start | bytes 786440 | tf_op jit(solution)/shard_map/to_neighbour/ppermute | solution.py:401
  133.9 32.5 %all-to-all-start = ((f32[32,6,8,128]{3,2,1,0:T(8,128)}), f32[32,6,8,128]{3,2,1,0:T(8,128)S(1)}, u32[]{:S(2)}, u32[]{:S(2)}) async-start(f32[32,6,8,128]{3,2,1,0:T(8,128)} %route.1), calls=%async_computation | async-start | bytes 1572864 | tf_op jit(solution)/shard_map/to_holders/all_to_all | solution.py:416
  167.1 6.9 %collective-permute-start.10 = (f32[20,8,128]{2,1,0:T(8,128)S(1)}, f32[20,8,128]{2,1,0:T(8,128)S(1)}, u32[]{:S(2)}, u32[]{:S(2)}) collective-permute-start(f32[20,8,128]{2,1,0:T(8,128)S(1)} %collect.1.r0), channel_id=1, source_target_pairs={{0,3},{1,0},{2,1},{3,2},{4,7},{5,4},{6,5},{7,6},{8,11},{9,8},{10,9... | collective-permute-start | bytes 245768 | tf_op jit(solution)/shard_map/direct_copies/ppermute | solution.py:428
  169.9 14.0 %collective-permute-start.8 = (f32[20,8,128]{2,1,0:T(8,128)S(1)}, f32[20,8,128]{2,1,0:T(8,128)S(1)}, u32[]{:S(2)}, u32[]{:S(2)}) collective-permute-start(f32[20,8,128]{2,1,0:T(8,128)S(1)} %collect.1.r0), channel_id=1, source_target_pairs={{0,1},{1,2},{2,3},{3,0},{4,5},{5,6},{6,7},{7,4},{8,9},{9,10},{10,1... | collective-permute-start | bytes 245768 | tf_op jit(solution)/shard_map/direct_copies/ppermute | solution.py:428
  170.0 13.9 %collective-permute-start.9 = (f32[20,8,128]{2,1,0:T(8,128)S(1)}, f32[20,8,128]{2,1,0:T(8,128)S(1)}, u32[]{:S(2)}, u32[]{:S(2)}) collective-permute-start(f32[20,8,128]{2,1,0:T(8,128)S(1)} %collect.1.r0), channel_id=1, source_target_pairs={{0,2},{1,3},{2,0},{3,1},{4,6},{5,7},{6,4},{7,5},{8,10},{9,11},{10,... | collective-permute-start | bytes 245768 | tf_op jit(solution)/shard_map/direct_copies/ppermute | solution.py:428
  178.2 7.1 %collective-permute-start.11 = (f32[20,8,128]{2,1,0:T(8,128)S(1)}, f32[20,8,128]{2,1,0:T(8,128)S(1)}, u32[]{:S(2)}, u32[]{:S(2)}) collective-permute-start(f32[20,8,128]{2,1,0:T(8,128)S(1)} %exchange.1.r0), channel_id=1, source_target_pairs={{0,1},{1,2},{2,3},{3,0},{4,5},{5,6},{6,7},{7,4},{8,9},{9,10},{10,1... | collective-permute-start | bytes 245768 | tf_op jit(solution)/shard_map/exchange_copies/ppermute | solution.py:457
  179.7 7.0 %collective-permute-start.12 = (f32[20,8,128]{2,1,0:T(8,128)S(1)}, f32[20,8,128]{2,1,0:T(8,128)S(1)}, u32[]{:S(2)}, u32[]{:S(2)}) collective-permute-start(f32[20,8,128]{2,1,0:T(8,128)S(1)} %exchange.1.r0), channel_id=1, source_target_pairs={{0,2},{1,3},{2,0},{3,1},{4,6},{5,7},{6,4},{7,5},{8,10},{9,11},{10,... | collective-permute-start | bytes 245768 | tf_op jit(solution)/shard_map/exchange_copies/ppermute | solution.py:457
  182.4 4.4 %collective-permute-start.13 = (f32[20,8,128]{2,1,0:T(8,128)S(1)}, f32[20,8,128]{2,1,0:T(8,128)S(1)}, u32[]{:S(2)}, u32[]{:S(2)}) collective-permute-start(f32[20,8,128]{2,1,0:T(8,128)S(1)} %exchange.1.r0), channel_id=1, source_target_pairs={{0,3},{1,0},{2,1},{3,2},{4,7},{5,4},{6,5},{7,6},{8,11},{9,8},{10,9... | collective-permute-start | bytes 245768 | tf_op jit(solution)/shard_map/exchange_copies/ppermute | solution.py:457
Sparse Core Ops, SparseCore 0:
  20.6 94.6 all-gather.3
  118.2 55.7 all-gather.5

commit v10 on v9

--- a/solution.py
+++ b/solution.py
@@ -30,7 +30,7 @@
     return jnp.concatenate([even, odd], axis=1)
 
 
-def direct_kernel(plan, big, w, keep, away, xs, ys, us, prod, kept, sent, sx, sy):
+def direct_kernel(plan, big, wk, keep, away, w, xs, ys, us, prod, kept, sent, sw, sx, sy):
     half = prod.shape[0] // CH
     nt = 2 * half
     deep = xs.shape[3]
@@ -76,9 +76,17 @@
             kept[t] = jnp.where(parity == 0, tiles[0], tiles[1])
             sent[t] = jnp.where(parity == 0, tiles[1], tiles[0])
 
+    loads = [pltpu.make_async_copy(wk.at[i], w.at[i], sw.at[i]) for i in range(w.shape[0])]
+    loads[0].start()
+
     @pl.when(chunks > 0)
     def _():
         begin(0)
+
+    for c in loads[1:]:
+        c.start()
+    for c in loads:
+        c.wait()
 
     def chunk(c, carry):
         @pl.when(c + 1 < chunks)
@@ -382,19 +390,21 @@
     keep, away = pl.pallas_call(
         direct_kernel,
         out_shape=(jax.ShapeDtypeStruct((nslot, 8, 128), F32),) * 2,
-        in_specs=[SMEM, ANY, *in_vmem(1)],
+        in_specs=[SMEM, ANY, ANY],
         out_specs=tuple(in_vmem(2)),
         scratch_shapes=[
+            pltpu.VMEM((qs, 4 * QW, 2 * QW), BF16),
             pltpu.VMEM((2, CH, nt, 2 * QW), BF16),
             pltpu.VMEM((3, CH, nt, 2 * QW), BF16),
             pltpu.VMEM((2, CH * half, 2 * QW), BF16),
             pltpu.VMEM((CH * half, 128), F32),
             pltpu.VMEM((nslot + 1, 8, 128), F32),
             pltpu.VMEM((nslot + 1, 8, 128), F32),
+            pltpu.SemaphoreType.DMA((qs,)),
             pltpu.SemaphoreType.DMA((2, CH)),
             pltpu.SemaphoreType.DMA((3, CH)),
         ],
-        compiler_params=pltpu.CompilerParams(vmem_limit_bytes=32 * 1024 * 1024),
+        compiler_params=pltpu.CompilerParams(vmem_limit_bytes=52 * 1024 * 1024),
         name="direct",
     )(plan, big, wk)
     with jax.named_scope("to_neighbour"):

time: 198 us -> 196 us (0.990)
  local copies, waits for them, and re-layouts: 12.1 us -> 9.73 us
  Pallas kernels: 16 us -> 18.1 us
    unnamed x17 -> x15, local copies, waits for them, and re-layouts: 2.72 us -> 0.38 us
  transfers between devices with their start and end apart: 17 -> 17, of which waited for: 10 -> 10; matrix products, arithmetic and copies ran while one was open for 12% -> 12% of each run, Pallas kernels for 7% -> 8%
where the time goes in v10:
time: 196 us; the launch traced here: 195 us
  waiting for transfers between devices  60.2 us (31%)
  blocking collectives  40.3 us (21%)
  starting transfers between devices  35.6 us (18%)
  Pallas kernels  18.1 us (9%)
  between operations  15.9 us (8%)
  other arithmetic  15.6 us (8%)
  local copies, waits for them, and re-layouts  9.73 us (5%)
    all_gather x1, blocking collectives, per_device(): lax.all_gather(pairs, 'ka', axis=0, tiled=True).reshape(n_ka, npair, 3)  25.7 us
    all_to_all x1, waiting for transfers between devices, per_device(): got = lax.all_to_all(send, 'ka', 0, 0, tiled=True)  18.4 us
    ppermute x3, waiting for transfers between devices, per_device(): wk.append(lax.ppermute(v, 'ga', shift(r)) if r else v)  15.2 us
    all_gather x1, blocking collectives, per_device(): full = lax.all_gather(widen(held), 'ga', axis=1, tiled=True)  14.6 us
    all_gather x1, waiting for transfers between devices, per_device(): big = lax.all_gather(payload, 'ka', axis=0, tiled=True)  13.2 us
    all_to_all x1, starting transfers between devices, per_device(): got = lax.all_to_all(send, 'ka', 0, 0, tiled=True)  12.1 us
    pallas_call x1, Pallas kernels, per_device(): pl.pallas_call(direct_kernel, out_shape=(jax.ShapeDtypeStruct((nslot, 8,...  6.92 us
    ppermute x1, waiting for transfers between devices, per_device(): came = lax.ppermute(away, 'ga', [(0, 1), (1, 0), (2, 3), (3, 2)])  5.79 us
  transfers between devices with their start and end apart: 17, of which 10 were waited for; matrix products, arithmetic and copies ran while one was open for 12% of the time, Pallas kernels for 8%

profile of v10, /device:TPU:0, one launch (start us, length us, event | category | flops | bytes accessed | tf_op | source)
XLA Modules:
  0.0 195.4 jit_solution(5490283481739456212)
XLA Ops:
  7.2 2.9 %collective-permute-start.3 = (bf16[4,64,375]{2,1,0:T(8,128)(2,1)}, bf16[4,64,375]{2,1,0:T(8,128)(2,1)S(1)}, u32[]{:S(2)}, u32[]{:S(2)}) collective-permute-start(bf16[4,64,375]{2,1,0:T(8,128)(2,1)} %param.8), channel_id=1, source_target_pairs={{0,3},{1,2},{2,1},{3,0},{4,7},{5,6},{6,5},{7,4},{8,11},{9,10},{10,... | collective-permute-start | bytes 576008 | tf_op jit(solution)/shard_map/pack/ppermute | solution.py:286
  11.4 1.6 collective-permute-start.1
  14.6 3.4 %collective-permute-done.3 = bf16[4,64,375]{2,1,0:T(8,128)(2,1)S(1)} collective-permute-done((bf16[4,64,375]{2,1,0:T(8,128)(2,1)}, bf16[4,64,375]{2,1,0:T(8,128)(2,1)S(1)}, u32[]{:S(2)}, u32[]{:S(2)}) %collective-permute-start.3) | collective-permute-done | bytes 192032 | tf_op jit(solution)/shard_map/pack/ppermute | solution.py:286
  20.7 14.6 %all_gather.14.full = bf16[272,1536]{1,0:T(8,128)(2,1)S(1)} all-gather(bf16[272,384]{1,0:T(8,128)(2,1)S(1)} %fusion.33), channel_id=1, replica_groups=mesh['ka'=32,'ga'=4] {'ga'}, dimensions={1}, use_global_device_ids=true | all-gather | bytes 1044480 | tf_op jit(solution)/shard_map/exchange_pack/all_gather | solution.py:318
  36.3 1.6 constant_dynamic-slice_fusion
  38.0 3.6 %fusion.54 = (bf16[2,375,375]{2,0,1:T(2,128)(2,1)S(1)}, bf16[2,375,375]{2,0,1:T(2,128)(2,1)S(1)}, bf16[2,375,375]{2,0,1:T(2,128)(2,1)S(1)}, bf16[2,375,375]{2,0,1:T(2,128)(2,1)S(1)}) fusion(bf16[2,375,1500]{2,0,1:T(2,128)(2,1)S(1)} %copy-done), kind=kLoop, calls=%fused_computation.156 | loop fusion | bytes 4500000 | tf_op jit(solution)/shard_map/weights/slice | solution.py:300
  41.9 2.4 %broadcast_select_fusion.3 = (bf16[2,384,768]{2,1,0:T(8,128)(2,1)}, bf16[2,384,768]{2,1,0:T(8,128)(2,1)}, bf16[2,384,768]{2,1,0:T(8,128)(2,1)}) fusion(pred[]{:T(512)S(6)} %or.12, bf16[2,375,375]{2,1,0:T(8,128)(2,1)S(1)} %copy.90, bf16[2,375,375]{2,1,0:T(8,128)(2,1)S(1)} %copy.89, bf16[2,375,375]{2,1,0:T(8,128)(2,1)S(1)} %copy.88, ...), kind=kLoop, calls=%fused_computation.39 | loop fusion | flops 10027008 | bytes 5788947 | tf_op jit(solution)/shard_map/weights/jit(_where)/select_n | solution.py:308
  44.3 2.0 %collective-permute-start.4 = (bf16[2,384,768]{2,1,0:T(8,128)(2,1)}, bf16[2,384,768]{2,1,0:T(8,128)(2,1)}, u32[]{:S(2)}, u32[]{:S(2)}) collective-permute-start(bf16[2,384,768]{2,1,0:T(8,128)(2,1)} %get-tuple-element.26), channel_id=1, source_target_pairs={{0,1},{1,2},{2,3},{3,0},{4,5},{5,6},{6,7},{7,4},{8,9},{9,10},{10,1... | collective-permute-start | bytes 3538952 | tf_op jit(solution)/shard_map/weights/ppermute | solution.py:309
  46.3 2.5 %collective-permute-start.5 = (bf16[2,384,768]{2,1,0:T(8,128)(2,1)}, bf16[2,384,768]{2,1,0:T(8,128)(2,1)}, u32[]{:S(2)}, u32[]{:S(2)}) collective-permute-start(bf16[2,384,768]{2,1,0:T(8,128)(2,1)} %get-tuple-element.27), channel_id=1, source_target_pairs={{0,2},{1,3},{2,0},{3,1},{4,6},{5,7},{6,4},{7,5},{8,10},{9,11},{10,... | collective-permute-start | bytes 3538952 | tf_op jit(solution)/shard_map/weights/ppermute | solution.py:309
  50.3 25.7 %all-gather = s32[32,16,3]{1,2,0:T(4,128)S(1)} all-gather(s32[1,16,3]{1,2,0:T(4,128)S(1)} %bitcast.49), channel_id=1, replica_groups=mesh['ka'=32,'ga'=4] {'ka'}, dimensions={0}, use_global_device_ids=true | all-gather | bytes 6336 | tf_op jit(solution)/shard_map/tables/all_gather | solution.py:329
  81.9 14.7 %collective-permute-done.4 = bf16[2,384,768]{2,1,0:T(8,128)(2,1)} collective-permute-done((bf16[2,384,768]{2,1,0:T(8,128)(2,1)}, bf16[2,384,768]{2,1,0:T(8,128)(2,1)}, u32[]{:S(2)}, u32[]{:S(2)}) %collective-permute-start.4) | collective-permute-done | bytes 1179680 | tf_op jit(solution)/shard_map/weights/ppermute | solution.py:309
  97.1 5.1 %pad_maximum_fusion.wk = bf16[2,1536,768]{2,1,0:T(8,128)(2,1)} fusion(bf16[2,384,768]{2,1,0:T(8,128)(2,1)S(1)} %collective-permute-done.6, bf16[2,384,768]{2,1,0:T(8,128)(2,1)} %collective-permute-done.5, bf16[2,384,768]{2,1,0:T(8,128)(2,1)} %collective-permute-done.4, bf16[2,384,768]{2,1,0:T(8,128)(2,1)} %get-tuple-element.25), kind=kLoop, calls=%fused_computation | loop fusion | flops 18874368 | bytes 9437184 | tf_op jit(solution)/shard_map/weights/concatenate | solution.py:310
  102.1 13.2 %all-gather.4.cloned.1.call-done.big = bf16[128,128,768]{2,1,0:T(8,128)(2,1)} async-done(((bf16[4,128,768]{2,1,0:T(8,128)(2,1)}), bf16[128,128,768]{2,1,0:T(8,128)(2,1)}) %all-gather.4.cloned.1.call-update) | async-done | bytes 25165840 | tf_op jit(solution)/shard_map/spread/all_gather | solution.py:296
  115.3 6.9 %direct.1 = (f32[64,8,128]{2,1,0:T(8,128)S(1)}, f32[64,8,128]{2,1,0:T(8,128)S(1)}) custom-call(s32[4,80]{1,0:T(4,128)S(1)} %pad_add_fusion.1.plan, bf16[128,128,768]{2,1,0:T(8,128)(2,1)} %all-gather.4.cloned.1.call-done.big, bf16[2,1536,768]{2,1,0:T(8,128)(2,1)} %pad_maximum_fusion.wk), custom_call_target="tpu_custom_call" | custom-call | tf_op jit(solution)/shard_map/direct/pallas_call | solution.py:390
  125.0 5.8 %collective-permute-done.7.came = f32[64,8,128]{2,1,0:T(8,128)S(1)} collective-permute-done((f32[64,8,128]{2,1,0:T(8,128)S(1)}, f32[64,8,128]{2,1,0:T(8,128)S(1)}, u32[]{:S(2)}, u32[]{:S(2)}) %collective-permute-start.7) | collective-permute-done | bytes 262176 | tf_op jit(solution)/shard_map/to_neighbour/ppermute | solution.py:411
  130.8 2.3 %route.1 = f32[32,6,8,128]{3,2,1,0:T(8,128)} custom-call(s32[7,64]{1,0:T(8,128)S(1)} %stack.83.tab, f32[64,8,128]{2,1,0:T(8,128)S(1)} %get-tuple-element.4.keep, f32[64,8,128]{2,1,0:T(8,128)S(1)} %collective-permute-done.7.came), custom_call_target="tpu_custom_call" | custom-call | tf_op jit(solution)/shard_map/route/pallas_call | solution.py:412
  133.1 12.1 %all-to-all-start = ((f32[32,6,8,128]{3,2,1,0:T(8,128)}), f32[32,6,8,128]{3,2,1,0:T(8,128)S(1)}, u32[]{:S(2)}, u32[]{:S(2)}) async-start(f32[32,6,8,128]{3,2,1,0:T(8,128)} %route.1), calls=%async_computation | async-start | bytes 1572864 | tf_op jit(solution)/shard_map/to_holders/all_to_all | solution.py:426
  146.6 18.4 %all-to-all-done.got = f32[32,6,8,128]{3,2,1,0:T(8,128)S(1)} async-done(((f32[32,6,8,128]{3,2,1,0:T(8,128)}), f32[32,6,8,128]{3,2,1,0:T(8,128)S(1)}, u32[]{:S(2)}, u32[]{:S(2)}) %all-to-all-start) | async-done | bytes 786464 | tf_op jit(solution)/shard_map/to_holders/all_to_all | solution.py:426
  165.8 2.8 %collective-permute-start.10 = (f32[20,8,128]{2,1,0:T(8,128)S(1)}, f32[20,8,128]{2,1,0:T(8,128)S(1)}, u32[]{:S(2)}, u32[]{:S(2)}) collective-permute-start(f32[20,8,128]{2,1,0:T(8,128)S(1)} %collect.1.r0), channel_id=1, source_target_pairs={{0,3},{1,0},{2,1},{3,2},{4,7},{5,4},{6,5},{7,6},{8,11},{9,8},{10,9... | collective-permute-start | bytes 245768 | tf_op jit(solution)/shard_map/direct_copies/ppermute | solution.py:438
  168.7 2.3 %collective-permute-start.9 = (f32[20,8,128]{2,1,0:T(8,128)S(1)}, f32[20,8,128]{2,1,0:T(8,128)S(1)}, u32[]{:S(2)}, u32[]{:S(2)}) collective-permute-start(f32[20,8,128]{2,1,0:T(8,128)S(1)} %collect.1.r0), channel_id=1, source_target_pairs={{0,2},{1,3},{2,0},{3,1},{4,6},{5,7},{6,4},{7,5},{8,10},{9,11},{10,... | collective-permute-start | bytes 245768 | tf_op jit(solution)/shard_map/direct_copies/ppermute | solution.py:438
  171.0 2.1 %all-gather.6.cloned.1.call-done.big = bf16[128,16,1536]{2,1,0:T(8,128)(2,1)} async-done(((bf16[4,16,1536]{2,1,0:T(8,128)(2,1)}), bf16[128,16,1536]{2,1,0:T(8,128)(2,1)}) %all-gather.6.cloned.1.call-update) | async-done | bytes 6291472 | tf_op jit(solution)/shard_map/exchange_pack/all_gather | solution.py:321
  173.1 4.4 %exchange.1.r0 = f32[20,8,128]{2,1,0:T(8,128)S(1)} custom-call(s32[3,64]{1,0:T(4,128)S(1)} %add_add_fusion.firsts, s32[4,16]{1,0:T(4,128)S(1)} %pad_add_fusion.own, bf16[128,16,1536]{2,1,0:T(8,128)(2,1)} %all-gather.6.cloned.1.call-done.big, f32[20,8,128]{2,1,0:T(8,128)S(1)} %collective-permute-done.10.r3.early, bf16[272,1536]{1,0:T(8,128)(2,1)S(1)} %all_gather.14.full, ...), custom_call_target="tpu_custom_call" | custom-call | tf_op jit(solution)/shard_map/exchange/pallas_call | solution.py:449
  179.1 2.7 %collective-permute-start.12 = (f32[20,8,128]{2,1,0:T(8,128)S(1)}, f32[20,8,128]{2,1,0:T(8,128)S(1)}, u32[]{:S(2)}, u32[]{:S(2)}) collective-permute-start(f32[20,8,128]{2,1,0:T(8,128)S(1)} %exchange.1.r0), channel_id=1, source_target_pairs={{0,2},{1,3},{2,0},{3,1},{4,6},{5,7},{6,4},{7,5},{8,10},{9,11},{10,... | collective-permute-start | bytes 245768 | tf_op jit(solution)/shard_map/exchange_copies/ppermute | solution.py:467
  186.2 2.4 %finish.1 = (f32[16,4096]{1,0:T(8,128)}, f32[4,4096]{1,0:T(4,128)}) custom-call(s32[4]{0:T(128)S(1)} %pad_add_fusion.2.place, f32[20,64,64]{2,1,0:T(8,128)S(1)} %arrange.1.dmat, f32[20,8,128]{2,1,0:T(8,128)S(1)} %exchange.1.r0, f32[20,8,128]{2,1,0:T(8,128)S(1)} %collective-permute-done.11.r1, f32[20,8,128]{2,1,0:T(8,128)S(1)} %collective-permute-done.12.r2, ...), custom_call_target="tpu_custom_call" | custom-call | tf_op jit(solution)/shard_map/finish/pallas_call | solution.py:468
  (109 shorter events, 24.1 us)
Async XLA Ops:
  7.2 108.2 %all-gather.4.cloned.1.call-start = ((), (), s32[]{:S(2)}) async-start(), calls=%async_computation.1 | async-start | bytes 25952256 | tf_op jit(solution)/shard_map/spread/all_gather | solution.py:296
  7.2 10.8 %collective-permute-start.3 = (bf16[4,64,375]{2,1,0:T(8,128)(2,1)}, bf16[4,64,375]{2,1,0:T(8,128)(2,1)S(1)}, u32[]{:S(2)}, u32[]{:S(2)}) collective-permute-start(bf16[4,64,375]{2,1,0:T(8,128)(2,1)} %param.8), channel_id=1, source_target_pairs={{0,3},{1,2},{2,1},{3,0},{4,7},{5,6},{6,5},{7,4},{8,11},{9,10},{10,... | collective-permute-start | bytes 576008 | tf_op jit(solution)/shard_map/pack/ppermute | solution.py:286
  11.1 8.3 %collective-permute-start = (bf16[4,32,375]{2,1,0:T(8,128)(2,1)S(1)}, bf16[4,32,375]{2,1,0:T(8,128)(2,1)S(1)}, u32[]{:S(2)}, u32[]{:S(2)}) collective-permute-start(bf16[4,32,375]{2,1,0:T(8,128)(2,1)S(1)} %get-tuple-element.39), channel_id=1, source_target_pairs={{0,1},{1,2},{2,3},{3,0},{4,5},{5,6},{6,7},{7,4},{8,9},{9,10},{10,1... | collective-permute-start | bytes 288008 | tf_op jit(solution)/shard_map/pack/ppermute | solution.py:288
  11.4 8.1 %collective-permute-start.1 = (bf16[4,32,375]{2,1,0:T(8,128)(2,1)S(1)}, bf16[4,32,375]{2,1,0:T(8,128)(2,1)S(1)}, u32[]{:S(2)}, u32[]{:S(2)}) collective-permute-start(bf16[4,32,375]{2,1,0:T(8,128)(2,1)S(1)} %get-tuple-element.37), channel_id=1, source_target_pairs={{0,2},{1,3},{2,0},{3,1},{4,6},{5,7},{6,4},{7,5},{8,10},{9,11},{10,... | collective-permute-start | bytes 288008 | tf_op jit(solution)/shard_map/pack/ppermute | solution.py:288
  13.0 6.4 %collective-permute-start.2 = (bf16[4,32,375]{2,1,0:T(8,128)(2,1)S(1)}, bf16[4,32,375]{2,1,0:T(8,128)(2,1)S(1)}, u32[]{:S(2)}, u32[]{:S(2)}) collective-permute-start(bf16[4,32,375]{2,1,0:T(8,128)(2,1)S(1)} %get-tuple-element.38), channel_id=1, source_target_pairs={{0,3},{1,0},{2,1},{3,2},{4,7},{5,4},{6,5},{7,6},{8,11},{9,8},{10,9... | collective-permute-start | bytes 288008 | tf_op jit(solution)/shard_map/pack/ppermute | solution.py:288
  14.6 5.9 %copy-start.3 = (f32[375]{0:T(512)S(1)}, f32[375]{0:T(512)}, u32[]{:S(2)}) copy-start(f32[375]{0:T(512)} %param.10) | copy-start | bytes 4504
  14.6 6.0 %copy-start.1 = (bf16[4,64,375]{2,1,0:T(8,128)(2,1)S(1)}, bf16[4,64,375]{2,1,0:T(8,128)(2,1)}, u32[]{:S(2)}) copy-start(bf16[4,64,375]{2,1,0:T(8,128)(2,1)} %param.9) | copy-start | bytes 576004
  20.5 152.6 %all-gather.6.cloned.1.call-start = ((), (), s32[]{:S(2)}) async-start(), calls=%async_computation.2 | async-start | bytes 6488064 | tf_op jit(solution)/shard_map/exchange_pack/all_gather | solution.py:321
  20.7 17.3 %copy-start = (bf16[2,375,1500]{2,0,1:T(2,128)(2,1)S(1)}, bf16[2,375,1500]{2,0,1:T(2,128)(2,1)}, u32[]{:S(2)}) copy-start(bf16[2,375,1500]{2,0,1:T(2,128)(2,1)} %param.11) | copy-start | bytes 6750004
  44.3 52.3 %collective-permute-start.4 = (bf16[2,384,768]{2,1,0:T(8,128)(2,1)}, bf16[2,384,768]{2,1,0:T(8,128)(2,1)}, u32[]{:S(2)}, u32[]{:S(2)}) collective-permute-start(bf16[2,384,768]{2,1,0:T(8,128)(2,1)} %get-tuple-element.26), channel_id=1, source_target_pairs={{0,1},{1,2},{2,3},{3,0},{4,5},{5,6},{6,7},{7,4},{8,9},{9,10},{10,1... | collective-permute-start | bytes 3538952 | tf_op jit(solution)/shard_map/weights/ppermute | solution.py:309
  46.3 50.3 %collective-permute-start.5 = (bf16[2,384,768]{2,1,0:T(8,128)(2,1)}, bf16[2,384,768]{2,1,0:T(8,128)(2,1)}, u32[]{:S(2)}, u32[]{:S(2)}) collective-permute-start(bf16[2,384,768]{2,1,0:T(8,128)(2,1)} %get-tuple-element.27), channel_id=1, source_target_pairs={{0,2},{1,3},{2,0},{3,1},{4,6},{5,7},{6,4},{7,5},{8,10},{9,11},{10,... | collective-permute-start | bytes 3538952 | tf_op jit(solution)/shard_map/weights/ppermute | solution.py:309
  48.7 1.6 copy-start.2
  48.7 27.4 %copy-start.4 = (s32[64]{0:T(128)S(1)}, s32[64]{0:T(128)}, u32[]{:S(2)}) copy-start(s32[64]{0:T(128)} %param.13) | copy-start | bytes 772
  50.1 46.9 %collective-permute-start.6 = (bf16[2,384,768]{2,1,0:T(8,128)(2,1)}, bf16[2,384,768]{2,1,0:T(8,128)(2,1)S(1)}, u32[]{:S(2)}, u32[]{:S(2)}) collective-permute-start(bf16[2,384,768]{2,1,0:T(8,128)(2,1)} %broadcast_select_fusion), channel_id=1, source_target_pairs={{0,3},{1,0},{2,1},{3,2},{4,7},{5,4},{6,5},{7,6},{8,11},{9,8},{10,9... | collective-permute-start | bytes 3538952 | tf_op jit(solution)/shard_map/weights/ppermute | solution.py:309
  122.3 8.5 %collective-permute-start.7 = (f32[64,8,128]{2,1,0:T(8,128)S(1)}, f32[64,8,128]{2,1,0:T(8,128)S(1)}, u32[]{:S(2)}, u32[]{:S(2)}) collective-permute-start(f32[64,8,128]{2,1,0:T(8,128)S(1)} %get-tuple-element.5), channel_id=1, source_target_pairs={{0,1},{1,0},{2,3},{3,2},{4,5},{5,4},{6,7},{7,6},{8,9},{9,8},{10,11... | collective-permute-start | bytes 786440 | tf_op jit(solution)/shard_map/to_neighbour/ppermute | solution.py:411
  133.1 31.9 %all-to-all-start = ((f32[32,6,8,128]{3,2,1,0:T(8,128)}), f32[32,6,8,128]{3,2,1,0:T(8,128)S(1)}, u32[]{:S(2)}, u32[]{:S(2)}) async-start(f32[32,6,8,128]{3,2,1,0:T(8,128)} %route.1), calls=%async_computation | async-start | bytes 1572864 | tf_op jit(solution)/shard_map/to_holders/all_to_all | solution.py:426
  165.8 7.3 %collective-permute-start.10 = (f32[20,8,128]{2,1,0:T(8,128)S(1)}, f32[20,8,128]{2,1,0:T(8,128)S(1)}, u32[]{:S(2)}, u32[]{:S(2)}) collective-permute-start(f32[20,8,128]{2,1,0:T(8,128)S(1)} %collect.1.r0), channel_id=1, source_target_pairs={{0,3},{1,0},{2,1},{3,2},{4,7},{5,4},{6,5},{7,6},{8,11},{9,8},{10,9... | collective-permute-start | bytes 245768 | tf_op jit(solution)/shard_map/direct_copies/ppermute | solution.py:438
  168.6 14.7 %collective-permute-start.8 = (f32[20,8,128]{2,1,0:T(8,128)S(1)}, f32[20,8,128]{2,1,0:T(8,128)S(1)}, u32[]{:S(2)}, u32[]{:S(2)}) collective-permute-start(f32[20,8,128]{2,1,0:T(8,128)S(1)} %collect.1.r0), channel_id=1, source_target_pairs={{0,1},{1,2},{2,3},{3,0},{4,5},{5,6},{6,7},{7,4},{8,9},{9,10},{10,1... | collective-permute-start | bytes 245768 | tf_op jit(solution)/shard_map/direct_copies/ppermute | solution.py:438
  168.7 14.6 %collective-permute-start.9 = (f32[20,8,128]{2,1,0:T(8,128)S(1)}, f32[20,8,128]{2,1,0:T(8,128)S(1)}, u32[]{:S(2)}, u32[]{:S(2)}) collective-permute-start(f32[20,8,128]{2,1,0:T(8,128)S(1)} %collect.1.r0), channel_id=1, source_target_pairs={{0,2},{1,3},{2,0},{3,1},{4,6},{5,7},{6,4},{7,5},{8,10},{9,11},{10,... | collective-permute-start | bytes 245768 | tf_op jit(solution)/shard_map/direct_copies/ppermute | solution.py:438
  177.5 7.1 %collective-permute-start.11 = (f32[20,8,128]{2,1,0:T(8,128)S(1)}, f32[20,8,128]{2,1,0:T(8,128)S(1)}, u32[]{:S(2)}, u32[]{:S(2)}) collective-permute-start(f32[20,8,128]{2,1,0:T(8,128)S(1)} %exchange.1.r0), channel_id=1, source_target_pairs={{0,1},{1,2},{2,3},{3,0},{4,5},{5,6},{6,7},{7,4},{8,9},{9,10},{10,1... | collective-permute-start | bytes 245768 | tf_op jit(solution)/shard_map/exchange_copies/ppermute | solution.py:467
  179.1 6.8 %collective-permute-start.12 = (f32[20,8,128]{2,1,0:T(8,128)S(1)}, f32[20,8,128]{2,1,0:T(8,128)S(1)}, u32[]{:S(2)}, u32[]{:S(2)}) collective-permute-start(f32[20,8,128]{2,1,0:T(8,128)S(1)} %exchange.1.r0), channel_id=1, source_target_pairs={{0,2},{1,3},{2,0},{3,1},{4,6},{5,7},{6,4},{7,5},{8,10},{9,11},{10,... | collective-permute-start | bytes 245768 | tf_op jit(solution)/shard_map/exchange_copies/ppermute | solution.py:467
  181.7 4.4 %collective-permute-start.13 = (f32[20,8,128]{2,1,0:T(8,128)S(1)}, f32[20,8,128]{2,1,0:T(8,128)S(1)}, u32[]{:S(2)}, u32[]{:S(2)}) collective-permute-start(f32[20,8,128]{2,1,0:T(8,128)S(1)} %exchange.1.r0), channel_id=1, source_target_pairs={{0,3},{1,0},{2,1},{3,2},{4,7},{5,4},{6,5},{7,6},{8,11},{9,8},{10,9... | collective-permute-start | bytes 245768 | tf_op jit(solution)/shard_map/exchange_copies/ppermute | solution.py:467
Sparse Core Ops, SparseCore 0:
  20.6 94.6 all-gather.3
  118.2 54.8 all-gather.5

commit v11 on v9

--- a/solution.py
+++ b/solution.py
@@ -146,15 +146,22 @@
     def first(t):
         return pltpu.make_async_copy(big.at[firsts[0, t]], p1.at[t], s1.at[t])
 
-    for j in range(npair):
-        second(j).start()
 
     def begin(t, carry):
         first(t).start()
         return carry
 
     lax.fori_loop(0, count, begin, 0)
+    for j in range(npair):
+        second(j).start()
     tot[...] = jnp.zeros_like(tot)
+    def gather(t, carry):
+        first(t).wait()
+        k = firsts[1, t]
+        tot[k] = tot[k] + p1[t].astype(F32)
+        return carry
+
+    lax.fori_loop(0, count, gather, 0)
     for j in range(npair):
         second(j).wait()
 
@@ -170,13 +177,6 @@
         r = pl.ds(j * rows, rows)
         flat[r, :] = prod[own[0, j], r, :]
 
-    def gather(t, carry):
-        first(t).wait()
-        k = firsts[1, t]
-        tot[k] = tot[k] + p1[t].astype(F32)
-        return carry
-
-    lax.fori_loop(0, count, gather, 0)
     w = tot[...].reshape(nk * rows, wide) * cw[...]
     hi = w.astype(BF16)
     lo = (w - hi.astype(F32)).astype(BF16)

time: 198 us -> 195 us (0.985)
  no operation moved by 1% of the time
where the time goes in v11:
time: 195 us; the launch traced here: 194 us
  waiting for transfers between devices  60.2 us (31%)
  blocking collectives  40.3 us (21%)
  starting transfers between devices  34.5 us (18%)
  between operations  15.9 us (8%)
  Pallas kernels  15.7 us (8%)
  other arithmetic  15.6 us (8%)
  local copies, waits for them, and re-layouts  12.1 us (6%)
    all_gather x1, blocking collectives, per_device(): lax.all_gather(pairs, 'ka', axis=0, tiled=True).reshape(n_ka, npair, 3)  25.7 us
    all_to_all x1, waiting for transfers between devices, per_device(): got = lax.all_to_all(send, 'ka', 0, 0, tiled=True)  17.8 us
    ppermute x3, waiting for transfers between devices, per_device(): wk.append(lax.ppermute(v, 'ga', shift(r)) if r else v)  15.2 us
    all_gather x1, blocking collectives, per_device(): full = lax.all_gather(widen(held), 'ga', axis=1, tiled=True)  14.6 us
    all_gather x1, waiting for transfers between devices, per_device(): big = lax.all_gather(payload, 'ka', axis=0, tiled=True)  13.2 us
    all_to_all x1, starting transfers between devices, per_device(): got = lax.all_to_all(send, 'ka', 0, 0, tiled=True)  11 us
    ppermute x1, waiting for transfers between devices, per_device(): came = lax.ppermute(away, 'ga', [(0, 1), (1, 0), (2, 3), (3, 2)])  5.71 us
    ppermute x3, starting transfers between devices, per_device(): exch_others = [lax.ppermute(exch, 'ga', shift(r)) for r in range(1, 4)]  5.67 us
  transfers between devices with their start and end apart: 17, of which 10 were waited for; matrix products, arithmetic and copies ran while one was open for 12% of the time, Pallas kernels for 7%

profile of v11, /device:TPU:0, one launch (start us, length us, event | category | flops | bytes accessed | tf_op | source)
XLA Modules:
  0.0 194.3 jit_solution(7321013784468375476)
XLA Ops:
  7.2 2.9 %collective-permute-start.3 = (bf16[4,64,375]{2,1,0:T(8,128)(2,1)}, bf16[4,64,375]{2,1,0:T(8,128)(2,1)S(1)}, u32[]{:S(2)}, u32[]{:S(2)}) collective-permute-start(bf16[4,64,375]{2,1,0:T(8,128)(2,1)} %param.8), channel_id=1, source_target_pairs={{0,3},{1,2},{2,1},{3,0},{4,7},{5,6},{6,5},{7,4},{8,11},{9,10},{10,... | collective-permute-start | bytes 576008 | tf_op jit(solution)/shard_map/pack/ppermute | solution.py:278
  11.4 1.6 collective-permute-start.1
  14.6 3.4 %collective-permute-done.3 = bf16[4,64,375]{2,1,0:T(8,128)(2,1)S(1)} collective-permute-done((bf16[4,64,375]{2,1,0:T(8,128)(2,1)}, bf16[4,64,375]{2,1,0:T(8,128)(2,1)S(1)}, u32[]{:S(2)}, u32[]{:S(2)}) %collective-permute-start.3) | collective-permute-done | bytes 192032 | tf_op jit(solution)/shard_map/pack/ppermute | solution.py:278
  20.7 14.6 %all_gather.14.full = bf16[272,1536]{1,0:T(8,128)(2,1)S(1)} all-gather(bf16[272,384]{1,0:T(8,128)(2,1)S(1)} %fusion.33), channel_id=1, replica_groups=mesh['ka'=32,'ga'=4] {'ga'}, dimensions={1}, use_global_device_ids=true | all-gather | bytes 1044480 | tf_op jit(solution)/shard_map/exchange_pack/all_gather | solution.py:310
  38.0 3.6 %fusion.54 = (bf16[2,375,375]{2,0,1:T(2,128)(2,1)S(1)}, bf16[2,375,375]{2,0,1:T(2,128)(2,1)S(1)}, bf16[2,375,375]{2,0,1:T(2,128)(2,1)S(1)}, bf16[2,375,375]{2,0,1:T(2,128)(2,1)S(1)}) fusion(bf16[2,375,1500]{2,0,1:T(2,128)(2,1)S(1)} %copy-done.1), kind=kLoop, calls=%fused_computation.156 | loop fusion | bytes 4500000 | tf_op jit(solution)/shard_map/weights/slice | solution.py:292
  41.9 2.4 %broadcast_select_fusion.3 = (bf16[2,384,768]{2,1,0:T(8,128)(2,1)}, bf16[2,384,768]{2,1,0:T(8,128)(2,1)}, bf16[2,384,768]{2,1,0:T(8,128)(2,1)}) fusion(pred[]{:T(512)S(6)} %or.12, bf16[2,375,375]{2,1,0:T(8,128)(2,1)S(1)} %copy.90, bf16[2,375,375]{2,1,0:T(8,128)(2,1)S(1)} %copy.89, bf16[2,375,375]{2,1,0:T(8,128)(2,1)S(1)} %copy.88, ...), kind=kLoop, calls=%fused_computation.39 | loop fusion | flops 10027008 | bytes 5788947 | tf_op jit(solution)/shard_map/weights/jit(_where)/select_n | solution.py:300
  44.3 2.0 %collective-permute-start.4 = (bf16[2,384,768]{2,1,0:T(8,128)(2,1)}, bf16[2,384,768]{2,1,0:T(8,128)(2,1)}, u32[]{:S(2)}, u32[]{:S(2)}) collective-permute-start(bf16[2,384,768]{2,1,0:T(8,128)(2,1)} %get-tuple-element.26), channel_id=1, source_target_pairs={{0,1},{1,2},{2,3},{3,0},{4,5},{5,6},{6,7},{7,4},{8,9},{9,10},{10,1... | collective-permute-start | bytes 3538952 | tf_op jit(solution)/shard_map/weights/ppermute | solution.py:301
  46.3 2.5 %collective-permute-start.5 = (bf16[2,384,768]{2,1,0:T(8,128)(2,1)}, bf16[2,384,768]{2,1,0:T(8,128)(2,1)}, u32[]{:S(2)}, u32[]{:S(2)}) collective-permute-start(bf16[2,384,768]{2,1,0:T(8,128)(2,1)} %get-tuple-element.27), channel_id=1, source_target_pairs={{0,2},{1,3},{2,0},{3,1},{4,6},{5,7},{6,4},{7,5},{8,10},{9,11},{10,... | collective-permute-start | bytes 3538952 | tf_op jit(solution)/shard_map/weights/ppermute | solution.py:301
  50.3 25.7 %all-gather = s32[32,16,3]{1,2,0:T(4,128)S(1)} all-gather(s32[1,16,3]{1,2,0:T(4,128)S(1)} %bitcast.49), channel_id=1, replica_groups=mesh['ka'=32,'ga'=4] {'ka'}, dimensions={0}, use_global_device_ids=true | all-gather | bytes 6336 | tf_op jit(solution)/shard_map/tables/all_gather | solution.py:321
  81.9 14.7 %collective-permute-done.4 = bf16[2,384,768]{2,1,0:T(8,128)(2,1)} collective-permute-done((bf16[2,384,768]{2,1,0:T(8,128)(2,1)}, bf16[2,384,768]{2,1,0:T(8,128)(2,1)}, u32[]{:S(2)}, u32[]{:S(2)}) %collective-permute-start.4) | collective-permute-done | bytes 1179680 | tf_op jit(solution)/shard_map/weights/ppermute | solution.py:301
  97.1 5.1 %pad_maximum_fusion.w = bf16[2,1536,768]{2,1,0:T(8,128)(2,1)} fusion(bf16[2,384,768]{2,1,0:T(8,128)(2,1)S(1)} %collective-permute-done.6, bf16[2,384,768]{2,1,0:T(8,128)(2,1)} %collective-permute-done.5, bf16[2,384,768]{2,1,0:T(8,128)(2,1)} %collective-permute-done.4, bf16[2,384,768]{2,1,0:T(8,128)(2,1)} %get-tuple-element.25), kind=kLoop, calls=%fused_computation | loop fusion | flops 18874368 | bytes 9437184 | tf_op jit(solution)/shard_map/weights/concatenate | solution.py:302
  102.1 13.2 %all-gather.4.cloned.1.call-done.big = bf16[128,128,768]{2,1,0:T(8,128)(2,1)} async-done(((bf16[4,128,768]{2,1,0:T(8,128)(2,1)}), bf16[128,128,768]{2,1,0:T(8,128)(2,1)}) %all-gather.4.cloned.1.call-update) | async-done | bytes 25165840 | tf_op jit(solution)/shard_map/spread/all_gather | solution.py:288
  115.3 2.3 %copy-done = bf16[2,1536,768]{2,1,0:T(8,128)(2,1)S(1)} copy-done((bf16[2,1536,768]{2,1,0:T(8,128)(2,1)S(1)}, bf16[2,1536,768]{2,1,0:T(8,128)(2,1)}, u32[]{:S(2)}) %copy-start) | copy-done | bytes 4718616
  117.7 5.3 %direct.1 = (f32[64,8,128]{2,1,0:T(8,128)S(1)}, f32[64,8,128]{2,1,0:T(8,128)S(1)}) custom-call(s32[4,80]{1,0:T(4,128)S(1)} %pad_add_fusion.1.plan, bf16[128,128,768]{2,1,0:T(8,128)(2,1)} %all-gather.4.cloned.1.call-done.big, bf16[2,1536,768]{2,1,0:T(8,128)(2,1)S(1)} %copy-done), custom_call_target="tpu_custom_call" | custom-call | tf_op jit(solution)/shard_map/direct/pallas_call | solution.py:382
  125.8 5.7 %collective-permute-done.7.came = f32[64,8,128]{2,1,0:T(8,128)S(1)} collective-permute-done((f32[64,8,128]{2,1,0:T(8,128)S(1)}, f32[64,8,128]{2,1,0:T(8,128)S(1)}, u32[]{:S(2)}, u32[]{:S(2)}) %collective-permute-start.7) | collective-permute-done | bytes 262176 | tf_op jit(solution)/shard_map/to_neighbour/ppermute | solution.py:401
  131.5 2.4 %route.1 = f32[32,6,8,128]{3,2,1,0:T(8,128)} custom-call(s32[7,64]{1,0:T(8,128)S(1)} %stack.83.tab, f32[64,8,128]{2,1,0:T(8,128)S(1)} %get-tuple-element.4.keep, f32[64,8,128]{2,1,0:T(8,128)S(1)} %collective-permute-done.7.came), custom_call_target="tpu_custom_call" | custom-call | tf_op jit(solution)/shard_map/route/pallas_call | solution.py:402
  133.8 11.0 %all-to-all-start = ((f32[32,6,8,128]{3,2,1,0:T(8,128)}), f32[32,6,8,128]{3,2,1,0:T(8,128)S(1)}, u32[]{:S(2)}, u32[]{:S(2)}) async-start(f32[32,6,8,128]{3,2,1,0:T(8,128)} %route.1), calls=%async_computation | async-start | bytes 1572864 | tf_op jit(solution)/shard_map/to_holders/all_to_all | solution.py:416
  146.2 17.8 %all-to-all-done.got = f32[32,6,8,128]{3,2,1,0:T(8,128)S(1)} async-done(((f32[32,6,8,128]{3,2,1,0:T(8,128)}), f32[32,6,8,128]{3,2,1,0:T(8,128)S(1)}, u32[]{:S(2)}, u32[]{:S(2)}) %all-to-all-start) | async-done | bytes 786464 | tf_op jit(solution)/shard_map/to_holders/all_to_all | solution.py:416
  164.7 2.8 %collective-permute-start.10 = (f32[20,8,128]{2,1,0:T(8,128)S(1)}, f32[20,8,128]{2,1,0:T(8,128)S(1)}, u32[]{:S(2)}, u32[]{:S(2)}) collective-permute-start(f32[20,8,128]{2,1,0:T(8,128)S(1)} %collect.1.r0), channel_id=1, source_target_pairs={{0,3},{1,0},{2,1},{3,2},{4,7},{5,4},{6,5},{7,6},{8,11},{9,8},{10,9... | collective-permute-start | bytes 245768 | tf_op jit(solution)/shard_map/direct_copies/ppermute | solution.py:428
  167.6 2.3 %collective-permute-start.9 = (f32[20,8,128]{2,1,0:T(8,128)S(1)}, f32[20,8,128]{2,1,0:T(8,128)S(1)}, u32[]{:S(2)}, u32[]{:S(2)}) collective-permute-start(f32[20,8,128]{2,1,0:T(8,128)S(1)} %collect.1.r0), channel_id=1, source_target_pairs={{0,2},{1,3},{2,0},{3,1},{4,6},{5,7},{6,4},{7,5},{8,10},{9,11},{10,... | collective-permute-start | bytes 245768 | tf_op jit(solution)/shard_map/direct_copies/ppermute | solution.py:428
  169.9 2.8 %all-gather.6.cloned.1.call-done.big = bf16[128,16,1536]{2,1,0:T(8,128)(2,1)} async-done(((bf16[4,16,1536]{2,1,0:T(8,128)(2,1)}), bf16[128,16,1536]{2,1,0:T(8,128)(2,1)}) %all-gather.6.cloned.1.call-update) | async-done | bytes 6291472 | tf_op jit(solution)/shard_map/exchange_pack/all_gather | solution.py:313
  172.7 3.7 %exchange.1.r0 = f32[20,8,128]{2,1,0:T(8,128)S(1)} custom-call(s32[3,64]{1,0:T(4,128)S(1)} %add_add_fusion.firsts, s32[4,16]{1,0:T(4,128)S(1)} %pad_add_fusion.own, bf16[128,16,1536]{2,1,0:T(8,128)(2,1)} %all-gather.6.cloned.1.call-done.big, f32[20,8,128]{2,1,0:T(8,128)S(1)} %collective-permute-done.10.r3.early, bf16[272,1536]{1,0:T(8,128)(2,1)S(1)} %all_gather.14.full, ...), custom_call_target="tpu_custom_call" | custom-call | tf_op jit(solution)/shard_map/exchange/pallas_call | solution.py:439
  177.9 2.7 %collective-permute-start.12 = (f32[20,8,128]{2,1,0:T(8,128)S(1)}, f32[20,8,128]{2,1,0:T(8,128)S(1)}, u32[]{:S(2)}, u32[]{:S(2)}) collective-permute-start(f32[20,8,128]{2,1,0:T(8,128)S(1)} %exchange.1.r0), channel_id=1, source_target_pairs={{0,2},{1,3},{2,0},{3,1},{4,6},{5,7},{6,4},{7,5},{8,10},{9,11},{10,... | collective-permute-start | bytes 245768 | tf_op jit(solution)/shard_map/exchange_copies/ppermute | solution.py:457
  185.0 2.4 %finish.1 = (f32[16,4096]{1,0:T(8,128)}, f32[4,4096]{1,0:T(4,128)}) custom-call(s32[4]{0:T(128)S(1)} %pad_add_fusion.2.place, f32[20,64,64]{2,1,0:T(8,128)S(1)} %arrange.1.dmat, f32[20,8,128]{2,1,0:T(8,128)S(1)} %exchange.1.r0, f32[20,8,128]{2,1,0:T(8,128)S(1)} %collective-permute-done.11.r1, f32[20,8,128]{2,1,0:T(8,128)S(1)} %collective-permute-done.12.r2, ...), custom_call_target="tpu_custom_call" | custom-call | tf_op jit(solution)/shard_map/finish/pallas_call | solution.py:458
  (111 shorter events, 25.7 us)
Async XLA Ops:
  7.2 108.2 %all-gather.4.cloned.1.call-start = ((), (), s32[]{:S(2)}) async-start(), calls=%async_computation.1 | async-start | bytes 25952256 | tf_op jit(solution)/shard_map/spread/all_gather | solution.py:288
  7.2 10.8 %collective-permute-start.3 = (bf16[4,64,375]{2,1,0:T(8,128)(2,1)}, bf16[4,64,375]{2,1,0:T(8,128)(2,1)S(1)}, u32[]{:S(2)}, u32[]{:S(2)}) collective-permute-start(bf16[4,64,375]{2,1,0:T(8,128)(2,1)} %param.8), channel_id=1, source_target_pairs={{0,3},{1,2},{2,1},{3,0},{4,7},{5,6},{6,5},{7,4},{8,11},{9,10},{10,... | collective-permute-start | bytes 576008 | tf_op jit(solution)/shard_map/pack/ppermute | solution.py:278
  11.1 8.3 %collective-permute-start = (bf16[4,32,375]{2,1,0:T(8,128)(2,1)S(1)}, bf16[4,32,375]{2,1,0:T(8,128)(2,1)S(1)}, u32[]{:S(2)}, u32[]{:S(2)}) collective-permute-start(bf16[4,32,375]{2,1,0:T(8,128)(2,1)S(1)} %get-tuple-element.39), channel_id=1, source_target_pairs={{0,1},{1,2},{2,3},{3,0},{4,5},{5,6},{6,7},{7,4},{8,9},{9,10},{10,1... | collective-permute-start | bytes 288008 | tf_op jit(solution)/shard_map/pack/ppermute | solution.py:280
  11.4 8.1 %collective-permute-start.1 = (bf16[4,32,375]{2,1,0:T(8,128)(2,1)S(1)}, bf16[4,32,375]{2,1,0:T(8,128)(2,1)S(1)}, u32[]{:S(2)}, u32[]{:S(2)}) collective-permute-start(bf16[4,32,375]{2,1,0:T(8,128)(2,1)S(1)} %get-tuple-element.37), channel_id=1, source_target_pairs={{0,2},{1,3},{2,0},{3,1},{4,6},{5,7},{6,4},{7,5},{8,10},{9,11},{10,... | collective-permute-start | bytes 288008 | tf_op jit(solution)/shard_map/pack/ppermute | solution.py:280
  13.0 6.4 %collective-permute-start.2 = (bf16[4,32,375]{2,1,0:T(8,128)(2,1)S(1)}, bf16[4,32,375]{2,1,0:T(8,128)(2,1)S(1)}, u32[]{:S(2)}, u32[]{:S(2)}) collective-permute-start(bf16[4,32,375]{2,1,0:T(8,128)(2,1)S(1)} %get-tuple-element.38), channel_id=1, source_target_pairs={{0,3},{1,0},{2,1},{3,2},{4,7},{5,4},{6,5},{7,6},{8,11},{9,8},{10,9... | collective-permute-start | bytes 288008 | tf_op jit(solution)/shard_map/pack/ppermute | solution.py:280
  14.6 5.9 %copy-start.4 = (f32[375]{0:T(512)S(1)}, f32[375]{0:T(512)}, u32[]{:S(2)}) copy-start(f32[375]{0:T(512)} %param.10) | copy-start | bytes 4504
  14.6 6.0 %copy-start.2 = (bf16[4,64,375]{2,1,0:T(8,128)(2,1)S(1)}, bf16[4,64,375]{2,1,0:T(8,128)(2,1)}, u32[]{:S(2)}) copy-start(bf16[4,64,375]{2,1,0:T(8,128)(2,1)} %param.9) | copy-start | bytes 576004
  20.5 152.2 %all-gather.6.cloned.1.call-start = ((), (), s32[]{:S(2)}) async-start(), calls=%async_computation.2 | async-start | bytes 6488064 | tf_op jit(solution)/shard_map/exchange_pack/all_gather | solution.py:313
  20.7 17.3 %copy-start.1 = (bf16[2,375,1500]{2,0,1:T(2,128)(2,1)S(1)}, bf16[2,375,1500]{2,0,1:T(2,128)(2,1)}, u32[]{:S(2)}) copy-start(bf16[2,375,1500]{2,0,1:T(2,128)(2,1)} %param.11) | copy-start | bytes 6750004
  44.3 52.3 %collective-permute-start.4 = (bf16[2,384,768]{2,1,0:T(8,128)(2,1)}, bf16[2,384,768]{2,1,0:T(8,128)(2,1)}, u32[]{:S(2)}, u32[]{:S(2)}) collective-permute-start(bf16[2,384,768]{2,1,0:T(8,128)(2,1)} %get-tuple-element.26), channel_id=1, source_target_pairs={{0,1},{1,2},{2,3},{3,0},{4,5},{5,6},{6,7},{7,4},{8,9},{9,10},{10,1... | collective-permute-start | bytes 3538952 | tf_op jit(solution)/shard_map/weights/ppermute | solution.py:301
  46.3 50.3 %collective-permute-start.5 = (bf16[2,384,768]{2,1,0:T(8,128)(2,1)}, bf16[2,384,768]{2,1,0:T(8,128)(2,1)}, u32[]{:S(2)}, u32[]{:S(2)}) collective-permute-start(bf16[2,384,768]{2,1,0:T(8,128)(2,1)} %get-tuple-element.27), channel_id=1, source_target_pairs={{0,2},{1,3},{2,0},{3,1},{4,6},{5,7},{6,4},{7,5},{8,10},{9,11},{10,... | collective-permute-start | bytes 3538952 | tf_op jit(solution)/shard_map/weights/ppermute | solution.py:301
  48.7 1.6 copy-start.3
  48.7 27.4 %copy-start.5 = (s32[64]{0:T(128)S(1)}, s32[64]{0:T(128)}, u32[]{:S(2)}) copy-start(s32[64]{0:T(128)} %param.13) | copy-start | bytes 772
  50.1 46.9 %collective-permute-start.6 = (bf16[2,384,768]{2,1,0:T(8,128)(2,1)}, bf16[2,384,768]{2,1,0:T(8,128)(2,1)S(1)}, u32[]{:S(2)}, u32[]{:S(2)}) collective-permute-start(bf16[2,384,768]{2,1,0:T(8,128)(2,1)} %broadcast_select_fusion), channel_id=1, source_target_pairs={{0,3},{1,0},{2,1},{3,2},{4,7},{5,4},{6,5},{7,6},{8,11},{9,8},{10,9... | collective-permute-start | bytes 3538952 | tf_op jit(solution)/shard_map/weights/ppermute | solution.py:301
  115.3 2.3 %copy-start = (bf16[2,1536,768]{2,1,0:T(8,128)(2,1)S(1)}, bf16[2,1536,768]{2,1,0:T(8,128)(2,1)}, u32[]{:S(2)}) copy-start(bf16[2,1536,768]{2,1,0:T(8,128)(2,1)} %pad_maximum_fusion.w) | copy-start | bytes 14155780
  123.0 8.4 %collective-permute-start.7 = (f32[64,8,128]{2,1,0:T(8,128)S(1)}, f32[64,8,128]{2,1,0:T(8,128)S(1)}, u32[]{:S(2)}, u32[]{:S(2)}) collective-permute-start(f32[64,8,128]{2,1,0:T(8,128)S(1)} %get-tuple-element.5), channel_id=1, source_target_pairs={{0,1},{1,0},{2,3},{3,2},{4,5},{5,4},{6,7},{7,6},{8,9},{9,8},{10,11... | collective-permute-start | bytes 786440 | tf_op jit(solution)/shard_map/to_neighbour/ppermute | solution.py:401
  133.8 30.2 %all-to-all-start = ((f32[32,6,8,128]{3,2,1,0:T(8,128)}), f32[32,6,8,128]{3,2,1,0:T(8,128)S(1)}, u32[]{:S(2)}, u32[]{:S(2)}) async-start(f32[32,6,8,128]{3,2,1,0:T(8,128)} %route.1), calls=%async_computation | async-start | bytes 1572864 | tf_op jit(solution)/shard_map/to_holders/all_to_all | solution.py:416
  164.7 8.0 %collective-permute-start.10 = (f32[20,8,128]{2,1,0:T(8,128)S(1)}, f32[20,8,128]{2,1,0:T(8,128)S(1)}, u32[]{:S(2)}, u32[]{:S(2)}) collective-permute-start(f32[20,8,128]{2,1,0:T(8,128)S(1)} %collect.1.r0), channel_id=1, source_target_pairs={{0,3},{1,0},{2,1},{3,2},{4,7},{5,4},{6,5},{7,6},{8,11},{9,8},{10,9... | collective-permute-start | bytes 245768 | tf_op jit(solution)/shard_map/direct_copies/ppermute | solution.py:428
  167.5 14.6 %collective-permute-start.8 = (f32[20,8,128]{2,1,0:T(8,128)S(1)}, f32[20,8,128]{2,1,0:T(8,128)S(1)}, u32[]{:S(2)}, u32[]{:S(2)}) collective-permute-start(f32[20,8,128]{2,1,0:T(8,128)S(1)} %collect.1.r0), channel_id=1, source_target_pairs={{0,1},{1,2},{2,3},{3,0},{4,5},{5,6},{6,7},{7,4},{8,9},{9,10},{10,1... | collective-permute-start | bytes 245768 | tf_op jit(solution)/shard_map/direct_copies/ppermute | solution.py:428
  167.6 14.5 %collective-permute-start.9 = (f32[20,8,128]{2,1,0:T(8,128)S(1)}, f32[20,8,128]{2,1,0:T(8,128)S(1)}, u32[]{:S(2)}, u32[]{:S(2)}) collective-permute-start(f32[20,8,128]{2,1,0:T(8,128)S(1)} %collect.1.r0), channel_id=1, source_target_pairs={{0,2},{1,3},{2,0},{3,1},{4,6},{5,7},{6,4},{7,5},{8,10},{9,11},{10,... | collective-permute-start | bytes 245768 | tf_op jit(solution)/shard_map/direct_copies/ppermute | solution.py:428
  176.4 7.1 %collective-permute-start.11 = (f32[20,8,128]{2,1,0:T(8,128)S(1)}, f32[20,8,128]{2,1,0:T(8,128)S(1)}, u32[]{:S(2)}, u32[]{:S(2)}) collective-permute-start(f32[20,8,128]{2,1,0:T(8,128)S(1)} %exchange.1.r0), channel_id=1, source_target_pairs={{0,1},{1,2},{2,3},{3,0},{4,5},{5,6},{6,7},{7,4},{8,9},{9,10},{10,1... | collective-permute-start | bytes 245768 | tf_op jit(solution)/shard_map/exchange_copies/ppermute | solution.py:457
  177.9 7.0 %collective-permute-start.12 = (f32[20,8,128]{2,1,0:T(8,128)S(1)}, f32[20,8,128]{2,1,0:T(8,128)S(1)}, u32[]{:S(2)}, u32[]{:S(2)}) collective-permute-start(f32[20,8,128]{2,1,0:T(8,128)S(1)} %exchange.1.r0), channel_id=1, source_target_pairs={{0,2},{1,3},{2,0},{3,1},{4,6},{5,7},{6,4},{7,5},{8,10},{9,11},{10,... | collective-permute-start | bytes 245768 | tf_op jit(solution)/shard_map/exchange_copies/ppermute | solution.py:457
  180.6 4.4 %collective-permute-start.13 = (f32[20,8,128]{2,1,0:T(8,128)S(1)}, f32[20,8,128]{2,1,0:T(8,128)S(1)}, u32[]{:S(2)}, u32[]{:S(2)}) collective-permute-start(f32[20,8,128]{2,1,0:T(8,128)S(1)} %exchange.1.r0), channel_id=1, source_target_pairs={{0,3},{1,0},{2,1},{3,2},{4,7},{5,4},{6,5},{7,6},{8,11},{9,8},{10,9... | collective-permute-start | bytes 245768 | tf_op jit(solution)/shard_map/exchange_copies/ppermute | solution.py:457
Sparse Core Ops, SparseCore 0:
  20.6 94.6 all-gather.3
  118.2 54.4 all-gather.5

commit v12 on v11

--- a/solution.py
+++ b/solution.py
@@ -146,14 +146,14 @@
     def first(t):
         return pltpu.make_async_copy(big.at[firsts[0, t]], p1.at[t], s1.at[t])
 
+    for j in range(npair):
+        second(j).start()
 
     def begin(t, carry):
         first(t).start()
         return carry
 
     lax.fori_loop(0, count, begin, 0)
-    for j in range(npair):
-        second(j).start()
     tot[...] = jnp.zeros_like(tot)
     def gather(t, carry):
         first(t).wait()

time: 195 us -> 196 us (level)
  transfers between devices with their start and end apart: 17 -> 17, of which waited for: 10 -> 10; matrix products, arithmetic and copies ran while one was open for 12% -> 13% of each run, Pallas kernels for 7% -> 7%
where the time goes in v12:
time: 196 us; the launch traced here: 194 us
  waiting for transfers between devices  59.8 us (31%)
  blocking collectives  40.3 us (21%)
  starting transfers between devices  34.4 us (18%)
  Pallas kernels  16.1 us (8%)
  between operations  15.9 us (8%)
  other arithmetic  15.6 us (8%)
  local copies, waits for them, and re-layouts  12.1 us (6%)
    all_gather x1, blocking collectives, per_device(): lax.all_gather(pairs, 'ka', axis=0, tiled=True).reshape(n_ka, npair, 3)  25.7 us
    all_to_all x1, waiting for transfers between devices, per_device(): got = lax.all_to_all(send, 'ka', 0, 0, tiled=True)  17.5 us
    ppermute x3, waiting for transfers between devices, per_device(): wk.append(lax.ppermute(v, 'ga', shift(r)) if r else v)  15.2 us
    all_gather x1, blocking collectives, per_device(): full = lax.all_gather(widen(held), 'ga', axis=1, tiled=True)  14.6 us
    all_gather x1, waiting for transfers between devices, per_device(): big = lax.all_gather(payload, 'ka', axis=0, tiled=True)  13.2 us
    all_to_all x1, starting transfers between devices, per_device(): got = lax.all_to_all(send, 'ka', 0, 0, tiled=True)  11 us
    ppermute x3, starting transfers between devices, per_device(): exch_others = [lax.ppermute(exch, 'ga', shift(r)) for r in range(1, 4)]  5.66 us
    pallas_call x1, Pallas kernels, per_device(): pl.pallas_call(direct_kernel, out_shape=(jax.ShapeDtypeStruct((nslot, 8,...  5.53 us
  transfers between devices with their start and end apart: 17, of which 10 were waited for; matrix products, arithmetic and copies ran while one was open for 13% of the time, Pallas kernels for 7%

profile of v12, /device:TPU:0, one launch (start us, length us, event | category | flops | bytes accessed | tf_op | source)
XLA Modules:
  0.0 194.1 jit_solution(15753706165668613158)
XLA Ops:
  7.2 2.9 %collective-permute-start.3 = (bf16[4,64,375]{2,1,0:T(8,128)(2,1)}, bf16[4,64,375]{2,1,0:T(8,128)(2,1)S(1)}, u32[]{:S(2)}, u32[]{:S(2)}) collective-permute-start(bf16[4,64,375]{2,1,0:T(8,128)(2,1)} %param.8), channel_id=1, source_target_pairs={{0,3},{1,2},{2,1},{3,0},{4,7},{5,6},{6,5},{7,4},{8,11},{9,10},{10,... | collective-permute-start | bytes 576008 | tf_op jit(solution)/shard_map/pack/ppermute | solution.py:278
  11.4 1.6 collective-permute-start.1
  14.6 3.4 %collective-permute-done.3 = bf16[4,64,375]{2,1,0:T(8,128)(2,1)S(1)} collective-permute-done((bf16[4,64,375]{2,1,0:T(8,128)(2,1)}, bf16[4,64,375]{2,1,0:T(8,128)(2,1)S(1)}, u32[]{:S(2)}, u32[]{:S(2)}) %collective-permute-start.3) | collective-permute-done | bytes 192032 | tf_op jit(solution)/shard_map/pack/ppermute | solution.py:278
  20.7 14.6 %all_gather.14.full = bf16[272,1536]{1,0:T(8,128)(2,1)S(1)} all-gather(bf16[272,384]{1,0:T(8,128)(2,1)S(1)} %fusion.33), channel_id=1, replica_groups=mesh['ka'=32,'ga'=4] {'ga'}, dimensions={1}, use_global_device_ids=true | all-gather | bytes 1044480 | tf_op jit(solution)/shard_map/exchange_pack/all_gather | solution.py:310
  38.0 3.6 %fusion.54 = (bf16[2,375,375]{2,0,1:T(2,128)(2,1)S(1)}, bf16[2,375,375]{2,0,1:T(2,128)(2,1)S(1)}, bf16[2,375,375]{2,0,1:T(2,128)(2,1)S(1)}, bf16[2,375,375]{2,0,1:T(2,128)(2,1)S(1)}) fusion(bf16[2,375,1500]{2,0,1:T(2,128)(2,1)S(1)} %copy-done.1), kind=kLoop, calls=%fused_computation.156 | loop fusion | bytes 4500000 | tf_op jit(solution)/shard_map/weights/slice | solution.py:292
  41.9 2.4 %broadcast_select_fusion.3 = (bf16[2,384,768]{2,1,0:T(8,128)(2,1)}, bf16[2,384,768]{2,1,0:T(8,128)(2,1)}, bf16[2,384,768]{2,1,0:T(8,128)(2,1)}) fusion(pred[]{:T(512)S(6)} %or.12, bf16[2,375,375]{2,1,0:T(8,128)(2,1)S(1)} %copy.90, bf16[2,375,375]{2,1,0:T(8,128)(2,1)S(1)} %copy.89, bf16[2,375,375]{2,1,0:T(8,128)(2,1)S(1)} %copy.88, ...), kind=kLoop, calls=%fused_computation.39 | loop fusion | flops 10027008 | bytes 5788947 | tf_op jit(solution)/shard_map/weights/jit(_where)/select_n | solution.py:300
  44.3 2.0 %collective-permute-start.4 = (bf16[2,384,768]{2,1,0:T(8,128)(2,1)}, bf16[2,384,768]{2,1,0:T(8,128)(2,1)}, u32[]{:S(2)}, u32[]{:S(2)}) collective-permute-start(bf16[2,384,768]{2,1,0:T(8,128)(2,1)} %get-tuple-element.26), channel_id=1, source_target_pairs={{0,1},{1,2},{2,3},{3,0},{4,5},{5,6},{6,7},{7,4},{8,9},{9,10},{10,1... | collective-permute-start | bytes 3538952 | tf_op jit(solution)/shard_map/weights/ppermute | solution.py:301
  46.3 2.5 %collective-permute-start.5 = (bf16[2,384,768]{2,1,0:T(8,128)(2,1)}, bf16[2,384,768]{2,1,0:T(8,128)(2,1)}, u32[]{:S(2)}, u32[]{:S(2)}) collective-permute-start(bf16[2,384,768]{2,1,0:T(8,128)(2,1)} %get-tuple-element.27), channel_id=1, source_target_pairs={{0,2},{1,3},{2,0},{3,1},{4,6},{5,7},{6,4},{7,5},{8,10},{9,11},{10,... | collective-permute-start | bytes 3538952 | tf_op jit(solution)/shard_map/weights/ppermute | solution.py:301
  50.3 25.7 %all-gather = s32[32,16,3]{1,2,0:T(4,128)S(1)} all-gather(s32[1,16,3]{1,2,0:T(4,128)S(1)} %bitcast.49), channel_id=1, replica_groups=mesh['ka'=32,'ga'=4] {'ka'}, dimensions={0}, use_global_device_ids=true | all-gather | bytes 6336 | tf_op jit(solution)/shard_map/tables/all_gather | solution.py:321
  81.9 14.7 %collective-permute-done.4 = bf16[2,384,768]{2,1,0:T(8,128)(2,1)} collective-permute-done((bf16[2,384,768]{2,1,0:T(8,128)(2,1)}, bf16[2,384,768]{2,1,0:T(8,128)(2,1)}, u32[]{:S(2)}, u32[]{:S(2)}) %collective-permute-start.4) | collective-permute-done | bytes 1179680 | tf_op jit(solution)/shard_map/weights/ppermute | solution.py:301
  97.1 5.1 %pad_maximum_fusion.w = bf16[2,1536,768]{2,1,0:T(8,128)(2,1)} fusion(bf16[2,384,768]{2,1,0:T(8,128)(2,1)S(1)} %collective-permute-done.6, bf16[2,384,768]{2,1,0:T(8,128)(2,1)} %collective-permute-done.5, bf16[2,384,768]{2,1,0:T(8,128)(2,1)} %collective-permute-done.4, bf16[2,384,768]{2,1,0:T(8,128)(2,1)} %get-tuple-element.25), kind=kLoop, calls=%fused_computation | loop fusion | flops 18874368 | bytes 9437184 | tf_op jit(solution)/shard_map/weights/concatenate | solution.py:302
  102.1 13.2 %all-gather.4.cloned.1.call-done.big = bf16[128,128,768]{2,1,0:T(8,128)(2,1)} async-done(((bf16[4,128,768]{2,1,0:T(8,128)(2,1)}), bf16[128,128,768]{2,1,0:T(8,128)(2,1)}) %all-gather.4.cloned.1.call-update) | async-done | bytes 25165840 | tf_op jit(solution)/shard_map/spread/all_gather | solution.py:288
  115.3 2.3 %copy-done = bf16[2,1536,768]{2,1,0:T(8,128)(2,1)S(1)} copy-done((bf16[2,1536,768]{2,1,0:T(8,128)(2,1)S(1)}, bf16[2,1536,768]{2,1,0:T(8,128)(2,1)}, u32[]{:S(2)}) %copy-start) | copy-done | bytes 4718616
  117.7 5.5 %direct.1 = (f32[64,8,128]{2,1,0:T(8,128)S(1)}, f32[64,8,128]{2,1,0:T(8,128)S(1)}) custom-call(s32[4,80]{1,0:T(4,128)S(1)} %pad_add_fusion.1.plan, bf16[128,128,768]{2,1,0:T(8,128)(2,1)} %all-gather.4.cloned.1.call-done.big, bf16[2,1536,768]{2,1,0:T(8,128)(2,1)S(1)} %copy-done), custom_call_target="tpu_custom_call" | custom-call | tf_op jit(solution)/shard_map/direct/pallas_call | solution.py:382
  125.9 5.2 %collective-permute-done.7.came = f32[64,8,128]{2,1,0:T(8,128)S(1)} collective-permute-done((f32[64,8,128]{2,1,0:T(8,128)S(1)}, f32[64,8,128]{2,1,0:T(8,128)S(1)}, u32[]{:S(2)}, u32[]{:S(2)}) %collective-permute-start.7) | collective-permute-done | bytes 262176 | tf_op jit(solution)/shard_map/to_neighbour/ppermute | solution.py:401
  131.1 2.3 %route.1 = f32[32,6,8,128]{3,2,1,0:T(8,128)} custom-call(s32[7,64]{1,0:T(8,128)S(1)} %stack.83.tab, f32[64,8,128]{2,1,0:T(8,128)S(1)} %get-tuple-element.4.keep, f32[64,8,128]{2,1,0:T(8,128)S(1)} %collective-permute-done.7.came), custom_call_target="tpu_custom_call" | custom-call | tf_op jit(solution)/shard_map/route/pallas_call | solution.py:402
  133.5 11.0 %all-to-all-start = ((f32[32,6,8,128]{3,2,1,0:T(8,128)}), f32[32,6,8,128]{3,2,1,0:T(8,128)S(1)}, u32[]{:S(2)}, u32[]{:S(2)}) async-start(f32[32,6,8,128]{3,2,1,0:T(8,128)} %route.1), calls=%async_computation | async-start | bytes 1572864 | tf_op jit(solution)/shard_map/to_holders/all_to_all | solution.py:416
  145.8 17.5 %all-to-all-done.got = f32[32,6,8,128]{3,2,1,0:T(8,128)S(1)} async-done(((f32[32,6,8,128]{3,2,1,0:T(8,128)}), f32[32,6,8,128]{3,2,1,0:T(8,128)S(1)}, u32[]{:S(2)}, u32[]{:S(2)}) %all-to-all-start) | async-done | bytes 786464 | tf_op jit(solution)/shard_map/to_holders/all_to_all | solution.py:416
  164.0 2.7 %collective-permute-start.10 = (f32[20,8,128]{2,1,0:T(8,128)S(1)}, f32[20,8,128]{2,1,0:T(8,128)S(1)}, u32[]{:S(2)}, u32[]{:S(2)}) collective-permute-start(f32[20,8,128]{2,1,0:T(8,128)S(1)} %collect.1.r0), channel_id=1, source_target_pairs={{0,3},{1,0},{2,1},{3,2},{4,7},{5,4},{6,5},{7,6},{8,11},{9,8},{10,9... | collective-permute-start | bytes 245768 | tf_op jit(solution)/shard_map/direct_copies/ppermute | solution.py:428
  166.9 2.3 %collective-permute-start.9 = (f32[20,8,128]{2,1,0:T(8,128)S(1)}, f32[20,8,128]{2,1,0:T(8,128)S(1)}, u32[]{:S(2)}, u32[]{:S(2)}) collective-permute-start(f32[20,8,128]{2,1,0:T(8,128)S(1)} %collect.1.r0), channel_id=1, source_target_pairs={{0,2},{1,3},{2,0},{3,1},{4,6},{5,7},{6,4},{7,5},{8,10},{9,11},{10,... | collective-permute-start | bytes 245768 | tf_op jit(solution)/shard_map/direct_copies/ppermute | solution.py:428
  169.2 3.1 %all-gather.6.cloned.1.call-done.big = bf16[128,16,1536]{2,1,0:T(8,128)(2,1)} async-done(((bf16[4,16,1536]{2,1,0:T(8,128)(2,1)}), bf16[128,16,1536]{2,1,0:T(8,128)(2,1)}) %all-gather.6.cloned.1.call-update) | async-done | bytes 6291472 | tf_op jit(solution)/shard_map/exchange_pack/all_gather | solution.py:313
  172.3 3.9 %exchange.1.r0 = f32[20,8,128]{2,1,0:T(8,128)S(1)} custom-call(s32[3,64]{1,0:T(4,128)S(1)} %add_add_fusion.firsts, s32[4,16]{1,0:T(4,128)S(1)} %pad_add_fusion.own, bf16[128,16,1536]{2,1,0:T(8,128)(2,1)} %all-gather.6.cloned.1.call-done.big, f32[20,8,128]{2,1,0:T(8,128)S(1)} %collective-permute-done.10.r3.early, bf16[272,1536]{1,0:T(8,128)(2,1)S(1)} %all_gather.14.full, ...), custom_call_target="tpu_custom_call" | custom-call | tf_op jit(solution)/shard_map/exchange/pallas_call | solution.py:439
  177.7 2.7 %collective-permute-start.12 = (f32[20,8,128]{2,1,0:T(8,128)S(1)}, f32[20,8,128]{2,1,0:T(8,128)S(1)}, u32[]{:S(2)}, u32[]{:S(2)}) collective-permute-start(f32[20,8,128]{2,1,0:T(8,128)S(1)} %exchange.1.r0), channel_id=1, source_target_pairs={{0,2},{1,3},{2,0},{3,1},{4,6},{5,7},{6,4},{7,5},{8,10},{9,11},{10,... | collective-permute-start | bytes 245768 | tf_op jit(solution)/shard_map/exchange_copies/ppermute | solution.py:457
  184.9 2.4 %finish.1 = (f32[16,4096]{1,0:T(8,128)}, f32[4,4096]{1,0:T(4,128)}) custom-call(s32[4]{0:T(128)S(1)} %pad_add_fusion.2.place, f32[20,64,64]{2,1,0:T(8,128)S(1)} %arrange.1.dmat, f32[20,8,128]{2,1,0:T(8,128)S(1)} %exchange.1.r0, f32[20,8,128]{2,1,0:T(8,128)S(1)} %collective-permute-done.11.r1, f32[20,8,128]{2,1,0:T(8,128)S(1)} %collective-permute-done.12.r2, ...), custom_call_target="tpu_custom_call" | custom-call | tf_op jit(solution)/shard_map/finish/pallas_call | solution.py:458
  (111 shorter events, 25.7 us)
Async XLA Ops:
  7.2 108.2 %all-gather.4.cloned.1.call-start = ((), (), s32[]{:S(2)}) async-start(), calls=%async_computation.1 | async-start | bytes 25952256 | tf_op jit(solution)/shard_map/spread/all_gather | solution.py:288
  7.2 10.8 %collective-permute-start.3 = (bf16[4,64,375]{2,1,0:T(8,128)(2,1)}, bf16[4,64,375]{2,1,0:T(8,128)(2,1)S(1)}, u32[]{:S(2)}, u32[]{:S(2)}) collective-permute-start(bf16[4,64,375]{2,1,0:T(8,128)(2,1)} %param.8), channel_id=1, source_target_pairs={{0,3},{1,2},{2,1},{3,0},{4,7},{5,6},{6,5},{7,4},{8,11},{9,10},{10,... | collective-permute-start | bytes 576008 | tf_op jit(solution)/shard_map/pack/ppermute | solution.py:278
  11.1 8.3 %collective-permute-start = (bf16[4,32,375]{2,1,0:T(8,128)(2,1)S(1)}, bf16[4,32,375]{2,1,0:T(8,128)(2,1)S(1)}, u32[]{:S(2)}, u32[]{:S(2)}) collective-permute-start(bf16[4,32,375]{2,1,0:T(8,128)(2,1)S(1)} %get-tuple-element.39), channel_id=1, source_target_pairs={{0,1},{1,2},{2,3},{3,0},{4,5},{5,6},{6,7},{7,4},{8,9},{9,10},{10,1... | collective-permute-start | bytes 288008 | tf_op jit(solution)/shard_map/pack/ppermute | solution.py:280
  11.4 8.1 %collective-permute-start.1 = (bf16[4,32,375]{2,1,0:T(8,128)(2,1)S(1)}, bf16[4,32,375]{2,1,0:T(8,128)(2,1)S(1)}, u32[]{:S(2)}, u32[]{:S(2)}) collective-permute-start(bf16[4,32,375]{2,1,0:T(8,128)(2,1)S(1)} %get-tuple-element.37), channel_id=1, source_target_pairs={{0,2},{1,3},{2,0},{3,1},{4,6},{5,7},{6,4},{7,5},{8,10},{9,11},{10,... | collective-permute-start | bytes 288008 | tf_op jit(solution)/shard_map/pack/ppermute | solution.py:280
  13.0 6.4 %collective-permute-start.2 = (bf16[4,32,375]{2,1,0:T(8,128)(2,1)S(1)}, bf16[4,32,375]{2,1,0:T(8,128)(2,1)S(1)}, u32[]{:S(2)}, u32[]{:S(2)}) collective-permute-start(bf16[4,32,375]{2,1,0:T(8,128)(2,1)S(1)} %get-tuple-element.38), channel_id=1, source_target_pairs={{0,3},{1,0},{2,1},{3,2},{4,7},{5,4},{6,5},{7,6},{8,11},{9,8},{10,9... | collective-permute-start | bytes 288008 | tf_op jit(solution)/shard_map/pack/ppermute | solution.py:280
  14.6 5.9 %copy-start.4 = (f32[375]{0:T(512)S(1)}, f32[375]{0:T(512)}, u32[]{:S(2)}) copy-start(f32[375]{0:T(512)} %param.10) | copy-start | bytes 4504
  14.6 6.0 %copy-start.2 = (bf16[4,64,375]{2,1,0:T(8,128)(2,1)S(1)}, bf16[4,64,375]{2,1,0:T(8,128)(2,1)}, u32[]{:S(2)}) copy-start(bf16[4,64,375]{2,1,0:T(8,128)(2,1)} %param.9) | copy-start | bytes 576004
  20.5 151.8 %all-gather.6.cloned.1.call-start = ((), (), s32[]{:S(2)}) async-start(), calls=%async_computation.2 | async-start | bytes 6488064 | tf_op jit(solution)/shard_map/exchange_pack/all_gather | solution.py:313
  20.7 17.3 %copy-start.1 = (bf16[2,375,1500]{2,0,1:T(2,128)(2,1)S(1)}, bf16[2,375,1500]{2,0,1:T(2,128)(2,1)}, u32[]{:S(2)}) copy-start(bf16[2,375,1500]{2,0,1:T(2,128)(2,1)} %param.11) | copy-start | bytes 6750004
  44.3 52.3 %collective-permute-start.4 = (bf16[2,384,768]{2,1,0:T(8,128)(2,1)}, bf16[2,384,768]{2,1,0:T(8,128)(2,1)}, u32[]{:S(2)}, u32[]{:S(2)}) collective-permute-start(bf16[2,384,768]{2,1,0:T(8,128)(2,1)} %get-tuple-element.26), channel_id=1, source_target_pairs={{0,1},{1,2},{2,3},{3,0},{4,5},{5,6},{6,7},{7,4},{8,9},{9,10},{10,1... | collective-permute-start | bytes 3538952 | tf_op jit(solution)/shard_map/weights/ppermute | solution.py:301
  46.3 50.3 %collective-permute-start.5 = (bf16[2,384,768]{2,1,0:T(8,128)(2,1)}, bf16[2,384,768]{2,1,0:T(8,128)(2,1)}, u32[]{:S(2)}, u32[]{:S(2)}) collective-permute-start(bf16[2,384,768]{2,1,0:T(8,128)(2,1)} %get-tuple-element.27), channel_id=1, source_target_pairs={{0,2},{1,3},{2,0},{3,1},{4,6},{5,7},{6,4},{7,5},{8,10},{9,11},{10,... | collective-permute-start | bytes 3538952 | tf_op jit(solution)/shard_map/weights/ppermute | solution.py:301
  48.7 1.6 copy-start.3
  48.7 27.4 %copy-start.5 = (s32[64]{0:T(128)S(1)}, s32[64]{0:T(128)}, u32[]{:S(2)}) copy-start(s32[64]{0:T(128)} %param.13) | copy-start | bytes 772
  50.1 46.9 %collective-permute-start.6 = (bf16[2,384,768]{2,1,0:T(8,128)(2,1)}, bf16[2,384,768]{2,1,0:T(8,128)(2,1)S(1)}, u32[]{:S(2)}, u32[]{:S(2)}) collective-permute-start(bf16[2,384,768]{2,1,0:T(8,128)(2,1)} %broadcast_select_fusion), channel_id=1, source_target_pairs={{0,3},{1,0},{2,1},{3,2},{4,7},{5,4},{6,5},{7,6},{8,11},{9,8},{10,9... | collective-permute-start | bytes 3538952 | tf_op jit(solution)/shard_map/weights/ppermute | solution.py:301
  115.3 2.3 %copy-start = (bf16[2,1536,768]{2,1,0:T(8,128)(2,1)S(1)}, bf16[2,1536,768]{2,1,0:T(8,128)(2,1)}, u32[]{:S(2)}) copy-start(bf16[2,1536,768]{2,1,0:T(8,128)(2,1)} %pad_maximum_fusion.w) | copy-start | bytes 14155780
  123.2 7.9 %collective-permute-start.7 = (f32[64,8,128]{2,1,0:T(8,128)S(1)}, f32[64,8,128]{2,1,0:T(8,128)S(1)}, u32[]{:S(2)}, u32[]{:S(2)}) collective-permute-start(f32[64,8,128]{2,1,0:T(8,128)S(1)} %get-tuple-element.5), channel_id=1, source_target_pairs={{0,1},{1,0},{2,3},{3,2},{4,5},{5,4},{6,7},{7,6},{8,9},{9,8},{10,11... | collective-permute-start | bytes 786440 | tf_op jit(solution)/shard_map/to_neighbour/ppermute | solution.py:401
  133.5 29.9 %all-to-all-start = ((f32[32,6,8,128]{3,2,1,0:T(8,128)}), f32[32,6,8,128]{3,2,1,0:T(8,128)S(1)}, u32[]{:S(2)}, u32[]{:S(2)}) async-start(f32[32,6,8,128]{3,2,1,0:T(8,128)} %route.1), calls=%async_computation | async-start | bytes 1572864 | tf_op jit(solution)/shard_map/to_holders/all_to_all | solution.py:416
  164.0 8.3 %collective-permute-start.10 = (f32[20,8,128]{2,1,0:T(8,128)S(1)}, f32[20,8,128]{2,1,0:T(8,128)S(1)}, u32[]{:S(2)}, u32[]{:S(2)}) collective-permute-start(f32[20,8,128]{2,1,0:T(8,128)S(1)} %collect.1.r0), channel_id=1, source_target_pairs={{0,3},{1,0},{2,1},{3,2},{4,7},{5,4},{6,5},{7,6},{8,11},{9,8},{10,9... | collective-permute-start | bytes 245768 | tf_op jit(solution)/shard_map/direct_copies/ppermute | solution.py:428
  166.8 15.1 %collective-permute-start.8 = (f32[20,8,128]{2,1,0:T(8,128)S(1)}, f32[20,8,128]{2,1,0:T(8,128)S(1)}, u32[]{:S(2)}, u32[]{:S(2)}) collective-permute-start(f32[20,8,128]{2,1,0:T(8,128)S(1)} %collect.1.r0), channel_id=1, source_target_pairs={{0,1},{1,2},{2,3},{3,0},{4,5},{5,6},{6,7},{7,4},{8,9},{9,10},{10,1... | collective-permute-start | bytes 245768 | tf_op jit(solution)/shard_map/direct_copies/ppermute | solution.py:428
  166.9 15.0 %collective-permute-start.9 = (f32[20,8,128]{2,1,0:T(8,128)S(1)}, f32[20,8,128]{2,1,0:T(8,128)S(1)}, u32[]{:S(2)}, u32[]{:S(2)}) collective-permute-start(f32[20,8,128]{2,1,0:T(8,128)S(1)} %collect.1.r0), channel_id=1, source_target_pairs={{0,2},{1,3},{2,0},{3,1},{4,6},{5,7},{6,4},{7,5},{8,10},{9,11},{10,... | collective-permute-start | bytes 245768 | tf_op jit(solution)/shard_map/direct_copies/ppermute | solution.py:428
  176.2 7.1 %collective-permute-start.11 = (f32[20,8,128]{2,1,0:T(8,128)S(1)}, f32[20,8,128]{2,1,0:T(8,128)S(1)}, u32[]{:S(2)}, u32[]{:S(2)}) collective-permute-start(f32[20,8,128]{2,1,0:T(8,128)S(1)} %exchange.1.r0), channel_id=1, source_target_pairs={{0,1},{1,2},{2,3},{3,0},{4,5},{5,6},{6,7},{7,4},{8,9},{9,10},{10,1... | collective-permute-start | bytes 245768 | tf_op jit(solution)/shard_map/exchange_copies/ppermute | solution.py:457
  177.7 7.0 %collective-permute-start.12 = (f32[20,8,128]{2,1,0:T(8,128)S(1)}, f32[20,8,128]{2,1,0:T(8,128)S(1)}, u32[]{:S(2)}, u32[]{:S(2)}) collective-permute-start(f32[20,8,128]{2,1,0:T(8,128)S(1)} %exchange.1.r0), channel_id=1, source_target_pairs={{0,2},{1,3},{2,0},{3,1},{4,6},{5,7},{6,4},{7,5},{8,10},{9,11},{10,... | collective-permute-start | bytes 245768 | tf_op jit(solution)/shard_map/exchange_copies/ppermute | solution.py:457
  180.4 4.4 %collective-permute-start.13 = (f32[20,8,128]{2,1,0:T(8,128)S(1)}, f32[20,8,128]{2,1,0:T(8,128)S(1)}, u32[]{:S(2)}, u32[]{:S(2)}) collective-permute-start(f32[20,8,128]{2,1,0:T(8,128)S(1)} %exchange.1.r0), channel_id=1, source_target_pairs={{0,3},{1,0},{2,1},{3,2},{4,7},{5,4},{6,5},{7,6},{8,11},{9,8},{10,9... | collective-permute-start | bytes 245768 | tf_op jit(solution)/shard_map/exchange_copies/ppermute | solution.py:457
Sparse Core Ops, SparseCore 0:
  20.6 94.6 all-gather.3
  118.2 54.0 all-gather.5

commit v13 on v12

--- a/solution.py
+++ b/solution.py
@@ -227,17 +227,17 @@
                 )
 
 
-def finish_kernel(place, dmat, r0, r1, r2, r3, blocks, mirrored, whole, emat, bmat, rows, sem):
-    bring(place, (r0, r1, r2, r3), whole, sem)
+def finish_kernel(place, dmat, r0, r1, r2, r3, blocks, mirrored, emat, bmat, rows):
     npair, nk = blocks.shape[0], mirrored.shape[0]
     nt = dmat.shape[1]
     half = nt // 2
     n = npair + nk
-    for j in range(n):
-        for a in range(4):
-            tile = whole[a, j]
-            emat[j, pl.ds(16 * a, 8, stride=2), :] = tile[:, :nt]
-            emat[j, pl.ds(16 * a + 1, 8, stride=2), :] = tile[:, nt:]
+    for i, r in enumerate((r0, r1, r2, r3)):
+        top = pl.multiple_of(16 * place[i], 16)
+        for j in range(n):
+            tile = r[j]
+            emat[j, pl.ds(top, 8, stride=2), :] = tile[:, :nt]
+            emat[j, pl.ds(top + 1, 8, stride=2), :] = tile[:, nt:]
     for j in range(n):
         if j < npair:
             bmat[j] = emat[j].T - dmat[j]
@@ -461,14 +461,12 @@
             jax.ShapeDtypeStruct((npair, nt * nt), F32),
             jax.ShapeDtypeStruct((nk, nt * nt), F32),
         ),
-        in_specs=[SMEM, *in_vmem(2), ANY, ANY, ANY],
+        in_specs=[SMEM, *in_vmem(5)],
         out_specs=tuple(in_vmem(2)),
         scratch_shapes=[
-            pltpu.VMEM((4, n, 8, 128), F32),
             pltpu.VMEM((n, nt, nt), F32),
             pltpu.VMEM((n, nt, nt), F32),
             pltpu.VMEM((n * half, 2 * nt), F32),
-            pltpu.SemaphoreType.DMA((4,)),
         ],
         compiler_params=pltpu.CompilerParams(vmem_limit_bytes=16 * 1024 * 1024),
         name="finish",

time: 196 us -> 196 us (level)
  Pallas kernels: 16.1 us -> 23.2 us
  starting transfers between devices: 34.4 us -> 29.2 us
    pallas_call x1, Pallas kernels: 5.53 us -> 12.8 us  [per_device(): pl.pallas_call(direct_kernel, out_shape=(jax.ShapeDtypeStruct((nslot, 8,...]
    all_to_all x1, starting transfers between devices: 11 us -> 5.72 us  [per_device(): got = lax.all_to_all(send, 'ka', 0, 0, tiled=True)]
  transfers between devices with their start and end apart: 17 -> 17, of which waited for: 10 -> 9; matrix products, arithmetic and copies ran while one was open for 13% -> 12% of each run, Pallas kernels for 7% -> 11%
where the time goes in v13:
time: 196 us; the launch traced here: 194 us
  waiting for transfers between devices  58.3 us (30%)
  blocking collectives  40.3 us (21%)
  starting transfers between devices  29.2 us (15%)
  Pallas kernels  23.2 us (12%)
  between operations  15.9 us (8%)
  other arithmetic  15.6 us (8%)
  local copies, waits for them, and re-layouts  12.1 us (6%)
    all_gather x1, blocking collectives, per_device(): lax.all_gather(pairs, 'ka', axis=0, tiled=True).reshape(n_ka, npair, 3)  25.7 us
    all_to_all x1, waiting for transfers between devices, per_device(): got = lax.all_to_all(send, 'ka', 0, 0, tiled=True)  18.6 us
    ppermute x3, waiting for transfers between devices, per_device(): wk.append(lax.ppermute(v, 'ga', shift(r)) if r else v)  15.2 us
    all_gather x1, blocking collectives, per_device(): full = lax.all_gather(widen(held), 'ga', axis=1, tiled=True)  14.6 us
    all_gather x1, waiting for transfers between devices, per_device(): big = lax.all_gather(payload, 'ka', axis=0, tiled=True)  13.2 us
    pallas_call x1, Pallas kernels, per_device(): pl.pallas_call(direct_kernel, out_shape=(jax.ShapeDtypeStruct((nslot, 8,...  12.8 us
    all_to_all x1, starting transfers between devices, per_device(): got = lax.all_to_all(send, 'ka', 0, 0, tiled=True)  5.72 us
    ppermute x3, starting transfers between devices, per_device(): exch_others = [lax.ppermute(exch, 'ga', shift(r)) for r in range(1, 4)]  5.67 us
  transfers between devices with their start and end apart: 17, of which 9 were waited for; matrix products, arithmetic and copies ran while one was open for 12% of the time, Pallas kernels for 11%

profile of v13, /device:TPU:0, one launch (start us, length us, event | category | flops | bytes accessed | tf_op | source)
XLA Modules:
  0.0 194.5 jit_solution(12217388386619778976)
XLA Ops:
  7.2 2.9 %collective-permute-start.3 = (bf16[4,64,375]{2,1,0:T(8,128)(2,1)}, bf16[4,64,375]{2,1,0:T(8,128)(2,1)S(1)}, u32[]{:S(2)}, u32[]{:S(2)}) collective-permute-start(bf16[4,64,375]{2,1,0:T(8,128)(2,1)} %param.8), channel_id=1, source_target_pairs={{0,3},{1,2},{2,1},{3,0},{4,7},{5,6},{6,5},{7,4},{8,11},{9,10},{10,... | collective-permute-start | bytes 576008 | tf_op jit(solution)/shard_map/pack/ppermute | solution.py:278
  11.4 1.6 collective-permute-start.1
  14.6 3.4 %collective-permute-done.3 = bf16[4,64,375]{2,1,0:T(8,128)(2,1)S(1)} collective-permute-done((bf16[4,64,375]{2,1,0:T(8,128)(2,1)}, bf16[4,64,375]{2,1,0:T(8,128)(2,1)S(1)}, u32[]{:S(2)}, u32[]{:S(2)}) %collective-permute-start.3) | collective-permute-done | bytes 192032 | tf_op jit(solution)/shard_map/pack/ppermute | solution.py:278
  20.7 14.6 %all_gather.14.full = bf16[272,1536]{1,0:T(8,128)(2,1)S(1)} all-gather(bf16[272,384]{1,0:T(8,128)(2,1)S(1)} %fusion.33), channel_id=1, replica_groups=mesh['ka'=32,'ga'=4] {'ga'}, dimensions={1}, use_global_device_ids=true | all-gather | bytes 1044480 | tf_op jit(solution)/shard_map/exchange_pack/all_gather | solution.py:310
  38.0 3.6 %fusion.54 = (bf16[2,375,375]{2,0,1:T(2,128)(2,1)S(1)}, bf16[2,375,375]{2,0,1:T(2,128)(2,1)S(1)}, bf16[2,375,375]{2,0,1:T(2,128)(2,1)S(1)}, bf16[2,375,375]{2,0,1:T(2,128)(2,1)S(1)}) fusion(bf16[2,375,1500]{2,0,1:T(2,128)(2,1)S(1)} %copy-done.1), kind=kLoop, calls=%fused_computation.156 | loop fusion | bytes 4500000 | tf_op jit(solution)/shard_map/weights/slice | solution.py:292
  41.9 2.4 %broadcast_select_fusion.3 = (bf16[2,384,768]{2,1,0:T(8,128)(2,1)}, bf16[2,384,768]{2,1,0:T(8,128)(2,1)}, bf16[2,384,768]{2,1,0:T(8,128)(2,1)}) fusion(pred[]{:T(512)S(6)} %or.12, bf16[2,375,375]{2,1,0:T(8,128)(2,1)S(1)} %copy.90, bf16[2,375,375]{2,1,0:T(8,128)(2,1)S(1)} %copy.89, bf16[2,375,375]{2,1,0:T(8,128)(2,1)S(1)} %copy.88, ...), kind=kLoop, calls=%fused_computation.39 | loop fusion | flops 10027008 | bytes 5788947 | tf_op jit(solution)/shard_map/weights/jit(_where)/select_n | solution.py:300
  44.3 2.0 %collective-permute-start.4 = (bf16[2,384,768]{2,1,0:T(8,128)(2,1)}, bf16[2,384,768]{2,1,0:T(8,128)(2,1)}, u32[]{:S(2)}, u32[]{:S(2)}) collective-permute-start(bf16[2,384,768]{2,1,0:T(8,128)(2,1)} %get-tuple-element.26), channel_id=1, source_target_pairs={{0,1},{1,2},{2,3},{3,0},{4,5},{5,6},{6,7},{7,4},{8,9},{9,10},{10,1... | collective-permute-start | bytes 3538952 | tf_op jit(solution)/shard_map/weights/ppermute | solution.py:301
  46.3 2.5 %collective-permute-start.5 = (bf16[2,384,768]{2,1,0:T(8,128)(2,1)}, bf16[2,384,768]{2,1,0:T(8,128)(2,1)}, u32[]{:S(2)}, u32[]{:S(2)}) collective-permute-start(bf16[2,384,768]{2,1,0:T(8,128)(2,1)} %get-tuple-element.27), channel_id=1, source_target_pairs={{0,2},{1,3},{2,0},{3,1},{4,6},{5,7},{6,4},{7,5},{8,10},{9,11},{10,... | collective-permute-start | bytes 3538952 | tf_op jit(solution)/shard_map/weights/ppermute | solution.py:301
  50.3 25.7 %all-gather = s32[32,16,3]{1,2,0:T(4,128)S(1)} all-gather(s32[1,16,3]{1,2,0:T(4,128)S(1)} %bitcast.49), channel_id=1, replica_groups=mesh['ka'=32,'ga'=4] {'ka'}, dimensions={0}, use_global_device_ids=true | all-gather | bytes 6336 | tf_op jit(solution)/shard_map/tables/all_gather | solution.py:321
  81.9 14.7 %collective-permute-done.4 = bf16[2,384,768]{2,1,0:T(8,128)(2,1)} collective-permute-done((bf16[2,384,768]{2,1,0:T(8,128)(2,1)}, bf16[2,384,768]{2,1,0:T(8,128)(2,1)}, u32[]{:S(2)}, u32[]{:S(2)}) %collective-permute-start.4) | collective-permute-done | bytes 1179680 | tf_op jit(solution)/shard_map/weights/ppermute | solution.py:301
  97.1 5.1 %pad_maximum_fusion.w = bf16[2,1536,768]{2,1,0:T(8,128)(2,1)} fusion(bf16[2,384,768]{2,1,0:T(8,128)(2,1)S(1)} %collective-permute-done.6, bf16[2,384,768]{2,1,0:T(8,128)(2,1)} %collective-permute-done.5, bf16[2,384,768]{2,1,0:T(8,128)(2,1)} %collective-permute-done.4, bf16[2,384,768]{2,1,0:T(8,128)(2,1)} %get-tuple-element.25), kind=kLoop, calls=%fused_computation | loop fusion | flops 18874368 | bytes 9437184 | tf_op jit(solution)/shard_map/weights/concatenate | solution.py:302
  102.1 13.2 %all-gather.4.cloned.1.call-done.big = bf16[128,128,768]{2,1,0:T(8,128)(2,1)} async-done(((bf16[4,128,768]{2,1,0:T(8,128)(2,1)}), bf16[128,128,768]{2,1,0:T(8,128)(2,1)}) %all-gather.4.cloned.1.call-update) | async-done | bytes 25165840 | tf_op jit(solution)/shard_map/spread/all_gather | solution.py:288
  115.3 2.3 %copy-done = bf16[2,1536,768]{2,1,0:T(8,128)(2,1)S(1)} copy-done((bf16[2,1536,768]{2,1,0:T(8,128)(2,1)S(1)}, bf16[2,1536,768]{2,1,0:T(8,128)(2,1)}, u32[]{:S(2)}) %copy-start) | copy-done | bytes 4718616
  117.7 12.8 %direct.1 = (f32[64,8,128]{2,1,0:T(8,128)S(1)}, f32[64,8,128]{2,1,0:T(8,128)S(1)}) custom-call(s32[4,80]{1,0:T(4,128)S(1)} %pad_add_fusion.1.plan, bf16[128,128,768]{2,1,0:T(8,128)(2,1)} %all-gather.4.cloned.1.call-done.big, bf16[2,1536,768]{2,1,0:T(8,128)(2,1)S(1)} %copy-done), custom_call_target="tpu_custom_call" | custom-call | tf_op jit(solution)/shard_map/direct/pallas_call | solution.py:382
  133.2 3.7 %collective-permute-done.7.came = f32[64,8,128]{2,1,0:T(8,128)S(1)} collective-permute-done((f32[64,8,128]{2,1,0:T(8,128)S(1)}, f32[64,8,128]{2,1,0:T(8,128)S(1)}, u32[]{:S(2)}, u32[]{:S(2)}) %collective-permute-start.7) | collective-permute-done | bytes 262176 | tf_op jit(solution)/shard_map/to_neighbour/ppermute | solution.py:401
  136.9 2.8 %route.1 = f32[32,6,8,128]{3,2,1,0:T(8,128)} custom-call(s32[7,64]{1,0:T(8,128)S(1)} %stack.83.tab, f32[64,8,128]{2,1,0:T(8,128)S(1)} %get-tuple-element.4.keep, f32[64,8,128]{2,1,0:T(8,128)S(1)} %collective-permute-done.7.came), custom_call_target="tpu_custom_call" | custom-call | tf_op jit(solution)/shard_map/route/pallas_call | solution.py:402
  139.7 5.7 %all-to-all-start = ((f32[32,6,8,128]{3,2,1,0:T(8,128)}), f32[32,6,8,128]{3,2,1,0:T(8,128)S(1)}, u32[]{:S(2)}, u32[]{:S(2)}) async-start(f32[32,6,8,128]{3,2,1,0:T(8,128)} %route.1), calls=%async_computation | async-start | bytes 1572864 | tf_op jit(solution)/shard_map/to_holders/all_to_all | solution.py:416
  146.8 18.6 %all-to-all-done.got = f32[32,6,8,128]{3,2,1,0:T(8,128)S(1)} async-done(((f32[32,6,8,128]{3,2,1,0:T(8,128)}), f32[32,6,8,128]{3,2,1,0:T(8,128)S(1)}, u32[]{:S(2)}, u32[]{:S(2)}) %all-to-all-start) | async-done | bytes 786464 | tf_op jit(solution)/shard_map/to_holders/all_to_all | solution.py:416
  166.1 2.7 %collective-permute-start.10 = (f32[20,8,128]{2,1,0:T(8,128)S(1)}, f32[20,8,128]{2,1,0:T(8,128)S(1)}, u32[]{:S(2)}, u32[]{:S(2)}) collective-permute-start(f32[20,8,128]{2,1,0:T(8,128)S(1)} %collect.1.r0), channel_id=1, source_target_pairs={{0,3},{1,0},{2,1},{3,2},{4,7},{5,4},{6,5},{7,6},{8,11},{9,8},{10,9... | collective-permute-start | bytes 245768 | tf_op jit(solution)/shard_map/direct_copies/ppermute | solution.py:428
  169.0 2.3 %collective-permute-start.9 = (f32[20,8,128]{2,1,0:T(8,128)S(1)}, f32[20,8,128]{2,1,0:T(8,128)S(1)}, u32[]{:S(2)}, u32[]{:S(2)}) collective-permute-start(f32[20,8,128]{2,1,0:T(8,128)S(1)} %collect.1.r0), channel_id=1, source_target_pairs={{0,2},{1,3},{2,0},{3,1},{4,6},{5,7},{6,4},{7,5},{8,10},{9,11},{10,... | collective-permute-start | bytes 245768 | tf_op jit(solution)/shard_map/direct_copies/ppermute | solution.py:428
  171.3 2.0 %all-gather.6.cloned.1.call-done.big = bf16[128,16,1536]{2,1,0:T(8,128)(2,1)} async-done(((bf16[4,16,1536]{2,1,0:T(8,128)(2,1)}), bf16[128,16,1536]{2,1,0:T(8,128)(2,1)}) %all-gather.6.cloned.1.call-update) | async-done | bytes 6291472 | tf_op jit(solution)/shard_map/exchange_pack/all_gather | solution.py:313
  173.3 3.7 %exchange.1.r0 = f32[20,8,128]{2,1,0:T(8,128)S(1)} custom-call(s32[3,64]{1,0:T(4,128)S(1)} %add_add_fusion.firsts, s32[4,16]{1,0:T(4,128)S(1)} %pad_add_fusion.own, bf16[128,16,1536]{2,1,0:T(8,128)(2,1)} %all-gather.6.cloned.1.call-done.big, f32[20,8,128]{2,1,0:T(8,128)S(1)} %collective-permute-done.10.r3.early, bf16[272,1536]{1,0:T(8,128)(2,1)S(1)} %all_gather.14.full, ...), custom_call_target="tpu_custom_call" | custom-call | tf_op jit(solution)/shard_map/exchange/pallas_call | solution.py:439
  178.5 2.7 %collective-permute-start.12 = (f32[20,8,128]{2,1,0:T(8,128)S(1)}, f32[20,8,128]{2,1,0:T(8,128)S(1)}, u32[]{:S(2)}, u32[]{:S(2)}) collective-permute-start(f32[20,8,128]{2,1,0:T(8,128)S(1)} %exchange.1.r0), channel_id=1, source_target_pairs={{0,2},{1,3},{2,0},{3,1},{4,6},{5,7},{6,4},{7,5},{8,10},{9,11},{10,... | collective-permute-start | bytes 245768 | tf_op jit(solution)/shard_map/exchange_copies/ppermute | solution.py:457
  185.7 1.9 finish.1
  (111 shorter events, 25.7 us)
Async XLA Ops:
  7.2 108.2 %all-gather.4.cloned.1.call-start = ((), (), s32[]{:S(2)}) async-start(), calls=%async_computation.1 | async-start | bytes 25952256 | tf_op jit(solution)/shard_map/spread/all_gather | solution.py:288
  7.2 10.8 %collective-permute-start.3 = (bf16[4,64,375]{2,1,0:T(8,128)(2,1)}, bf16[4,64,375]{2,1,0:T(8,128)(2,1)S(1)}, u32[]{:S(2)}, u32[]{:S(2)}) collective-permute-start(bf16[4,64,375]{2,1,0:T(8,128)(2,1)} %param.8), channel_id=1, source_target_pairs={{0,3},{1,2},{2,1},{3,0},{4,7},{5,6},{6,5},{7,4},{8,11},{9,10},{10,... | collective-permute-start | bytes 576008 | tf_op jit(solution)/shard_map/pack/ppermute | solution.py:278
  11.1 8.3 %collective-permute-start = (bf16[4,32,375]{2,1,0:T(8,128)(2,1)S(1)}, bf16[4,32,375]{2,1,0:T(8,128)(2,1)S(1)}, u32[]{:S(2)}, u32[]{:S(2)}) collective-permute-start(bf16[4,32,375]{2,1,0:T(8,128)(2,1)S(1)} %get-tuple-element.39), channel_id=1, source_target_pairs={{0,1},{1,2},{2,3},{3,0},{4,5},{5,6},{6,7},{7,4},{8,9},{9,10},{10,1... | collective-permute-start | bytes 288008 | tf_op jit(solution)/shard_map/pack/ppermute | solution.py:280
  11.4 8.1 %collective-permute-start.1 = (bf16[4,32,375]{2,1,0:T(8,128)(2,1)S(1)}, bf16[4,32,375]{2,1,0:T(8,128)(2,1)S(1)}, u32[]{:S(2)}, u32[]{:S(2)}) collective-permute-start(bf16[4,32,375]{2,1,0:T(8,128)(2,1)S(1)} %get-tuple-element.37), channel_id=1, source_target_pairs={{0,2},{1,3},{2,0},{3,1},{4,6},{5,7},{6,4},{7,5},{8,10},{9,11},{10,... | collective-permute-start | bytes 288008 | tf_op jit(solution)/shard_map/pack/ppermute | solution.py:280
  13.0 6.4 %collective-permute-start.2 = (bf16[4,32,375]{2,1,0:T(8,128)(2,1)S(1)}, bf16[4,32,375]{2,1,0:T(8,128)(2,1)S(1)}, u32[]{:S(2)}, u32[]{:S(2)}) collective-permute-start(bf16[4,32,375]{2,1,0:T(8,128)(2,1)S(1)} %get-tuple-element.38), channel_id=1, source_target_pairs={{0,3},{1,0},{2,1},{3,2},{4,7},{5,4},{6,5},{7,6},{8,11},{9,8},{10,9... | collective-permute-start | bytes 288008 | tf_op jit(solution)/shard_map/pack/ppermute | solution.py:280
  14.6 5.9 %copy-start.4 = (f32[375]{0:T(512)S(1)}, f32[375]{0:T(512)}, u32[]{:S(2)}) copy-start(f32[375]{0:T(512)} %param.10) | copy-start | bytes 4504
  14.6 6.0 %copy-start.2 = (bf16[4,64,375]{2,1,0:T(8,128)(2,1)S(1)}, bf16[4,64,375]{2,1,0:T(8,128)(2,1)}, u32[]{:S(2)}) copy-start(bf16[4,64,375]{2,1,0:T(8,128)(2,1)} %param.9) | copy-start | bytes 576004
  20.5 152.8 %all-gather.6.cloned.1.call-start = ((), (), s32[]{:S(2)}) async-start(), calls=%async_computation.2 | async-start | bytes 6488064 | tf_op jit(solution)/shard_map/exchange_pack/all_gather | solution.py:313
  20.7 17.3 %copy-start.1 = (bf16[2,375,1500]{2,0,1:T(2,128)(2,1)S(1)}, bf16[2,375,1500]{2,0,1:T(2,128)(2,1)}, u32[]{:S(2)}) copy-start(bf16[2,375,1500]{2,0,1:T(2,128)(2,1)} %param.11) | copy-start | bytes 6750004
  44.3 52.3 %collective-permute-start.4 = (bf16[2,384,768]{2,1,0:T(8,128)(2,1)}, bf16[2,384,768]{2,1,0:T(8,128)(2,1)}, u32[]{:S(2)}, u32[]{:S(2)}) collective-permute-start(bf16[2,384,768]{2,1,0:T(8,128)(2,1)} %get-tuple-element.26), channel_id=1, source_target_pairs={{0,1},{1,2},{2,3},{3,0},{4,5},{5,6},{6,7},{7,4},{8,9},{9,10},{10,1... | collective-permute-start | bytes 3538952 | tf_op jit(solution)/shard_map/weights/ppermute | solution.py:301
  46.3 50.3 %collective-permute-start.5 = (bf16[2,384,768]{2,1,0:T(8,128)(2,1)}, bf16[2,384,768]{2,1,0:T(8,128)(2,1)}, u32[]{:S(2)}, u32[]{:S(2)}) collective-permute-start(bf16[2,384,768]{2,1,0:T(8,128)(2,1)} %get-tuple-element.27), channel_id=1, source_target_pairs={{0,2},{1,3},{2,0},{3,1},{4,6},{5,7},{6,4},{7,5},{8,10},{9,11},{10,... | collective-permute-start | bytes 3538952 | tf_op jit(solution)/shard_map/weights/ppermute | solution.py:301
  48.7 1.6 copy-start.3
  48.7 27.4 %copy-start.5 = (s32[64]{0:T(128)S(1)}, s32[64]{0:T(128)}, u32[]{:S(2)}) copy-start(s32[64]{0:T(128)} %param.13) | copy-start | bytes 772
  50.1 46.9 %collective-permute-start.6 = (bf16[2,384,768]{2,1,0:T(8,128)(2,1)}, bf16[2,384,768]{2,1,0:T(8,128)(2,1)S(1)}, u32[]{:S(2)}, u32[]{:S(2)}) collective-permute-start(bf16[2,384,768]{2,1,0:T(8,128)(2,1)} %broadcast_select_fusion), channel_id=1, source_target_pairs={{0,3},{1,0},{2,1},{3,2},{4,7},{5,4},{6,5},{7,6},{8,11},{9,8},{10,9... | collective-permute-start | bytes 3538952 | tf_op jit(solution)/shard_map/weights/ppermute | solution.py:301
  115.3 2.3 %copy-start = (bf16[2,1536,768]{2,1,0:T(8,128)(2,1)S(1)}, bf16[2,1536,768]{2,1,0:T(8,128)(2,1)}, u32[]{:S(2)}) copy-start(bf16[2,1536,768]{2,1,0:T(8,128)(2,1)} %pad_maximum_fusion.w) | copy-start | bytes 14155780
  130.5 6.5 %collective-permute-start.7 = (f32[64,8,128]{2,1,0:T(8,128)S(1)}, f32[64,8,128]{2,1,0:T(8,128)S(1)}, u32[]{:S(2)}, u32[]{:S(2)}) collective-permute-start(f32[64,8,128]{2,1,0:T(8,128)S(1)} %get-tuple-element.5), channel_id=1, source_target_pairs={{0,1},{1,0},{2,3},{3,2},{4,5},{5,4},{6,7},{7,6},{8,9},{9,8},{10,11... | collective-permute-start | bytes 786440 | tf_op jit(solution)/shard_map/to_neighbour/ppermute | solution.py:401
  139.7 25.7 %all-to-all-start = ((f32[32,6,8,128]{3,2,1,0:T(8,128)}), f32[32,6,8,128]{3,2,1,0:T(8,128)S(1)}, u32[]{:S(2)}, u32[]{:S(2)}) async-start(f32[32,6,8,128]{3,2,1,0:T(8,128)} %route.1), calls=%async_computation | async-start | bytes 1572864 | tf_op jit(solution)/shard_map/to_holders/all_to_all | solution.py:416
  166.1 7.2 %collective-permute-start.10 = (f32[20,8,128]{2,1,0:T(8,128)S(1)}, f32[20,8,128]{2,1,0:T(8,128)S(1)}, u32[]{:S(2)}, u32[]{:S(2)}) collective-permute-start(f32[20,8,128]{2,1,0:T(8,128)S(1)} %collect.1.r0), channel_id=1, source_target_pairs={{0,3},{1,0},{2,1},{3,2},{4,7},{5,4},{6,5},{7,6},{8,11},{9,8},{10,9... | collective-permute-start | bytes 245768 | tf_op jit(solution)/shard_map/direct_copies/ppermute | solution.py:428
  168.9 13.9 %collective-permute-start.8 = (f32[20,8,128]{2,1,0:T(8,128)S(1)}, f32[20,8,128]{2,1,0:T(8,128)S(1)}, u32[]{:S(2)}, u32[]{:S(2)}) collective-permute-start(f32[20,8,128]{2,1,0:T(8,128)S(1)} %collect.1.r0), channel_id=1, source_target_pairs={{0,1},{1,2},{2,3},{3,0},{4,5},{5,6},{6,7},{7,4},{8,9},{9,10},{10,1... | collective-permute-start | bytes 245768 | tf_op jit(solution)/shard_map/direct_copies/ppermute | solution.py:428
  169.0 13.8 %collective-permute-start.9 = (f32[20,8,128]{2,1,0:T(8,128)S(1)}, f32[20,8,128]{2,1,0:T(8,128)S(1)}, u32[]{:S(2)}, u32[]{:S(2)}) collective-permute-start(f32[20,8,128]{2,1,0:T(8,128)S(1)} %collect.1.r0), channel_id=1, source_target_pairs={{0,2},{1,3},{2,0},{3,1},{4,6},{5,7},{6,4},{7,5},{8,10},{9,11},{10,... | collective-permute-start | bytes 245768 | tf_op jit(solution)/shard_map/direct_copies/ppermute | solution.py:428
  177.0 7.1 %collective-permute-start.11 = (f32[20,8,128]{2,1,0:T(8,128)S(1)}, f32[20,8,128]{2,1,0:T(8,128)S(1)}, u32[]{:S(2)}, u32[]{:S(2)}) collective-permute-start(f32[20,8,128]{2,1,0:T(8,128)S(1)} %exchange.1.r0), channel_id=1, source_target_pairs={{0,1},{1,2},{2,3},{3,0},{4,5},{5,6},{6,7},{7,4},{8,9},{9,10},{10,1... | collective-permute-start | bytes 245768 | tf_op jit(solution)/shard_map/exchange_copies/ppermute | solution.py:457
  178.5 7.2 %collective-permute-start.12 = (f32[20,8,128]{2,1,0:T(8,128)S(1)}, f32[20,8,128]{2,1,0:T(8,128)S(1)}, u32[]{:S(2)}, u32[]{:S(2)}) collective-permute-start(f32[20,8,128]{2,1,0:T(8,128)S(1)} %exchange.1.r0), channel_id=1, source_target_pairs={{0,2},{1,3},{2,0},{3,1},{4,6},{5,7},{6,4},{7,5},{8,10},{9,11},{10,... | collective-permute-start | bytes 245768 | tf_op jit(solution)/shard_map/exchange_copies/ppermute | solution.py:457
  181.2 4.5 %collective-permute-start.13 = (f32[20,8,128]{2,1,0:T(8,128)S(1)}, f32[20,8,128]{2,1,0:T(8,128)S(1)}, u32[]{:S(2)}, u32[]{:S(2)}) collective-permute-start(f32[20,8,128]{2,1,0:T(8,128)S(1)} %exchange.1.r0), channel_id=1, source_target_pairs={{0,3},{1,0},{2,1},{3,2},{4,7},{5,4},{6,5},{7,6},{8,11},{9,8},{10,9... | collective-permute-start | bytes 245768 | tf_op jit(solution)/shard_map/exchange_copies/ppermute | solution.py:457
Sparse Core Ops, SparseCore 0:
  20.6 94.6 all-gather.3
  118.2 55.0 all-gather.5
